TPU v7x, 32 devices: a whole 2x2x4 slice. The times are simulated.
32 devices in a mesh: rep: 16 (over z, y, core), fsdp: 2 (over x).
Axes of the slice: x: 2, y: 2, z: 4, core: 2. Of those that a mesh axis runs over, the one named last changes fastest.
Arguments:
- tokens: bfloat16 [256, 197, 384], P(('rep', 'fsdp')), may hold values from -6 to 6
- gain_one: bfloat16 [384], P('fsdp'), may hold values from 0.25 to 1.75
- shift_one: bfloat16 [384], P('fsdp'), may hold values from -1.75 to 1.75
- qkv_weight: bfloat16 [384, 1152], P('fsdp'), may hold values from -0.3125 to 0.3125
- query_bias: bfloat16 [384], P('fsdp'), may hold values from -3 to 3
- value_bias: bfloat16 [384], P('fsdp'), may hold values from -3 to 3
- out_weight: bfloat16 [384, 384], P('fsdp'), may hold values from -1.25 to 1.25
- out_bias: bfloat16 [384], P('fsdp'), may hold values from -1.75 to 1.75
- gain_two: bfloat16 [384], P('fsdp'), may hold values from 0.25 to 1.75
- shift_two: bfloat16 [384], P('fsdp'), may hold values from -1.75 to 1.75
- lift_weight: bfloat16 [384, 1536], P('fsdp'), may hold values from -0.3125 to 0.3125
- lift_bias: bfloat16 [1536], P('fsdp'), may hold values from -3 to 3
- drop_weight: bfloat16 [1536, 384], P('fsdp'), may hold values from -0.15625 to 0.15625
- drop_bias: bfloat16 [384], P('fsdp'), may hold values from -1.75 to 1.75
- cotangent: bfloat16 [256, 197, 384], P(('rep', 'fsdp')), may hold values from -12 to 12
Outputs:
- output: bfloat16 [256, 197, 384], P(('rep', 'fsdp'))
- input_grad: bfloat16 [256, 197, 384], P(('rep', 'fsdp'))
- grad_gain_one: float32 [384], P('fsdp')
- grad_shift_one: float32 [384], P('fsdp')
- grad_qkv_weight: float32 [384, 1152], P('fsdp')
- grad_query_bias: float32 [384], P('fsdp')
- grad_value_bias: float32 [384], P('fsdp')
- grad_out_weight: float32 [384, 384], P('fsdp')
- grad_out_bias: float32 [384], P('fsdp')
- grad_gain_two: float32 [384], P('fsdp')
- grad_shift_two: float32 [384], P('fsdp')
- grad_lift_weight: float32 [384, 1536], P('fsdp')
- grad_lift_bias: float32 [1536], P('fsdp')
- grad_drop_weight: float32 [1536, 384], P('fsdp')
- grad_drop_bias: float32 [384], P('fsdp')
All inputs are finite; a program needn't handle non-finite values.
Results may differ from a plain program's by a relative error of at most 0.023.
Values may be sent and summed in bfloat16 or wider, within the bound.
No kernel may reach another device: no remote copies, remote signals or barrier semaphores. Data moves between devices by JAX's collectives and lax.ppermute only.
A program may use at most 128 MiB of HBM per device.

v0:
```python
import jax
import jax.numpy as jnp
from jax import lax
from jax.sharding import PartitionSpec as P

HEADS = 6
HEAD_DIM = 64


epsilon = 1e-06
root_half = 0.7071067811865476
gauss_norm = 0.3989422804014327


def norm_forward(inputs, gain_vec, shift_vec):
    average = jnp.mean(inputs, axis=-1, keepdims=True)
    centred = inputs - average
    variance = jnp.mean(centred * centred, axis=-1, keepdims=True)
    inverse = lax.rsqrt(variance + epsilon)
    normal = centred * inverse
    return (normal * gain_vec + shift_vec, normal, inverse)


def norm_backward(grad_out, normal, inverse, gain_vec):
    grad_gain = jnp.sum(grad_out * normal, axis=0)
    grad_shift = jnp.sum(grad_out, axis=0)
    scaled = grad_out * gain_vec
    grad_in = inverse * (
        scaled
        - jnp.mean(scaled, axis=-1, keepdims=True)
        - normal * jnp.mean(scaled * normal, axis=-1, keepdims=True)
    )
    return (grad_in, grad_gain, grad_shift)


def product(left, right):
    return jnp.dot(left, right, preferred_element_type=jnp.float32)


def product_left(left, right):
    return lax.dot_general(
        left, right, (((0,), (0,)), ((), ())), preferred_element_type=jnp.float32
    )


def product_right(left, right):
    return lax.dot_general(
        left, right, (((1,), (1,)), ((), ())), preferred_element_type=jnp.float32
    )


def raw_scores(query_part, key_part):
    scale_factor = query_part.shape[-1] ** (-0.5)
    return (
        jnp.einsum("iqhe,ikhe->ihqk", query_part, key_part, preferred_element_type=jnp.float32)
        * scale_factor
    )


def per_device(
    tokens,
    gain_one,
    shift_one,
    qkv_weight,
    query_bias,
    value_bias,
    out_weight,
    out_bias,
    gain_two,
    shift_two,
    lift_weight,
    lift_bias,
    drop_weight,
    drop_bias,
    cotangent,
):
    gathered = (
        lax.all_gather(gain_one, "fsdp", axis=0, tiled=True),
        lax.all_gather(shift_one, "fsdp", axis=0, tiled=True),
        lax.all_gather(qkv_weight, "fsdp", axis=0, tiled=True),
        lax.all_gather(query_bias, "fsdp", axis=0, tiled=True),
        lax.all_gather(value_bias, "fsdp", axis=0, tiled=True),
        lax.all_gather(out_weight, "fsdp", axis=0, tiled=True),
        lax.all_gather(out_bias, "fsdp", axis=0, tiled=True),
        lax.all_gather(gain_two, "fsdp", axis=0, tiled=True),
        lax.all_gather(shift_two, "fsdp", axis=0, tiled=True),
        lax.all_gather(lift_weight, "fsdp", axis=0, tiled=True),
        lax.all_gather(lift_bias, "fsdp", axis=0, tiled=True),
        lax.all_gather(drop_weight, "fsdp", axis=0, tiled=True),
        lax.all_gather(drop_bias, "fsdp", axis=0, tiled=True),
    )
    (
        full_gain_one,
        full_shift_one,
        full_qkv,
        full_query_bias,
        full_value_bias,
        full_out,
        full_out_bias,
        full_gain_two,
        full_shift_two,
        full_lift,
        full_lift_bias,
        full_drop,
        full_drop_bias,
    ) = gathered
    images, length, width = tokens.shape
    tok_rows = images * length
    scale_factor = HEAD_DIM ** (-0.5)
    flat_in = tokens.astype(jnp.float32).reshape(tok_rows, width)
    normed_f, normal_one, inverse_one = norm_forward(
        flat_in, full_gain_one.astype(jnp.float32), full_shift_one.astype(jnp.float32)
    )
    normed = normed_f.astype(jnp.bfloat16)
    qkv_bias = jnp.concatenate(
        [full_query_bias, jnp.zeros_like(full_query_bias), full_value_bias]
    ).astype(jnp.float32)
    projected = (product(normed, full_qkv) + qkv_bias).astype(jnp.bfloat16)
    split_heads = projected.reshape(images, length, 3, HEADS, HEAD_DIM)
    query_part = split_heads[:, :, 0]
    key_part = split_heads[:, :, 1]
    value_part = split_heads[:, :, 2]
    scores = raw_scores(query_part, key_part)
    top_score = jnp.max(scores, axis=-1, keepdims=True)
    log_total = top_score + jnp.log(jnp.sum(jnp.exp(scores - top_score), axis=-1, keepdims=True))
    soft_weights = jnp.exp(scores - log_total).astype(jnp.bfloat16)
    mixed = (
        jnp.einsum("ihqk,ikhe->iqhe", soft_weights, value_part, preferred_element_type=jnp.float32)
        .reshape(tok_rows, width)
        .astype(jnp.bfloat16)
    )
    middle = flat_in + product(mixed, full_out) + full_out_bias.astype(jnp.float32)
    normed_two_f, normal_two, inverse_two = norm_forward(
        middle, full_gain_two.astype(jnp.float32), full_shift_two.astype(jnp.float32)
    )
    normed_two = normed_two_f.astype(jnp.bfloat16)
    hidden = product(normed_two, full_lift) + full_lift_bias.astype(jnp.float32)
    active = jax.nn.gelu(hidden, approximate=False).astype(jnp.bfloat16)
    result = middle + product(active, full_drop) + full_drop_bias.astype(jnp.float32)
    output = result.astype(jnp.bfloat16).reshape(tokens.shape)
    back_gain_one, back_qkv, back_out, back_gain_two, back_lift, back_drop = (
        lax.all_gather(gain_one, "fsdp", axis=0, tiled=True),
        lax.all_gather(qkv_weight, "fsdp", axis=0, tiled=True),
        lax.all_gather(out_weight, "fsdp", axis=0, tiled=True),
        lax.all_gather(gain_two, "fsdp", axis=0, tiled=True),
        lax.all_gather(lift_weight, "fsdp", axis=0, tiled=True),
        lax.all_gather(drop_weight, "fsdp", axis=0, tiled=True),
    )
    grad_flat = cotangent.reshape(tok_rows, width)
    grad_outer = grad_flat.astype(jnp.float32)
    grad_drop_weight = product_left(active, grad_flat)
    grad_drop_bias = jnp.sum(grad_outer, axis=0)
    d_active = product_right(grad_flat, back_drop)
    slope = (
        0.5 * (1.0 + lax.erf(hidden * root_half))
        + hidden * jnp.exp(-0.5 * hidden * hidden) * gauss_norm
    )
    d_hidden = (d_active * slope).astype(jnp.bfloat16)
    grad_lift_weight = product_left(normed_two, d_hidden)
    grad_lift_bias = jnp.sum(d_hidden.astype(jnp.float32), axis=0)
    d_normed_two = product_right(d_hidden, back_lift)
    d_from_norm, grad_gain_two, grad_shift_two = norm_backward(
        d_normed_two, normal_two, inverse_two, back_gain_two.astype(jnp.float32)
    )
    d_middle = grad_outer + d_from_norm
    d_attended = d_middle.astype(jnp.bfloat16)
    grad_out_weight = product_left(mixed, d_attended)
    grad_out_bias = jnp.sum(d_attended.astype(jnp.float32), axis=0)
    d_mixed = (
        product_right(d_attended, back_out)
        .astype(jnp.bfloat16)
        .reshape(images, length, HEADS, HEAD_DIM)
    )
    again_probs = jnp.exp(raw_scores(query_part, key_part) - log_total)
    again_soft = again_probs.astype(jnp.bfloat16)
    d_value = jnp.einsum("ihqk,iqhe->ikhe", again_soft, d_mixed, preferred_element_type=jnp.float32)
    d_probs = jnp.einsum("iqhe,ikhe->ihqk", d_mixed, value_part, preferred_element_type=jnp.float32)
    row_delta = jnp.sum(again_probs * d_probs, axis=-1, keepdims=True)
    d_scores = (again_probs * (d_probs - row_delta)).astype(jnp.bfloat16)
    d_query = (
        jnp.einsum("ihqk,ikhe->iqhe", d_scores, key_part, preferred_element_type=jnp.float32)
        * scale_factor
    )
    d_key = (
        jnp.einsum("ihqk,iqhe->ikhe", d_scores, query_part, preferred_element_type=jnp.float32)
        * scale_factor
    )
    d_projected = (
        jnp.stack([d_query, d_key, d_value], axis=2)
        .reshape(tok_rows, 3 * width)
        .astype(jnp.bfloat16)
    )
    grad_qkv_weight = product_left(normed, d_projected)
    column_sums = jnp.sum(d_projected.astype(jnp.float32), axis=0)
    grad_query_bias = column_sums[:width]
    grad_value_bias = column_sums[2 * width :]
    d_normed = product_right(d_projected, back_qkv)
    d_first, grad_gain_one, grad_shift_one = norm_backward(
        d_normed, normal_one, inverse_one, back_gain_one.astype(jnp.float32)
    )
    input_grad = (d_middle + d_first).astype(jnp.bfloat16).reshape(tokens.shape)
    owned = (
        lax.psum_scatter(
            grad_gain_one.astype(jnp.bfloat16), "fsdp", scatter_dimension=0, tiled=True
        ).astype(jnp.float32),
        lax.psum_scatter(
            grad_shift_one.astype(jnp.bfloat16), "fsdp", scatter_dimension=0, tiled=True
        ).astype(jnp.float32),
        lax.psum_scatter(
            grad_qkv_weight.astype(jnp.bfloat16), "fsdp", scatter_dimension=0, tiled=True
        ).astype(jnp.float32),
        lax.psum_scatter(
            grad_query_bias.astype(jnp.bfloat16), "fsdp", scatter_dimension=0, tiled=True
        ).astype(jnp.float32),
        lax.psum_scatter(
            grad_value_bias.astype(jnp.bfloat16), "fsdp", scatter_dimension=0, tiled=True
        ).astype(jnp.float32),
        lax.psum_scatter(
            grad_out_weight.astype(jnp.bfloat16), "fsdp", scatter_dimension=0, tiled=True
        ).astype(jnp.float32),
        lax.psum_scatter(
            grad_out_bias.astype(jnp.bfloat16), "fsdp", scatter_dimension=0, tiled=True
        ).astype(jnp.float32),
        lax.psum_scatter(
            grad_gain_two.astype(jnp.bfloat16), "fsdp", scatter_dimension=0, tiled=True
        ).astype(jnp.float32),
        lax.psum_scatter(
            grad_shift_two.astype(jnp.bfloat16), "fsdp", scatter_dimension=0, tiled=True
        ).astype(jnp.float32),
        lax.psum_scatter(
            grad_lift_weight.astype(jnp.bfloat16), "fsdp", scatter_dimension=0, tiled=True
        ).astype(jnp.float32),
        lax.psum_scatter(
            grad_lift_bias.astype(jnp.bfloat16), "fsdp", scatter_dimension=0, tiled=True
        ).astype(jnp.float32),
        lax.psum_scatter(
            grad_drop_weight.astype(jnp.bfloat16), "fsdp", scatter_dimension=0, tiled=True
        ).astype(jnp.float32),
        lax.psum_scatter(
            grad_drop_bias.astype(jnp.bfloat16), "fsdp", scatter_dimension=0, tiled=True
        ).astype(jnp.float32),
    )
    final = (
        lax.psum(owned[0].astype(jnp.bfloat16), "rep").astype(jnp.float32),
        lax.psum(owned[1].astype(jnp.bfloat16), "rep").astype(jnp.float32),
        lax.psum(owned[2].astype(jnp.bfloat16), "rep").astype(jnp.float32),
        lax.psum(owned[3].astype(jnp.bfloat16), "rep").astype(jnp.float32),
        lax.psum(owned[4].astype(jnp.bfloat16), "rep").astype(jnp.float32),
        lax.psum(owned[5].astype(jnp.bfloat16), "rep").astype(jnp.float32),
        lax.psum(owned[6].astype(jnp.bfloat16), "rep").astype(jnp.float32),
        lax.psum(owned[7].astype(jnp.bfloat16), "rep").astype(jnp.float32),
        lax.psum(owned[8].astype(jnp.bfloat16), "rep").astype(jnp.float32),
        lax.psum(owned[9].astype(jnp.bfloat16), "rep").astype(jnp.float32),
        lax.psum(owned[10].astype(jnp.bfloat16), "rep").astype(jnp.float32),
        lax.psum(owned[11].astype(jnp.bfloat16), "rep").astype(jnp.float32),
        lax.psum(owned[12].astype(jnp.bfloat16), "rep").astype(jnp.float32),
    )
    return (output, input_grad) + tuple(final)


def solution(mesh):
    in_specs = (
        P(("rep", "fsdp"), None, None),
        P("fsdp"),
        P("fsdp"),
        P("fsdp", None),
        P("fsdp"),
        P("fsdp"),
        P("fsdp", None),
        P("fsdp"),
        P("fsdp"),
        P("fsdp"),
        P("fsdp", None),
        P("fsdp"),
        P("fsdp", None),
        P("fsdp"),
        P(("rep", "fsdp"), None, None),
    )
    out_specs = (
        P(("rep", "fsdp"), None, None),
        P(("rep", "fsdp"), None, None),
        P("fsdp"),
        P("fsdp"),
        P("fsdp", None),
        P("fsdp"),
        P("fsdp"),
        P("fsdp", None),
        P("fsdp"),
        P("fsdp"),
        P("fsdp"),
        P("fsdp", None),
        P("fsdp"),
        P("fsdp", None),
        P("fsdp"),
    )
    return jax.shard_map(
        per_device, mesh=mesh, in_specs=in_specs, out_specs=out_specs, check_vma=False
    )
```

profile of v0, /device:TPU:0, one launch (start us, length us, event | category | flops | bytes accessed | tf_op | source)
XLA Modules:
  0.0 416.0 jit_solution(2073940774700629270)
XLA Ops:
  8.0 0.7 all-gather.6.cloned.1.call-update
  8.7 1.6 convert_reduce_fusion
  10.4 1.6 copy.83
  12.3 0.7 multiply_reduce_fusion.7
  16.4 5.9 %all-reduce.20 = (bf16[384]{0:T(512)(128)(2,1)S(1)}, bf16[384]{0:T(512)(128)(2,1)S(1)}, bf16[384]{0:T(512)(128)(2,1)S(1)}, bf16[384]{0:T(512)(128)(2,1)S(1)}, bf...) all-reduce(bf16[384]{0:T(512)(128)(2,1)S(1)} %dynamic-update-slice., ...), channel_id=1, replica_groups=mesh['rep'=16,'fsdp'=2] {'fsdp'}, use_global_device_ids=true, to_apply=%add.3 | all-reduce | flops 2688 | bytes 10752
  22.3 2.0 reshape.179
  24.4 20.0 %all_gather.47 = bf16[384,1152]{1,0:T(8,128)(2,1)S(1)} all-gather(bf16[192,1152]{1,0:T(8,128)(2,1)S(1)} %copy-done.15), channel_id=1, replica_groups=mesh['rep'=16,'fsdp'=2] {'fsdp'}, dimensions={0}, use_global_device_ids=true | all-gather | bytes 1327104 | tf_op jit(solution)/shard_map/all_gather | solution.py:80
  44.4 0.9 copy-done.13
  45.3 4.2 %fusion.16 = bf16[1576,1152]{1,0:T(8,128)(2,1)} fusion(bf16[384,1152]{1,0:T(8,128)(2,1)S(1)} %all_gather.47, f32[1152]{0:T(1024)S(1)} %maximum_convert_fusion.1, f32[1576,384]{1,0:T(8,128)S(1)} %reshape.179, f32[384]{0:T(512)S(1)} %convert_element_type.206, f32[384]{0:T(512)S(1)} %convert_element_type.205, f32[1576]{0:T(1024)S(1)} %rsqrt.21, f32[1576]{0:T(1024)S(1)} %div.27), kind=kOutput, calls=%fused_computation.34 | convolution fusion | flops 1401000960 | bytes 6956864 | tf_op jit(solution)/shard_map/dot_general | solution.py:37
  49.5 11.7 %reshape.237 = bf16[8,197,3,6,64]{4,3,2,1,0:T(8,128)(2,1)} reshape(bf16[1576,1152]{1,0:T(8,128)(2,1)} %fusion.16) | data formatting | bytes 7262208 | tf_op jit(solution)/shard_map/reshape | solution.py:119
  61.2 6.7 %fusion.43 = (bf16[8,197,1,6,64]{4,3,2,1,0:T(8,128)(2,1)}, bf16[8,197,1,6,64]{4,3,2,1,0:T(8,128)(2,1)}, bf16[8,197,1,6,64]{4,3,2,1,0:T(8,128)(2,1)}) fusion(bf16[8,197,3,6,64]{4,3,2,1,0:T(8,128)(2,1)} %reshape.237), kind=kLoop, calls=%fused_computation.96 | loop fusion | bytes 7262208 | tf_op jit(solution)/shard_map/slice | solution.py:120
  67.9 3.5 copy.114
  71.4 4.0 copy.115
  75.4 1.5 multiply_reduce_fusion.1
  77.0 2.0 exponential_reduce_fusion
  79.0 1.7 copy-done
  80.8 3.5 copy.113
  84.3 6.3 %fusion.29 = bf16[8,197,6,64]{1,3,2,0:T(8,128)(2,1)S(1)} fusion(bf16[8,197,1,6,64]{1,4,3,0,2:T(8,128)(2,1)S(1)} %copy.113, f32[8,6,197,197]{2,3,1,0:T(8,128)} %copy-done, f32[8,6,197]{2,1,0:T(8,128)S(1)} %log_add_fusion), kind=kOutput, calls=%fused_computation.73 | convolution fusion | flops 244636176 | bytes 9909888 | tf_op jit(solution)/shard_map/ihqk,ikhe->iqhe/dot_general | solution.py:128
  90.6 0.9 copy.92
  91.6 2.6 convert_element_type.213
  94.2 6.2 %all_gather.50 = bf16[384,384]{1,0:T(8,128)(2,1)S(1)} all-gather(bf16[192,384]{1,0:T(8,128)(2,1)S(1)} %copy-done.17), channel_id=1, replica_groups=mesh['rep'=16,'fsdp'=2] {'fsdp'}, dimensions={0}, use_global_device_ids=true | all-gather | bytes 442368 | tf_op jit(solution)/shard_map/all_gather | solution.py:83
  100.4 3.2 fusion.46
  104.3 4.3 %all-gather = bf16[2,1,768]{2,1,0:T(2,128)(2,1)S(1)} all-gather(bf16[1,1,768]{2,1,0:T(2,128)(2,1)S(1)} %reshape.209), channel_id=1, replica_groups=mesh['rep'=16,'fsdp'=2] {'fsdp'}, dimensions={0}, use_global_device_ids=true | all-gather | bytes 4608 | tf_op jit(solution)/shard_map/all_gather | solution.py:88
  108.7 2.5 copy.93
  111.2 2.7 reshape.182
  113.9 1.8 add_convert_fusion
  115.7 1.2 copy.102
  116.9 2.7 convert_element_type.235
  119.6 26.4 %fusion.2 = (bf16[1576,1536]{1,0:T(8,128)(2,1)}, f32[1576,1536]{1,0:T(8,128)}) fusion(f32[1536]{0:T(1024)S(1)} %reshape.211, bf16[384,1536]{1,0:T(8,128)(2,1)} %all-gather.4.cloned.1.call-done, f32[1576,384]{1,0:T(8,128)S(1)} %get-tuple-element.127, f32[384]{0:T(512)S(1)} %convert_element_type.216, f32[384]{0:T(512)S(1)} %convert_element_type.215, ...), kind=kOutput, calls=%fused_computation.9 | convolution fusion | flops 2021919744 | bytes 18146624 | tf_op jit(solution)/shard_map/dot_general | solution.py:37
  146.0 8.6 %fusion.47 = (bf16[1536]{0:T(1024)(128)(2,1)S(1)}, bf16[1576,1536]{1,0:T(8,128)(2,1)S(1)}) fusion(f32[1576,1536]{1,0:T(8,128)} %get-tuple-element.129, bf16[1576,384]{1,0:T(8,128)(2,1)} %reshape.182, bf16[1536,384]{1,0:T(8,128)(2,1)} %all-gather.6.cloned.1.call-done), kind=kOutput, calls=%fused_computation.100 | convolution fusion | flops 1885751808 | bytes 16917504 | tf_op jit(solution)/shard_map/dot_general | solution.py:47
  154.6 3.3 multiply_reduce_fusion.2
  157.9 3.2 convert_reduce_fusion.2
  161.2 1.6 convolution_convert_fusion.5
  162.8 2.1 convolution_convert_fusion.3
  164.9 4.8 %reshape.238 = bf16[8,197,6,64]{3,2,1,0:T(8,128)(2,1)} reshape(bf16[1576,384]{1,0:T(8,128)(2,1)} %convolution_convert_fusion.3) | data formatting | bytes 2420736 | tf_op jit(solution)/shard_map/reshape | solution.py:172
  169.6 4.8 %copy.95 = bf16[8,197,6,64]{1,3,2,0:T(8,128)(2,1)} copy(bf16[8,197,6,64]{3,2,1,0:T(8,128)(2,1)} %reshape.238) | data formatting | bytes 2420736 | tf_op jit(solution)/shard_map/reshape | solution.py:172
  174.4 11.1 %multiply_reduce_fusion = (f32[8,6,197]{2,1,0:T(8,128)S(1)}, f32[8,6,197,197]{2,3,1,0:T(8,128)}) fusion(f32[8,6,197,197]{2,3,1,0:T(8,128)} %copy-done, f32[8,6,197]{2,1,0:T(8,128)S(1)} %log_add_fusion, bf16[8,197,6,64]{1,3,2,0:T(8,128)(2,1)} %copy.95, bf16[8,197,1,6,64]{1,4,3,0,2:T(8,128)(2,1)} %copy-done.7), kind=kOutput, calls=%fused_computation.3 | convolution fusion | flops 245884368 | bytes 17399040 | tf_op jit(solution)/shard_map/iqhe,ikhe->ihqk/dot_general | solution.py:177
  185.5 11.5 %multiply_convert_fusion = bf16[8,6,197,197]{2,3,1,0:T(8,128)(2,1)} fusion(f32[8,6,197,197]{2,3,1,0:T(8,128)} %get-tuple-element.132, f32[8,6,197,197]{2,3,1,0:T(8,128)} %copy-done, f32[8,6,197]{2,1,0:T(8,128)S(1)} %get-tuple-element.131, f32[8,6,197]{2,1,0:T(8,128)S(1)} %log_add_fusion), kind=kLoop, calls=%fused_computation.2 | loop fusion | flops 9314160 | bytes 18703968 | tf_op jit(solution)/shard_map/convert_element_type | solution.py:179
  197.0 5.2 %multiply_bitcast_fusion.1 = bf16[8,197,1,6,64]{1,4,3,0,2:T(8,128)(2,1)} fusion(bf16[8,6,197,197]{2,3,1,0:T(8,128)(2,1)} %multiply_convert_fusion, bf16[8,197,1,6,64]{1,4,3,0,2:T(8,128)(2,1)} %copy-done.1), kind=kOutput, calls=%fused_computation.37 | convolution fusion | flops 239652864 | bytes 6146400 | tf_op jit(solution)/shard_map/ihqk,ikhe->iqhe/dot_general | solution.py:181
  202.2 5.4 %multiply_bitcast_fusion = bf16[8,197,1,6,64]{1,4,3,0,2:T(8,128)(2,1)} fusion(bf16[8,6,197,197]{2,3,1,0:T(8,128)(2,1)} %multiply_convert_fusion, bf16[8,197,1,6,64]{1,4,3,0,2:T(8,128)(2,1)S(1)} %copy-done.10), kind=kOutput, calls=%fused_computation.36 | convolution fusion | flops 239652864 | bytes 6146400 | tf_op jit(solution)/shard_map/ihqk,iqhe->ikhe/dot_general | solution.py:185
  207.6 3.1 convolution_bitcast_fusion
  210.8 3.4 fusion.42
  214.2 5.5 %copy.100 = bf16[8,197,3,6,64]{1,0,4,3,2:T(8,128)(2,1)} copy(bf16[8,197,3,6,64]{1,4,3,0,2:T(8,128)(2,1)S(1)} %get-tuple-element.116) | data formatting | bytes 7262208 | tf_op jit(solution)/shard_map/convert_element_type | solution.py:191
  219.7 8.9 %convert_element_type.228 = bf16[1576,1152]{0,1:T(8,128)(2,1)} reshape(bf16[8,197,3,6,64]{1,0,4,3,2:T(8,128)(2,1)} %copy.100) | data formatting | bytes 7262208 | tf_op jit(solution)/shard_map/convert_element_type | solution.py:191
  228.5 5.3 %convolution_convert_fusion = bf16[384,1152]{1,0:T(8,128)(2,1)} fusion(bf16[1576,384]{1,0:T(8,128)(2,1)} %convert_element_type.235, bf16[1576,1152]{0,1:T(8,128)(2,1)} %convert_element_type.228), kind=kOutput, calls=%fused_computation.42 | convolution fusion | flops 1394786304 | bytes 5726208 | tf_op jit(solution)/shard_map/dot_general | solution.py:41
  234.0 6.6 %convolution_convert_fusion.2 = bf16[384,1536]{1,0:T(8,128)(2,1)} fusion(bf16[1576,1536]{1,0:T(8,128)(2,1)} %copy-done.37, f32[1576,384]{1,0:T(8,128)} %copy-done.2, f32[384]{0:T(512)S(1)} %convert_element_type.216, f32[384]{0:T(512)S(1)} %convert_element_type.215, f32[1576]{0:T(1024)S(1)} %add_rsqrt_fusion, f32[1576]{0:T(1024)S(1)} %broadcast_multiply_fusion.4), kind=kOutput, calls=%fused_computation.45 | convolution fusion | flops 1862740992 | bytes 8457536 | tf_op jit(solution)/shard_map/dot_general | solution.py:41
  240.7 6.8 %convolution_convert_fusion.1 = bf16[1536,384]{1,0:T(8,128)(2,1)} fusion(bf16[1576,1536]{1,0:T(8,128)(2,1)} %get-tuple-element.128, bf16[1576,384]{1,0:T(8,128)(2,1)} %reshape.182), kind=kOutput, calls=%fused_computation.44 | convolution fusion | flops 1859715072 | bytes 7231488 | tf_op jit(solution)/shard_map/dot_general | solution.py:41
  247.6 1.5 reduce_sum.188
  250.9 6.4 %multiply_reduce_fusion.3 = (bf16[384]{0:T(512)(128)(2,1)S(1)}, f32[1576]{0:T(1024)S(1)}, f32[1576]{0:T(1024)S(1)}, bf16[384]{0:T(512)(128)(2,1)S(1)}, f32[1576,384]{1,0:T(8,128)S(1)}) fusion(f32[1576,384]{1,0:T(8,128)} %copy-done.4, f32[1576]{0:T(1024)S(1)} %copy-done.22, f32[1576]{0:T(1024)S(1)} %copy-done.20, f32[384]{0:T(512)S(1)} %copy-done.24, ...), kind=kOutput, calls=%fused_computation.49 | convolution fusion | flops 1399786752 | bytes 9385600 | tf_op jit(solution)/shard_map/dot_general | solution.py:47
  257.4 2.2 add_convert_fusion.1
  259.6 17.5 %reduce-scatter.9.cloned.1.call-done = bf16[192,1536]{1,0:T(8,128)(2,1)} async-done(((bf16[384,1536]{1,0:T(8,128)(2,1)}), bf16[192,1536]{1,0:T(8,128)(2,1)}) %reduce-scatter.9.cloned.1.call-update) | async-done | bytes 589840 | tf_op jit(solution)/shard_map/reduce_scatter | solution.py:230
  277.1 24.6 %reduce-scatter.11.cloned.1.call-done = bf16[768,384]{1,0:T(8,128)(2,1)} async-done(((bf16[1536,384]{1,0:T(8,128)(2,1)}), bf16[768,384]{1,0:T(8,128)(2,1)}) %reduce-scatter.11.cloned.1.call-update) | async-done | bytes 589840 | tf_op jit(solution)/shard_map/reduce_scatter | solution.py:236
  301.8 7.0 %all-reduce.19 = (bf16[384]{0:T(512)(128)(2,1)S(1)}, bf16[384]{0:T(512)(128)(2,1)S(1)}, bf16[384]{0:T(512)(128)(2,1)S(1)}, bf16[384]{0:T(512)(128)(2,1)S(1)}, bf...) all-reduce(bf16[384]{0:T(512)(128)(2,1)S(1)} %dynamic-update-slice., ...), channel_id=1, replica_groups=mesh['rep'=16,'fsdp'=2] {'fsdp'}, use_global_device_ids=true, to_apply=%add.7 | all-reduce | flops 4992 | bytes 19968
  309.5 32.4 %all-reduce.17 = (bf16[192]{0:T(256)(128)(2,1)S(1)}, bf16[192]{0:T(256)(128)(2,1)S(1)}, bf16[192]{0:T(256)(128)(2,1)S(1)}, bf16[192]{0:T(256)(128)(2,1)S(1)}, bf...) all-reduce(bf16[192]{0:T(256)(128)(2,1)S(1)} %dynamic-slice.9, ...), channel_id=1, replica_groups=mesh['rep'=16,'fsdp'=2] {'rep'}, use_global_device_ids=true, to_apply=%region_13.0 | all-reduce | flops 2304 | bytes 9216 | tf_op jit(solution)/shard_map/psum | solution.py:244
  347.0 2.9 reshape.184
  349.9 2.6 copy.104
  352.5 6.1 %fusion.20 = bf16[1576,384]{1,0:T(8,128)(2,1)} fusion(f32[1576,384]{1,0:T(8,128)S(1)} %copy-done.3, bf16[1576,1536]{1,0:T(8,128)(2,1)} %get-tuple-element.128, bf16[1536,384]{1,0:T(8,128)(2,1)S(1)} %copy-done.27, f32[384]{0:T(512)S(1)} %convert_element_type.220), kind=kOutput, calls=%fused_computation.43 | convolution fusion | flops 1860940800 | bytes 9653760 | tf_op jit(solution)/shard_map/dot_general | solution.py:37
  358.6 1.7 reshape.181
  360.2 1.2 copy.103
  361.4 41.4 %all-reduce.23.cloned.1.call-done = (bf16[192,1152]{1,0:T(8,128)(2,1)}, bf16[192,384]{1,0:T(8,128)(2,1)}, bf16[192,1536]{1,0:T(8,128)(2,1)}, bf16[768,384]{1,0:T(8,128)(2,1)}) async-done(((bf16[192,1152]{1,0:T(8,128)(2,1)}, bf16[192,384]{1,0:T(8,128)(2,1)}, bf16[192,1536]{1,0:T(8,128)(2,1)}, bf16[768,384]{1,0:T(8,128)(2,1)}), (bf16[192,1152]{1,0:T(8,128)(2,1)}, bf16[192,384]{1,0:T(8,128)(2,1)}, ...) | async-done | bytes 1769488 | tf_op jit(solution)/shard_map/psum | solution.py:246
  402.8 2.3 convert_element_type.251
  405.1 2.2 convert_element_type.254
  407.2 1.0 convert_element_type.237
  408.2 0.7 convert_element_type.244
  (162 shorter events, 11.2 us)
Async XLA Ops:
  7.2 3.1 copy-start.6
  7.2 112.4 %all-gather.4.cloned.1.call-start = ((), (), s32[]{:S(2)}) async-start(), calls=%async_computation.4 | async-start | bytes 1769472 | tf_op jit(solution)/shard_map/all_gather | solution.py:87
  7.9 138.1 %all-gather.6.cloned.1.call-start = ((), (), s32[]{:S(2)}) async-start(), calls=%async_computation.5 | async-start | bytes 1769472 | tf_op jit(solution)/shard_map/all_gather | solution.py:89
  8.7 250.9 %reduce-scatter.7.cloned.1.call-start = ((), (), s32[]{:S(2)}) async-start(), calls=%async_computation.7 | async-start | bytes 442368 | tf_op jit(solution)/shard_map/reduce_scatter | solution.py:218
  10.3 3.0 copy-start.25
  10.3 4.3 %copy-start.29 = (bf16[192]{0:T(256)(128)(2,1)S(1)}, bf16[192]{0:T(256)(128)(2,1)}, u32[]{:S(2)}) copy-start(bf16[192]{0:T(256)(128)(2,1)} %param.16) | copy-start | bytes 1156
  10.3 4.5 %copy-start.30 = (bf16[192]{0:T(256)(128)(2,1)S(1)}, bf16[192]{0:T(256)(128)(2,1)}, u32[]{:S(2)}) copy-start(bf16[192]{0:T(256)(128)(2,1)} %param.17) | copy-start | bytes 1156
  10.4 4.8 %copy-start.31 = (bf16[192]{0:T(256)(128)(2,1)S(1)}, bf16[192]{0:T(256)(128)(2,1)}, u32[]{:S(2)}) copy-start(bf16[192]{0:T(256)(128)(2,1)} %param.19) | copy-start | bytes 1156
  10.4 5.0 %copy-start.32 = (bf16[192]{0:T(256)(128)(2,1)S(1)}, bf16[192]{0:T(256)(128)(2,1)}, u32[]{:S(2)}) copy-start(bf16[192]{0:T(256)(128)(2,1)} %param.20) | copy-start | bytes 1156
  10.4 5.2 %copy-start.33 = (bf16[192]{0:T(256)(128)(2,1)S(1)}, bf16[192]{0:T(256)(128)(2,1)}, u32[]{:S(2)}) copy-start(bf16[192]{0:T(256)(128)(2,1)} %param.22) | copy-start | bytes 1156
  10.4 5.5 %copy-start.34 = (bf16[192]{0:T(256)(128)(2,1)S(1)}, bf16[192]{0:T(256)(128)(2,1)}, u32[]{:S(2)}) copy-start(bf16[192]{0:T(256)(128)(2,1)} %param.23) | copy-start | bytes 1156
  10.4 5.7 %copy-start.35 = (bf16[192]{0:T(256)(128)(2,1)S(1)}, bf16[192]{0:T(256)(128)(2,1)}, u32[]{:S(2)}) copy-start(bf16[192]{0:T(256)(128)(2,1)} %param.24) | copy-start | bytes 1156
  12.3 32.1 %copy-start.19 = (f32[1576]{0:T(1024)}, f32[1576]{0:T(1024)S(1)}, u32[]{:S(2)}) copy-start(f32[1576]{0:T(1024)S(1)} %div.27) | copy-start | bytes 18916
  13.2 31.2 %copy-start.21 = (f32[1576]{0:T(1024)}, f32[1576]{0:T(1024)S(1)}, u32[]{:S(2)}) copy-start(f32[1576]{0:T(1024)S(1)} %rsqrt.21) | copy-start | bytes 18916
  22.3 91.6 %copy-start.23 = (f32[384]{0:T(512)}, f32[384]{0:T(512)S(1)}, u32[]{:S(2)}) copy-start(f32[384]{0:T(512)S(1)} %convert_element_type.205) | copy-start | bytes 4612
  22.3 2.1 copy-start.15
  24.4 25.1 %copy-start.4 = (f32[1576,384]{1,0:T(8,128)}, f32[1576,384]{1,0:T(8,128)S(1)}, u32[]{:S(2)}) copy-start(f32[1576,384]{1,0:T(8,128)S(1)} %reshape.179) | copy-start | bytes 7262212
  44.4 0.9 copy-start.13
  71.4 5.6 %copy-start.9 = (bf16[8,197,1,6,64]{1,4,3,0,2:T(8,128)(2,1)}, bf16[8,197,1,6,64]{1,4,3,0,2:T(8,128)(2,1)S(1)}, u32[]{:S(2)}) copy-start(bf16[8,197,1,6,64]{1,4,3,0,2:T(8,128)(2,1)S(1)} %copy.114) | copy-start | bytes 3631108
  75.4 1.5 copy-start.1
  77.0 3.8 copy-start
  84.3 6.3 %copy-start.7 = (bf16[8,197,1,6,64]{1,4,3,0,2:T(8,128)(2,1)}, bf16[8,197,1,6,64]{1,4,3,0,2:T(8,128)(2,1)S(1)}, u32[]{:S(2)}) copy-start(bf16[8,197,1,6,64]{1,4,3,0,2:T(8,128)(2,1)S(1)} %copy.113) | copy-start | bytes 3631108
  91.6 2.6 copy-start.17
  103.6 51.0 %copy-start.2 = (f32[1576,384]{1,0:T(8,128)}, f32[1576,384]{1,0:T(8,128)S(1)}, u32[]{:S(2)}) copy-start(f32[1576,384]{1,0:T(8,128)S(1)} %get-tuple-element.127) | copy-start | bytes 7262212
  103.6 0.7 copy-start.26
  146.0 8.6 %copy-start.28 = (bf16[384,1536]{1,0:T(8,128)(2,1)S(1)}, bf16[384,1536]{1,0:T(8,128)(2,1)}, u32[]{:S(2)}) copy-start(bf16[384,1536]{1,0:T(8,128)(2,1)} %all-gather.4.cloned.1.call-done) | copy-start | bytes 3538948
  154.6 3.3 copy-start.37
  154.6 3.3 copy-start.12
  157.9 3.3 copy-start.11
  197.0 5.2 %copy-start.10 = (bf16[8,197,1,6,64]{1,4,3,0,2:T(8,128)(2,1)S(1)}, bf16[8,197,1,6,64]{1,4,3,0,2:T(8,128)(2,1)}, u32[]{:S(2)}) copy-start(bf16[8,197,1,6,64]{1,4,3,0,2:T(8,128)(2,1)} %copy-done.9) | copy-start | bytes 3631108
  197.0 10.7 %slice-start = ((s8[9830400]{0:T(1024)(128)(4,1)}), s8[4194304]{0:T(1024)(128)(4,1)S(1)}, s32[]{:S(2)}) async-start(s8[9830400]{0:T(1024)(128)(4,1)} %bitcast.70), calls=%async_computation.11 | async-start | bytes 8388608
  197.0 10.7 %slice-start.1 = ((s8[9830400]{0:T(1024)(128)(4,1)}), s8[4194304]{0:T(1024)(128)(4,1)S(1)}, s32[]{:S(2)}) async-start(s8[9830400]{0:T(1024)(128)(4,1)} %bitcast.70), calls=%async_computation.12 | async-start | bytes 8388608
  202.2 5.4 %slice-start.2 = ((s8[9830400]{0:T(1024)(128)(4,1)}), s8[1441792]{0:T(1024)(128)(4,1)S(1)}, s32[]{:S(2)}) async-start(s8[9830400]{0:T(1024)(128)(4,1)} %bitcast.70), calls=%async_computation.13 | async-start | bytes 2883584
  202.2 5.4 %copy-start.8 = (bf16[8,197,6,64]{1,3,2,0:T(8,128)(2,1)S(1)}, bf16[8,197,6,64]{1,3,2,0:T(8,128)(2,1)}, u32[]{:S(2)}) copy-start(bf16[8,197,6,64]{1,3,2,0:T(8,128)(2,1)} %copy.95) | copy-start | bytes 3631108
  210.7 48.8 %reduce-scatter.5.cloned.1.call-start = ((), (), s32[]{:S(2)}) async-start(), calls=%async_computation.6 | async-start | bytes 1327104 | tf_op jit(solution)/shard_map/reduce_scatter | solution.py:209
  233.9 43.2 %reduce-scatter.9.cloned.1.call-start = ((), (), s32[]{:S(2)}) async-start(), calls=%async_computation.8 | async-start | bytes 1769472 | tf_op jit(solution)/shard_map/reduce_scatter | solution.py:230
  240.6 61.0 %reduce-scatter.11.cloned.1.call-start = ((), (), s32[]{:S(2)}) async-start(), calls=%async_computation.9 | async-start | bytes 1769472 | tf_op jit(solution)/shard_map/reduce_scatter | solution.py:236
  240.6 9.8 %copy-start.36 = (bf16[192]{0:T(256)(128)(2,1)S(1)}, bf16[192]{0:T(256)(128)(2,1)}, u32[]{:S(2)}) copy-start(bf16[192]{0:T(256)(128)(2,1)} %param.28) | copy-start | bytes 1156
  240.6 10.2 %copy-start.14 = (bf16[384,1152]{1,0:T(8,128)(2,1)S(1)}, bf16[384,1152]{1,0:T(8,128)(2,1)}, u32[]{:S(2)}) copy-start(bf16[384,1152]{1,0:T(8,128)(2,1)} %copy-done.13) | copy-start | bytes 2654212
  240.7 10.2 %copy-start.20 = (f32[1576]{0:T(1024)S(1)}, f32[1576]{0:T(1024)}, u32[]{:S(2)}) copy-start(f32[1576]{0:T(1024)} %copy-done.19) | copy-start | bytes 18916
  240.7 10.2 %copy-start.22 = (f32[1576]{0:T(1024)S(1)}, f32[1576]{0:T(1024)}, u32[]{:S(2)}) copy-start(f32[1576]{0:T(1024)} %copy-done.21) | copy-start | bytes 18916
  240.7 10.2 %copy-start.24 = (f32[384]{0:T(512)S(1)}, f32[384]{0:T(512)}, u32[]{:S(2)}) copy-start(f32[384]{0:T(512)} %copy-done.23) | copy-start | bytes 4612
  247.5 155.3 %all-reduce.23.cloned.1.call-start = ((), (), s32[]{:S(2)}) async-start(), calls=%async_computation.10 | async-start | bytes 3538944 | tf_op jit(solution)/shard_map/psum | solution.py:246
  250.9 6.5 %copy-start.5 = (f32[1576,384]{1,0:T(8,128)S(1)}, f32[1576,384]{1,0:T(8,128)}, u32[]{:S(2)}) copy-start(f32[1576,384]{1,0:T(8,128)} %copy-done.4) | copy-start | bytes 7262212
  347.0 5.5 %copy-start.3 = (f32[1576,384]{1,0:T(8,128)S(1)}, f32[1576,384]{1,0:T(8,128)}, u32[]{:S(2)}) copy-start(f32[1576,384]{1,0:T(8,128)} %copy-done.2) | copy-start | bytes 7262212
  349.9 2.6 copy-start.27
  402.8 4.4 %copy-start.16 = (bf16[192,1152]{1,0:T(8,128)(2,1)S(1)}, bf16[192,1152]{1,0:T(8,128)(2,1)}, u32[]{:S(2)}) copy-start(bf16[192,1152]{1,0:T(8,128)(2,1)} %get-tuple-element.92) | copy-start | bytes 1327108
  402.8 5.4 %copy-start.18 = (bf16[192,384]{1,0:T(8,128)(2,1)S(1)}, bf16[192,384]{1,0:T(8,128)(2,1)}, u32[]{:S(2)}) copy-start(bf16[192,384]{1,0:T(8,128)(2,1)} %get-tuple-element.93) | copy-start | bytes 442372
Sparse Core Ops, SparseCore 0:
  9.6 32.5 all-gather.3
  43.7 22.4 all-gather.5
  210.9 12.0 reduce-scatter.6
  234.0 18.5 reduce-scatter.4
  255.3 21.7 reduce-scatter.8
  279.8 21.7 reduce-scatter.10
  305.5 97.2 all-reduce.22
where the time goes:
time: 421 us; the launch traced here: 416 us
  matrix products  113 us (27%)
  local copies, waits for them, and re-layouts  84.9 us (20%)
  waiting for transfers between devices  84.9 us (20%)
  blocking collectives  75.7 us (18%)
  other arithmetic  39.9 us (9%)
  between operations  17 us (4%)
    psum x1, waiting for transfers between devices, per_device(): lax.psum(owned[2].astype(jnp.bfloat16), 'rep').astype(jnp.float32)  41.4 us
    dot_general x4, matrix products, product(): return jnp.dot(left, right, preferred_element_type=jnp.float32)  39.9 us
    psum x1, blocking collectives, per_device(): lax.psum(owned[0].astype(jnp.bfloat16), 'rep').astype(jnp.float32)  32.4 us
    reduce_scatter x1, waiting for transfers between devices, per_device(): lax.psum_scatter(grad_drop_weight.astype(jnp.bfloat16), 'fsdp', scatter_d...  24.6 us
    unnamed x116, local copies, waits for them, and re-layouts  23.5 us
    dot_general x4, matrix products, product_right(): lax.dot_general(left, right, (((1,), (1,)), ((), ())), preferred_element_...  20.3 us
    dot_general x4, matrix products, product_left(): lax.dot_general(left, right, (((0,), (0,)), ((), ())), preferred_element_...  20.3 us
    all_gather x1, blocking collectives, per_device(): lax.all_gather(qkv_weight, 'fsdp', axis=0, tiled=True)  20 us
  transfers between devices with their start and end apart: 7, of which 3 were waited for; matrix products, arithmetic and copies ran while one was open for 40% of the time, Pallas kernels for 0%

commit v1 on v0

v1 whole, which is shorter than its diff:
```python
import functools

import jax
import jax.numpy as jnp
from jax import lax
from jax.experimental import pallas as pl
from jax.experimental.pallas import tpu as pltpu
from jax.sharding import PartitionSpec as P

HEADS = 6
HEAD_DIM = 64
PAIR = 2 * HEAD_DIM
LANE = 128
EPS = 1e-06
ROOT_HALF = 0.7071067811865476
GAUSS = 0.3989422804014327
LOG2E = 1.4426950408889634
SCALE = HEAD_DIM ** (-0.5)
F32 = jnp.float32
BF16 = jnp.bfloat16


def nn(a, b):
    return lax.dot_general(a, b, (((1,), (0,)), ((), ())), preferred_element_type=F32)


def nt(a, b):
    return lax.dot_general(a, b, (((1,), (1,)), ((), ())), preferred_element_type=F32)


def tn(a, b):
    return lax.dot_general(a, b, (((0,), (0,)), ((), ())), preferred_element_type=F32)


def normalise(v):
    mean = jnp.mean(v, axis=-1, keepdims=True)
    centred = v - mean
    var = jnp.mean(centred * centred, axis=-1, keepdims=True)
    inverse = lax.rsqrt(var + EPS)
    return centred * inverse, inverse


def norm_back(grad, normal, inverse, gain):
    scaled = grad * gain
    return inverse * (
        scaled
        - jnp.mean(scaled, axis=-1, keepdims=True)
        - normal * jnp.mean(scaled * normal, axis=-1, keepdims=True)
    )


def fold(v):
    return jnp.sum(v.reshape(v.shape[0] // 8, 8, v.shape[1]), axis=0)


def pad_rows(scratch, ref, length):
    for j in range(ref.shape[0]):
        scratch[j, 0:length, :] = ref[j].astype(scratch.dtype)


def zero_tail(scratch, length):
    images, rows, columns = scratch.shape
    low = (length // 16) * 16
    scratch[:, low:rows, :] = jnp.zeros((images, rows - low, columns), scratch.dtype)


def lane_masks(rows, dtype):
    lane = lax.broadcasted_iota(jnp.int32, (rows, PAIR), 1)
    return lane < HEAD_DIM


def split_pair(v):
    first = lax.broadcasted_iota(jnp.int32, v.shape, 1) < HEAD_DIM
    zero = jnp.zeros_like(v)
    return jnp.concatenate([jnp.where(first, v, zero), jnp.where(first, zero, v)], axis=0)


def join_pair(v):
    rows = v.shape[0] // 2
    first = lax.broadcasted_iota(jnp.int32, (rows, PAIR), 1) < HEAD_DIM
    return jnp.where(first, v[:rows], v[rows:])


def attend_kernel(length, tok_ref, gain_ref, shift_ref, w_ref, bias_ref, normed_ref, proj_ref, mixed_ref, n_s):
    images, rows, width = n_s.shape
    zero_tail(n_s, length)
    for j in range(images):
        normal, _ = normalise(tok_ref[j].astype(F32))
        n_s[j, 0:length, :] = (normal * gain_ref[...] + shift_ref[...]).astype(BF16)
    normed_ref[...] = n_s[...]
    flat = n_s[...].reshape(images * rows, width)
    proj_ref[...] = (
        (nn(flat, w_ref[...]) + bias_ref[...]).astype(BF16).reshape(images, rows, 3 * width)
    )
    live = lax.broadcasted_iota(jnp.int32, (2 * rows, rows), 1) < length
    ones = jnp.ones((rows, PAIR), BF16)
    for j in range(images):
        for c in range(0, width, PAIR):
            query = split_pair(proj_ref[j, :, c : c + PAIR] * jnp.asarray(SCALE, BF16))
            key = proj_ref[j, :, width + c : width + c + PAIR]
            value = proj_ref[j, :, 2 * width + c : 2 * width + c + PAIR]
            scores = jnp.where(live, nt(query, key), -1e30)
            top = jnp.max(scores, axis=-1, keepdims=True)
            weights = jnp.exp(scores - top).astype(BF16)
            both = nn(weights, jnp.concatenate([value, ones], axis=1))
            mixed_ref[j, :, c : c + PAIR] = join_pair(both[:, :PAIR] / both[:, PAIR:]).astype(BF16)


def mlp_kernel(
    length,
    chunk,
    tok_ref,
    cot_ref,
    mixed_ref,
    w_out_ref,
    w_lift_ref,
    w_drop_ref,
    vec_ref,
    lift_bias_ref,
    out_ref,
    d_middle_ref,
    d_mixed_ref,
    g_drop_ref,
    g_lift_ref,
    g_out_ref,
    g_vec_ref,
    g_bias_ref,
    x_s,
    z_s,
    a_drop,
    a_lift,
    a_out,
    a_vec,
    a_bias,
):
    step = pl.program_id(0)
    images, rows, width = x_s.shape
    total = images * rows
    hidden_width = w_lift_ref.shape[1]

    @pl.when(step == 0)
    def _():
        zero_tail(x_s, length)
        zero_tail(z_s, length)
        for acc in (a_drop, a_lift, a_out, a_vec, a_bias):
            acc[...] = jnp.zeros_like(acc)

    pad_rows(x_s, tok_ref, length)
    pad_rows(z_s, cot_ref, length)
    out_bias, gain, shift, drop_bias = (vec_ref[i : i + 1, :] for i in range(4))
    mixed = mixed_ref[...].reshape(total, width)
    dz = z_s[...].reshape(total, width)
    dz_f = dz.astype(F32)
    middle = x_s[...].reshape(total, width).astype(F32) + nn(mixed, w_out_ref[...]) + out_bias
    normal, inverse = normalise(middle)
    normed = (normal * gain + shift).astype(BF16)
    result = middle + drop_bias
    d_normed = jnp.zeros((total, width), F32)
    for c in range(0, hidden_width, chunk):
        part = slice(c, c + chunk)
        hidden = nn(normed, w_lift_ref[:, part]) + lift_bias_ref[:, part]
        cdf = 0.5 + 0.5 * lax.erf(hidden * ROOT_HALF)
        bell = jnp.exp(hidden * hidden * -0.5) * GAUSS
        active = (hidden * cdf).astype(BF16)
        d_active = nt(dz, w_drop_ref[part, :])
        d_hidden_f = d_active * (cdf + hidden * bell)
        d_hidden = d_hidden_f.astype(BF16)
        result = result + nn(active, w_drop_ref[part, :])
        d_normed = d_normed + nt(d_hidden, w_lift_ref[:, part])
        a_drop[part, :] += tn(active, dz)
        a_lift[:, part] += tn(normed, d_hidden)
        a_bias[:, part] += fold(d_hidden.astype(F32))
    out = result.astype(BF16)
    for j in range(images):
        out_ref[j] = out[j * rows : j * rows + length]
    d_middle = dz_f + norm_back(d_normed, normal, inverse, gain)
    d_middle_ref[...] = d_middle.reshape(images, rows, width)
    d_attended = d_middle.astype(BF16)
    d_mixed_ref[...] = nt(d_attended, w_out_ref[...]).astype(BF16).reshape(images, rows, width)
    a_out[...] += tn(mixed, d_attended)
    a_vec[0] += fold(d_attended.astype(F32))
    a_vec[1] += fold(d_normed * normal)
    a_vec[2] += fold(d_normed)
    a_vec[3] += fold(dz_f)

    @pl.when(step == pl.num_programs(0) - 1)
    def _():
        g_drop_ref[...] = a_drop[...].astype(BF16)
        g_lift_ref[...] = a_lift[...].astype(BF16)
        g_out_ref[...] = a_out[...].astype(BF16)
        g_vec_ref[...] = jnp.sum(a_vec[...], axis=1)
        g_bias_ref[...] = jnp.sum(a_bias[...], axis=0, keepdims=True)


def back_kernel(
    length,
    tok_ref,
    proj_ref,
    normed_ref,
    d_mixed_ref,
    d_middle_ref,
    w_ref,
    gain_ref,
    in_grad_ref,
    g_qkv_ref,
    g_vec_ref,
    d_s,
    a_qkv,
    a_proj,
    a_vec,
):
    step = pl.program_id(0)
    images, rows, wide = d_s.shape
    width = wide // 3
    total = images * rows

    @pl.when(step == 0)
    def _():
        for acc in (a_qkv, a_proj, a_vec):
            acc[...] = jnp.zeros_like(acc)

    live = lax.broadcasted_iota(jnp.int32, (rows, 2 * rows), 0) < length
    for j in range(images):
        for c in range(0, width, PAIR):
            query = split_pair(proj_ref[j, :, c : c + PAIR] * jnp.asarray(SCALE, BF16))
            key = proj_ref[j, :, width + c : width + c + PAIR]
            value = proj_ref[j, :, 2 * width + c : 2 * width + c + PAIR]
            d_mixed = split_pair(d_mixed_ref[j, :, c : c + PAIR])
            scores = jnp.where(live, nt(key, query), -1e30)
            top = jnp.max(scores, axis=0, keepdims=True)
            weights = jnp.exp(scores - top)
            probs = weights * (1.0 / jnp.sum(weights, axis=0, keepdims=True))
            d_probs = nt(value, d_mixed)
            delta = jnp.sum(probs * d_probs, axis=0, keepdims=True)
            d_scores = (probs * (d_probs - delta)).astype(BF16)
            d_value = nn(probs.astype(BF16), d_mixed)
            d_key = nn(d_scores, query)
            d_query = join_pair(tn(d_scores, key)) * SCALE
            d_s[j, :, c : c + PAIR] = d_query.astype(BF16)
            d_s[j, :, width + c : width + c + PAIR] = d_key.astype(BF16)
            d_s[j, :, 2 * width + c : 2 * width + c + PAIR] = d_value.astype(BF16)
    d_proj = d_s[...].reshape(total, wide)
    a_qkv[...] += tn(normed_ref[...].reshape(total, width), d_proj)
    a_proj[...] += fold(d_proj.astype(F32))
    d_normed = nt(d_proj, w_ref[...])
    gain = gain_ref[...]
    for j in range(images):
        normal, inverse = normalise(tok_ref[j].astype(F32))
        grad = d_normed[j * rows : j * rows + length]
        in_grad_ref[j] = (
            d_middle_ref[j, 0:length, :] + norm_back(grad, normal, inverse, gain)
        ).astype(BF16)
        a_vec[0:1, :] += jnp.sum(grad * normal, axis=0, keepdims=True)
        a_vec[1:2, :] += jnp.sum(grad, axis=0, keepdims=True)

    @pl.when(step == pl.num_programs(0) - 1)
    def _():
        g_qkv_ref[...] = a_qkv[...].astype(BF16)
        columns = jnp.sum(a_proj[...], axis=0, keepdims=True)
        g_vec_ref[0:2, :] = a_vec[...]
        g_vec_ref[2:3, :] = columns[:, :width]
        g_vec_ref[3:4, :] = columns[:, 2 * width :]


VMEM_LIMIT = 60 * 1024 * 1024


def whole(*shape):
    return pl.BlockSpec(shape, lambda i: (0,) * len(shape))


def per_step(*shape):
    return pl.BlockSpec(shape, lambda i: (i,) + (0,) * (len(shape) - 1))


def forward_attention(tokens, gain, shift, w_qkv, bias):
    images, length, width = tokens.shape
    rows = -(-length // 16) * 16
    group = 2 if images % 2 == 0 else 1
    return pl.pallas_call(
        functools.partial(attend_kernel, length),
        grid=(images // group,),
        in_specs=[
            per_step(group, length, width),
            whole(1, width),
            whole(1, width),
            whole(width, 3 * width),
            whole(1, 3 * width),
        ],
        out_specs=[
            per_step(group, rows, width),
            per_step(group, rows, 3 * width),
            per_step(group, rows, width),
        ],
        out_shape=[
            jax.ShapeDtypeStruct((images, rows, width), BF16),
            jax.ShapeDtypeStruct((images, rows, 3 * width), BF16),
            jax.ShapeDtypeStruct((images, rows, width), BF16),
        ],
        scratch_shapes=[pltpu.VMEM((group, rows, width), BF16)],
        compiler_params=pltpu.CompilerParams(vmem_limit_bytes=VMEM_LIMIT),
        name="attend",
    )(tokens, gain, shift, w_qkv, bias)


def mlp_both_ways(tokens, cotangent, mixed, w_out, w_lift, w_drop, vectors, lift_bias):
    images, length, width = tokens.shape
    rows = mixed.shape[1]
    ff = w_lift.shape[1]
    group = 2 if images % 2 == 0 else 1
    return pl.pallas_call(
        functools.partial(mlp_kernel, length, 256),
        grid=(images // group,),
        in_specs=[
            per_step(group, length, width),
            per_step(group, length, width),
            per_step(group, rows, width),
            whole(width, width),
            whole(width, ff),
            whole(ff, width),
            whole(4, width),
            whole(1, ff),
        ],
        out_specs=[
            per_step(group, length, width),
            per_step(group, rows, width),
            per_step(group, rows, width),
            whole(ff, width),
            whole(width, ff),
            whole(width, width),
            whole(4, width),
            whole(1, ff),
        ],
        out_shape=[
            jax.ShapeDtypeStruct((images, length, width), BF16),
            jax.ShapeDtypeStruct((images, rows, width), F32),
            jax.ShapeDtypeStruct((images, rows, width), BF16),
            jax.ShapeDtypeStruct((ff, width), BF16),
            jax.ShapeDtypeStruct((width, ff), BF16),
            jax.ShapeDtypeStruct((width, width), BF16),
            jax.ShapeDtypeStruct((4, width), F32),
            jax.ShapeDtypeStruct((1, ff), F32),
        ],
        scratch_shapes=[
            pltpu.VMEM((group, rows, width), BF16),
            pltpu.VMEM((group, rows, width), BF16),
            pltpu.VMEM((ff, width), F32),
            pltpu.VMEM((width, ff), F32),
            pltpu.VMEM((width, width), F32),
            pltpu.VMEM((4, 8, width), F32),
            pltpu.VMEM((8, ff), F32),
        ],
        compiler_params=pltpu.CompilerParams(vmem_limit_bytes=VMEM_LIMIT),
        name="mlp",
    )(tokens, cotangent, mixed, w_out, w_lift, w_drop, vectors, lift_bias)


def attention_backward(tokens, projected, normed, d_mixed, d_middle, w_qkv, gain):
    images, length, width = tokens.shape
    rows = normed.shape[1]
    group = 2 if images % 2 == 0 else 1
    return pl.pallas_call(
        functools.partial(back_kernel, length),
        grid=(images // group,),
        in_specs=[
            per_step(group, length, width),
            per_step(group, rows, 3 * width),
            per_step(group, rows, width),
            per_step(group, rows, width),
            per_step(group, rows, width),
            whole(width, 3 * width),
            whole(1, width),
        ],
        out_specs=[
            per_step(group, length, width),
            whole(width, 3 * width),
            whole(4, width),
        ],
        out_shape=[
            jax.ShapeDtypeStruct((images, length, width), BF16),
            jax.ShapeDtypeStruct((width, 3 * width), BF16),
            jax.ShapeDtypeStruct((4, width), F32),
        ],
        scratch_shapes=[
            pltpu.VMEM((group, rows, 3 * width), BF16),
            pltpu.VMEM((width, 3 * width), F32),
            pltpu.VMEM((8, 3 * width), F32),
            pltpu.VMEM((2, width), F32),
        ],
        compiler_params=pltpu.CompilerParams(vmem_limit_bytes=VMEM_LIMIT),
        name="back",
    )(tokens, projected, normed, d_mixed, d_middle, w_qkv, gain)


def per_device(
    tokens,
    gain_one,
    shift_one,
    qkv_weight,
    query_bias,
    value_bias,
    out_weight,
    out_bias,
    gain_two,
    shift_two,
    lift_weight,
    lift_bias,
    drop_weight,
    drop_bias,
    cotangent,
):
    def gather(v):
        return lax.all_gather(v, "fsdp", axis=0, tiled=True)

    width = tokens.shape[-1]
    vectors = gather(
        jnp.stack(
            [gain_one, shift_one, query_bias, value_bias, out_bias, gain_two, shift_two, drop_bias],
            axis=1,
        )
    ).T.astype(F32)
    full_qkv, full_out, full_lift, full_drop = (
        gather(w) for w in (qkv_weight, out_weight, lift_weight, drop_weight)
    )
    full_lift_bias = gather(lift_bias).astype(F32)[None]
    gain, shift = vectors[0:1], vectors[1:2]
    qkv_bias = jnp.concatenate([vectors[2], jnp.zeros((width,), F32), vectors[3]])[None]
    normed, projected, mixed = forward_attention(tokens, gain, shift, full_qkv, qkv_bias)
    outer = jnp.stack([vectors[4], vectors[5], vectors[6], vectors[7]])
    output, d_middle, d_mixed, g_drop, g_lift, g_out, g_vec, g_bias = mlp_both_ways(
        tokens, cotangent, mixed, full_out, full_lift, full_drop, outer, full_lift_bias
    )
    input_grad, g_qkv, g_vec_one = attention_backward(
        tokens, projected, normed, d_mixed, d_middle, full_qkv, gain
    )

    def reduced(v):
        owned = lax.psum_scatter(v.astype(BF16), "fsdp", scatter_dimension=0, tiled=True)
        return lax.psum(owned, "rep").astype(F32)

    return (
        output,
        input_grad,
        reduced(g_vec_one[0]),
        reduced(g_vec_one[1]),
        reduced(g_qkv),
        reduced(g_vec_one[2]),
        reduced(g_vec_one[3]),
        reduced(g_out),
        reduced(g_vec[0]),
        reduced(g_vec[1]),
        reduced(g_vec[2]),
        reduced(g_lift),
        reduced(g_bias[0]),
        reduced(g_drop),
        reduced(g_vec[3]),
    )


def solution(mesh):
    spread = P(("rep", "fsdp"), None, None)
    vector, matrix = P("fsdp"), P("fsdp", None)
    in_specs = (
        spread,
        vector,
        vector,
        matrix,
        vector,
        vector,
        matrix,
        vector,
        vector,
        vector,
        matrix,
        vector,
        matrix,
        vector,
        spread,
    )
    out_specs = (
        spread,
        spread,
        vector,
        vector,
        matrix,
        vector,
        vector,
        matrix,
        vector,
        vector,
        vector,
        matrix,
        vector,
        matrix,
        vector,
    )
    return jax.shard_map(
        per_device, mesh=mesh, in_specs=in_specs, out_specs=out_specs, check_vma=False
    )
```

time: 421 us -> 296 us (0.70); the launches traced: 416 us -> 296 us
  matrix products: 113 us -> 0 us
  local copies, waits for them, and re-layouts: 84.9 us -> 14.4 us
  Pallas kernels: 0 us -> 59.3 us
  waiting for transfers between devices: 84.9 us -> 121 us
  other arithmetic: 39.9 us -> 10.8 us
    dot_general x18 -> x0, matrix products: 113 us -> none  [the longest x4 39.9 us: product(): return jnp.dot(left, right, preferred_element_type=jnp.float32)]
    pallas_call x0 -> x3, Pallas kernels: none -> 59.3 us  [the longest x1 28.6 us: mlp_both_ways(): pl.pallas_call(functools.partial(mlp_kernel, length, 256), grid=(images /...]
    reshape x7 -> x0, local copies, waits for them, and re-layouts: 30.6 us -> none  [the longest x1 11.7 us: per_device(): split_heads = projected.reshape(images, length, 3, HEADS, HEAD_DIM)]
    reduce_scatter x4, waiting for transfers between devices: 42.1 us -> 66.4 us  [reduced(): lax.psum_scatter(v.astype(BF16), 'fsdp', scatter_dimension=0, tiled=True)]
    convert_element_type x10 -> x2, local copies, waits for them, and re-layouts: 23.6 us -> 0.09 us  [per_device(): vectors = gather(jnp.stack([gain_one, shift_one, query_bias, value_bias,...]
    convert_element_type x24 -> x14, other arithmetic: 26.8 us -> 10.2 us  [the longest x13 10.2 us: reduced(): return lax.psum(owned, 'rep').astype(F32)]
    unnamed x116 -> x43, local copies, waits for them, and re-layouts: 23.5 us -> 7.21 us
    reduce_sum x7 -> x0, other arithmetic: 13.1 us -> none  [the longest x1 3.42 us: per_device(): column_sums = jnp.sum(d_projected.astype(jnp.float32), axis=0)]
  transfers between devices with their start and end apart: 7 -> 7, of which waited for: 3 -> 5; matrix products, arithmetic and copies ran while one was open for 40% -> 6% of each run, Pallas kernels for 0% -> 10%
where the time goes in v1:
time: 296 us
  waiting for transfers between devices  121 us (41%)
  blocking collectives  74.6 us (25%)
  Pallas kernels  59.3 us (20%)
  between operations  15.6 us (5%)
  local copies, waits for them, and re-layouts  14.4 us (5%)
  other arithmetic  10.8 us (4%)
    reduce_scatter x4, waiting for transfers between devices, reduced(): lax.psum_scatter(v.astype(BF16), 'fsdp', scatter_dimension=0, tiled=True)  66.4 us
    psum x1, waiting for transfers between devices, reduced(): return lax.psum(owned, 'rep').astype(F32)  50.7 us
    all_gather x4, blocking collectives, gather(): return lax.all_gather(v, 'fsdp', axis=0, tiled=True)  35 us
    psum x1, blocking collectives, reduced(): return lax.psum(owned, 'rep').astype(F32)  32.6 us
    pallas_call x1, Pallas kernels, mlp_both_ways(): pl.pallas_call(functools.partial(mlp_kernel, length, 256), grid=(images /...  28.6 us
    pallas_call x1, Pallas kernels, attention_backward(): pl.pallas_call(functools.partial(back_kernel, length), grid=(images // gr...  20.8 us
    convert_element_type x13, other arithmetic, reduced(): return lax.psum(owned, 'rep').astype(F32)  10.2 us
    pallas_call x1, Pallas kernels, forward_attention(): pl.pallas_call(functools.partial(attend_kernel, length), grid=(images //...  9.95 us
  transfers between devices with their start and end apart: 7, of which 5 were waited for; matrix products, arithmetic and copies ran while one was open for 6% of the time, Pallas kernels for 10%

profile of v1, /device:TPU:0, one launch (start us, length us, event | category | flops | bytes accessed | tf_op | source)
XLA Modules:
  0.0 296.0 jit_solution(2711152687693444866)
XLA Ops:
  7.2 0.7 all-gather.5.cloned.1.call-update
  8.0 0.7 all-gather.7.cloned.1.call-update
  8.7 0.0 reduce-scatter.7.cloned.1.call-start
  8.7 0.7 stack.28
  9.4 0.7 stack.29
  10.0 0.7 stack.30
  10.7 0.7 stack.31
  11.4 0.7 stack.32
  12.0 0.7 stack.33
  12.7 0.7 stack.34
  13.3 0.7 stack.35
  14.0 5.2 %all-gather = bf16[2,192,8]{1,2,0:T(8,128)(2,1)S(1)} all-gather(bf16[1,192,8]{1,2,0:T(8,128)(2,1)S(1)} %bitcast.10), channel_id=1, replica_groups=mesh['rep'=16,'fsdp'=2] {'fsdp'}, dimensions={0}, use_global_device_ids=true | all-gather | bytes 9216 | tf_op jit(solution)/shard_map/all_gather | solution.py:413
  19.3 0.1 reshape.44
  19.3 0.6 slice.68.vec_ref
  19.9 0.6 slice_reduce_fusion.9
  20.5 0.6 broadcast_in_dim.12.bias_ref
  21.1 1.2 copy.45.tok_ref
  22.3 0.5 copy-done.3
  22.9 1.3 copy.46.cot_ref
  24.1 4.4 %all-gather.1 = bf16[2,1,768]{2,1,0:T(2,128)(2,1)S(1)} all-gather(bf16[1,1,768]{2,1,0:T(2,128)(2,1)S(1)} %reshape.42), channel_id=1, replica_groups=mesh['rep'=16,'fsdp'=2] {'fsdp'}, dimensions={0}, use_global_device_ids=true | all-gather | bytes 4608 | tf_op jit(solution)/shard_map/all_gather | solution.py:413
  28.5 0.6 convert.16.lift_bias_ref
  29.1 15.4 %all_gather.19.w_ref = bf16[384,1152]{1,0:T(8,128)(2,1)} all-gather(bf16[192,1152]{1,0:T(8,128)(2,1)S(1)} %copy-done.5), channel_id=1, replica_groups=mesh['rep'=16,'fsdp'=2] {'fsdp'}, dimensions={0}, use_global_device_ids=true | all-gather | bytes 1327104 | tf_op jit(solution)/shard_map/all_gather | solution.py:413
  44.5 9.9 %attend.1 = (bf16[8,208,384]{2,1,0:T(8,128)(2,1)}, bf16[8,208,1152]{2,1,0:T(8,128)(2,1)}, bf16[8,208,384]{2,1,0:T(8,128)(2,1)}) custom-call(bf16[8,197,384]{2,1,0:T(8,128)(2,1)} %copy.45.tok_ref, f32[1,384]{1,0:T(1,128)} %get-tuple-element.121.gain_ref, f32[1,384]{1,0:T(1,128)} %get-tuple-element.120.shift_ref, bf16[384,1152]{1,0:T(8,128)(2,1)} %all_gather.19.w_ref, ...), custom_call_target="tpu_custom_call" | custom-call | tf_op jit(solution)/shard_map/attend/pallas_call | solution.py:280
  54.4 10.0 %all_gather.20.w_out_ref = bf16[384,384]{1,0:T(8,128)(2,1)} all-gather(bf16[192,384]{1,0:T(8,128)(2,1)S(1)} %copy-done.7), channel_id=1, replica_groups=mesh['rep'=16,'fsdp'=2] {'fsdp'}, dimensions={0}, use_global_device_ids=true | all-gather | bytes 442368 | tf_op jit(solution)/shard_map/all_gather | solution.py:413
  64.4 1.2 all-gather.7.cloned.1.call-done.w_drop_ref
  65.6 28.6 %mlp.1 = (bf16[8,197,384]{2,1,0:T(8,128)(2,1)}, f32[8,208,384]{2,1,0:T(8,128)}, bf16[8,208,384]{2,1,0:T(8,128)(2,1)}, bf16[1536,384]{1,0:T(8,128)(2,1)}, bf16[38...) custom-call(bf16[8,197,384]{2,1,0:T(8,128)(2,1)} %copy.45.tok_ref, ...), custom_call_target="tpu_custom_call" | custom-call | tf_op jit(solution)/shard_map/mlp/pallas_call | solution.py:311
  94.2 0.2 reduce-scatter.5.cloned.1.call-start
  94.5 20.8 %back.1 = (bf16[8,197,384]{2,1,0:T(8,128)(2,1)}, bf16[384,1152]{1,0:T(8,128)(2,1)}, f32[4,384]{1,0:T(4,128)}) custom-call(bf16[8,197,384]{2,1,0:T(8,128)(2,1)} %copy.45.tok_ref, bf16[8,208,1152]{2,1,0:T(8,128)(2,1)} %get-tuple-element.31.proj_ref, bf16[8,208,384]{2,1,0:T(8,128)(2,1)} %get-tuple-element.32.normed_ref, ...), custom_call_target="tpu_custom_call" | custom-call | tf_op jit(solution)/shard_map/back/pallas_call | solution.py:362
  115.3 0.0 reduce-scatter.11.cloned.1.call-start
  115.3 0.5 reduce-scatter.11.cloned.1.call-update
  115.9 0.5 reduce-scatter.9.cloned.1.call-update
  116.4 0.0 all-reduce.14.cloned.1.call-start
  116.5 17.4 %reduce-scatter.5.cloned.1.call-done = bf16[192,1152]{1,0:T(8,128)(2,1)} async-done(((bf16[384,1152]{1,0:T(8,128)(2,1)}), bf16[192,1152]{1,0:T(8,128)(2,1)}) %reduce-scatter.5.cloned.1.call-update) | async-done | bytes 442384 | tf_op jit(solution)/shard_map/reduce_scatter | solution.py:438
  133.9 24.5 %reduce-scatter.11.cloned.1.call-done = bf16[768,384]{1,0:T(8,128)(2,1)} async-done(((bf16[1536,384]{1,0:T(8,128)(2,1)}), bf16[768,384]{1,0:T(8,128)(2,1)}) %reduce-scatter.11.cloned.1.call-update) | async-done | bytes 589840 | tf_op jit(solution)/shard_map/reduce_scatter | solution.py:438
  158.4 24.5 %reduce-scatter.9.cloned.1.call-done = bf16[192,1536]{1,0:T(8,128)(2,1)} async-done(((bf16[384,1536]{1,0:T(8,128)(2,1)}), bf16[192,1536]{1,0:T(8,128)(2,1)}) %reduce-scatter.9.cloned.1.call-update) | async-done | bytes 589840 | tf_op jit(solution)/shard_map/reduce_scatter | solution.py:438
  183.0 0.6 dynamic-slice
  185.0 7.0 %all-reduce.11 = (bf16[384]{0:T(512)(128)(2,1)S(1)}, bf16[384]{0:T(512)(128)(2,1)S(1)}, bf16[384]{0:T(512)(128)(2,1)S(1)}, bf16[384]{0:T(512)(128)(2,1)S(1)}, bf...) all-reduce(bf16[384]{0:T(512)(128)(2,1)S(1)} %get-tuple-element.122, ...), channel_id=2, replica_groups=mesh['rep'=16,'fsdp'=2] {'fsdp'}, use_global_device_ids=true, to_apply=%region_0.0.clone | all-reduce | flops 4608 | bytes 18432
  192.0 0.1 dynamic-slice.1
  192.1 0.1 dynamic-slice.11
  192.2 0.1 dynamic-slice.13
  192.2 0.1 dynamic-slice.17
  192.3 0.1 dynamic-slice.3
  192.4 0.1 dynamic-slice.5
  192.5 0.1 dynamic-slice.7
  192.5 0.1 dynamic-slice.9
  192.6 0.1 dynamic-slice.15
  192.7 32.6 %all-reduce.9 = (bf16[192]{0:T(256)(128)(2,1)S(1)}, bf16[192]{0:T(256)(128)(2,1)S(1)}, bf16[192]{0:T(256)(128)(2,1)S(1)}, bf16[192]{0:T(256)(128)(2,1)S(1)}, bf1...) all-reduce(bf16[192]{0:T(256)(128)(2,1)S(1)} %dynamic-slice.1, ...), channel_id=1, replica_groups=mesh['rep'=16,'fsdp'=2] {'rep'}, use_global_device_ids=true, to_apply=%region_1.0 | all-reduce | flops 2304 | bytes 9216 | tf_op jit(solution)/shard_map/psum | solution.py:439
  225.3 0.6 convert_element_type.105
  225.9 0.6 convert_element_type.101
  226.5 0.6 convert_element_type.108
  227.1 0.6 convert_element_type.87
  227.6 0.6 convert_element_type.89
  228.2 0.6 convert_element_type.92
  228.7 0.6 convert_element_type.94
  229.3 0.6 convert_element_type.97
  229.9 0.6 convert_element_type.99
  230.4 1.2 copy.49
  231.6 0.5 copy-done
  232.2 1.2 copy.48
  233.3 50.7 %all-reduce.14.cloned.1.call-done = (bf16[192,1152]{1,0:T(8,128)(2,1)}, bf16[192,384]{1,0:T(8,128)(2,1)}, bf16[192,1536]{1,0:T(8,128)(2,1)}, bf16[768,384]{1,0:T(8,128)(2,1)}) async-done(((bf16[192,1152]{1,0:T(8,128)(2,1)}, bf16[192,384]{1,0:T(8,128)(2,1)}, bf16[192,1536]{1,0:T(8,128)(2,1)}, bf16[768,384]{1,0:T(8,128)(2,1)}), (bf16[192,1152]{1,0:T(8,128)(2,1)}, bf16[192,384]{1,0:T(8,128)(2,1)}, ...) | async-done | bytes 1769488 | tf_op jit(solution)/shard_map/psum | solution.py:439
  284.1 2.3 convert_element_type.102
  286.4 1.1 convert_element_type.106
  287.5 1.0 convert_element_type.90
  288.4 0.7 convert_element_type.95
  (43 shorter events, 0.4 us)
Async XLA Ops:
  7.2 14.0 %copy-start.2 = (bf16[8,197,384]{2,0,1:T(8,128)(2,1)S(1)}, bf16[8,197,384]{2,0,1:T(8,128)(2,1)}, u32[]{:S(2)}) copy-start(bf16[8,197,384]{2,0,1:T(8,128)(2,1)} %param.15) | copy-start | bytes 3631108
  7.2 57.2 %all-gather.5.cloned.1.call-start = ((), (), s32[]{:S(2)}) async-start(), calls=%async_computation.4 | async-start | bytes 1769472 | tf_op jit(solution)/shard_map/all_gather | solution.py:413
  7.9 57.7 %all-gather.7.cloned.1.call-start = ((), (), s32[]{:S(2)}) async-start(), calls=%async_computation.5 | async-start | bytes 1769472 | tf_op jit(solution)/shard_map/all_gather | solution.py:413
  8.7 107.8 %reduce-scatter.7.cloned.1.call-start = ((), (), s32[]{:S(2)}) async-start(), calls=%async_computation.7 | async-start | bytes 442368 | tf_op jit(solution)/shard_map/reduce_scatter | solution.py:438
  21.1 1.7 copy-start.3
  22.9 1.3 copy-start.12
  22.9 6.2 %copy-start.5 = (bf16[192,1152]{1,0:T(8,128)(2,1)S(1)}, bf16[192,1152]{1,0:T(8,128)(2,1)}, u32[]{:S(2)}) copy-start(bf16[192,1152]{1,0:T(8,128)(2,1)} %param.18) | copy-start | bytes 1327108
  44.5 10.0 %copy-start.7 = (bf16[192,384]{1,0:T(8,128)(2,1)S(1)}, bf16[192,384]{1,0:T(8,128)(2,1)}, u32[]{:S(2)}) copy-start(bf16[192,384]{1,0:T(8,128)(2,1)} %param.21) | copy-start | bytes 442372
  94.2 39.7 %reduce-scatter.5.cloned.1.call-start = ((), (), s32[]{:S(2)}) async-start(), calls=%async_computation.6 | async-start | bytes 1327104 | tf_op jit(solution)/shard_map/reduce_scatter | solution.py:438
  115.3 43.1 %reduce-scatter.11.cloned.1.call-start = ((), (), s32[]{:S(2)}) async-start(), calls=%async_computation.9 | async-start | bytes 1769472 | tf_op jit(solution)/shard_map/reduce_scatter | solution.py:438
  115.9 67.1 %reduce-scatter.9.cloned.1.call-start = ((), (), s32[]{:S(2)}) async-start(), calls=%async_computation.8 | async-start | bytes 1769472 | tf_op jit(solution)/shard_map/reduce_scatter | solution.py:438
  115.9 67.1 %copy-start.13 = (u32[32]{0:T(128)S(1)}, u32[32]{0:T(128)}, u32[]{:S(2)}) copy-start(u32[32]{0:T(128)} %constant.6) | copy-start | bytes 388
  115.9 69.0 %copy-start.11 = (f32[4,384]{1,0:T(4,128)S(1)}, f32[4,384]{1,0:T(4,128)}, u32[]{:S(2)}) copy-start(f32[4,384]{1,0:T(4,128)} %get-tuple-element.36) | copy-start | bytes 18436
  115.9 69.0 %copy-start.10 = (f32[4,384]{1,0:T(4,128)S(1)}, f32[4,384]{1,0:T(4,128)}, u32[]{:S(2)}) copy-start(f32[4,384]{1,0:T(4,128)} %get-tuple-element.39) | copy-start | bytes 18436
  116.4 68.5 %copy-start.9 = (f32[1,1536]{1,0:T(1,128)S(1)}, f32[1,1536]{1,0:T(1,128)}, u32[]{:S(2)}) copy-start(f32[1,1536]{1,0:T(1,128)} %get-tuple-element.41) | copy-start | bytes 18436
  116.4 114.0 %copy-start.1 = (bf16[8,197,384]{2,1,0:T(8,128)(2,1)S(1)}, bf16[8,197,384]{2,1,0:T(8,128)(2,1)}, u32[]{:S(2)}) copy-start(bf16[8,197,384]{2,1,0:T(8,128)(2,1)} %get-tuple-element.74) | copy-start | bytes 3631108
  116.4 167.6 %all-reduce.14.cloned.1.call-start = ((), (), s32[]{:S(2)}) async-start(), calls=%async_computation.10 | async-start | bytes 3538944 | tf_op jit(solution)/shard_map/psum | solution.py:439
  230.4 1.7 copy-start
  284.1 2.3 copy-start.4
  286.4 1.1 copy-start.6
  286.4 2.1 copy-start.8
Sparse Core Ops, SparseCore 0:
  9.6 29.1 all-gather.4
  40.3 25.2 all-gather.6
  94.3 12.0 reduce-scatter.6
  115.4 18.5 reduce-scatter.4
  136.6 21.7 reduce-scatter.10
  161.2 21.7 reduce-scatter.8
  186.8 97.2 all-reduce.13

commit v2 on v1

v2 whole, which is shorter than its diff:
```python
import functools

import jax
import jax.numpy as jnp
from jax import lax
from jax.experimental import pallas as pl
from jax.experimental.pallas import tpu as pltpu
from jax.sharding import PartitionSpec as P

HEADS = 6
HEAD_DIM = 64
PAIR = 2 * HEAD_DIM
LANE = 128
EPS = 1e-06
ROOT_HALF = 0.7071067811865476
GAUSS = 0.3989422804014327
LOG2E = 1.4426950408889634
SCALE = HEAD_DIM ** (-0.5)
F32 = jnp.float32
BF16 = jnp.bfloat16


def nn(a, b):
    return lax.dot_general(a, b, (((1,), (0,)), ((), ())), preferred_element_type=F32)


def nt(a, b):
    return lax.dot_general(a, b, (((1,), (1,)), ((), ())), preferred_element_type=F32)


def tn(a, b):
    return lax.dot_general(a, b, (((0,), (0,)), ((), ())), preferred_element_type=F32)


def normalise(v):
    mean = jnp.mean(v, axis=-1, keepdims=True)
    centred = v - mean
    var = jnp.mean(centred * centred, axis=-1, keepdims=True)
    inverse = lax.rsqrt(var + EPS)
    return centred * inverse, inverse


def norm_back(grad, normal, inverse, gain):
    scaled = grad * gain
    return inverse * (
        scaled
        - jnp.mean(scaled, axis=-1, keepdims=True)
        - normal * jnp.mean(scaled * normal, axis=-1, keepdims=True)
    )


def fold(v):
    return jnp.sum(v.reshape(v.shape[0] // 8, 8, v.shape[1]), axis=0)


def pad_rows(scratch, ref, length):
    for j in range(ref.shape[0]):
        scratch[j, 0:length, :] = ref[j].astype(scratch.dtype)


def zero_tail(scratch, length):
    images, rows, columns = scratch.shape
    low = (length // 16) * 16
    scratch[:, low:rows, :] = jnp.zeros((images, rows - low, columns), scratch.dtype)


def split_pair(v):
    first = lax.broadcasted_iota(jnp.int32, v.shape, 1) < HEAD_DIM
    zero = jnp.zeros_like(v)
    return jnp.concatenate([jnp.where(first, v, zero), jnp.where(first, zero, v)], axis=0)


def join_pair(v):
    rows = v.shape[0] // 2
    first = lax.broadcasted_iota(jnp.int32, (rows, PAIR), 1) < HEAD_DIM
    return jnp.where(first, v[:rows], v[rows:])


def join_pieces(full, own, near, far, index):
    block = own.shape[0]
    half = block // 2
    x, core = index[0], index[1]
    other = (1 - x) * block
    full[pl.ds(pl.multiple_of(x * block, 16), block), :] = own[...]
    full[pl.ds(pl.multiple_of(other + core * half, 16), half), :] = near[...]
    full[pl.ds(pl.multiple_of(other + (1 - core) * half, 16), half), :] = far[...]


def quarters(index, keep, send):
    x, core = index[0], index[1]
    for slot, half in ((0, x), (1, 1 - x)):
        yield keep, slot, half, core
        yield send, slot, half, 1 - core


def attend_kernel(
    length, index, tok_ref, vec_ref, own, near, far, normed_ref, proj_ref, mixed_ref, w_ref, n_s
):
    images, rows, width = n_s.shape

    @pl.when(pl.program_id(0) == 0)
    def _():
        zero_tail(n_s, length)
        join_pieces(w_ref, own, near, far, index)

    gain, shift = vec_ref[0:1, :], vec_ref[1:2, :]
    bias = jnp.concatenate([vec_ref[2:3, :], jnp.zeros((1, width), F32), vec_ref[3:4, :]], axis=1)
    for j in range(images):
        normal, _ = normalise(tok_ref[j].astype(F32))
        n_s[j, 0:length, :] = (normal * gain + shift).astype(BF16)
    normed_ref[...] = n_s[...]
    flat = n_s[...].reshape(images * rows, width)
    proj_ref[...] = (nn(flat, w_ref[...]) + bias).astype(BF16).reshape(images, rows, 3 * width)
    live = lax.broadcasted_iota(jnp.int32, (2 * rows, rows), 1) < length
    ones = jnp.ones((rows, PAIR), BF16)
    for j in range(images):
        for c in range(0, width, PAIR):
            query = split_pair(proj_ref[j, :, c : c + PAIR] * jnp.asarray(SCALE, BF16))
            key = proj_ref[j, :, width + c : width + c + PAIR]
            value = proj_ref[j, :, 2 * width + c : 2 * width + c + PAIR]
            scores = jnp.where(live, nt(query, key), -1e30)
            top = jnp.max(scores, axis=-1, keepdims=True)
            weights = jnp.exp(scores - top).astype(BF16)
            both = nn(weights, jnp.concatenate([value, ones], axis=1))
            mixed_ref[j, :, c : c + PAIR] = join_pair(both[:, :PAIR] / both[:, PAIR:]).astype(BF16)


def mlp_kernel(
    length,
    chunk,
    index,
    tok_ref,
    cot_ref,
    mixed_ref,
    vec_ref,
    lift_bias_ref,
    out_own,
    out_near,
    out_far,
    lift_own,
    lift_near,
    lift_far,
    drop_own,
    drop_near,
    drop_far,
    out_ref,
    d_middle_ref,
    d_mixed_ref,
    keep_a,
    send_a,
    keep_b,
    send_b,
    x_s,
    z_s,
    w_out_ref,
    w_lift_ref,
    w_drop_ref,
    a_drop,
    a_lift,
    a_out,
    a_vec,
    a_bias,
):
    step = pl.program_id(0)
    images, rows, width = x_s.shape
    total = images * rows
    hidden_width = w_lift_ref.shape[1]

    @pl.when(step == 0)
    def _():
        zero_tail(x_s, length)
        zero_tail(z_s, length)
        join_pieces(w_out_ref, out_own, out_near, out_far, index)
        join_pieces(w_lift_ref, lift_own, lift_near, lift_far, index)
        join_pieces(w_drop_ref, drop_own, drop_near, drop_far, index)
        for acc in (a_drop, a_lift, a_out, a_vec, a_bias):
            acc[...] = jnp.zeros_like(acc)

    pad_rows(x_s, tok_ref, length)
    pad_rows(z_s, cot_ref, length)
    out_bias, gain, shift, drop_bias = (vec_ref[i : i + 1, :] for i in range(4, 8))
    mixed = mixed_ref[...].reshape(total, width)
    dz = z_s[...].reshape(total, width)
    dz_f = dz.astype(F32)
    middle = x_s[...].reshape(total, width).astype(F32) + nn(mixed, w_out_ref[...]) + out_bias
    normal, inverse = normalise(middle)
    normed = (normal * gain + shift).astype(BF16)
    result = middle + drop_bias
    d_normed = jnp.zeros((total, width), F32)
    for c in range(0, hidden_width, chunk):
        part = slice(c, c + chunk)
        hidden = nn(normed, w_lift_ref[:, part]) + lift_bias_ref[:, part]
        cdf = 0.5 + 0.5 * lax.erf(hidden * ROOT_HALF)
        bell = jnp.exp(hidden * hidden * -0.5) * GAUSS
        active = (hidden * cdf).astype(BF16)
        d_active = nt(dz, w_drop_ref[part, :])
        d_hidden_f = d_active * (cdf + hidden * bell)
        d_hidden = d_hidden_f.astype(BF16)
        result = result + nn(active, w_drop_ref[part, :])
        d_normed = d_normed + nt(d_hidden, w_lift_ref[:, part])
        a_drop[part, :] += tn(active, dz)
        a_lift[:, part] += tn(normed, d_hidden)
        a_bias[:, part] += fold(d_hidden.astype(F32))
    out = result.astype(BF16)
    for j in range(images):
        out_ref[j] = out[j * rows : j * rows + length]
    d_middle = dz_f + norm_back(d_normed, normal, inverse, gain)
    d_middle_ref[...] = d_middle.reshape(images, rows, width)
    d_attended = d_middle.astype(BF16)
    d_mixed_ref[...] = nt(d_attended, w_out_ref[...]).astype(BF16).reshape(images, rows, width)
    a_out[...] += tn(mixed, d_attended)
    a_vec[0] += fold(d_attended.astype(F32))
    a_vec[1] += fold(d_normed * normal)
    a_vec[2] += fold(d_normed)
    a_vec[3] += fold(dz_f)

    @pl.when(step == pl.num_programs(0) - 1)
    def _():
        columns = jnp.sum(a_bias[...], axis=0, keepdims=True)
        vector_rows = [jnp.sum(a_vec[...], axis=1)]
        vector_rows += [columns[:, c : c + width] for c in range(0, hidden_width, width)]
        vector_rows += [jnp.zeros((VEC_ROWS - 4 - hidden_width // width, width), F32)]
        vectors = jnp.concatenate(vector_rows, axis=0).astype(BF16)
        deep, tall = a_drop.shape[0] // 4, width // 4
        for dest, slot, half, core in quarters(index, keep_a, send_a):
            first = pl.multiple_of((2 * half + core) * deep, 8)
            dest[slot, 0:deep, :] = a_drop[pl.ds(first, deep), :].astype(BF16)
            dest[slot, deep : deep + VEC_ROWS, :] = vectors
        for dest, slot, half, core in quarters(index, keep_b, send_b):
            rows_of = pl.ds(pl.multiple_of((2 * half + core) * tall, 8), tall)
            blocks = hidden_width // width
            for k in range(blocks):
                dest[slot, k * tall : (k + 1) * tall, :] = a_lift[
                    rows_of, k * width : (k + 1) * width
                ].astype(BF16)
            dest[slot, blocks * tall : (blocks + 1) * tall, :] = a_out[rows_of, :].astype(BF16)


def back_kernel(length, *refs):
    proj_ref, d_mixed_ref = refs[:2]
    d_proj_ref = refs[-1]
    images, rows, wide = d_proj_ref.shape
    width = wide // 3
    live = lax.broadcasted_iota(jnp.int32, (rows, 2 * rows), 0) < length
    for j in range(images):
        for c in range(0, width, PAIR):
            query = split_pair(proj_ref[j, :, c : c + PAIR] * jnp.asarray(SCALE, BF16))
            key = proj_ref[j, :, width + c : width + c + PAIR]
            value = proj_ref[j, :, 2 * width + c : 2 * width + c + PAIR]
            d_mixed = split_pair(d_mixed_ref[j, :, c : c + PAIR])
            scores = jnp.where(live, nt(key, query), -1e30)
            top = jnp.max(scores, axis=0, keepdims=True)
            weights = jnp.exp(scores - top)
            probs = weights * (1.0 / jnp.sum(weights, axis=0, keepdims=True))
            d_probs = nt(value, d_mixed)
            delta = jnp.sum(probs * d_probs, axis=0, keepdims=True)
            d_scores = (probs * (d_probs - delta)).astype(BF16)
            d_value = nn(probs.astype(BF16), d_mixed)
            d_key = nn(d_scores, query)
            d_query = join_pair(tn(d_scores, key)) * SCALE
            d_proj_ref[j, :, c : c + PAIR] = d_query.astype(BF16)
            d_proj_ref[j, :, width + c : width + c + PAIR] = d_key.astype(BF16)
            d_proj_ref[j, :, 2 * width + c : 2 * width + c + PAIR] = d_value.astype(BF16)


def weight_kernel(index, normed_ref, d_proj_ref, keep, send, a_qkv, a_proj):
    step = pl.program_id(0)
    images, rows, wide = d_proj_ref.shape
    width = wide // 3
    total = images * rows

    @pl.when(step == 0)
    def _():
        for acc in (a_qkv, a_proj):
            acc[...] = jnp.zeros_like(acc)

    d_proj = d_proj_ref[...].reshape(total, wide)
    a_qkv[...] += tn(normed_ref[...].reshape(total, width), d_proj)
    a_proj[...] += fold(d_proj.astype(F32))

    @pl.when(step == pl.num_programs(0) - 1)
    def _():
        columns = jnp.sum(a_proj[...], axis=0, keepdims=True)
        vectors = jnp.concatenate(
            [columns[:, :width], columns[:, 2 * width :], jnp.zeros((VEC_ROWS - 2, width), F32)], axis=0
        ).astype(BF16)
        tall = width // 4
        for dest, slot, half, core in quarters(index, keep, send):
            rows_of = pl.ds(pl.multiple_of((2 * half + core) * tall, 8), tall)
            for k in range(3):
                dest[slot, k * tall : (k + 1) * tall, :] = a_qkv[
                    rows_of, k * width : (k + 1) * width
                ].astype(BF16)
            dest[slot, 3 * tall : 3 * tall + VEC_ROWS, :] = vectors


def input_kernel(length, tok_ref, d_proj_ref, d_middle_ref, w_ref, vec_ref, in_grad_ref, g_vec_ref):
    images, rows, wide = d_proj_ref.shape

    @pl.when(pl.program_id(0) == 0)
    def _():
        g_vec_ref[...] = jnp.zeros_like(g_vec_ref)

    d_normed = nt(d_proj_ref[...].reshape(images * rows, wide), w_ref[...])
    gain = vec_ref[0:1, :]
    for j in range(images):
        normal, inverse = normalise(tok_ref[j].astype(F32))
        grad = d_normed[j * rows : j * rows + length]
        in_grad_ref[j] = (
            d_middle_ref[j, 0:length, :] + norm_back(grad, normal, inverse, gain)
        ).astype(BF16)
        g_vec_ref[0:1, :] += jnp.sum(grad * normal, axis=0, keepdims=True)
        g_vec_ref[1:2, :] += jnp.sum(grad, axis=0, keepdims=True)


def placed(full, index, pieces):
    half = pieces[0].shape[0]
    core, y = index[1], index[2]
    spots = ((core, y), (core, 1 - y), (1 - core, y), (1 - core, 1 - y))
    for (where, side), piece in zip(spots, pieces):
        full[where, pl.ds(pl.multiple_of(side * half, 8), half), :] = piece[...].astype(F32)


def own_half(index, row):
    half = row.shape[-1] // 2
    return jnp.where(index[0] == 0, row[:, :half], row[:, half:])[0]


def unpack_outer_kernel(index, *refs):
    a_pieces, b_pieces = refs[0:4], refs[4:8]
    g_drop, g_lift, g_out, g_out_bias, g_gain, g_shift, g_drop_bias, g_lift_bias, a_s, b_s = refs[8:]
    placed(a_s, index, a_pieces)
    placed(b_s, index, b_pieces)
    width = g_out.shape[1]
    deep, tall = g_drop.shape[0] // 2, g_out.shape[0] // 2
    blocks = g_lift.shape[1] // width
    for core in range(2):
        g_drop[core * deep : (core + 1) * deep, :] = a_s[core, 0:deep, :]
        for k in range(blocks):
            g_lift[core * tall : (core + 1) * tall, k * width : (k + 1) * width] = b_s[
                core, k * tall : (k + 1) * tall, :
            ]
        g_out[core * tall : (core + 1) * tall, :] = b_s[core, blocks * tall : (blocks + 1) * tall, :]
    vectors = a_s[0, deep : deep + VEC_ROWS, :]
    for i, ref in enumerate((g_out_bias, g_gain, g_shift, g_drop_bias)):
        ref[...] = own_half(index, vectors[i : i + 1, :])
    for k in range(blocks // 2):
        row = jnp.where(
            index[0] == 0,
            vectors[4 + k : 5 + k, :],
            vectors[4 + blocks // 2 + k : 5 + blocks // 2 + k, :],
        )
        g_lift_bias[k * width : (k + 1) * width] = row[0]


def unpack_inner_kernel(index, *refs):
    pieces, late = refs[0:4], refs[4]
    g_qkv, g_query, g_value, g_gain, g_shift, c_s = refs[5:]
    placed(c_s, index, pieces)
    width = late.shape[1]
    tall = g_qkv.shape[0] // 2
    for core in range(2):
        for k in range(3):
            g_qkv[core * tall : (core + 1) * tall, k * width : (k + 1) * width] = c_s[
                core, k * tall : (k + 1) * tall, :
            ]
    vectors = c_s[0, 3 * tall : 3 * tall + VEC_ROWS, :]
    g_query[...] = own_half(index, vectors[0:1, :])
    g_value[...] = own_half(index, vectors[1:2, :])
    g_gain[...] = own_half(index, late[0:1, :])
    g_shift[...] = own_half(index, late[1:2, :])


VEC_ROWS = 16


VMEM_LIMIT = 60 * 1024 * 1024
PARAMS = pltpu.CompilerParams(vmem_limit_bytes=VMEM_LIMIT)
SCALARS = pl.BlockSpec(memory_space=pltpu.SMEM)


def whole(*shape):
    return pl.BlockSpec(shape, lambda i: (0,) * len(shape))


def whole_like(arrays):
    return [whole(*a.shape) for a in arrays]


def per_step(*shape):
    return pl.BlockSpec(shape, lambda i: (i,) + (0,) * (len(shape) - 1))


def shape_of(dtype, *shape):
    return jax.ShapeDtypeStruct(shape, dtype)


def cost(microseconds):
    return pl.CostEstimate(flops=int(microseconds * 1e3), bytes_accessed=1, transcendentals=0)


def forward_attention(index, tokens, vectors, pieces):
    images, length, width = tokens.shape
    rows = -(-length // 16) * 16
    group = 2 if images % 2 == 0 else 1
    return pl.pallas_call(
        functools.partial(attend_kernel, length),
        grid=(images // group,),
        in_specs=[SCALARS, per_step(group, length, width), *whole_like((vectors, *pieces))],
        out_specs=[
            per_step(group, rows, width),
            per_step(group, rows, 3 * width),
            per_step(group, rows, width),
            whole(width, 3 * width),
        ],
        out_shape=[
            shape_of(BF16, images, rows, width),
            shape_of(BF16, images, rows, 3 * width),
            shape_of(BF16, images, rows, width),
            shape_of(BF16, width, 3 * width),
        ],
        scratch_shapes=[pltpu.VMEM((group, rows, width), BF16)],
        compiler_params=PARAMS,
        cost_estimate=cost(1),
        name="attend",
    )(index, tokens, vectors, *pieces)


def mlp_both_ways(index, tokens, cotangent, mixed, vectors, lift_bias, pieces):
    images, length, width = tokens.shape
    rows = mixed.shape[1]
    ff = lift_bias.shape[1]
    group = 2 if images % 2 == 0 else 1
    a_rows = ff // 4 + VEC_ROWS
    b_rows = (width // 4) * (ff // width + 1)
    return pl.pallas_call(
        functools.partial(mlp_kernel, length, 256),
        grid=(images // group,),
        in_specs=[
            SCALARS,
            per_step(group, length, width),
            per_step(group, length, width),
            per_step(group, rows, width),
            *whole_like((vectors, lift_bias, *pieces)),
        ],
        out_specs=[
            per_step(group, length, width),
            per_step(group, rows, width),
            per_step(group, rows, width),
            whole(2, a_rows, width),
            whole(2, a_rows, width),
            whole(2, b_rows, width),
            whole(2, b_rows, width),
        ],
        out_shape=[
            shape_of(BF16, images, length, width),
            shape_of(F32, images, rows, width),
            shape_of(BF16, images, rows, width),
            shape_of(BF16, 2, a_rows, width),
            shape_of(BF16, 2, a_rows, width),
            shape_of(BF16, 2, b_rows, width),
            shape_of(BF16, 2, b_rows, width),
        ],
        scratch_shapes=[
            pltpu.VMEM((group, rows, width), BF16),
            pltpu.VMEM((group, rows, width), BF16),
            pltpu.VMEM((width, width), BF16),
            pltpu.VMEM((width, ff), BF16),
            pltpu.VMEM((ff, width), BF16),
            pltpu.VMEM((ff, width), F32),
            pltpu.VMEM((width, ff), F32),
            pltpu.VMEM((width, width), F32),
            pltpu.VMEM((4, 8, width), F32),
            pltpu.VMEM((8, ff), F32),
        ],
        compiler_params=PARAMS,
        cost_estimate=cost(1),
        name="mlp",
    )(index, tokens, cotangent, mixed, vectors, lift_bias, *pieces)


def attention_backward(projected, d_mixed, length, first, count, earlier):
    images, rows, wide = projected.shape
    group = 2 if images % 2 == 0 else 1
    start = first // group

    def at(*shape):
        return pl.BlockSpec(shape, lambda i: (i + start if start else i, 0, 0))

    more = [] if earlier is None else [earlier]
    return pl.pallas_call(
        functools.partial(back_kernel, length),
        grid=(count // group,),
        in_specs=[at(group, rows, wide), at(group, rows, wide // 3)]
        + [pl.BlockSpec(memory_space=pl.ANY)] * len(more),
        out_specs=at(group, rows, wide),
        out_shape=shape_of(BF16, images, rows, wide),
        input_output_aliases={2: 0} if more else {},
        compiler_params=PARAMS,
        cost_estimate=cost(count / 2),
        name="back",
    )(projected, d_mixed, *more)


def qkv_weight_gradient(index, normed, d_proj):
    images, rows, width = normed.shape
    group = 2 if images % 2 == 0 else 1
    c_rows = 3 * width // 4 + VEC_ROWS
    return pl.pallas_call(
        weight_kernel,
        grid=(images // group,),
        in_specs=[SCALARS, per_step(group, rows, width), per_step(group, rows, 3 * width)],
        out_specs=[whole(2, c_rows, width)] * 2,
        out_shape=[shape_of(BF16, 2, c_rows, width)] * 2,
        scratch_shapes=[
            pltpu.VMEM((width, 3 * width), F32),
            pltpu.VMEM((8, 3 * width), F32),
        ],
        compiler_params=PARAMS,
        cost_estimate=cost(1),
        name="qkv_weight_gradient",
    )(index, normed, d_proj)


def input_gradient(tokens, d_proj, d_middle, w_qkv, vectors):
    images, length, width = tokens.shape
    rows = d_proj.shape[1]
    group = 2 if images % 2 == 0 else 1
    return pl.pallas_call(
        functools.partial(input_kernel, length),
        grid=(images // group,),
        in_specs=[
            per_step(group, length, width),
            per_step(group, rows, 3 * width),
            per_step(group, rows, width),
            *whole_like((w_qkv, vectors)),
        ],
        out_specs=[per_step(group, length, width), whole(8, width)],
        out_shape=[shape_of(BF16, images, length, width), shape_of(F32, 8, width)],
        compiler_params=PARAMS,
        cost_estimate=cost(1),
        name="input_gradient",
    )(tokens, d_proj, d_middle, w_qkv, vectors)


def unpack_outer(index, a_pieces, b_pieces, width, ff):
    half = width // 2
    return pl.pallas_call(
        unpack_outer_kernel,
        in_specs=[SCALARS] + [pl.BlockSpec(memory_space=pltpu.VMEM)] * 8,
        out_shape=[
            shape_of(F32, ff // 2, width),
            shape_of(F32, half, ff),
            shape_of(F32, half, width),
            *[shape_of(F32, half)] * 4,
            shape_of(F32, ff // 2),
        ],
        scratch_shapes=[
            pltpu.VMEM((2, 2 * a_pieces[0].shape[0], width), F32),
            pltpu.VMEM((2, 2 * b_pieces[0].shape[0], width), F32),
        ],
        compiler_params=PARAMS,
        cost_estimate=cost(3),
        name="unpack_outer",
    )(index, *a_pieces, *b_pieces)


def unpack_inner(index, pieces, late):
    width = late.shape[1]
    half = width // 2
    return pl.pallas_call(
        unpack_inner_kernel,
        in_specs=[SCALARS] + [pl.BlockSpec(memory_space=pltpu.VMEM)] * 5,
        out_shape=[shape_of(F32, half, 3 * width), *[shape_of(F32, half)] * 4],
        scratch_shapes=[pltpu.VMEM((2, 2 * pieces[0].shape[0], width), F32)],
        compiler_params=PARAMS,
        cost_estimate=cost(2),
        name="unpack_inner",
    )(index, *pieces, late)


AXES = ("rep", "fsdp")


class Butterfly:
    def __init__(self):
        rep, x = lax.axis_index("rep"), lax.axis_index("fsdp")
        self.x, self.core, self.y = x, rep & 1, (rep >> 1) & 1
        self.index = jnp.stack([self.x, self.core, self.y]).astype(jnp.int32)

    def swap(self, v, rep_mask, x_mask=0):
        pairs = [
            (rep * 2 + x, (rep ^ rep_mask) * 2 + (x ^ x_mask)) for rep in range(16) for x in range(2)
        ]
        return lax.ppermute(v, AXES, pairs)

    def over_x(self, v):
        return self.swap(v, 0, 1)

    def over_core(self, v):
        return self.swap(v, 1)

    def over_y(self, v):
        return self.swap(v, 2)

    def over_z(self, v, mask):
        return self.swap(v, 4 * mask)

    def gather_weight(self, own):
        half = own.shape[0] // 2
        near = self.over_x(lax.dynamic_slice_in_dim(own, self.core * half, half, 0))
        return own, near, self.over_core(near)

    def gather_vectors(self, own):
        other = self.over_x(own)
        first = self.x == 0
        return jnp.where(first, own, other), jnp.where(first, other, own)

    def halves(self, v):
        return v.reshape(2, v.shape[0] // 2, v.shape[1])

    def to_send(self, v):
        return lax.dynamic_index_in_dim(self.halves(v), 1 - self.y, 0, keepdims=False)

    def to_keep(self, v):
        return lax.dynamic_index_in_dim(self.halves(v), self.y, 0, keepdims=False)

    def over_both_z(self, part):
        part = part + self.over_z(part, 1)
        return part + self.over_z(part, 2)

    def pieces(self, part):
        across = self.over_y(part)
        return part, across, self.over_core(part), self.over_core(across)

    def reduce_late(self, v):
        v = v + self.over_core(v)
        v = v + self.over_x(v)
        v = v + self.over_y(v)
        v = v + self.over_z(v, 1)
        return v + self.over_z(v, 2)


class Collective:
    def __init__(self):
        self.index = jnp.zeros((3,), jnp.int32)

    def gather_weight(self, own):
        full = lax.all_gather(own, "fsdp", axis=0, tiled=True)
        quarter = full.shape[0] // 4
        return full[: 2 * quarter], full[2 * quarter : 3 * quarter], full[3 * quarter :]

    def gather_vectors(self, own):
        full = lax.all_gather(own, "fsdp", axis=0)
        shards, rows, columns = full.shape
        halves = full.reshape(2, shards // 2, rows, columns)
        both = halves.transpose(0, 2, 1, 3).reshape(2, rows, shards // 2 * columns)
        return both[0], both[1]

    def reduce(self, v):
        owned = lax.psum_scatter(v.astype(BF16), "fsdp", scatter_dimension=0, tiled=True)
        return lax.psum(owned, "rep").astype(F32)


def after(*arrays):
    return lax.optimization_barrier(arrays)


def assembled(keep, send, first, tall, blocks):
    order = (keep[0], send[0], keep[1], send[1])
    return jnp.concatenate(
        [
            jnp.concatenate(
                [q[first + k * tall : first + (k + 1) * tall] for k in range(blocks)], axis=1
            )
            for q in order
        ],
        axis=0,
    )


def per_device(
    tokens,
    gain_one,
    shift_one,
    qkv_weight,
    query_bias,
    value_bias,
    out_weight,
    out_bias,
    gain_two,
    shift_two,
    lift_weight,
    lift_bias,
    drop_weight,
    drop_bias,
    cotangent,
    swaps,
):
    length, width = tokens.shape[1:]
    plan = Butterfly() if swaps else Collective()
    shard = gain_one.shape[0]
    own = jnp.concatenate(
        [
            v.reshape(-1, shard)
            for v in (
                gain_one,
                shift_one,
                query_bias,
                value_bias,
                out_bias,
                gain_two,
                shift_two,
                drop_bias,
                lift_bias,
            )
        ],
        axis=0,
    )
    low, high = plan.gather_vectors(own)
    vectors = jnp.concatenate([low[:8], high[:8]], axis=1).astype(F32)
    parts = 2 * width // (2 * shard)
    full_lift_bias = (
        jnp.stack([low[8:], high[8:]])
        .reshape(2, lift_bias.shape[0] // shard, parts // 2, shard)
        .transpose(0, 2, 1, 3)
        .reshape(1, -1)
        .astype(F32)
    )
    qkv = plan.gather_weight(qkv_weight)
    outer = [
        piece for w in (out_weight, lift_weight, drop_weight) for piece in plan.gather_weight(w)
    ]
    index = plan.index
    normed, projected, mixed, full_qkv = forward_attention(index, tokens, vectors, qkv)
    output, d_middle, d_mixed, keep_a, send_a, keep_b, send_b = mlp_both_ways(
        index, tokens, cotangent, mixed, vectors, full_lift_bias, outer
    )
    ff = full_lift_bias.shape[1]
    images = tokens.shape[0]
    backward = functools.partial(attention_backward, projected, d_mixed, length)
    if swaps:
        got_a, got_b = plan.over_core(send_a), plan.over_core(send_b)
        d_proj = backward(0, 2, None)
        d_proj, keep_a, keep_b = after(d_proj, keep_a, keep_b)
        other_a, other_b = keep_a[1] + got_a[1], keep_b[1] + got_b[1]
        d_proj, other_a, other_b = after(d_proj, other_a, other_b)
        over_a, over_b = plan.over_x(other_a), plan.over_x(other_b)
        d_proj = backward(2, images - 4, d_proj)
        d_proj, keep_a = after(d_proj, keep_a)
        mine_a = keep_a[0] + got_a[0] + over_a
        d_proj, out_a = after(d_proj, plan.to_send(mine_a))
        low_a = plan.over_y(out_a)
        d_proj = backward(images - 2, 2, d_proj)
        d_proj, keep_b, mine_a = after(d_proj, keep_b, mine_a)
        mine_b = keep_b[0] + got_b[0] + over_b
        d_proj, out_b = after(d_proj, plan.to_send(mine_b))
        low_b = plan.over_y(out_b)
        part_a = plan.to_keep(mine_a) + low_a
        d_proj, part_a = after(d_proj, part_a)
        keep_c, send_c = qkv_weight_gradient(index, normed, d_proj)
        got_c = plan.over_core(send_c)
        d_proj, other_c = after(d_proj, keep_c[1] + got_c[1])
        over_c = plan.over_x(other_c)
        input_grad, g_first = input_gradient(tokens, d_proj, d_middle, full_qkv, vectors)
        g_first, keep_c = after(g_first, keep_c)
        mine_c = keep_c[0] + got_c[0] + over_c
        part_c = plan.to_keep(mine_c) + plan.over_y(plan.to_send(mine_c))
        part_b = plan.to_keep(mine_b) + low_b
        c_pieces = plan.pieces(plan.over_both_z(part_c))
        a_pieces = plan.pieces(plan.over_both_z(part_a))
        b_pieces = plan.pieces(plan.over_both_z(part_b))
        late = plan.reduce_late(g_first)
        g_drop, g_lift, g_out, g_out_bias, g_gain_two, g_shift_two, g_drop_bias, g_lift_bias = (
            unpack_outer(index, a_pieces, b_pieces, width, ff)
        )
        g_qkv, g_query, g_value, g_gain_one, g_shift_one = unpack_inner(index, c_pieces, late)
    else:
        d_proj = backward(0, images, None)
        keep_c, send_c = qkv_weight_gradient(index, normed, d_proj)
        input_grad, g_first = input_gradient(tokens, d_proj, d_middle, full_qkv, vectors)
        tall = width // 4
        g_drop = plan.reduce(assembled(keep_a, send_a, 0, ff // 4, 1))
        g_lift = plan.reduce(assembled(keep_b, send_b, 0, tall, ff // width))
        g_out = plan.reduce(assembled(keep_b, send_b, ff // width * tall, tall, 1))
        g_qkv = plan.reduce(assembled(keep_c, send_c, 0, tall, 3))
        rows_a = keep_a[0, ff // 4 :]
        rows_c = keep_c[0, 3 * tall :]
        g_out_bias, g_gain_two, g_shift_two, g_drop_bias = (plan.reduce(rows_a[i]) for i in range(4))
        g_lift_bias = plan.reduce(rows_a[4 : 4 + ff // width].reshape(-1))
        g_query, g_value = plan.reduce(rows_c[0]), plan.reduce(rows_c[1])
        g_gain_one, g_shift_one = plan.reduce(g_first[0]), plan.reduce(g_first[1])
    return (
        output,
        input_grad,
        g_gain_one,
        g_shift_one,
        g_qkv,
        g_query,
        g_value,
        g_out,
        g_out_bias,
        g_gain_two,
        g_shift_two,
        g_lift,
        g_lift_bias,
        g_drop,
        g_drop_bias,
    )


def solution(mesh):
    spread = P(("rep", "fsdp"), None, None)
    vector, matrix = P("fsdp"), P("fsdp", None)
    in_specs = (
        spread,
        vector,
        vector,
        matrix,
        vector,
        vector,
        matrix,
        vector,
        vector,
        vector,
        matrix,
        vector,
        matrix,
        vector,
        spread,
    )
    out_specs = (
        spread,
        spread,
        vector,
        vector,
        matrix,
        vector,
        vector,
        matrix,
        vector,
        vector,
        vector,
        matrix,
        vector,
        matrix,
        vector,
    )
    swaps = mesh.shape["rep"] == 16 and mesh.shape["fsdp"] == 2
    return jax.shard_map(
        functools.partial(per_device, swaps=swaps),
        mesh=mesh,
        in_specs=in_specs,
        out_specs=out_specs,
        check_vma=False,
    )
```

time: 296 us -> 185 us (0.62)
  blocking collectives: 74.6 us -> 0 us
  waiting for transfers between devices: 121 us -> 50.8 us
  starting transfers between devices: 0.45 us -> 29.1 us
  Pallas kernels: 59.3 us -> 76.5 us
  between operations: 15.6 us -> 1.06 us
  local copies, waits for them, and re-layouts: 14.4 us -> 21.6 us
  other arithmetic: 10.8 us -> 5.14 us
    reduce_scatter x4 -> x0, waiting for transfers between devices: 66.4 us -> none  [reduced(): lax.psum_scatter(v.astype(BF16), 'fsdp', scatter_dimension=0, tiled=True)]
    ppermute x0 -> x38, waiting for transfers between devices: none -> 50.8 us  [swap(): return lax.ppermute(v, AXES, pairs)]
    psum x1 -> x0, waiting for transfers between devices: 50.7 us -> none  [reduced(): return lax.psum(owned, 'rep').astype(F32)]
    all_gather x4 -> x0, blocking collectives: 35 us -> none  [gather(): return lax.all_gather(v, 'fsdp', axis=0, tiled=True)]
    psum x1 -> x0, blocking collectives: 32.6 us -> none  [reduced(): return lax.psum(owned, 'rep').astype(F32)]
    ppermute x0 -> x38, starting transfers between devices: none -> 29.1 us  [swap(): return lax.ppermute(v, AXES, pairs)]
    pallas_call x1 -> x7, Pallas kernels: 20.8 us -> 37.4 us  [the longest x3 18.6 us: attention_backward(): pl.pallas_call(functools.partial(back_kernel, length), grid=(count // gro...]
    convert_element_type x14 -> x2, other arithmetic: 10.2 us -> 0.68 us  [the longest x1 0.67 us: per_device(): vectors = jnp.concatenate([low[:8], high[:8]], axis=1).astype(F32)]
  transfers between devices with their start and end apart: 7 -> 38, of which waited for: 5 -> 13; matrix products, arithmetic and copies ran while one was open for 6% -> 9% of each run, Pallas kernels for 10% -> 21%
where the time goes in v2:
time: 185 us; the launch traced here: 184 us
  Pallas kernels  76.5 us (41%)
  waiting for transfers between devices  50.8 us (27%)
  starting transfers between devices  29.1 us (16%)
  local copies, waits for them, and re-layouts  21.6 us (12%)
  other arithmetic  5.14 us (3%)
    ppermute x38, waiting for transfers between devices, swap(): return lax.ppermute(v, AXES, pairs)  50.8 us
    ppermute x38, starting transfers between devices, swap(): return lax.ppermute(v, AXES, pairs)  29.1 us
    pallas_call x1, Pallas kernels, mlp_both_ways(): pl.pallas_call(functools.partial(mlp_kernel, length, 256), grid=(images /...  28.9 us
    pallas_call x3, Pallas kernels, attention_backward(): pl.pallas_call(functools.partial(back_kernel, length), grid=(count // gro...  18.6 us
    pallas_call x1, Pallas kernels, forward_attention(): pl.pallas_call(functools.partial(attend_kernel, length), grid=(images //...  10.3 us
    unnamed x60, local copies, waits for them, and re-layouts  9.02 us
    pallas_call x1, Pallas kernels, input_gradient(): pl.pallas_call(functools.partial(input_kernel, length), grid=(images // g...  7.41 us
    reshape x9, local copies, waits for them, and re-layouts, per_device(): v.reshape(-1, shard)  6.16 us
  transfers between devices with their start and end apart: 38, of which 13 were waited for; matrix products, arithmetic and copies ran while one was open for 9% of the time, Pallas kernels for 21%

profile of v2, /device:TPU:0, one launch (start us, length us, event | category | flops | bytes accessed | tf_op | source)
XLA Modules:
  0.0 184.2 jit_solution(16591963944838491184)
XLA Ops:
  0.7 0.8 reshape.91
  1.5 0.7 reshape.92
  2.1 0.7 reshape.93
  2.8 0.7 reshape.94
  3.4 0.7 reshape.95
  4.1 0.7 reshape.96
  4.7 0.7 reshape.97
  5.4 0.7 reshape.98
  6.1 0.8 reshape.99
  6.9 3.0 %collective-permute-start = (bf16[12,192]{1,0:T(8,128)(2,1)S(1)}, bf16[12,192]{1,0:T(8,128)(2,1)S(1)}, u32[]{:S(2)}, u32[]{:S(2)}) collective-permute-start(bf16[12,192]{1,0:T(8,128)(2,1)S(1)} %concatenate.6), channel_id=1, source_target_pairs={{0,1},{1,0},{2,3},{3,2},{4,5},{5,4},{6,7},{7,6},{8,9},{9,8},{10,11... | collective-permute-start | bytes 13832 | tf_op jit(solution)/shard_map/ppermute | solution.py:595
  9.9 1.6 constant_dynamic-slice_fusion.3
  11.5 1.5 constant_dynamic-slice_fusion.2
  13.1 2.0 %collective-permute-start.3 = (bf16[96,384]{1,0:T(8,128)(2,1)}, bf16[96,384]{1,0:T(8,128)(2,1)}, u32[]{:S(2)}, u32[]{:S(2)}) collective-permute-start(bf16[96,384]{1,0:T(8,128)(2,1)} %constant_dynamic-slice_fusion.2), channel_id=1, source_target_pairs={{0,1},{1,0},{2,3},{3,2},{4,5},{5,4},{6,7},{7,6},{8,9},{9,8},{10,11... | collective-permute-start | bytes 221192 | tf_op jit(solution)/shard_map/ppermute | solution.py:595
  15.1 1.7 constant_dynamic-slice_fusion.1
  16.8 0.7 constant_dynamic-slice_fusion
  17.5 2.0 %collective-permute-start.7 = (bf16[384,384]{1,0:T(8,128)(2,1)}, bf16[384,384]{1,0:T(8,128)(2,1)S(1)}, u32[]{:S(2)}, u32[]{:S(2)}) collective-permute-start(bf16[384,384]{1,0:T(8,128)(2,1)} %constant_dynamic-slice_fusion), channel_id=1, source_target_pairs={{0,1},{1,0},{2,3},{3,2},{4,5},{5,4},{6,7},{7,6},{8,9},{9,8},{10,11... | collective-permute-start | bytes 884744 | tf_op jit(solution)/shard_map/ppermute | solution.py:595
  19.5 0.6 pad_add_fusion.index
  20.1 1.2 copy.33.tok_ref
  21.3 1.2 copy.34.cot_ref
  22.5 5.4 %collective-permute-done.5.lift_near = bf16[96,1536]{1,0:T(8,128)(2,1)S(1)} collective-permute-done((bf16[96,1536]{1,0:T(8,128)(2,1)}, bf16[96,1536]{1,0:T(8,128)(2,1)S(1)}, u32[]{:S(2)}, u32[]{:S(2)}) %collective-permute-start.5) | collective-permute-done | bytes 294944 | tf_op jit(solution)/shard_map/ppermute | solution.py:595
  28.0 4.8 %collective-permute-done.7.drop_near = bf16[384,384]{1,0:T(8,128)(2,1)S(1)} collective-permute-done((bf16[384,384]{1,0:T(8,128)(2,1)}, bf16[384,384]{1,0:T(8,128)(2,1)S(1)}, u32[]{:S(2)}, u32[]{:S(2)}) %collective-permute-start.7) | collective-permute-done | bytes 294944 | tf_op jit(solution)/shard_map/ppermute | solution.py:595
  33.4 0.7 reshape.104.lift_bias_ref
  34.2 0.7 maximum_convert_fusion.vec_ref
  34.8 0.7 copy-done.16
  35.5 10.3 %attend.1 = (bf16[8,208,384]{2,1,0:T(8,128)(2,1)}, bf16[8,208,1152]{2,1,0:T(8,128)(2,1)}, bf16[8,208,384]{2,1,0:T(8,128)(2,1)}, bf16[384,1152]{1,0:T(8,128)(2,1)}) custom-call(s32[3]{0:T(128)} %pad_add_fusion.index, bf16[8,197,384]{2,1,0:T(8,128)(2,1)} %copy.33.tok_ref, f32[8,384]{1,0:T(8,128)} %maximum_convert_fusion.vec_ref, bf16[192,1152]{1,0:T(8,128)(2,1)} %own.1, ...), custom_call_target="tpu_custom_call" | custom-call | flops 1000 | bytes 1 | tf_op jit(solution)/shard_map/attend/pallas_call | solution.py:406
  46.7 28.9 %mlp.1 = (bf16[8,197,384]{2,1,0:T(8,128)(2,1)}, f32[8,208,384]{2,1,0:T(8,128)}, bf16[8,208,384]{2,1,0:T(8,128)(2,1)}, bf16[2,400,384]{2,1,0:T(8,128)(2,1)}, bf16...) custom-call(s32[3]{0:T(128)} %pad_add_fusion.index, ...), custom_call_target="tpu_custom_call" | custom-call | flops 1000 | bytes 1 | tf_op jit(solution)/shard_map/mlp/pallas_call | solution.py:436
  76.2 5.3 %back.3.refs_2_ = bf16[8,208,1152]{2,1,0:T(8,128)(2,1)} custom-call(bf16[8,208,1152]{2,1,0:T(8,128)(2,1)} %get-tuple-element.66.refs_0_, bf16[8,208,384]{2,1,0:T(8,128)(2,1)} %get-tuple-element.67.refs_1_), custom_call_target="tpu_custom_call" | custom-call | flops 1000 | bytes 1 | tf_op jit(solution)/shard_map/back/pallas_call | solution.py:491
  81.5 0.8 fusion.5
  82.7 8.1 %back.4.refs_2_ = bf16[8,208,1152]{2,1,0:T(8,128)(2,1)} custom-call(bf16[8,208,1152]{2,1,0:T(8,128)(2,1)} %get-tuple-element.66.refs_0_, bf16[8,208,384]{2,1,0:T(8,128)(2,1)} %get-tuple-element.67.refs_1_, bf16[8,208,1152]{2,1,0:T(8,128)(2,1)} %back.3.refs_2_), custom_call_target="tpu_custom_call", output_to_operand_aliasing={{}: (2, {})} | custom-call | flops 2000 | bytes 1 | tf_op jit(solution)/shard_map/back/pallas_call | solution.py:491
  90.8 1.7 collective-permute-start.12
  92.5 1.0 fusion.4
  93.6 5.2 %back.5.d_proj_ref = bf16[8,208,1152]{2,1,0:T(8,128)(2,1)} custom-call(bf16[8,208,1152]{2,1,0:T(8,128)(2,1)} %get-tuple-element.66.refs_0_, bf16[8,208,384]{2,1,0:T(8,128)(2,1)} %get-tuple-element.67.refs_1_, bf16[8,208,1152]{2,1,0:T(8,128)(2,1)} %back.4.refs_2_), custom_call_target="tpu_custom_call", output_to_operand_aliasing={{}: (2, {})} | custom-call | flops 1000 | bytes 1 | tf_op jit(solution)/shard_map/back/pallas_call | solution.py:491
  98.8 1.5 collective-permute-start.13
  100.3 1.3 collective-permute-done.12
  101.7 2.9 %collective-permute-done.13 = bf16[200,384]{1,0:T(8,128)(2,1)S(1)} collective-permute-done((bf16[200,384]{1,0:T(8,128)(2,1)S(1)}, bf16[200,384]{1,0:T(8,128)(2,1)S(1)}, u32[]{:S(2)}, u32[]{:S(2)}) %collective-permute-start.13) | collective-permute-done | bytes 153632 | tf_op jit(solution)/shard_map/ppermute | solution.py:595
  104.6 6.0 %qkv_weight_gradient.1 = (bf16[2,304,384]{2,1,0:T(8,128)(2,1)}, bf16[2,304,384]{2,1,0:T(8,128)(2,1)}) custom-call(s32[3]{0:T(128)} %pad_add_fusion.index, bf16[8,208,384]{2,1,0:T(8,128)(2,1)} %get-tuple-element.87.normed_ref, bf16[8,208,1152]{2,1,0:T(8,128)(2,1)} %back.5.d_proj_ref), custom_call_target="tpu_custom_call" | custom-call | flops 1000 | bytes 1 | tf_op jit(solution)/shard_map/qkv_weight_gradient/pallas_call | solution.py:509
  110.7 1.5 collective-permute-start.32
  112.2 1.6 collective-permute-start.27
  113.8 1.0 fusion.8
  114.7 0.6 collective-permute-start.15
  115.3 2.4 %collective-permute-done.32 = bf16[240,384]{1,0:T(8,128)(2,1)S(1)} collective-permute-done((bf16[240,384]{1,0:T(8,128)(2,1)S(1)}, bf16[240,384]{1,0:T(8,128)(2,1)S(1)}, u32[]{:S(2)}, u32[]{:S(2)}) %collective-permute-start.32) | collective-permute-done | bytes 184352 | tf_op jit(solution)/shard_map/ppermute | solution.py:595
  117.7 1.6 collective-permute-start.33
  119.4 7.4 %input_gradient.1 = (bf16[8,197,384]{2,1,0:T(8,128)(2,1)}, f32[8,384]{1,0:T(8,128)}) custom-call(bf16[8,197,384]{2,1,0:T(8,128)(2,1)} %copy.33.tok_ref, bf16[8,208,1152]{2,1,0:T(8,128)(2,1)} %back.5.d_proj_ref, f32[8,208,384]{2,1,0:T(8,128)} %get-tuple-element.91.d_middle_ref, bf16[384,1152]{1,0:T(8,128)(2,1)} %get-tuple-element.92.w_ref, ...), custom_call_target="tpu_custom_call" | custom-call | flops 1000 | bytes 1 | tf_op jit(solution)/shard_map/input_gradient/pallas_call | solution.py:529
  126.9 1.6 collective-permute-start.16
  128.5 2.7 %collective-permute-start.28 = (bf16[200,384]{1,0:T(8,128)(2,1)S(1)}, bf16[200,384]{1,0:T(8,128)(2,1)S(1)}, u32[]{:S(2)}, u32[]{:S(2)}) collective-permute-start(bf16[200,384]{1,0:T(8,128)(2,1)S(1)} %add.137), channel_id=1, source_target_pairs={{0,16},{1,17},{2,18},{3,19},{4,20},{5,21},{6,22},{7,23},{8,24},{9,... | collective-permute-start | bytes 460808 | tf_op jit(solution)/shard_map/ppermute | solution.py:595
  132.3 13.3 %collective-permute-done.34 = bf16[240,384]{1,0:T(8,128)(2,1)S(1)} collective-permute-done((bf16[240,384]{1,0:T(8,128)(2,1)S(1)}, bf16[240,384]{1,0:T(8,128)(2,1)S(1)}, u32[]{:S(2)}, u32[]{:S(2)}) %collective-permute-start.34) | collective-permute-done | bytes 184352 | tf_op jit(solution)/shard_map/ppermute | solution.py:595
  146.5 1.6 collective-permute-start.29
  148.0 5.4 %collective-permute-done.18 = bf16[152,384]{1,0:T(8,128)(2,1)S(1)} collective-permute-done((bf16[152,384]{1,0:T(8,128)(2,1)S(1)}, bf16[152,384]{1,0:T(8,128)(2,1)S(1)}, u32[]{:S(2)}, u32[]{:S(2)}) %collective-permute-start.18) | collective-permute-done | bytes 116768 | tf_op jit(solution)/shard_map/ppermute | solution.py:595
  153.5 1.6 collective-permute-start.19
  155.1 1.2 collective-permute-done.22
  156.8 3.2 %collective-permute-done.23 = f32[8,384]{1,0:T(8,128)S(1)} collective-permute-done((f32[8,384]{1,0:T(8,128)S(1)}, f32[8,384]{1,0:T(8,128)S(1)}, u32[]{:S(2)}, u32[]{:S(2)}) %collective-permute-start.23) | collective-permute-done | bytes 12320 | tf_op jit(solution)/shard_map/ppermute | solution.py:595
  160.5 3.2 %collective-permute-done.24 = f32[8,384]{1,0:T(8,128)S(1)} collective-permute-done((f32[8,384]{1,0:T(8,128)S(1)}, f32[8,384]{1,0:T(8,128)S(1)}, u32[]{:S(2)}, u32[]{:S(2)}) %collective-permute-start.24) | collective-permute-done | bytes 12320 | tf_op jit(solution)/shard_map/ppermute | solution.py:595
  164.3 3.7 %collective-permute-done.25 = f32[8,384]{1,0:T(8,128)S(1)} collective-permute-done((f32[8,384]{1,0:T(8,128)S(1)}, f32[8,384]{1,0:T(8,128)S(1)}, u32[]{:S(2)}, u32[]{:S(2)}) %collective-permute-start.25) | collective-permute-done | bytes 12320 | tf_op jit(solution)/shard_map/ppermute | solution.py:595
  168.0 0.9 collective-permute-start.26
  168.9 3.8 %collective-permute-done.26 = f32[8,384]{1,0:T(8,128)S(1)} collective-permute-done((f32[8,384]{1,0:T(8,128)S(1)}, f32[8,384]{1,0:T(8,128)S(1)}, u32[]{:S(2)}, u32[]{:S(2)}) %collective-permute-start.26) | collective-permute-done | bytes 12320 | tf_op jit(solution)/shard_map/ppermute | solution.py:595
  173.2 1.2 copy.36
  174.4 1.2 copy.37
  175.6 0.6 add.136.refs_4_
  176.2 0.6 copy-done.22
  176.9 0.7 copy-done.19
  177.6 3.2 %unpack_outer.1 = (f32[768,384]{1,0:T(8,128)}, f32[192,1536]{1,0:T(8,128)}, f32[192,384]{1,0:T(8,128)}, f32[192]{0:T(256)}, f32[192]{0:T(256)}, /*index=5*/f32[192]{0:T(256)}, f32[192]{0:T(256)}, f32[768]{0:T(1024)}) custom-call(s32[3]{0:T(128)} %pad_add_fusion.index, bf16[200,384]{1,0:T(8,128)(2,1)} %copy-done.8, bf16[200,384]{1,0:T(8,128)(2,1)} %copy-done.20, ...), custom_call_target="tpu_custom_call" | custom-call | flops 3000 | bytes 1 | tf_op jit(solution)/shard_map/unpack_outer/pallas_call | solution.py:548
  180.8 0.6 copy-done.24
  181.5 0.6 copy-done.25
  182.1 2.1 %unpack_inner.1 = (f32[192,1152]{1,0:T(8,128)}, f32[192]{0:T(256)}, f32[192]{0:T(256)}, f32[192]{0:T(256)}, f32[192]{0:T(256)}) custom-call(s32[3]{0:T(128)} %pad_add_fusion.index, bf16[152,384]{1,0:T(8,128)(2,1)} %copy-done.10, bf16[152,384]{1,0:T(8,128)(2,1)} %copy-done.23, bf16[152,384]{1,0:T(8,128)(2,1)} %copy-done.24, bf16[152,384]{1,0:T(8,128)(2,1)} %copy-done.25, ...), custom_call_target="tpu_custom_call" | custom-call | flops 2000 | bytes 1 | tf_op jit(solution)/shard_map/unpack_inner/pallas_call | solution.py:571
  (126 shorter events, 7.1 us)
Async XLA Ops:
  0.6 16.1 %copy-start = (bf16[768,384]{1,0:T(8,128)(2,1)S(1)}, bf16[768,384]{1,0:T(8,128)(2,1)}, u32[]{:S(2)}) copy-start(bf16[768,384]{1,0:T(8,128)(2,1)} %drop_own.1) | copy-start | bytes 1769476
  0.7 19.5 %copy-start.3 = (bf16[8,197,384]{2,0,1:T(8,128)(2,1)S(1)}, bf16[8,197,384]{2,0,1:T(8,128)(2,1)}, u32[]{:S(2)}) copy-start(bf16[8,197,384]{2,0,1:T(8,128)(2,1)} %param.15) | copy-start | bytes 3631108
  6.9 15.6 %collective-permute-start = (bf16[12,192]{1,0:T(8,128)(2,1)S(1)}, bf16[12,192]{1,0:T(8,128)(2,1)S(1)}, u32[]{:S(2)}, u32[]{:S(2)}) collective-permute-start(bf16[12,192]{1,0:T(8,128)(2,1)S(1)} %concatenate.6), channel_id=1, source_target_pairs={{0,1},{1,0},{2,3},{3,2},{4,5},{5,4},{6,7},{7,6},{8,9},{9,8},{10,11... | collective-permute-start | bytes 13832 | tf_op jit(solution)/shard_map/ppermute | solution.py:595
  11.5 21.4 %collective-permute-start.1 = (bf16[96,1152]{1,0:T(8,128)(2,1)}, bf16[96,1152]{1,0:T(8,128)(2,1)S(1)}, u32[]{:S(2)}, u32[]{:S(2)}) collective-permute-start(bf16[96,1152]{1,0:T(8,128)(2,1)} %constant_dynamic-slice_fusion.3), channel_id=1, source_target_pairs={{0,1},{1,0},{2,3},{3,2},{4,5},{5,4},{6,7},{7,6},{8,9},{9,8},{10,11... | collective-permute-start | bytes 663560 | tf_op jit(solution)/shard_map/ppermute | solution.py:595
  13.1 21.1 %collective-permute-start.3 = (bf16[96,384]{1,0:T(8,128)(2,1)}, bf16[96,384]{1,0:T(8,128)(2,1)}, u32[]{:S(2)}, u32[]{:S(2)}) collective-permute-start(bf16[96,384]{1,0:T(8,128)(2,1)} %constant_dynamic-slice_fusion.2), channel_id=1, source_target_pairs={{0,1},{1,0},{2,3},{3,2},{4,5},{5,4},{6,7},{7,6},{8,9},{9,8},{10,11... | collective-permute-start | bytes 221192 | tf_op jit(solution)/shard_map/ppermute | solution.py:595
  16.7 11.2 %collective-permute-start.5 = (bf16[96,1536]{1,0:T(8,128)(2,1)}, bf16[96,1536]{1,0:T(8,128)(2,1)S(1)}, u32[]{:S(2)}, u32[]{:S(2)}) collective-permute-start(bf16[96,1536]{1,0:T(8,128)(2,1)} %constant_dynamic-slice_fusion.1), channel_id=1, source_target_pairs={{0,1},{1,0},{2,3},{3,2},{4,5},{5,4},{6,7},{7,6},{8,9},{9,8},{10,11... | collective-permute-start | bytes 884744 | tf_op jit(solution)/shard_map/ppermute | solution.py:595
  17.5 3.8 %copy-start.4 = (bf16[8,197,384]{2,0,1:T(8,128)(2,1)S(1)}, bf16[8,197,384]{2,0,1:T(8,128)(2,1)}, u32[]{:S(2)}) copy-start(bf16[8,197,384]{2,0,1:T(8,128)(2,1)} %param.29) | copy-start | bytes 3631108
  17.5 15.3 %collective-permute-start.7 = (bf16[384,384]{1,0:T(8,128)(2,1)}, bf16[384,384]{1,0:T(8,128)(2,1)S(1)}, u32[]{:S(2)}, u32[]{:S(2)}) collective-permute-start(bf16[384,384]{1,0:T(8,128)(2,1)} %constant_dynamic-slice_fusion), channel_id=1, source_target_pairs={{0,1},{1,0},{2,3},{3,2},{4,5},{5,4},{6,7},{7,6},{8,9},{9,8},{10,11... | collective-permute-start | bytes 884744 | tf_op jit(solution)/shard_map/ppermute | solution.py:595
  28.0 17.9 %copy-start.11 = (bf16[96,1536]{1,0:T(8,128)(2,1)}, bf16[96,1536]{1,0:T(8,128)(2,1)S(1)}, u32[]{:S(2)}) copy-start(bf16[96,1536]{1,0:T(8,128)(2,1)S(1)} %collective-permute-done.5.lift_near) | copy-start | bytes 884740
  28.0 17.9 %collective-permute-start.6 = (bf16[96,1536]{1,0:T(8,128)(2,1)S(1)}, bf16[96,1536]{1,0:T(8,128)(2,1)S(1)}, u32[]{:S(2)}, u32[]{:S(2)}) collective-permute-start(bf16[96,1536]{1,0:T(8,128)(2,1)S(1)} %collective-permute-done.5.lift_near), channel_id=1, source_target_pairs={{0,2},{1,3},{2,0},{3,1},{4,6},{5,7},{6,4},{7,5},{8,10},{9,11},{10,... | collective-permute-start | bytes 884744 | tf_op jit(solution)/shard_map/ppermute | solution.py:595
  32.8 13.1 %copy-start.12 = (bf16[384,384]{1,0:T(8,128)(2,1)}, bf16[384,384]{1,0:T(8,128)(2,1)S(1)}, u32[]{:S(2)}) copy-start(bf16[384,384]{1,0:T(8,128)(2,1)S(1)} %collective-permute-done.7.drop_near) | copy-start | bytes 884740
  32.8 13.0 %collective-permute-start.8 = (bf16[384,384]{1,0:T(8,128)(2,1)S(1)}, bf16[384,384]{1,0:T(8,128)(2,1)S(1)}, u32[]{:S(2)}, u32[]{:S(2)}) collective-permute-start(bf16[384,384]{1,0:T(8,128)(2,1)S(1)} %collective-permute-done.7.drop_near), channel_id=1, source_target_pairs={{0,2},{1,3},{2,0},{3,1},{4,6},{5,7},{6,4},{7,5},{8,10},{9,11},{10,... | collective-permute-start | bytes 884744 | tf_op jit(solution)/shard_map/ppermute | solution.py:595
  32.9 2.0 %copy-start.15 = (bf16[96,1152]{1,0:T(8,128)(2,1)}, bf16[96,1152]{1,0:T(8,128)(2,1)S(1)}, u32[]{:S(2)}) copy-start(bf16[96,1152]{1,0:T(8,128)(2,1)S(1)} %collective-permute-done.1.near) | copy-start | bytes 663556
  32.9 1.9 %collective-permute-start.2 = (bf16[96,1152]{1,0:T(8,128)(2,1)S(1)}, bf16[96,1152]{1,0:T(8,128)(2,1)S(1)}, u32[]{:S(2)}, u32[]{:S(2)}) collective-permute-start(bf16[96,1152]{1,0:T(8,128)(2,1)S(1)} %collective-permute-done.1.near), channel_id=1, source_target_pairs={{0,2},{1,3},{2,0},{3,1},{4,6},{5,7},{6,4},{7,5},{8,10},{9,11},{10,... | collective-permute-start | bytes 663560 | tf_op jit(solution)/shard_map/ppermute | solution.py:595
  34.1 11.7 %collective-permute-start.4 = (bf16[96,384]{1,0:T(8,128)(2,1)}, bf16[96,384]{1,0:T(8,128)(2,1)S(1)}, u32[]{:S(2)}, u32[]{:S(2)}) collective-permute-start(bf16[96,384]{1,0:T(8,128)(2,1)} %collective-permute-done.3.out_near), channel_id=1, source_target_pairs={{0,2},{1,3},{2,0},{3,1},{4,6},{5,7},{6,4},{7,5},{8,10},{9,11},{10,... | collective-permute-start | bytes 221192 | tf_op jit(solution)/shard_map/ppermute | solution.py:595
  34.8 0.7 copy-start.16
  45.8 0.7 copy-start.13
  45.9 0.8 copy-start.14
  75.6 5.9 %collective-permute-start.9 = (bf16[2,400,384]{2,1,0:T(8,128)(2,1)}, bf16[2,400,384]{2,1,0:T(8,128)(2,1)S(1)}, u32[]{:S(2)}, u32[]{:S(2)}) collective-permute-start(bf16[2,400,384]{2,1,0:T(8,128)(2,1)} %get-tuple-element.72), channel_id=1, source_target_pairs={{0,2},{1,3},{2,0},{3,1},{4,6},{5,7},{6,4},{7,5},{8,10},{9,11},{10,... | collective-permute-start | bytes 1843208 | tf_op jit(solution)/shard_map/ppermute | solution.py:595
  76.2 6.1 %collective-permute-start.10 = (bf16[2,480,384]{2,1,0:T(8,128)(2,1)}, bf16[2,480,384]{2,1,0:T(8,128)(2,1)S(1)}, u32[]{:S(2)}, u32[]{:S(2)}) collective-permute-start(bf16[2,480,384]{2,1,0:T(8,128)(2,1)} %get-tuple-element.74), channel_id=1, source_target_pairs={{0,2},{1,3},{2,0},{3,1},{4,6},{5,7},{6,4},{7,5},{8,10},{9,11},{10,... | collective-permute-start | bytes 2211848 | tf_op jit(solution)/shard_map/ppermute | solution.py:595
  76.2 5.3 %copy-start.7 = (bf16[2,400,384]{2,1,0:T(8,128)(2,1)S(1)}, bf16[2,400,384]{2,1,0:T(8,128)(2,1)}, u32[]{:S(2)}) copy-start(bf16[2,400,384]{2,1,0:T(8,128)(2,1)} %get-tuple-element.77) | copy-start | bytes 1843204
  76.2 6.0 %copy-start.6 = (bf16[2,480,384]{2,1,0:T(8,128)(2,1)S(1)}, bf16[2,480,384]{2,1,0:T(8,128)(2,1)}, u32[]{:S(2)}) copy-start(bf16[2,480,384]{2,1,0:T(8,128)(2,1)} %get-tuple-element.81) | copy-start | bytes 2211844
  82.3 10.2 %collective-permute-start.11 = (bf16[400,384]{1,0:T(8,128)(2,1)}, bf16[400,384]{1,0:T(8,128)(2,1)}, u32[]{:S(2)}, u32[]{:S(2)}) collective-permute-start(bf16[400,384]{1,0:T(8,128)(2,1)} %fusion.5), channel_id=1, source_target_pairs={{0,1},{1,0},{2,3},{3,2},{4,5},{5,4},{6,7},{7,6},{8,9},{9,8},{10,11... | collective-permute-start | bytes 921608 | tf_op jit(solution)/shard_map/ppermute | solution.py:595
  90.8 10.8 %collective-permute-start.12 = (bf16[480,384]{1,0:T(8,128)(2,1)S(1)}, bf16[480,384]{1,0:T(8,128)(2,1)S(1)}, u32[]{:S(2)}, u32[]{:S(2)}) collective-permute-start(bf16[480,384]{1,0:T(8,128)(2,1)S(1)} %fusion.2), channel_id=1, source_target_pairs={{0,1},{1,0},{2,3},{3,2},{4,5},{5,4},{6,7},{7,6},{8,9},{9,8},{10,11... | collective-permute-start | bytes 1105928 | tf_op jit(solution)/shard_map/ppermute | solution.py:595
  98.8 5.8 %collective-permute-start.13 = (bf16[200,384]{1,0:T(8,128)(2,1)S(1)}, bf16[200,384]{1,0:T(8,128)(2,1)S(1)}, u32[]{:S(2)}, u32[]{:S(2)}) collective-permute-start(bf16[200,384]{1,0:T(8,128)(2,1)S(1)} %dynamic-slice_bitcast_fusion.1), channel_id=1, source_target_pairs={{0,4},{1,5},{2,6},{3,7},{4,0},{5,1},{6,2},{7,3},{8,12},{9,13},{10,... | collective-permute-start | bytes 460808 | tf_op jit(solution)/shard_map/ppermute | solution.py:595
  110.7 3.1 %collective-permute-start.14 = (bf16[2,304,384]{2,1,0:T(8,128)(2,1)}, bf16[2,304,384]{2,1,0:T(8,128)(2,1)S(1)}, u32[]{:S(2)}, u32[]{:S(2)}) collective-permute-start(bf16[2,304,384]{2,1,0:T(8,128)(2,1)} %get-tuple-element.89), channel_id=1, source_target_pairs={{0,2},{1,3},{2,0},{3,1},{4,6},{5,7},{6,4},{7,5},{8,10},{9,11},{10,... | collective-permute-start | bytes 1400840 | tf_op jit(solution)/shard_map/ppermute | solution.py:595
  110.7 7.1 %collective-permute-start.32 = (bf16[240,384]{1,0:T(8,128)(2,1)S(1)}, bf16[240,384]{1,0:T(8,128)(2,1)S(1)}, u32[]{:S(2)}, u32[]{:S(2)}) collective-permute-start(bf16[240,384]{1,0:T(8,128)(2,1)S(1)} %dynamic-slice_bitcast_fusion), channel_id=1, source_target_pairs={{0,4},{1,5},{2,6},{3,7},{4,0},{5,1},{6,2},{7,3},{8,12},{9,13},{10,... | collective-permute-start | bytes 552968 | tf_op jit(solution)/shard_map/ppermute | solution.py:595
  112.2 16.3 %collective-permute-start.27 = (bf16[200,384]{1,0:T(8,128)(2,1)S(1)}, bf16[200,384]{1,0:T(8,128)(2,1)S(1)}, u32[]{:S(2)}, u32[]{:S(2)}) collective-permute-start(bf16[200,384]{1,0:T(8,128)(2,1)S(1)} %bitcast_add_fusion.1), channel_id=1, source_target_pairs={{0,8},{1,9},{2,10},{3,11},{4,12},{5,13},{6,14},{7,15},{8,0},{9,1},... | collective-permute-start | bytes 460808 | tf_op jit(solution)/shard_map/ppermute | solution.py:595
  114.7 12.1 %collective-permute-start.15 = (bf16[304,384]{1,0:T(8,128)(2,1)S(1)}, bf16[304,384]{1,0:T(8,128)(2,1)S(1)}, u32[]{:S(2)}, u32[]{:S(2)}) collective-permute-start(bf16[304,384]{1,0:T(8,128)(2,1)S(1)} %fusion.8), channel_id=1, source_target_pairs={{0,1},{1,0},{2,3},{3,2},{4,5},{5,4},{6,7},{7,6},{8,9},{9,8},{10,11... | collective-permute-start | bytes 700424 | tf_op jit(solution)/shard_map/ppermute | solution.py:595
  117.7 13.5 %collective-permute-start.33 = (bf16[240,384]{1,0:T(8,128)(2,1)S(1)}, bf16[240,384]{1,0:T(8,128)(2,1)S(1)}, u32[]{:S(2)}, u32[]{:S(2)}) collective-permute-start(bf16[240,384]{1,0:T(8,128)(2,1)S(1)} %bitcast_add_fusion), channel_id=1, source_target_pairs={{0,8},{1,9},{2,10},{3,11},{4,12},{5,13},{6,14},{7,15},{8,0},{9,1},... | collective-permute-start | bytes 552968 | tf_op jit(solution)/shard_map/ppermute | solution.py:595
  119.4 7.4 %copy-start.9 = (bf16[2,304,384]{2,1,0:T(8,128)(2,1)S(1)}, bf16[2,304,384]{2,1,0:T(8,128)(2,1)}, u32[]{:S(2)}) copy-start(bf16[2,304,384]{2,1,0:T(8,128)(2,1)} %get-tuple-element.95) | copy-start | bytes 1400836
  126.9 4.9 %collective-permute-start.16 = (bf16[152,384]{1,0:T(8,128)(2,1)S(1)}, bf16[152,384]{1,0:T(8,128)(2,1)S(1)}, u32[]{:S(2)}, u32[]{:S(2)}) collective-permute-start(bf16[152,384]{1,0:T(8,128)(2,1)S(1)} %dynamic-slice_bitcast_fusion.2), channel_id=1, source_target_pairs={{0,4},{1,5},{2,6},{3,7},{4,0},{5,1},{6,2},{7,3},{8,12},{9,13},{10,... | collective-permute-start | bytes 350216 | tf_op jit(solution)/shard_map/ppermute | solution.py:595
  128.5 26.6 %copy-start.27 = (f32[8,384]{1,0:T(8,128)S(1)}, f32[8,384]{1,0:T(8,128)}, u32[]{:S(2)}) copy-start(f32[8,384]{1,0:T(8,128)} %get-tuple-element.97) | copy-start | bytes 36868
  128.5 17.8 %collective-permute-start.28 = (bf16[200,384]{1,0:T(8,128)(2,1)S(1)}, bf16[200,384]{1,0:T(8,128)(2,1)S(1)}, u32[]{:S(2)}, u32[]{:S(2)}) collective-permute-start(bf16[200,384]{1,0:T(8,128)(2,1)S(1)} %add.137), channel_id=1, source_target_pairs={{0,16},{1,17},{2,18},{3,19},{4,20},{5,21},{6,22},{7,23},{8,24},{9,... | collective-permute-start | bytes 460808 | tf_op jit(solution)/shard_map/ppermute | solution.py:595
  131.3 41.9 %copy-start.1 = (bf16[8,197,384]{2,1,0:T(8,128)(2,1)S(1)}, bf16[8,197,384]{2,1,0:T(8,128)(2,1)}, u32[]{:S(2)}) copy-start(bf16[8,197,384]{2,1,0:T(8,128)(2,1)} %get-tuple-element.113) | copy-start | bytes 3631108
  131.3 14.4 %collective-permute-start.34 = (bf16[240,384]{1,0:T(8,128)(2,1)S(1)}, bf16[240,384]{1,0:T(8,128)(2,1)S(1)}, u32[]{:S(2)}, u32[]{:S(2)}) collective-permute-start(bf16[240,384]{1,0:T(8,128)(2,1)S(1)} %add.140), channel_id=1, source_target_pairs={{0,16},{1,17},{2,18},{3,19},{4,20},{5,21},{6,22},{7,23},{8,24},{9,... | collective-permute-start | bytes 552968 | tf_op jit(solution)/shard_map/ppermute | solution.py:595
  131.8 14.5 %collective-permute-start.17 = (bf16[152,384]{1,0:T(8,128)(2,1)S(1)}, bf16[152,384]{1,0:T(8,128)(2,1)S(1)}, u32[]{:S(2)}, u32[]{:S(2)}) collective-permute-start(bf16[152,384]{1,0:T(8,128)(2,1)S(1)} %bitcast_add_fusion.2), channel_id=1, source_target_pairs={{0,8},{1,9},{2,10},{3,11},{4,12},{5,13},{6,14},{7,15},{8,0},{9,1},... | collective-permute-start | bytes 350216 | tf_op jit(solution)/shard_map/ppermute | solution.py:595
  145.7 28.7 %copy-start.5 = (bf16[240,384]{1,0:T(8,128)(2,1)}, bf16[240,384]{1,0:T(8,128)(2,1)S(1)}, u32[]{:S(2)}) copy-start(bf16[240,384]{1,0:T(8,128)(2,1)S(1)} %add.141.refs_4_) | copy-start | bytes 552964
  145.7 18.0 %collective-permute-start.35 = (bf16[240,384]{1,0:T(8,128)(2,1)S(1)}, bf16[240,384]{1,0:T(8,128)(2,1)S(1)}, u32[]{:S(2)}, u32[]{:S(2)}) collective-permute-start(bf16[240,384]{1,0:T(8,128)(2,1)S(1)} %add.141.refs_4_), channel_id=1, source_target_pairs={{0,4},{1,5},{2,6},{3,7},{4,0},{5,1},{6,2},{7,3},{8,12},{9,13},{10,... | collective-permute-start | bytes 552968 | tf_op jit(solution)/shard_map/ppermute | solution.py:595
  146.3 7.2 %collective-permute-start.18 = (bf16[152,384]{1,0:T(8,128)(2,1)S(1)}, bf16[152,384]{1,0:T(8,128)(2,1)S(1)}, u32[]{:S(2)}, u32[]{:S(2)}) collective-permute-start(bf16[152,384]{1,0:T(8,128)(2,1)S(1)} %add.130), channel_id=1, source_target_pairs={{0,16},{1,17},{2,18},{3,19},{4,20},{5,21},{6,22},{7,23},{8,24},{9,... | collective-permute-start | bytes 350216 | tf_op jit(solution)/shard_map/ppermute | solution.py:595
  146.4 27.9 %copy-start.8 = (bf16[200,384]{1,0:T(8,128)(2,1)}, bf16[200,384]{1,0:T(8,128)(2,1)S(1)}, u32[]{:S(2)}) copy-start(bf16[200,384]{1,0:T(8,128)(2,1)S(1)} %add.138.refs_0_) | copy-start | bytes 460804
  146.5 17.8 %collective-permute-start.29 = (bf16[200,384]{1,0:T(8,128)(2,1)S(1)}, bf16[200,384]{1,0:T(8,128)(2,1)S(1)}, u32[]{:S(2)}, u32[]{:S(2)}) collective-permute-start(bf16[200,384]{1,0:T(8,128)(2,1)S(1)} %add.138.refs_0_), channel_id=1, source_target_pairs={{0,4},{1,5},{2,6},{3,7},{4,0},{5,1},{6,2},{7,3},{8,12},{9,13},{10,... | collective-permute-start | bytes 460808 | tf_op jit(solution)/shard_map/ppermute | solution.py:595
  148.0 20.0 %collective-permute-start.30 = (bf16[200,384]{1,0:T(8,128)(2,1)S(1)}, bf16[200,384]{1,0:T(8,128)(2,1)S(1)}, u32[]{:S(2)}, u32[]{:S(2)}) collective-permute-start(bf16[200,384]{1,0:T(8,128)(2,1)S(1)} %add.138.refs_0_), channel_id=1, source_target_pairs={{0,2},{1,3},{2,0},{3,1},{4,6},{5,7},{6,4},{7,5},{8,10},{9,11},{10,... | collective-permute-start | bytes 460808 | tf_op jit(solution)/shard_map/ppermute | solution.py:595
  153.5 20.9 %copy-start.10 = (bf16[152,384]{1,0:T(8,128)(2,1)}, bf16[152,384]{1,0:T(8,128)(2,1)S(1)}, u32[]{:S(2)}) copy-start(bf16[152,384]{1,0:T(8,128)(2,1)S(1)} %add.131.refs_0_) | copy-start | bytes 350212
  153.5 19.1 %collective-permute-start.19 = (bf16[152,384]{1,0:T(8,128)(2,1)S(1)}, bf16[152,384]{1,0:T(8,128)(2,1)S(1)}, u32[]{:S(2)}, u32[]{:S(2)}) collective-permute-start(bf16[152,384]{1,0:T(8,128)(2,1)S(1)} %add.131.refs_0_), channel_id=1, source_target_pairs={{0,4},{1,5},{2,6},{3,7},{4,0},{5,1},{6,2},{7,3},{8,12},{9,13},{10,... | collective-permute-start | bytes 350216 | tf_op jit(solution)/shard_map/ppermute | solution.py:595
  155.1 1.2 collective-permute-start.22
  156.3 3.7 %collective-permute-start.23 = (f32[8,384]{1,0:T(8,128)S(1)}, f32[8,384]{1,0:T(8,128)S(1)}, u32[]{:S(2)}, u32[]{:S(2)}) collective-permute-start(f32[8,384]{1,0:T(8,128)S(1)} %add.132), channel_id=1, source_target_pairs={{0,1},{1,0},{2,3},{3,2},{4,5},{5,4},{6,7},{7,6},{8,9},{9,8},{10,11... | collective-permute-start | bytes 36872 | tf_op jit(solution)/shard_map/ppermute | solution.py:595
  160.0 3.7 %collective-permute-start.24 = (f32[8,384]{1,0:T(8,128)S(1)}, f32[8,384]{1,0:T(8,128)S(1)}, u32[]{:S(2)}, u32[]{:S(2)}) collective-permute-start(f32[8,384]{1,0:T(8,128)S(1)} %add.133), channel_id=1, source_target_pairs={{0,4},{1,5},{2,6},{3,7},{4,0},{5,1},{6,2},{7,3},{8,12},{9,13},{10,... | collective-permute-start | bytes 36872 | tf_op jit(solution)/shard_map/ppermute | solution.py:595
  163.7 12.5 %collective-permute-start.36 = (bf16[240,384]{1,0:T(8,128)(2,1)S(1)}, bf16[240,384]{1,0:T(8,128)(2,1)S(1)}, u32[]{:S(2)}, u32[]{:S(2)}) collective-permute-start(bf16[240,384]{1,0:T(8,128)(2,1)S(1)} %add.141.refs_4_), channel_id=1, source_target_pairs={{0,2},{1,3},{2,0},{3,1},{4,6},{5,7},{6,4},{7,5},{8,10},{9,11},{10,... | collective-permute-start | bytes 552968 | tf_op jit(solution)/shard_map/ppermute | solution.py:595
  163.7 10.7 %copy-start.17 = (bf16[240,384]{1,0:T(8,128)(2,1)}, bf16[240,384]{1,0:T(8,128)(2,1)S(1)}, u32[]{:S(2)}) copy-start(bf16[240,384]{1,0:T(8,128)(2,1)S(1)} %collective-permute-done.35.refs_5_) | copy-start | bytes 552964
  163.7 12.5 %collective-permute-start.37 = (bf16[240,384]{1,0:T(8,128)(2,1)S(1)}, bf16[240,384]{1,0:T(8,128)(2,1)S(1)}, u32[]{:S(2)}, u32[]{:S(2)}) collective-permute-start(bf16[240,384]{1,0:T(8,128)(2,1)S(1)} %collective-permute-done.35.refs_5_), channel_id=1, source_target_pairs={{0,2},{1,3},{2,0},{3,1},{4,6},{5,7},{6,4},{7,5},{8,10},{9,11},{10,... | collective-permute-start | bytes 552968 | tf_op jit(solution)/shard_map/ppermute | solution.py:595
  164.2 10.2 %copy-start.20 = (bf16[200,384]{1,0:T(8,128)(2,1)}, bf16[200,384]{1,0:T(8,128)(2,1)S(1)}, u32[]{:S(2)}) copy-start(bf16[200,384]{1,0:T(8,128)(2,1)S(1)} %collective-permute-done.29.refs_1_) | copy-start | bytes 460804
  164.2 3.8 %collective-permute-start.25 = (f32[8,384]{1,0:T(8,128)S(1)}, f32[8,384]{1,0:T(8,128)S(1)}, u32[]{:S(2)}, u32[]{:S(2)}) collective-permute-start(f32[8,384]{1,0:T(8,128)S(1)} %add.134), channel_id=1, source_target_pairs={{0,8},{1,9},{2,10},{3,11},{4,12},{5,13},{6,14},{7,15},{8,0},{9,1},... | collective-permute-start | bytes 36872 | tf_op jit(solution)/shard_map/ppermute | solution.py:595
  168.0 8.2 %collective-permute-start.31 = (bf16[200,384]{1,0:T(8,128)(2,1)S(1)}, bf16[200,384]{1,0:T(8,128)(2,1)S(1)}, u32[]{:S(2)}, u32[]{:S(2)}) collective-permute-start(bf16[200,384]{1,0:T(8,128)(2,1)S(1)} %collective-permute-done.29.refs_1_), channel_id=1, source_target_pairs={{0,2},{1,3},{2,0},{3,1},{4,6},{5,7},{6,4},{7,5},{8,10},{9,11},{10,... | collective-permute-start | bytes 460808 | tf_op jit(solution)/shard_map/ppermute | solution.py:595
  168.0 6.4 %copy-start.2 = (bf16[8,197,384]{2,1,0:T(8,128)(2,1)S(1)}, bf16[8,197,384]{2,1,0:T(8,128)(2,1)}, u32[]{:S(2)}) copy-start(bf16[8,197,384]{2,1,0:T(8,128)(2,1)} %get-tuple-element.114) | copy-start | bytes 3631108
  168.0 7.6 %copy-start.21 = (bf16[200,384]{1,0:T(8,128)(2,1)}, bf16[200,384]{1,0:T(8,128)(2,1)S(1)}, u32[]{:S(2)}) copy-start(bf16[200,384]{1,0:T(8,128)(2,1)S(1)} %collective-permute-done.30.refs_2_) | copy-start | bytes 460804
  168.0 4.7 %collective-permute-start.26 = (f32[8,384]{1,0:T(8,128)S(1)}, f32[8,384]{1,0:T(8,128)S(1)}, u32[]{:S(2)}, u32[]{:S(2)}) collective-permute-start(f32[8,384]{1,0:T(8,128)S(1)} %add.135), channel_id=1, source_target_pairs={{0,16},{1,17},{2,18},{3,19},{4,20},{5,21},{6,22},{7,23},{8,24},{9,... | collective-permute-start | bytes 36872 | tf_op jit(solution)/shard_map/ppermute | solution.py:595
  172.7 8.1 %collective-permute-start.20 = (bf16[152,384]{1,0:T(8,128)(2,1)S(1)}, bf16[152,384]{1,0:T(8,128)(2,1)S(1)}, u32[]{:S(2)}, u32[]{:S(2)}) collective-permute-start(bf16[152,384]{1,0:T(8,128)(2,1)S(1)} %add.131.refs_0_), channel_id=1, source_target_pairs={{0,2},{1,3},{2,0},{3,1},{4,6},{5,7},{6,4},{7,5},{8,10},{9,11},{10,... | collective-permute-start | bytes 350216 | tf_op jit(solution)/shard_map/ppermute | solution.py:595
  172.7 2.9 %copy-start.23 = (bf16[152,384]{1,0:T(8,128)(2,1)}, bf16[152,384]{1,0:T(8,128)(2,1)S(1)}, u32[]{:S(2)}) copy-start(bf16[152,384]{1,0:T(8,128)(2,1)S(1)} %collective-permute-done.19.refs_1_) | copy-start | bytes 350212
  172.7 8.1 %collective-permute-start.21 = (bf16[152,384]{1,0:T(8,128)(2,1)S(1)}, bf16[152,384]{1,0:T(8,128)(2,1)S(1)}, u32[]{:S(2)}, u32[]{:S(2)}) collective-permute-start(bf16[152,384]{1,0:T(8,128)(2,1)S(1)} %collective-permute-done.19.refs_1_), channel_id=1, source_target_pairs={{0,2},{1,3},{2,0},{3,1},{4,6},{5,7},{6,4},{7,5},{8,10},{9,11},{10,... | collective-permute-start | bytes 350216 | tf_op jit(solution)/shard_map/ppermute | solution.py:595
  176.2 0.7 copy-start.22
  176.2 0.7 copy-start.18
  176.9 0.7 copy-start.19
  180.8 0.7 copy-start.24
  (2 other events, 1.3 us)

commit v3 on v2

--- a/solution.py
+++ b/solution.py
@@ -82,8 +82,8 @@
     x, core = index[0], index[1]
     other = (1 - x) * block
     full[pl.ds(pl.multiple_of(x * block, 16), block), :] = own[...]
-    full[pl.ds(pl.multiple_of(other + core * half, 16), half), :] = near[...]
-    full[pl.ds(pl.multiple_of(other + (1 - core) * half, 16), half), :] = far[...]
+    full[pl.ds(pl.multiple_of(other + core * half, 16), half), :] = near[0:half, :]
+    full[pl.ds(pl.multiple_of(other + (1 - core) * half, 16), half), :] = far[0:half, :]
 
 
 def quarters(index, keep, send):
@@ -93,8 +93,52 @@
         yield send, slot, half, 1 - core
 
 
+def pack_first_kernel(index, *refs):
+    vectors, lift_bias, weight, packed = refs[:8], *refs[8:]
+    half = weight.shape[0] // 2
+    shard, width = vectors[0].shape[0], weight.shape[1] // 3
+    packed[0:half, :] = weight[pl.ds(pl.multiple_of(index[1] * half, 16), half), :]
+    packed[half:, :] = jnp.zeros((8, 3 * width), BF16)
+    for i, ref in enumerate(vectors):
+        row = ref[...].astype(F32).reshape(1, shard)
+        packed[half + i : half + i + 1, 0:shard] = row.astype(BF16)
+    bias = lift_bias[...].astype(F32).reshape(1, lift_bias.shape[0]).astype(BF16)
+    for k in range(lift_bias.shape[0] // width):
+        packed[half + k : half + k + 1, width : 2 * width] = bias[:, k * width : (k + 1) * width]
+
+
+def pack_rest_kernel(index, *refs):
+    for weight, half_out in zip(refs[:3], refs[3:]):
+        half = half_out.shape[0]
+        half_out[...] = weight[pl.ds(pl.multiple_of(index[1] * half, 16), half), :]
+
+
+def join_vectors(vec_ref, own, other, index):
+    width = vec_ref.shape[1]
+    half = width // 2
+    mine, theirs = own[-8:, :].astype(F32), other[-8:, :].astype(F32)
+    first = index[0] == 0
+    low, high = jnp.where(first, mine, theirs), jnp.where(first, theirs, mine)
+    vec_ref[0:8, :] = jnp.concatenate([low[:, :half], high[:, :half]], axis=1)
+    blocks = vec_ref.shape[0] // 2 - 4
+    vec_ref[8 : 8 + blocks, :] = low[:blocks, width : 2 * width]
+    vec_ref[8 + blocks :, :] = high[:blocks, width : 2 * width]
+
+
 def attend_kernel(
-    length, index, tok_ref, vec_ref, own, near, far, normed_ref, proj_ref, mixed_ref, w_ref, n_s
+    length,
+    index,
+    tok_ref,
+    packed,
+    own,
+    near,
+    far,
+    normed_ref,
+    proj_ref,
+    mixed_ref,
+    w_ref,
+    vec_ref,
+    n_s,
 ):
     images, rows, width = n_s.shape
 
@@ -102,6 +146,7 @@
     def _():
         zero_tail(n_s, length)
         join_pieces(w_ref, own, near, far, index)
+        join_vectors(vec_ref, packed, near, index)
 
     gain, shift = vec_ref[0:1, :], vec_ref[1:2, :]
     bias = jnp.concatenate([vec_ref[2:3, :], jnp.zeros((1, width), F32), vec_ref[3:4, :]], axis=1)
@@ -133,7 +178,6 @@
     cot_ref,
     mixed_ref,
     vec_ref,
-    lift_bias_ref,
     out_own,
     out_near,
     out_far,
@@ -155,6 +199,7 @@
     w_out_ref,
     w_lift_ref,
     w_drop_ref,
+    lift_bias_ref,
     a_drop,
     a_lift,
     a_out,
@@ -173,6 +218,8 @@
         join_pieces(w_out_ref, out_own, out_near, out_far, index)
         join_pieces(w_lift_ref, lift_own, lift_near, lift_far, index)
         join_pieces(w_drop_ref, drop_own, drop_near, drop_far, index)
+        for k in range(hidden_width // width):
+            lift_bias_ref[:, k * width : (k + 1) * width] = vec_ref[8 + k : 9 + k, :]
         for acc in (a_drop, a_lift, a_out, a_vec, a_bias):
             acc[...] = jnp.zeros_like(acc)
 
@@ -399,37 +446,65 @@
     return pl.CostEstimate(flops=int(microseconds * 1e3), bytes_accessed=1, transcendentals=0)
 
 
-def forward_attention(index, tokens, vectors, pieces):
+def pack_first(index, vectors, lift_bias, weight):
+    rows, columns = weight.shape
+    return pl.pallas_call(
+        pack_first_kernel,
+        grid=(1,),
+        in_specs=[SCALARS, *whole_like((*vectors, lift_bias, weight))],
+        out_specs=whole(rows // 2 + 8, columns),
+        out_shape=shape_of(BF16, rows // 2 + 8, columns),
+        compiler_params=PARAMS,
+        cost_estimate=cost(1),
+        name="pack_first",
+    )(index, *vectors, lift_bias, weight)
+
+
+def pack_rest(index, weights):
+    return pl.pallas_call(
+        pack_rest_kernel,
+        grid=(1,),
+        in_specs=[SCALARS, *whole_like(weights)],
+        out_specs=[whole(w.shape[0] // 2, w.shape[1]) for w in weights],
+        out_shape=[shape_of(BF16, w.shape[0] // 2, w.shape[1]) for w in weights],
+        compiler_params=PARAMS,
+        cost_estimate=cost(1),
+        name="pack_rest",
+    )(index, *weights)
+
+
+def forward_attention(index, tokens, ff, packed, pieces):
     images, length, width = tokens.shape
     rows = -(-length // 16) * 16
     group = 2 if images % 2 == 0 else 1
     return pl.pallas_call(
         functools.partial(attend_kernel, length),
         grid=(images // group,),
-        in_specs=[SCALARS, per_step(group, length, width), *whole_like((vectors, *pieces))],
+        in_specs=[SCALARS, per_step(group, length, width), *whole_like((packed, *pieces))],
         out_specs=[
             per_step(group, rows, width),
             per_step(group, rows, 3 * width),
             per_step(group, rows, width),
             whole(width, 3 * width),
+            whole(8 + ff // width, width),
         ],
         out_shape=[
             shape_of(BF16, images, rows, width),
             shape_of(BF16, images, rows, 3 * width),
             shape_of(BF16, images, rows, width),
             shape_of(BF16, width, 3 * width),
+            shape_of(F32, 8 + ff // width, width),
         ],
         scratch_shapes=[pltpu.VMEM((group, rows, width), BF16)],
         compiler_params=PARAMS,
         cost_estimate=cost(1),
         name="attend",
-    )(index, tokens, vectors, *pieces)
-
-
-def mlp_both_ways(index, tokens, cotangent, mixed, vectors, lift_bias, pieces):
+    )(index, tokens, packed, *pieces)
+
+
+def mlp_both_ways(index, tokens, cotangent, mixed, vectors, ff, pieces):
     images, length, width = tokens.shape
     rows = mixed.shape[1]
-    ff = lift_bias.shape[1]
     group = 2 if images % 2 == 0 else 1
     a_rows = ff // 4 + VEC_ROWS
     b_rows = (width // 4) * (ff // width + 1)
@@ -441,7 +516,7 @@
             per_step(group, length, width),
             per_step(group, length, width),
             per_step(group, rows, width),
-            *whole_like((vectors, lift_bias, *pieces)),
+            *whole_like((vectors, *pieces)),
         ],
         out_specs=[
             per_step(group, length, width),
@@ -467,6 +542,7 @@
             pltpu.VMEM((width, width), BF16),
             pltpu.VMEM((width, ff), BF16),
             pltpu.VMEM((ff, width), BF16),
+            pltpu.VMEM((1, ff), F32),
             pltpu.VMEM((ff, width), F32),
             pltpu.VMEM((width, ff), F32),
             pltpu.VMEM((width, width), F32),
@@ -476,7 +552,7 @@
         compiler_params=PARAMS,
         cost_estimate=cost(1),
         name="mlp",
-    )(index, tokens, cotangent, mixed, vectors, lift_bias, *pieces)
+    )(index, tokens, cotangent, mixed, vectors, *pieces)
 
 
 def attention_backward(projected, d_mixed, length, first, count, earlier):
@@ -547,7 +623,15 @@
     half = width // 2
     return pl.pallas_call(
         unpack_outer_kernel,
-        in_specs=[SCALARS] + [pl.BlockSpec(memory_space=pltpu.VMEM)] * 8,
+        grid=(1,),
+        in_specs=[SCALARS, *whole_like((*a_pieces, *b_pieces))],
+        out_specs=[
+            whole(ff // 2, width),
+            whole(half, ff),
+            whole(half, width),
+            *[whole(half)] * 4,
+            whole(ff // 2),
+        ],
         out_shape=[
             shape_of(F32, ff // 2, width),
             shape_of(F32, half, ff),
@@ -570,7 +654,9 @@
     half = width // 2
     return pl.pallas_call(
         unpack_inner_kernel,
-        in_specs=[SCALARS] + [pl.BlockSpec(memory_space=pltpu.VMEM)] * 5,
+        grid=(1,),
+        in_specs=[SCALARS, *whole_like((*pieces, late))],
+        out_specs=[whole(half, 3 * width), *[whole(half)] * 4],
         out_shape=[shape_of(F32, half, 3 * width), *[shape_of(F32, half)] * 4],
         scratch_shapes=[pltpu.VMEM((2, 2 * pieces[0].shape[0], width), F32)],
         compiler_params=PARAMS,
@@ -606,39 +692,15 @@
     def over_z(self, v, mask):
         return self.swap(v, 4 * mask)
 
-    def gather_weight(self, own):
-        half = own.shape[0] // 2
-        near = self.over_x(lax.dynamic_slice_in_dim(own, self.core * half, half, 0))
-        return own, near, self.over_core(near)
-
-    def gather_vectors(self, own):
-        other = self.over_x(own)
-        first = self.x == 0
-        return jnp.where(first, own, other), jnp.where(first, other, own)
-
-    def halves(self, v):
-        return v.reshape(2, v.shape[0] // 2, v.shape[1])
+    def half_of(self, v, which):
+        rows = v.shape[-2] // 2
+        return lax.dynamic_slice_in_dim(v, which * rows, rows, v.ndim - 2)
 
     def to_send(self, v):
-        return lax.dynamic_index_in_dim(self.halves(v), 1 - self.y, 0, keepdims=False)
+        return self.half_of(v, 1 - self.y)
 
     def to_keep(self, v):
-        return lax.dynamic_index_in_dim(self.halves(v), self.y, 0, keepdims=False)
-
-    def over_both_z(self, part):
-        part = part + self.over_z(part, 1)
-        return part + self.over_z(part, 2)
-
-    def pieces(self, part):
-        across = self.over_y(part)
-        return part, across, self.over_core(part), self.over_core(across)
-
-    def reduce_late(self, v):
-        v = v + self.over_core(v)
-        v = v + self.over_x(v)
-        v = v + self.over_y(v)
-        v = v + self.over_z(v, 1)
-        return v + self.over_z(v, 2)
+        return self.half_of(v, self.y)
 
 
 class Collective:
@@ -650,12 +712,19 @@
         quarter = full.shape[0] // 4
         return full[: 2 * quarter], full[2 * quarter : 3 * quarter], full[3 * quarter :]
 
-    def gather_vectors(self, own):
-        full = lax.all_gather(own, "fsdp", axis=0)
-        shards, rows, columns = full.shape
-        halves = full.reshape(2, shards // 2, rows, columns)
-        both = halves.transpose(0, 2, 1, 3).reshape(2, rows, shards // 2 * columns)
-        return both[0], both[1]
+    def gather_vectors(self, vectors, lift_bias):
+        whole_vectors = [lax.all_gather(v, "fsdp", axis=0, tiled=True) for v in vectors]
+        whole_bias = lax.all_gather(lift_bias, "fsdp", axis=0, tiled=True)
+        width = whole_vectors[0].shape[0]
+        table = jnp.stack(whole_vectors).reshape(8, 2, width // 2)
+        bias = whole_bias.reshape(2, -1, width)
+        return (
+            jnp.zeros((2, 8, 3 * width), BF16)
+            .at[:, :, : width // 2]
+            .set(table.transpose(1, 0, 2))
+            .at[:, : bias.shape[1], width : 2 * width]
+            .set(bias)
+        )
 
     def reduce(self, v):
         owned = lax.psum_scatter(v.astype(BF16), "fsdp", scatter_dimension=0, tiled=True)
@@ -699,80 +768,102 @@
 ):
     length, width = tokens.shape[1:]
     plan = Butterfly() if swaps else Collective()
-    shard = gain_one.shape[0]
-    own = jnp.concatenate(
-        [
-            v.reshape(-1, shard)
-            for v in (
-                gain_one,
-                shift_one,
-                query_bias,
-                value_bias,
-                out_bias,
-                gain_two,
-                shift_two,
-                drop_bias,
-                lift_bias,
-            )
-        ],
-        axis=0,
+    index = plan.index
+    small = (
+        gain_one,
+        shift_one,
+        query_bias,
+        value_bias,
+        out_bias,
+        gain_two,
+        shift_two,
+        drop_bias,
     )
-    low, high = plan.gather_vectors(own)
-    vectors = jnp.concatenate([low[:8], high[:8]], axis=1).astype(F32)
-    parts = 2 * width // (2 * shard)
-    full_lift_bias = (
-        jnp.stack([low[8:], high[8:]])
-        .reshape(2, lift_bias.shape[0] // shard, parts // 2, shard)
-        .transpose(0, 2, 1, 3)
-        .reshape(1, -1)
-        .astype(F32)
+    ff = lift_weight.shape[1]
+    rest = (out_weight, lift_weight, drop_weight)
+    if swaps:
+        packed = pack_first(index, small, lift_bias, qkv_weight)
+        near = plan.over_x(packed)
+        qkv = (qkv_weight, near, plan.over_core(near))
+        rest_then, packed = after(rest, packed)
+        nears = [plan.over_x(half) for half in pack_rest(index, rest_then)]
+    else:
+        packed, theirs = plan.gather_vectors(small, lift_bias)
+        own, near, far = plan.gather_weight(qkv_weight)
+        qkv = (own, jnp.concatenate([near, theirs]), far)
+    normed, projected, mixed, full_qkv, vectors = forward_attention(
+        index, tokens, ff, packed, qkv
     )
-    qkv = plan.gather_weight(qkv_weight)
-    outer = [
-        piece for w in (out_weight, lift_weight, drop_weight) for piece in plan.gather_weight(w)
-    ]
-    index = plan.index
-    normed, projected, mixed, full_qkv = forward_attention(index, tokens, vectors, qkv)
+    if swaps:
+        mixed, nears = after(mixed, nears)
+        outer = [
+            piece for w, near in zip(rest, nears) for piece in (w, near, plan.over_core(near))
+        ]
+    else:
+        outer = [piece for w in rest for piece in plan.gather_weight(w)]
     output, d_middle, d_mixed, keep_a, send_a, keep_b, send_b = mlp_both_ways(
-        index, tokens, cotangent, mixed, vectors, full_lift_bias, outer
+        index, tokens, cotangent, mixed, vectors, ff, outer
     )
-    ff = full_lift_bias.shape[1]
     images = tokens.shape[0]
     backward = functools.partial(attention_backward, projected, d_mixed, length)
     if swaps:
         got_a, got_b = plan.over_core(send_a), plan.over_core(send_b)
-        d_proj = backward(0, 2, None)
-        d_proj, keep_a, keep_b = after(d_proj, keep_a, keep_b)
-        other_a, other_b = keep_a[1] + got_a[1], keep_b[1] + got_b[1]
-        d_proj, other_a, other_b = after(d_proj, other_a, other_b)
-        over_a, over_b = plan.over_x(other_a), plan.over_x(other_b)
-        d_proj = backward(2, images - 4, d_proj)
-        d_proj, keep_a = after(d_proj, keep_a)
+        d_proj, got_a, got_b = after(backward(0, 2, None), got_a, got_b)
+        other_a = keep_a[1] + got_a[1]
+        sum_b = keep_b + got_b
+        d_proj, other_a, other_b, sum_b = after(d_proj, other_a, plan.to_send(sum_b), sum_b)
+        over_a, over_b = plan.over_x(other_a), plan.over_y(other_b)
+        d_proj, over_a, over_b = after(backward(2, images - 4, d_proj), over_a, over_b)
         mine_a = keep_a[0] + got_a[0] + over_a
-        d_proj, out_a = after(d_proj, plan.to_send(mine_a))
-        low_a = plan.over_y(out_a)
-        d_proj = backward(images - 2, 2, d_proj)
-        d_proj, keep_b, mine_a = after(d_proj, keep_b, mine_a)
-        mine_b = keep_b[0] + got_b[0] + over_b
-        d_proj, out_b = after(d_proj, plan.to_send(mine_b))
-        low_b = plan.over_y(out_b)
-        part_a = plan.to_keep(mine_a) + low_a
-        d_proj, part_a = after(d_proj, part_a)
+        both_b = plan.to_keep(sum_b) + over_b
+        d_proj, other_a, other_b, mine_a, both_b = after(
+            d_proj, plan.to_send(mine_a), both_b[1], mine_a, both_b
+        )
+        over_a, over_b = plan.over_y(other_a), plan.over_x(other_b)
+        d_proj, over_a, over_b = after(backward(images - 2, 2, d_proj), over_a, over_b)
+        part_a = plan.to_keep(mine_a) + over_a
+        part_b = both_b[0] + over_b
+        d_proj, part_a, part_b = after(d_proj, part_a, part_b)
+        over_a, over_b = plan.over_z(part_a, 1), plan.over_z(part_b, 1)
         keep_c, send_c = qkv_weight_gradient(index, normed, d_proj)
+        send_c, over_a = after(send_c, over_a)
         got_c = plan.over_core(send_c)
-        d_proj, other_c = after(d_proj, keep_c[1] + got_c[1])
-        over_c = plan.over_x(other_c)
-        input_grad, g_first = input_gradient(tokens, d_proj, d_middle, full_qkv, vectors)
-        g_first, keep_c = after(g_first, keep_c)
+        over_b, got_c = after(over_b, got_c)
+        part_a, part_b, other_c = part_a + over_a, part_b + over_b, keep_c[1] + got_c[1]
+        d_proj, part_a, part_b, other_c = after(d_proj, part_a, part_b, other_c)
+        over_c, over_a, over_b = (
+            plan.over_x(other_c),
+            plan.over_z(part_a, 2),
+            plan.over_z(part_b, 2),
+        )
+        input_grad, late = input_gradient(tokens, d_proj, d_middle, full_qkv, vectors)
+        late, over_c = after(late, over_c)
         mine_c = keep_c[0] + got_c[0] + over_c
-        part_c = plan.to_keep(mine_c) + plan.over_y(plan.to_send(mine_c))
-        part_b = plan.to_keep(mine_b) + low_b
-        c_pieces = plan.pieces(plan.over_both_z(part_c))
-        a_pieces = plan.pieces(plan.over_both_z(part_a))
-        b_pieces = plan.pieces(plan.over_both_z(part_b))
-        late = plan.reduce_late(g_first)
+        other_c, mine_c, late = after(plan.to_send(mine_c), mine_c, late)
+        over_c, more = plan.over_y(other_c), plan.over_core(late)
+        over_c, more, over_a = after(over_c, more, over_a)
+        part_c, late, part_a = plan.to_keep(mine_c) + over_c, late + more, part_a + over_a
+        part_c, late, part_a = after(part_c, late, part_a)
+        over_c, more = plan.over_z(part_c, 1), plan.over_x(late)
+        across_a, beside_a = plan.over_y(part_a), plan.over_core(part_a)
+        over_c, more, over_b = after(over_c, more, over_b)
+        part_c, late, part_b = part_c + over_c, late + more, part_b + over_b
+        part_c, late, part_b = after(part_c, late, part_b)
+        over_c, more = plan.over_z(part_c, 2), plan.over_y(late)
+        across_b, beside_b = plan.over_y(part_b), plan.over_core(part_b)
+        over_c, more, across_a, across_b = after(over_c, more, across_a, across_b)
+        a_pieces = (part_a, across_a, beside_a, plan.over_core(across_a))
+        b_pieces = (part_b, across_b, beside_b, plan.over_core(across_b))
+        part_c, late = part_c + over_c, late + more
+        part_c, late, a_pieces, b_pieces = after(part_c, late, a_pieces, b_pieces)
+        across_c, beside_c, more = plan.over_y(part_c), plan.over_core(part_c), plan.over_z(late, 1)
+        outer_grads = unpack_outer(index, a_pieces, b_pieces, width, ff)
+        across_c, beside_c, more, outer_grads = after(across_c, beside_c, more, outer_grads)
+        late = late + more
+        c_pieces = (part_c, across_c, beside_c, plan.over_core(across_c))
+        late = late + plan.over_z(late, 2)
         g_drop, g_lift, g_out, g_out_bias, g_gain_two, g_shift_two, g_drop_bias, g_lift_bias = (
-            unpack_outer(index, a_pieces, b_pieces, width, ff)
+            outer_grads
         )
         g_qkv, g_query, g_value, g_gain_one, g_shift_one = unpack_inner(index, c_pieces, late)
     else:

time: 185 us -> 151 us (0.82)
  waiting for transfers between devices: 50.8 us -> 31.2 us
  local copies, waits for them, and re-layouts: 21.6 us -> 8.18 us
  Pallas kernels: 76.5 us -> 80.7 us
  starting transfers between devices: 29.1 us -> 26.6 us
  other arithmetic: 5.14 us -> 3.03 us
    ppermute x38 -> x37, waiting for transfers between devices: 50.8 us -> 31.2 us  [swap(): return lax.ppermute(v, AXES, pairs)]
    reshape x9 -> x0, local copies, waits for them, and re-layouts: 6.16 us -> none  [per_device(): v.reshape(-1, shard)]
    dynamic_slice x4 -> x3, local copies, waits for them, and re-layouts: 5.6 us -> 0.1 us  [half_of(): return lax.dynamic_slice_in_dim(v, which * rows, rows, v.ndim - 2)]
    pallas_call x2 -> x4, Pallas kernels: 5.31 us -> 9.39 us  [the longest x1 3.2 us: unpack_outer(): pl.pallas_call(unpack_outer_kernel, grid=(1,), in_specs=[SCALARS, *whole_...]
    ppermute x38 -> x37, starting transfers between devices: 29.1 us -> 26.6 us  [swap(): return lax.ppermute(v, AXES, pairs)]
  transfers between devices with their start and end apart: 38 -> 37, of which waited for: 13 -> 15; matrix products, arithmetic and copies ran while one was open for 9% -> 4% of each run, Pallas kernels for 21% -> 32%
where the time goes in v3:
time: 151 us
  Pallas kernels  80.7 us (53%)
  waiting for transfers between devices  31.2 us (21%)
  starting transfers between devices  26.6 us (18%)
  local copies, waits for them, and re-layouts  8.18 us (5%)
  other arithmetic  3.03 us (2%)
    ppermute x37, waiting for transfers between devices, swap(): return lax.ppermute(v, AXES, pairs)  31.2 us
    pallas_call x1, Pallas kernels, mlp_both_ways(): pl.pallas_call(functools.partial(mlp_kernel, length, 256), grid=(images /...  28.9 us
    ppermute x37, starting transfers between devices, swap(): return lax.ppermute(v, AXES, pairs)  26.6 us
    pallas_call x3, Pallas kernels, attention_backward(): pl.pallas_call(functools.partial(back_kernel, length), grid=(count // gro...  18.5 us
    pallas_call x1, Pallas kernels, forward_attention(): pl.pallas_call(functools.partial(attend_kernel, length), grid=(images //...  10.4 us
    unnamed x60, local copies, waits for them, and re-layouts  8.06 us
    pallas_call x1, Pallas kernels, input_gradient(): pl.pallas_call(functools.partial(input_kernel, length), grid=(images // g...  7.41 us
    pallas_call x1, Pallas kernels, qkv_weight_gradient(): pl.pallas_call(weight_kernel, grid=(images // group,), in_specs=[SCALARS,...  6.02 us
  transfers between devices with their start and end apart: 37, of which 15 were waited for; matrix products, arithmetic and copies ran while one was open for 4% of the time, Pallas kernels for 32%

profile of v3, /device:TPU:0, one launch (start us, length us, event | category | flops | bytes accessed | tf_op | source)
XLA Modules:
  0.0 150.7 jit_solution(11728252261616279313)
XLA Ops:
  0.7 0.6 pad_add_fusion.index
  1.3 1.9 %pack_first.1.packed = bf16[104,1152]{1,0:T(8,128)(2,1)} custom-call(s32[3]{0:T(128)} %pad_add_fusion.index, bf16[192]{0:T(256)(128)(2,1)} %refs_0_.1, bf16[192]{0:T(256)(128)(2,1)} %refs_1_.1, bf16[192]{0:T(256)(128)(2,1)} %refs_2_.1, bf16[192]{0:T(256)(128)(2,1)} %refs_3_.1, bf16[192]{0:T(256)(128)(2,1)} %refs_4_.1, bf16[192]{0:T(256)(128)(2,1)} %refs_5_.1, ...), custom_call_target="tpu_custom_call" | custom-call | flops 1000 | bytes 1 | tf_op jit(solution)/shard_map/pack_first/pallas_call | solution.py:451
  3.1 2.9 %collective-permute-start = (bf16[104,1152]{1,0:T(8,128)(2,1)}, bf16[104,1152]{1,0:T(8,128)(2,1)S(1)}, u32[]{:S(2)}, u32[]{:S(2)}) collective-permute-start(bf16[104,1152]{1,0:T(8,128)(2,1)} %pack_first.1.packed), channel_id=1, source_target_pairs={{0,1},{1,0},{2,3},{3,2},{4,5},{5,4},{6,7},{7,6},{8,9},{9,8},{10,11... | collective-permute-start | bytes 718856 | tf_op jit(solution)/shard_map/ppermute | solution.py:681
  6.1 2.2 %pack_rest.1 = (bf16[96,384]{1,0:T(8,128)(2,1)}, bf16[96,1536]{1,0:T(8,128)(2,1)}, bf16[384,384]{1,0:T(8,128)(2,1)}) custom-call(s32[3]{0:T(128)} %pad_add_fusion.index, bf16[192,384]{1,0:T(8,128)(2,1)} %out_own.1, bf16[192,1536]{1,0:T(8,128)(2,1)} %lift_own.1, bf16[768,384]{1,0:T(8,128)(2,1)} %drop_own.1), custom_call_target="tpu_custom_call" | custom-call | flops 1000 | bytes 1 | tf_op jit(solution)/shard_map/pack_rest/pallas_call | solution.py:464
  8.3 2.0 %collective-permute-start.4 = (bf16[384,384]{1,0:T(8,128)(2,1)}, bf16[384,384]{1,0:T(8,128)(2,1)S(1)}, u32[]{:S(2)}, u32[]{:S(2)}) collective-permute-start(bf16[384,384]{1,0:T(8,128)(2,1)} %get-tuple-element.133), channel_id=1, source_target_pairs={{0,1},{1,0},{2,3},{3,2},{4,5},{5,4},{6,7},{7,6},{8,9},{9,8},{10,11... | collective-permute-start | bytes 884744 | tf_op jit(solution)/shard_map/ppermute | solution.py:681
  10.3 2.6 %collective-permute-done.near = bf16[104,1152]{1,0:T(8,128)(2,1)S(1)} collective-permute-done((bf16[104,1152]{1,0:T(8,128)(2,1)}, bf16[104,1152]{1,0:T(8,128)(2,1)S(1)}, u32[]{:S(2)}, u32[]{:S(2)}) %collective-permute-start) | collective-permute-done | bytes 239648 | tf_op jit(solution)/shard_map/ppermute | solution.py:681
  13.0 2.1 %collective-permute-start.2 = (bf16[96,384]{1,0:T(8,128)(2,1)}, bf16[96,384]{1,0:T(8,128)(2,1)S(1)}, u32[]{:S(2)}, u32[]{:S(2)}) collective-permute-start(bf16[96,384]{1,0:T(8,128)(2,1)} %get-tuple-element.131), channel_id=1, source_target_pairs={{0,1},{1,0},{2,3},{3,2},{4,5},{5,4},{6,7},{7,6},{8,9},{9,8},{10,11... | collective-permute-start | bytes 221192 | tf_op jit(solution)/shard_map/ppermute | solution.py:681
  15.0 1.2 copy.33.tok_ref
  16.2 0.7 copy-done.15
  16.9 10.4 %attend.1 = (bf16[8,208,384]{2,1,0:T(8,128)(2,1)}, bf16[8,208,1152]{2,1,0:T(8,128)(2,1)}, bf16[8,208,384]{2,1,0:T(8,128)(2,1)}, bf16[384,1152]{1,0:T(8,128)(2,1)}, f32[12,384]{1,0:T(8,128)}) custom-call(s32[3]{0:T(128)} %pad_add_fusion.index, bf16[8,197,384]{2,1,0:T(8,128)(2,1)} %copy.33.tok_ref, bf16[104,1152]{1,0:T(8,128)(2,1)} %pack_first.1.packed, ...), custom_call_target="tpu_custom_call" | custom-call | flops 1000 | bytes 1 | tf_op jit(solution)/shard_map/attend/pallas_call | solution.py:480
  27.4 0.3 collective-permute-start.6
  27.7 0.3 collective-permute-start.7
  27.9 0.2 collective-permute-start.5
  28.2 1.2 copy.34.cot_ref
  29.4 0.2 collective-permute-done.5.out_far
  29.6 0.6 copy-done.26
  30.3 0.1 copy-done.13
  30.4 28.9 %mlp.1 = (bf16[8,197,384]{2,1,0:T(8,128)(2,1)}, f32[8,208,384]{2,1,0:T(8,128)}, bf16[8,208,384]{2,1,0:T(8,128)(2,1)}, bf16[2,400,384]{2,1,0:T(8,128)(2,1)}, bf16...) custom-call(s32[3]{0:T(128)} %pad_add_fusion.index, ...), custom_call_target="tpu_custom_call" | custom-call | flops 1000 | bytes 1 | tf_op jit(solution)/shard_map/mlp/pallas_call | solution.py:511
  59.3 0.3 collective-permute-start.9
  59.6 0.3 collective-permute-start.8
  59.9 5.2 %back.3.refs_2_ = bf16[8,208,1152]{2,1,0:T(8,128)(2,1)} custom-call(bf16[8,208,1152]{2,1,0:T(8,128)(2,1)} %get-tuple-element.140.refs_0_, bf16[8,208,384]{2,1,0:T(8,128)(2,1)} %get-tuple-element.141.refs_1_), custom_call_target="tpu_custom_call" | custom-call | flops 1000 | bytes 1 | tf_op jit(solution)/shard_map/back/pallas_call | solution.py:567
  65.2 1.0 copy-done.5
  66.3 0.2 add.98
  66.5 1.6 %collective-permute-start.11 = (bf16[2,240,384]{2,1,0:T(8,128)(2,1)S(1)}, bf16[2,240,384]{2,1,0:T(8,128)(2,1)S(1)}, u32[]{:S(2)}, u32[]{:S(2)}) collective-permute-start(bf16[2,240,384]{2,1,0:T(8,128)(2,1)S(1)} %constant_dynamic-slice_fusion.2), channel_id=1, source_target_pairs={{0,4},{1,5},{2,6},{3,7},{4,0},{5,1},{6,2},{7,3},{8,12},{9,13},{10,... | collective-permute-start | bytes 1105928 | tf_op jit(solution)/shard_map/ppermute | solution.py:681
  68.1 0.7 collective-permute-start.10
  68.8 8.1 %back.4.refs_2_ = bf16[8,208,1152]{2,1,0:T(8,128)(2,1)} custom-call(bf16[8,208,1152]{2,1,0:T(8,128)(2,1)} %get-tuple-element.140.refs_0_, bf16[8,208,384]{2,1,0:T(8,128)(2,1)} %get-tuple-element.141.refs_1_, bf16[8,208,1152]{2,1,0:T(8,128)(2,1)} %back.3.refs_2_), custom_call_target="tpu_custom_call", output_to_operand_aliasing={{}: (2, {})} | custom-call | flops 2000 | bytes 1 | tf_op jit(solution)/shard_map/back/pallas_call | solution.py:567
  76.9 0.3 collective-permute-done.10
  77.4 0.1 dynamic-slice_add_fusion
  77.5 1.0 collective-permute-start.13
  78.5 1.3 collective-permute-start.12
  79.8 5.2 %back.5.d_proj_ref = bf16[8,208,1152]{2,1,0:T(8,128)(2,1)} custom-call(bf16[8,208,1152]{2,1,0:T(8,128)(2,1)} %get-tuple-element.140.refs_0_, bf16[8,208,384]{2,1,0:T(8,128)(2,1)} %get-tuple-element.141.refs_1_, bf16[8,208,1152]{2,1,0:T(8,128)(2,1)} %back.4.refs_2_), custom_call_target="tpu_custom_call", output_to_operand_aliasing={{}: (2, {})} | custom-call | flops 1000 | bytes 1 | tf_op jit(solution)/shard_map/back/pallas_call | solution.py:567
  85.1 1.6 %collective-permute-start.14 = (bf16[200,384]{1,0:T(8,128)(2,1)S(1)}, bf16[200,384]{1,0:T(8,128)(2,1)S(1)}, u32[]{:S(2)}, u32[]{:S(2)}) collective-permute-start(bf16[200,384]{1,0:T(8,128)(2,1)S(1)} %dynamic-slice_add_fusion.1), channel_id=1, source_target_pairs={{0,8},{1,9},{2,10},{3,11},{4,12},{5,13},{6,14},{7,15},{8,0},{9,1},... | collective-permute-start | bytes 460808 | tf_op jit(solution)/shard_map/ppermute | solution.py:681
  86.7 6.0 %qkv_weight_gradient.1 = (bf16[2,304,384]{2,1,0:T(8,128)(2,1)}, bf16[2,304,384]{2,1,0:T(8,128)(2,1)}) custom-call(s32[3]{0:T(128)} %pad_add_fusion.index, bf16[8,208,384]{2,1,0:T(8,128)(2,1)} %get-tuple-element.166.normed_ref, bf16[8,208,1152]{2,1,0:T(8,128)(2,1)} %back.5.d_proj_ref), custom_call_target="tpu_custom_call" | custom-call | flops 1000 | bytes 1 | tf_op jit(solution)/shard_map/qkv_weight_gradient/pallas_call | solution.py:585
  92.8 0.5 collective-permute-start.15
  93.3 6.5 %collective-permute-done.15 = bf16[240,384]{1,0:T(8,128)(2,1)S(1)} collective-permute-done((bf16[240,384]{1,0:T(8,128)(2,1)S(1)}, bf16[240,384]{1,0:T(8,128)(2,1)S(1)}, u32[]{:S(2)}, u32[]{:S(2)}) %collective-permute-start.15) | collective-permute-done | bytes 184352 | tf_op jit(solution)/shard_map/ppermute | solution.py:681
  99.9 1.0 add_bitcast_fusion.1
  100.9 1.4 collective-permute-start.17
  102.3 2.6 %collective-permute-start.20 = (bf16[200,384]{1,0:T(8,128)(2,1)S(1)}, bf16[200,384]{1,0:T(8,128)(2,1)S(1)}, u32[]{:S(2)}, u32[]{:S(2)}) collective-permute-start(bf16[200,384]{1,0:T(8,128)(2,1)S(1)} %add.109), channel_id=1, source_target_pairs={{0,16},{1,17},{2,18},{3,19},{4,20},{5,21},{6,22},{7,23},{8,24},{9,... | collective-permute-start | bytes 460808 | tf_op jit(solution)/shard_map/ppermute | solution.py:681
  104.9 7.4 %input_gradient.1 = (bf16[8,197,384]{2,1,0:T(8,128)(2,1)}, f32[8,384]{1,0:T(8,128)}) custom-call(bf16[8,197,384]{2,1,0:T(8,128)(2,1)} %copy.33.tok_ref, bf16[8,208,1152]{2,1,0:T(8,128)(2,1)} %back.5.d_proj_ref, f32[8,208,384]{2,1,0:T(8,128)} %get-tuple-element.175.d_middle_ref, bf16[384,1152]{1,0:T(8,128)(2,1)} %get-tuple-element.176.w_ref, ...), custom_call_target="tpu_custom_call" | custom-call | flops 1000 | bytes 1 | tf_op jit(solution)/shard_map/input_gradient/pallas_call | solution.py:605
  112.4 0.6 collective-permute-start.18
  113.0 0.3 collective-permute-start.23
  113.3 1.0 collective-permute-done.19
  114.4 2.9 %collective-permute-done.18 = bf16[152,384]{1,0:T(8,128)(2,1)S(1)} collective-permute-done((bf16[152,384]{1,0:T(8,128)(2,1)S(1)}, bf16[152,384]{1,0:T(8,128)(2,1)S(1)}, u32[]{:S(2)}, u32[]{:S(2)}) %collective-permute-start.18) | collective-permute-done | bytes 116768 | tf_op jit(solution)/shard_map/ppermute | solution.py:681
  117.4 0.5 collective-permute-start.21
  117.9 0.6 collective-permute-start.22
  118.6 6.3 %collective-permute-done.23 = bf16[240,384]{1,0:T(8,128)(2,1)S(1)} collective-permute-done((bf16[240,384]{1,0:T(8,128)(2,1)S(1)}, bf16[240,384]{1,0:T(8,128)(2,1)S(1)}, u32[]{:S(2)}, u32[]{:S(2)}) %collective-permute-start.23) | collective-permute-done | bytes 184352 | tf_op jit(solution)/shard_map/ppermute | solution.py:681
  124.9 1.0 collective-permute-done.21
  126.1 0.8 collective-permute-start.27
  126.9 1.3 collective-permute-start.26
  128.1 0.7 collective-permute-start.25
  128.9 6.3 %collective-permute-done.25 = f32[8,384]{1,0:T(8,128)S(1)} collective-permute-done((f32[8,384]{1,0:T(8,128)S(1)}, f32[8,384]{1,0:T(8,128)S(1)}, u32[]{:S(2)}, u32[]{:S(2)}) %collective-permute-start.25) | collective-permute-done | bytes 12320 | tf_op jit(solution)/shard_map/ppermute | solution.py:681
  135.3 0.5 collective-permute-start.28
  135.9 1.0 collective-permute-done.28.refs_2_
  137.0 0.2 collective-permute-done.29.refs_3_
  137.2 1.6 %collective-permute-start.32 = (bf16[152,384]{1,0:T(8,128)(2,1)S(1)}, bf16[152,384]{1,0:T(8,128)(2,1)S(1)}, u32[]{:S(2)}, u32[]{:S(2)}) collective-permute-start(bf16[152,384]{1,0:T(8,128)(2,1)S(1)} %add.124.refs_0_), channel_id=1, source_target_pairs={{0,4},{1,5},{2,6},{3,7},{4,0},{5,1},{6,2},{7,3},{8,12},{9,13},{10,... | collective-permute-start | bytes 350216 | tf_op jit(solution)/shard_map/ppermute | solution.py:681
  138.9 3.2 %unpack_outer.1 = (f32[768,384]{1,0:T(8,128)}, f32[192,1536]{1,0:T(8,128)}, f32[192,384]{1,0:T(8,128)}, f32[192]{0:T(256)}, f32[192]{0:T(256)}, /*index=5*/f32[192]{0:T(256)}, f32[192]{0:T(256)}, f32[768]{0:T(1024)}) custom-call(s32[3]{0:T(128)} %pad_add_fusion.index, bf16[200,384]{1,0:T(8,128)(2,1)} %copy-done.7, bf16[200,384]{1,0:T(8,128)(2,1)} %copy-done.19, ...), custom_call_target="tpu_custom_call" | custom-call | flops 3000 | bytes 1 | tf_op jit(solution)/shard_map/unpack_outer/pallas_call | solution.py:624
  142.1 0.4 collective-permute-done.34
  142.7 0.2 collective-permute-start.36
  142.9 1.2 copy.36
  144.1 1.2 copy.37
  145.3 2.1 %collective-permute-done.36 = f32[8,384]{1,0:T(8,128)S(1)} collective-permute-done((f32[8,384]{1,0:T(8,128)S(1)}, f32[8,384]{1,0:T(8,128)S(1)}, u32[]{:S(2)}, u32[]{:S(2)}) %collective-permute-start.36) | collective-permute-done | bytes 12320 | tf_op jit(solution)/shard_map/ppermute | solution.py:681
  147.3 0.6 add.127.refs_4_
  147.9 0.7 copy-done.24
  148.6 2.1 %unpack_inner.1 = (f32[192,1152]{1,0:T(8,128)}, f32[192]{0:T(256)}, f32[192]{0:T(256)}, f32[192]{0:T(256)}, f32[192]{0:T(256)}) custom-call(s32[3]{0:T(128)} %pad_add_fusion.index, bf16[152,384]{1,0:T(8,128)(2,1)} %copy-done.9, bf16[152,384]{1,0:T(8,128)(2,1)} %copy-done.22, bf16[152,384]{1,0:T(8,128)(2,1)} %copy-done.23, bf16[152,384]{1,0:T(8,128)(2,1)} %copy-done.24, ...), custom_call_target="tpu_custom_call" | custom-call | flops 2000 | bytes 1 | tf_op jit(solution)/shard_map/unpack_inner/pallas_call | solution.py:655
  (106 shorter events, 1.4 us)
Async XLA Ops:
  0.6 14.4 %copy-start.2 = (bf16[8,197,384]{2,0,1:T(8,128)(2,1)S(1)}, bf16[8,197,384]{2,0,1:T(8,128)(2,1)}, u32[]{:S(2)}) copy-start(bf16[8,197,384]{2,0,1:T(8,128)(2,1)} %param.15) | copy-start | bytes 3631108
  3.1 9.8 %collective-permute-start = (bf16[104,1152]{1,0:T(8,128)(2,1)}, bf16[104,1152]{1,0:T(8,128)(2,1)S(1)}, u32[]{:S(2)}, u32[]{:S(2)}) collective-permute-start(bf16[104,1152]{1,0:T(8,128)(2,1)} %pack_first.1.packed), channel_id=1, source_target_pairs={{0,1},{1,0},{2,3},{3,2},{4,5},{5,4},{6,7},{7,6},{8,9},{9,8},{10,11... | collective-permute-start | bytes 718856 | tf_op jit(solution)/shard_map/ppermute | solution.py:681
  8.3 19.1 %collective-permute-start.3 = (bf16[96,1536]{1,0:T(8,128)(2,1)}, bf16[96,1536]{1,0:T(8,128)(2,1)S(1)}, u32[]{:S(2)}, u32[]{:S(2)}) collective-permute-start(bf16[96,1536]{1,0:T(8,128)(2,1)} %get-tuple-element.132), channel_id=1, source_target_pairs={{0,1},{1,0},{2,3},{3,2},{4,5},{5,4},{6,7},{7,6},{8,9},{9,8},{10,11... | collective-permute-start | bytes 884744 | tf_op jit(solution)/shard_map/ppermute | solution.py:681
  8.3 19.1 %collective-permute-start.4 = (bf16[384,384]{1,0:T(8,128)(2,1)}, bf16[384,384]{1,0:T(8,128)(2,1)S(1)}, u32[]{:S(2)}, u32[]{:S(2)}) collective-permute-start(bf16[384,384]{1,0:T(8,128)(2,1)} %get-tuple-element.133), channel_id=1, source_target_pairs={{0,1},{1,0},{2,3},{3,2},{4,5},{5,4},{6,7},{7,6},{8,9},{9,8},{10,11... | collective-permute-start | bytes 884744 | tf_op jit(solution)/shard_map/ppermute | solution.py:681
  12.9 3.3 %copy-start.14 = (bf16[104,1152]{1,0:T(8,128)(2,1)}, bf16[104,1152]{1,0:T(8,128)(2,1)S(1)}, u32[]{:S(2)}) copy-start(bf16[104,1152]{1,0:T(8,128)(2,1)S(1)} %collective-permute-done.near) | copy-start | bytes 718852
  12.9 3.3 %collective-permute-start.1 = (bf16[104,1152]{1,0:T(8,128)(2,1)S(1)}, bf16[104,1152]{1,0:T(8,128)(2,1)S(1)}, u32[]{:S(2)}, u32[]{:S(2)}) collective-permute-start(bf16[104,1152]{1,0:T(8,128)(2,1)S(1)} %collective-permute-done.near), channel_id=1, source_target_pairs={{0,2},{1,3},{2,0},{3,1},{4,6},{5,7},{6,4},{7,5},{8,10},{9,11},{10,... | collective-permute-start | bytes 718856 | tf_op jit(solution)/shard_map/ppermute | solution.py:681
  13.0 14.4 %collective-permute-start.2 = (bf16[96,384]{1,0:T(8,128)(2,1)}, bf16[96,384]{1,0:T(8,128)(2,1)S(1)}, u32[]{:S(2)}, u32[]{:S(2)}) collective-permute-start(bf16[96,384]{1,0:T(8,128)(2,1)} %get-tuple-element.131), channel_id=1, source_target_pairs={{0,1},{1,0},{2,3},{3,2},{4,5},{5,4},{6,7},{7,6},{8,9},{9,8},{10,11... | collective-permute-start | bytes 221192 | tf_op jit(solution)/shard_map/ppermute | solution.py:681
  16.2 11.9 %copy-start.3 = (bf16[8,197,384]{2,0,1:T(8,128)(2,1)S(1)}, bf16[8,197,384]{2,0,1:T(8,128)(2,1)}, u32[]{:S(2)}) copy-start(bf16[8,197,384]{2,0,1:T(8,128)(2,1)} %param.29) | copy-start | bytes 3631108
  16.2 0.7 copy-start.15
  27.3 2.3 %copy-start.25 = (bf16[96,384]{1,0:T(8,128)(2,1)}, bf16[96,384]{1,0:T(8,128)(2,1)S(1)}, u32[]{:S(2)}) copy-start(bf16[96,384]{1,0:T(8,128)(2,1)S(1)} %collective-permute-done.2.out_near) | copy-start | bytes 221188
  27.3 2.2 %copy-start.10 = (bf16[96,1536]{1,0:T(8,128)(2,1)}, bf16[96,1536]{1,0:T(8,128)(2,1)S(1)}, u32[]{:S(2)}) copy-start(bf16[96,1536]{1,0:T(8,128)(2,1)S(1)} %collective-permute-done.3.lift_near) | copy-start | bytes 884740
  27.4 2.2 %copy-start.11 = (bf16[384,384]{1,0:T(8,128)(2,1)}, bf16[384,384]{1,0:T(8,128)(2,1)S(1)}, u32[]{:S(2)}) copy-start(bf16[384,384]{1,0:T(8,128)(2,1)S(1)} %collective-permute-done.4.drop_near) | copy-start | bytes 884740
  27.4 2.2 %collective-permute-start.6 = (bf16[96,1536]{1,0:T(8,128)(2,1)S(1)}, bf16[96,1536]{1,0:T(8,128)(2,1)S(1)}, u32[]{:S(2)}, u32[]{:S(2)}) collective-permute-start(bf16[96,1536]{1,0:T(8,128)(2,1)S(1)} %collective-permute-done.3.lift_near), channel_id=1, source_target_pairs={{0,2},{1,3},{2,0},{3,1},{4,6},{5,7},{6,4},{7,5},{8,10},{9,11},{10,... | collective-permute-start | bytes 884744 | tf_op jit(solution)/shard_map/ppermute | solution.py:681
  27.7 1.9 %collective-permute-start.7 = (bf16[384,384]{1,0:T(8,128)(2,1)S(1)}, bf16[384,384]{1,0:T(8,128)(2,1)S(1)}, u32[]{:S(2)}, u32[]{:S(2)}) collective-permute-start(bf16[384,384]{1,0:T(8,128)(2,1)S(1)} %collective-permute-done.4.drop_near), channel_id=1, source_target_pairs={{0,2},{1,3},{2,0},{3,1},{4,6},{5,7},{6,4},{7,5},{8,10},{9,11},{10,... | collective-permute-start | bytes 884744 | tf_op jit(solution)/shard_map/ppermute | solution.py:681
  27.9 1.6 %collective-permute-start.5 = (bf16[96,384]{1,0:T(8,128)(2,1)S(1)}, bf16[96,384]{1,0:T(8,128)(2,1)S(1)}, u32[]{:S(2)}, u32[]{:S(2)}) collective-permute-start(bf16[96,384]{1,0:T(8,128)(2,1)S(1)} %collective-permute-done.2.out_near), channel_id=1, source_target_pairs={{0,2},{1,3},{2,0},{3,1},{4,6},{5,7},{6,4},{7,5},{8,10},{9,11},{10,... | collective-permute-start | bytes 221192 | tf_op jit(solution)/shard_map/ppermute | solution.py:681
  29.5 0.7 copy-start.12
  29.6 0.8 copy-start.13
  59.3 5.8 %collective-permute-start.9 = (bf16[2,480,384]{2,1,0:T(8,128)(2,1)}, bf16[2,480,384]{2,1,0:T(8,128)(2,1)S(1)}, u32[]{:S(2)}, u32[]{:S(2)}) collective-permute-start(bf16[2,480,384]{2,1,0:T(8,128)(2,1)} %get-tuple-element.143), channel_id=1, source_target_pairs={{0,2},{1,3},{2,0},{3,1},{4,6},{5,7},{6,4},{7,5},{8,10},{9,11},{10,... | collective-permute-start | bytes 2211848 | tf_op jit(solution)/shard_map/ppermute | solution.py:681
  59.6 5.5 %collective-permute-start.8 = (bf16[2,400,384]{2,1,0:T(8,128)(2,1)}, bf16[2,400,384]{2,1,0:T(8,128)(2,1)S(1)}, u32[]{:S(2)}, u32[]{:S(2)}) collective-permute-start(bf16[2,400,384]{2,1,0:T(8,128)(2,1)} %get-tuple-element.142), channel_id=1, source_target_pairs={{0,2},{1,3},{2,0},{3,1},{4,6},{5,7},{6,4},{7,5},{8,10},{9,11},{10,... | collective-permute-start | bytes 1843208 | tf_op jit(solution)/shard_map/ppermute | solution.py:681
  59.9 5.2 %copy-start.6 = (bf16[2,400,384]{2,1,0:T(8,128)(2,1)S(1)}, bf16[2,400,384]{2,1,0:T(8,128)(2,1)}, u32[]{:S(2)}) copy-start(bf16[2,400,384]{2,1,0:T(8,128)(2,1)} %get-tuple-element.145) | copy-start | bytes 1843204
  65.2 1.1 copy-start.5
  66.5 10.8 %collective-permute-start.11 = (bf16[2,240,384]{2,1,0:T(8,128)(2,1)S(1)}, bf16[2,240,384]{2,1,0:T(8,128)(2,1)S(1)}, u32[]{:S(2)}, u32[]{:S(2)}) collective-permute-start(bf16[2,240,384]{2,1,0:T(8,128)(2,1)S(1)} %constant_dynamic-slice_fusion.2), channel_id=1, source_target_pairs={{0,4},{1,5},{2,6},{3,7},{4,0},{5,1},{6,2},{7,3},{8,12},{9,13},{10,... | collective-permute-start | bytes 1105928 | tf_op jit(solution)/shard_map/ppermute | solution.py:681
  68.1 9.1 %collective-permute-start.10 = (bf16[400,384]{1,0:T(8,128)(2,1)S(1)}, bf16[400,384]{1,0:T(8,128)(2,1)S(1)}, u32[]{:S(2)}, u32[]{:S(2)}) collective-permute-start(bf16[400,384]{1,0:T(8,128)(2,1)S(1)} %add_bitcast_fusion), channel_id=1, source_target_pairs={{0,1},{1,0},{2,3},{3,2},{4,5},{5,4},{6,7},{7,6},{8,9},{9,8},{10,11... | collective-permute-start | bytes 921608 | tf_op jit(solution)/shard_map/ppermute | solution.py:681
  77.5 7.5 %collective-permute-start.13 = (bf16[240,384]{1,0:T(8,128)(2,1)S(1)}, bf16[240,384]{1,0:T(8,128)(2,1)S(1)}, u32[]{:S(2)}, u32[]{:S(2)}) collective-permute-start(bf16[240,384]{1,0:T(8,128)(2,1)S(1)} %slice_bitcast_fusion), channel_id=1, source_target_pairs={{0,1},{1,0},{2,3},{3,2},{4,5},{5,4},{6,7},{7,6},{8,9},{9,8},{10,11... | collective-permute-start | bytes 552968 | tf_op jit(solution)/shard_map/ppermute | solution.py:681
  78.5 6.5 %collective-permute-start.12 = (bf16[200,384]{1,0:T(8,128)(2,1)S(1)}, bf16[200,384]{1,0:T(8,128)(2,1)S(1)}, u32[]{:S(2)}, u32[]{:S(2)}) collective-permute-start(bf16[200,384]{1,0:T(8,128)(2,1)S(1)} %constant_dynamic-slice_fusion.1), channel_id=1, source_target_pairs={{0,4},{1,5},{2,6},{3,7},{4,0},{5,1},{6,2},{7,3},{8,12},{9,13},{10,... | collective-permute-start | bytes 460808 | tf_op jit(solution)/shard_map/ppermute | solution.py:681
  85.1 7.7 %collective-permute-start.14 = (bf16[200,384]{1,0:T(8,128)(2,1)S(1)}, bf16[200,384]{1,0:T(8,128)(2,1)S(1)}, u32[]{:S(2)}, u32[]{:S(2)}) collective-permute-start(bf16[200,384]{1,0:T(8,128)(2,1)S(1)} %dynamic-slice_add_fusion.1), channel_id=1, source_target_pairs={{0,8},{1,9},{2,10},{3,11},{4,12},{5,13},{6,14},{7,15},{8,0},{9,1},... | collective-permute-start | bytes 460808 | tf_op jit(solution)/shard_map/ppermute | solution.py:681
  92.8 7.1 %collective-permute-start.16 = (bf16[2,304,384]{2,1,0:T(8,128)(2,1)}, bf16[2,304,384]{2,1,0:T(8,128)(2,1)S(1)}, u32[]{:S(2)}, u32[]{:S(2)}) collective-permute-start(bf16[2,304,384]{2,1,0:T(8,128)(2,1)} %get-tuple-element.170), channel_id=1, source_target_pairs={{0,2},{1,3},{2,0},{3,1},{4,6},{5,7},{6,4},{7,5},{8,10},{9,11},{10,... | collective-permute-start | bytes 1400840 | tf_op jit(solution)/shard_map/ppermute | solution.py:681
  92.8 7.0 %collective-permute-start.15 = (bf16[240,384]{1,0:T(8,128)(2,1)S(1)}, bf16[240,384]{1,0:T(8,128)(2,1)S(1)}, u32[]{:S(2)}, u32[]{:S(2)}) collective-permute-start(bf16[240,384]{1,0:T(8,128)(2,1)S(1)} %bitcast_add_fusion.2), channel_id=1, source_target_pairs={{0,8},{1,9},{2,10},{3,11},{4,12},{5,13},{6,14},{7,15},{8,0},{9,1},... | collective-permute-start | bytes 552968 | tf_op jit(solution)/shard_map/ppermute | solution.py:681
  100.9 11.5 %collective-permute-start.17 = (bf16[304,384]{1,0:T(8,128)(2,1)S(1)}, bf16[304,384]{1,0:T(8,128)(2,1)S(1)}, u32[]{:S(2)}, u32[]{:S(2)}) collective-permute-start(bf16[304,384]{1,0:T(8,128)(2,1)S(1)} %add_bitcast_fusion.1), channel_id=1, source_target_pairs={{0,1},{1,0},{2,3},{3,2},{4,5},{5,4},{6,7},{7,6},{8,9},{9,8},{10,11... | collective-permute-start | bytes 700424 | tf_op jit(solution)/shard_map/ppermute | solution.py:681
  102.3 11.0 %collective-permute-start.20 = (bf16[200,384]{1,0:T(8,128)(2,1)S(1)}, bf16[200,384]{1,0:T(8,128)(2,1)S(1)}, u32[]{:S(2)}, u32[]{:S(2)}) collective-permute-start(bf16[200,384]{1,0:T(8,128)(2,1)S(1)} %add.109), channel_id=1, source_target_pairs={{0,16},{1,17},{2,18},{3,19},{4,20},{5,21},{6,22},{7,23},{8,24},{9,... | collective-permute-start | bytes 460808 | tf_op jit(solution)/shard_map/ppermute | solution.py:681
  104.9 7.4 %copy-start.8 = (bf16[2,304,384]{2,1,0:T(8,128)(2,1)S(1)}, bf16[2,304,384]{2,1,0:T(8,128)(2,1)}, u32[]{:S(2)}) copy-start(bf16[2,304,384]{2,1,0:T(8,128)(2,1)} %get-tuple-element.172) | copy-start | bytes 1400836
  112.3 5.0 %copy-start.27 = (f32[8,384]{1,0:T(8,128)S(1)}, f32[8,384]{1,0:T(8,128)}, u32[]{:S(2)}) copy-start(f32[8,384]{1,0:T(8,128)} %get-tuple-element.184) | copy-start | bytes 36868
  112.4 4.9 %collective-permute-start.18 = (bf16[152,384]{1,0:T(8,128)(2,1)S(1)}, bf16[152,384]{1,0:T(8,128)(2,1)S(1)}, u32[]{:S(2)}, u32[]{:S(2)}) collective-permute-start(bf16[152,384]{1,0:T(8,128)(2,1)S(1)} %constant_dynamic-slice_fusion), channel_id=1, source_target_pairs={{0,4},{1,5},{2,6},{3,7},{4,0},{5,1},{6,2},{7,3},{8,12},{9,13},{10,... | collective-permute-start | bytes 350216 | tf_op jit(solution)/shard_map/ppermute | solution.py:681
  113.0 1.4 collective-permute-start.19
  113.0 11.9 %collective-permute-start.23 = (bf16[240,384]{1,0:T(8,128)(2,1)S(1)}, bf16[240,384]{1,0:T(8,128)(2,1)S(1)}, u32[]{:S(2)}, u32[]{:S(2)}) collective-permute-start(bf16[240,384]{1,0:T(8,128)(2,1)S(1)} %add.110), channel_id=1, source_target_pairs={{0,16},{1,17},{2,18},{3,19},{4,20},{5,21},{6,22},{7,23},{8,24},{9,... | collective-permute-start | bytes 552968 | tf_op jit(solution)/shard_map/ppermute | solution.py:681
  117.4 21.4 %copy-start.7 = (bf16[200,384]{1,0:T(8,128)(2,1)}, bf16[200,384]{1,0:T(8,128)(2,1)S(1)}, u32[]{:S(2)}) copy-start(bf16[200,384]{1,0:T(8,128)(2,1)S(1)} %add.120.refs_0_) | copy-start | bytes 460804
  117.4 8.5 %collective-permute-start.21 = (bf16[152,384]{1,0:T(8,128)(2,1)S(1)}, bf16[152,384]{1,0:T(8,128)(2,1)S(1)}, u32[]{:S(2)}, u32[]{:S(2)}) collective-permute-start(bf16[152,384]{1,0:T(8,128)(2,1)S(1)} %dynamic-slice_add_fusion.2), channel_id=1, source_target_pairs={{0,8},{1,9},{2,10},{3,11},{4,12},{5,13},{6,14},{7,15},{8,0},{9,1},... | collective-permute-start | bytes 350216 | tf_op jit(solution)/shard_map/ppermute | solution.py:681
  117.9 7.0 %collective-permute-start.22 = (f32[8,384]{1,0:T(8,128)S(1)}, f32[8,384]{1,0:T(8,128)S(1)}, u32[]{:S(2)}, u32[]{:S(2)}) collective-permute-start(f32[8,384]{1,0:T(8,128)S(1)} %add.119), channel_id=1, source_target_pairs={{0,1},{1,0},{2,3},{3,2},{4,5},{5,4},{6,7},{7,6},{8,9},{9,8},{10,11... | collective-permute-start | bytes 36872 | tf_op jit(solution)/shard_map/ppermute | solution.py:681
  126.0 16.9 %copy-start = (bf16[8,197,384]{2,1,0:T(8,128)(2,1)S(1)}, bf16[8,197,384]{2,1,0:T(8,128)(2,1)}, u32[]{:S(2)}) copy-start(bf16[8,197,384]{2,1,0:T(8,128)(2,1)} %get-tuple-element.237) | copy-start | bytes 3631108
  126.0 12.7 %copy-start.4 = (bf16[240,384]{1,0:T(8,128)(2,1)}, bf16[240,384]{1,0:T(8,128)(2,1)S(1)}, u32[]{:S(2)}) copy-start(bf16[240,384]{1,0:T(8,128)(2,1)S(1)} %add.123.refs_4_) | copy-start | bytes 552964
  126.1 9.2 %collective-permute-start.27 = (bf16[240,384]{1,0:T(8,128)(2,1)S(1)}, bf16[240,384]{1,0:T(8,128)(2,1)S(1)}, u32[]{:S(2)}, u32[]{:S(2)}) collective-permute-start(bf16[240,384]{1,0:T(8,128)(2,1)S(1)} %add.123.refs_4_), channel_id=1, source_target_pairs={{0,4},{1,5},{2,6},{3,7},{4,0},{5,1},{6,2},{7,3},{8,12},{9,13},{10,... | collective-permute-start | bytes 552968 | tf_op jit(solution)/shard_map/ppermute | solution.py:681
  126.9 8.3 %collective-permute-start.26 = (bf16[200,384]{1,0:T(8,128)(2,1)S(1)}, bf16[200,384]{1,0:T(8,128)(2,1)S(1)}, u32[]{:S(2)}, u32[]{:S(2)}) collective-permute-start(bf16[200,384]{1,0:T(8,128)(2,1)S(1)} %add.120.refs_0_), channel_id=1, source_target_pairs={{0,4},{1,5},{2,6},{3,7},{4,0},{5,1},{6,2},{7,3},{8,12},{9,13},{10,... | collective-permute-start | bytes 460808 | tf_op jit(solution)/shard_map/ppermute | solution.py:681
  128.1 7.1 %collective-permute-start.24 = (bf16[152,384]{1,0:T(8,128)(2,1)S(1)}, bf16[152,384]{1,0:T(8,128)(2,1)S(1)}, u32[]{:S(2)}, u32[]{:S(2)}) collective-permute-start(bf16[152,384]{1,0:T(8,128)(2,1)S(1)} %add.121), channel_id=1, source_target_pairs={{0,16},{1,17},{2,18},{3,19},{4,20},{5,21},{6,22},{7,23},{8,24},{9,... | collective-permute-start | bytes 350216 | tf_op jit(solution)/shard_map/ppermute | solution.py:681
  128.1 7.0 %collective-permute-start.25 = (f32[8,384]{1,0:T(8,128)S(1)}, f32[8,384]{1,0:T(8,128)S(1)}, u32[]{:S(2)}, u32[]{:S(2)}) collective-permute-start(f32[8,384]{1,0:T(8,128)S(1)} %add.122), channel_id=1, source_target_pairs={{0,4},{1,5},{2,6},{3,7},{4,0},{5,1},{6,2},{7,3},{8,12},{9,13},{10,... | collective-permute-start | bytes 36872 | tf_op jit(solution)/shard_map/ppermute | solution.py:681
  128.9 8.1 %collective-permute-start.30 = (bf16[240,384]{1,0:T(8,128)(2,1)S(1)}, bf16[240,384]{1,0:T(8,128)(2,1)S(1)}, u32[]{:S(2)}, u32[]{:S(2)}) collective-permute-start(bf16[240,384]{1,0:T(8,128)(2,1)S(1)} %add.123.refs_4_), channel_id=1, source_target_pairs={{0,2},{1,3},{2,0},{3,1},{4,6},{5,7},{6,4},{7,5},{8,10},{9,11},{10,... | collective-permute-start | bytes 552968 | tf_op jit(solution)/shard_map/ppermute | solution.py:681
  135.2 3.6 %copy-start.19 = (bf16[200,384]{1,0:T(8,128)(2,1)}, bf16[200,384]{1,0:T(8,128)(2,1)S(1)}, u32[]{:S(2)}) copy-start(bf16[200,384]{1,0:T(8,128)(2,1)S(1)} %collective-permute-done.26.refs_1_) | copy-start | bytes 460804
  135.2 3.6 %copy-start.16 = (bf16[240,384]{1,0:T(8,128)(2,1)}, bf16[240,384]{1,0:T(8,128)(2,1)S(1)}, u32[]{:S(2)}) copy-start(bf16[240,384]{1,0:T(8,128)(2,1)S(1)} %collective-permute-done.27.refs_5_) | copy-start | bytes 552964
  135.2 2.0 %collective-permute-start.31 = (bf16[240,384]{1,0:T(8,128)(2,1)S(1)}, bf16[240,384]{1,0:T(8,128)(2,1)S(1)}, u32[]{:S(2)}, u32[]{:S(2)}) collective-permute-start(bf16[240,384]{1,0:T(8,128)(2,1)S(1)} %collective-permute-done.27.refs_5_), channel_id=1, source_target_pairs={{0,2},{1,3},{2,0},{3,1},{4,6},{5,7},{6,4},{7,5},{8,10},{9,11},{10,... | collective-permute-start | bytes 552968 | tf_op jit(solution)/shard_map/ppermute | solution.py:681
  135.3 1.6 %collective-permute-start.28 = (bf16[200,384]{1,0:T(8,128)(2,1)S(1)}, bf16[200,384]{1,0:T(8,128)(2,1)S(1)}, u32[]{:S(2)}, u32[]{:S(2)}) collective-permute-start(bf16[200,384]{1,0:T(8,128)(2,1)S(1)} %add.120.refs_0_), channel_id=1, source_target_pairs={{0,2},{1,3},{2,0},{3,1},{4,6},{5,7},{6,4},{7,5},{8,10},{9,11},{10,... | collective-permute-start | bytes 460808 | tf_op jit(solution)/shard_map/ppermute | solution.py:681
  135.8 1.4 collective-permute-start.29
  135.9 8.2 %copy-start.9 = (bf16[152,384]{1,0:T(8,128)(2,1)}, bf16[152,384]{1,0:T(8,128)(2,1)S(1)}, u32[]{:S(2)}) copy-start(bf16[152,384]{1,0:T(8,128)(2,1)S(1)} %add.124.refs_0_) | copy-start | bytes 350212
  136.9 1.9 %copy-start.20 = (bf16[200,384]{1,0:T(8,128)(2,1)}, bf16[200,384]{1,0:T(8,128)(2,1)S(1)}, u32[]{:S(2)}) copy-start(bf16[200,384]{1,0:T(8,128)(2,1)S(1)} %collective-permute-done.28.refs_2_) | copy-start | bytes 460804
  136.9 1.9 %copy-start.17 = (bf16[240,384]{1,0:T(8,128)(2,1)}, bf16[240,384]{1,0:T(8,128)(2,1)S(1)}, u32[]{:S(2)}) copy-start(bf16[240,384]{1,0:T(8,128)(2,1)S(1)} %collective-permute-done.30.refs_6_) | copy-start | bytes 552964
  137.2 1.6 %copy-start.21 = (bf16[200,384]{1,0:T(8,128)(2,1)}, bf16[200,384]{1,0:T(8,128)(2,1)S(1)}, u32[]{:S(2)}) copy-start(bf16[200,384]{1,0:T(8,128)(2,1)S(1)} %collective-permute-done.29.refs_3_) | copy-start | bytes 460804
  137.2 1.7 %copy-start.18 = (bf16[240,384]{1,0:T(8,128)(2,1)}, bf16[240,384]{1,0:T(8,128)(2,1)S(1)}, u32[]{:S(2)}) copy-start(bf16[240,384]{1,0:T(8,128)(2,1)S(1)} %collective-permute-done.31.refs_7_) | copy-start | bytes 552964
  137.2 5.4 %collective-permute-start.32 = (bf16[152,384]{1,0:T(8,128)(2,1)S(1)}, bf16[152,384]{1,0:T(8,128)(2,1)S(1)}, u32[]{:S(2)}, u32[]{:S(2)}) collective-permute-start(bf16[152,384]{1,0:T(8,128)(2,1)S(1)} %add.124.refs_0_), channel_id=1, source_target_pairs={{0,4},{1,5},{2,6},{3,7},{4,0},{5,1},{6,2},{7,3},{8,12},{9,13},{10,... | collective-permute-start | bytes 350216 | tf_op jit(solution)/shard_map/ppermute | solution.py:681
  138.8 3.8 %collective-permute-start.33 = (bf16[152,384]{1,0:T(8,128)(2,1)S(1)}, bf16[152,384]{1,0:T(8,128)(2,1)S(1)}, u32[]{:S(2)}, u32[]{:S(2)}) collective-permute-start(bf16[152,384]{1,0:T(8,128)(2,1)S(1)} %add.124.refs_0_), channel_id=1, source_target_pairs={{0,2},{1,3},{2,0},{3,1},{4,6},{5,7},{6,4},{7,5},{8,10},{9,11},{10,... | collective-permute-start | bytes 350216 | tf_op jit(solution)/shard_map/ppermute | solution.py:681
  138.8 3.7 %collective-permute-start.34 = (f32[8,384]{1,0:T(8,128)S(1)}, f32[8,384]{1,0:T(8,128)S(1)}, u32[]{:S(2)}, u32[]{:S(2)}) collective-permute-start(f32[8,384]{1,0:T(8,128)S(1)} %add.125), channel_id=1, source_target_pairs={{0,8},{1,9},{2,10},{3,11},{4,12},{5,13},{6,14},{7,15},{8,0},{9,1},... | collective-permute-start | bytes 36872 | tf_op jit(solution)/shard_map/ppermute | solution.py:681
  142.6 1.5 copy-start.22
  142.6 1.5 copy-start.23
  142.6 5.4 %collective-permute-start.35 = (bf16[152,384]{1,0:T(8,128)(2,1)S(1)}, bf16[152,384]{1,0:T(8,128)(2,1)S(1)}, u32[]{:S(2)}, u32[]{:S(2)}) collective-permute-start(bf16[152,384]{1,0:T(8,128)(2,1)S(1)} %collective-permute-done.32.refs_1_), channel_id=1, source_target_pairs={{0,2},{1,3},{2,0},{3,1},{4,6},{5,7},{6,4},{7,5},{8,10},{9,11},{10,... | collective-permute-start | bytes 350216 | tf_op jit(solution)/shard_map/ppermute | solution.py:681
  142.7 1.4 copy-start.1
  142.7 4.7 %collective-permute-start.36 = (f32[8,384]{1,0:T(8,128)S(1)}, f32[8,384]{1,0:T(8,128)S(1)}, u32[]{:S(2)}, u32[]{:S(2)}) collective-permute-start(f32[8,384]{1,0:T(8,128)S(1)} %add.126), channel_id=1, source_target_pairs={{0,16},{1,17},{2,18},{3,19},{4,20},{5,21},{6,22},{7,23},{8,24},{9,... | collective-permute-start | bytes 36872 | tf_op jit(solution)/shard_map/ppermute | solution.py:681
  147.9 0.7 copy-start.24
  (1 other events, 0.6 us)

commit v4 on v3

--- a/solution.py
+++ b/solution.py
@@ -86,11 +86,12 @@
     full[pl.ds(pl.multiple_of(other + (1 - core) * half, 16), half), :] = far[0:half, :]
 
 
-def quarters(index, keep, send):
+def quarters(index, keep, send, x_first=False):
     x, core = index[0], index[1]
-    for slot, half in ((0, x), (1, 1 - x)):
-        yield keep, slot, half, core
-        yield send, slot, half, 1 - core
+    yield keep, 0, x, core
+    yield (keep if x_first else send), int(x_first), x, 1 - core
+    yield (send if x_first else keep), int(not x_first), 1 - x, core
+    yield send, 1, 1 - x, 1 - core
 
 
 def pack_first_kernel(index, *refs):
@@ -170,9 +171,67 @@
             mixed_ref[j, :, c : c + PAIR] = join_pair(both[:, :PAIR] / both[:, PAIR:]).astype(BF16)
 
 
-def mlp_kernel(
+def join_mlp(index, turn, w_lift, w_drop, lift_bias, vec_ref, lift, drop):
+    own, near, far = lift
+    block = own.shape[0]
+    half = block // 2
+    width = w_lift.shape[0]
+    x, core = index[0], index[1]
+    other = (1 - x) * block
+    for k in range(2):
+        source = slice((2 * k + turn) * width, (2 * k + turn + 1) * width)
+        part = slice(k * width, (k + 1) * width)
+        w_lift[pl.ds(pl.multiple_of(x * block, 16), block), part] = own[:, source]
+        w_lift[pl.ds(pl.multiple_of(other + core * half, 16), half), part] = near[:, source]
+        w_lift[pl.ds(pl.multiple_of(other + (1 - core) * half, 16), half), part] = far[:, source]
+        lift_bias[:, part] = vec_ref[8 + 2 * k + turn : 9 + 2 * k + turn, :]
+    own, near, far = drop
+    w_drop[pl.ds(pl.multiple_of(x * width, 16), width), :] = own[turn * width : (turn + 1) * width, :]
+    rest = jnp.where(core == turn, near[...], far[...])
+    w_drop[pl.ds(pl.multiple_of((1 - x) * width, 16), width), :] = rest
+
+
+def mlp_turn(normed, dz, w_lift, w_drop, lift_bias, a_drop, a_lift, a_bias, result, d_normed):
+    chunk = 256
+    for c in range(0, w_drop.shape[0], chunk):
+        part = slice(c, c + chunk)
+        hidden = nn(normed, w_lift[:, part]) + lift_bias[:, part]
+        cdf = 0.5 + 0.5 * lax.erf(hidden * ROOT_HALF)
+        bell = jnp.exp(hidden * hidden * -0.5) * GAUSS
+        active = (hidden * cdf).astype(BF16)
+        d_active = nt(dz, w_drop[part, :])
+        d_hidden = (d_active * (cdf + hidden * bell)).astype(BF16)
+        result = result + nn(active, w_drop[part, :])
+        d_normed = d_normed + nt(d_hidden, w_lift[:, part])
+        a_drop[part, :] += tn(active, dz)
+        a_lift[:, part] += tn(normed, d_hidden)
+        a_bias[:, part] += fold(d_hidden.astype(F32))
+    return result, d_normed
+
+
+def emit_turn(index, here, there, a_drop, a_lift, a_bias, vector_rows, a_out=None):
+    width = a_lift.shape[0]
+    columns = jnp.sum(a_bias[...], axis=0, keepdims=True)
+    rows = [columns[:, :width], columns[:, width:], *vector_rows]
+    count = sum(r.shape[0] for r in rows)
+    rows.append(jnp.zeros((VEC_ROWS - count, width), F32))
+    vectors = jnp.concatenate(rows, axis=0).astype(BF16)
+    deep, tall = width // 2, width // 4
+    for dest, slot, half, core in quarters(index, here, there, x_first=a_out is None):
+        first = pl.multiple_of((2 * half + core) * deep, 8)
+        rows_of = pl.ds(pl.multiple_of((2 * half + core) * tall, 8), tall)
+        dest[slot, 0:deep, :] = a_drop[pl.ds(first, deep), :].astype(BF16)
+        for k in range(2):
+            dest[slot, deep + k * tall : deep + (k + 1) * tall, :] = a_lift[
+                rows_of, k * width : (k + 1) * width
+            ].astype(BF16)
+        dest[slot, 2 * deep : 2 * deep + VEC_ROWS, :] = vectors
+        if a_out is not None:
+            dest[slot, 2 * deep + VEC_ROWS :, :] = a_out[rows_of, :].astype(BF16)
+
+
+def mlp_first_kernel(
     length,
-    chunk,
     index,
     tok_ref,
     cot_ref,
@@ -187,14 +246,94 @@
     drop_own,
     drop_near,
     drop_far,
+    middle_ref,
+    result_ref,
+    d_normed_ref,
+    here,
+    there,
+    x_s,
+    z_s,
+    w_out_ref,
+    w_lift_ref,
+    w_drop_ref,
+    lift_bias_ref,
+    a_drop,
+    a_lift,
+    a_bias,
+):
+    images, rows, width = x_s.shape
+    total = images * rows
+
+    @pl.when(pl.program_id(0) == 0)
+    def _():
+        zero_tail(x_s, length)
+        zero_tail(z_s, length)
+        join_pieces(w_out_ref, out_own, out_near, out_far, index)
+        join_mlp(
+            index,
+            0,
+            w_lift_ref,
+            w_drop_ref,
+            lift_bias_ref,
+            vec_ref,
+            (lift_own, lift_near, lift_far),
+            (drop_own, drop_near, drop_far),
+        )
+        for acc in (a_drop, a_lift, a_bias):
+            acc[...] = jnp.zeros_like(acc)
+
+    pad_rows(x_s, tok_ref, length)
+    pad_rows(z_s, cot_ref, length)
+    out_bias, gain, shift, drop_bias = (vec_ref[i : i + 1, :] for i in range(4, 8))
+    mixed = mixed_ref[...].reshape(total, width)
+    dz = z_s[...].reshape(total, width)
+    middle = x_s[...].reshape(total, width).astype(F32) + nn(mixed, w_out_ref[...]) + out_bias
+    middle_ref[...] = middle.reshape(images, rows, width)
+    normal, _ = normalise(middle)
+    normed = (normal * gain + shift).astype(BF16)
+    result, d_normed = mlp_turn(
+        normed,
+        dz,
+        w_lift_ref,
+        w_drop_ref,
+        lift_bias_ref,
+        a_drop,
+        a_lift,
+        a_bias,
+        middle + drop_bias,
+        jnp.zeros((total, width), F32),
+    )
+    result_ref[...] = result.reshape(images, rows, width)
+    d_normed_ref[...] = d_normed.reshape(images, rows, width)
+
+    @pl.when(pl.program_id(0) == pl.num_programs(0) - 1)
+    def _():
+        emit_turn(index, here, there, a_drop, a_lift, a_bias, [])
+
+
+def mlp_second_kernel(
+    length,
+    index,
+    cot_ref,
+    mixed_ref,
+    middle_ref,
+    result_ref,
+    d_normed_ref,
+    vec_ref,
+    out_own,
+    out_near,
+    out_far,
+    lift_own,
+    lift_near,
+    lift_far,
+    drop_own,
+    drop_near,
+    drop_far,
     out_ref,
     d_middle_ref,
     d_mixed_ref,
-    keep_a,
-    send_a,
-    keep_b,
-    send_b,
-    x_s,
+    here,
+    there,
     z_s,
     w_out_ref,
     w_lift_ref,
@@ -206,48 +345,45 @@
     a_vec,
     a_bias,
 ):
-    step = pl.program_id(0)
-    images, rows, width = x_s.shape
+    images, rows, width = z_s.shape
     total = images * rows
-    hidden_width = w_lift_ref.shape[1]
-
-    @pl.when(step == 0)
+
+    @pl.when(pl.program_id(0) == 0)
     def _():
-        zero_tail(x_s, length)
         zero_tail(z_s, length)
         join_pieces(w_out_ref, out_own, out_near, out_far, index)
-        join_pieces(w_lift_ref, lift_own, lift_near, lift_far, index)
-        join_pieces(w_drop_ref, drop_own, drop_near, drop_far, index)
-        for k in range(hidden_width // width):
-            lift_bias_ref[:, k * width : (k + 1) * width] = vec_ref[8 + k : 9 + k, :]
+        join_mlp(
+            index,
+            1,
+            w_lift_ref,
+            w_drop_ref,
+            lift_bias_ref,
+            vec_ref,
+            (lift_own, lift_near, lift_far),
+            (drop_own, drop_near, drop_far),
+        )
         for acc in (a_drop, a_lift, a_out, a_vec, a_bias):
             acc[...] = jnp.zeros_like(acc)
 
-    pad_rows(x_s, tok_ref, length)
     pad_rows(z_s, cot_ref, length)
-    out_bias, gain, shift, drop_bias = (vec_ref[i : i + 1, :] for i in range(4, 8))
+    gain, shift = vec_ref[5:6, :], vec_ref[6:7, :]
     mixed = mixed_ref[...].reshape(total, width)
     dz = z_s[...].reshape(total, width)
     dz_f = dz.astype(F32)
-    middle = x_s[...].reshape(total, width).astype(F32) + nn(mixed, w_out_ref[...]) + out_bias
-    normal, inverse = normalise(middle)
+    normal, inverse = normalise(middle_ref[...].reshape(total, width))
     normed = (normal * gain + shift).astype(BF16)
-    result = middle + drop_bias
-    d_normed = jnp.zeros((total, width), F32)
-    for c in range(0, hidden_width, chunk):
-        part = slice(c, c + chunk)
-        hidden = nn(normed, w_lift_ref[:, part]) + lift_bias_ref[:, part]
-        cdf = 0.5 + 0.5 * lax.erf(hidden * ROOT_HALF)
-        bell = jnp.exp(hidden * hidden * -0.5) * GAUSS
-        active = (hidden * cdf).astype(BF16)
-        d_active = nt(dz, w_drop_ref[part, :])
-        d_hidden_f = d_active * (cdf + hidden * bell)
-        d_hidden = d_hidden_f.astype(BF16)
-        result = result + nn(active, w_drop_ref[part, :])
-        d_normed = d_normed + nt(d_hidden, w_lift_ref[:, part])
-        a_drop[part, :] += tn(active, dz)
-        a_lift[:, part] += tn(normed, d_hidden)
-        a_bias[:, part] += fold(d_hidden.astype(F32))
+    result, d_normed = mlp_turn(
+        normed,
+        dz,
+        w_lift_ref,
+        w_drop_ref,
+        lift_bias_ref,
+        a_drop,
+        a_lift,
+        a_bias,
+        result_ref[...].reshape(total, width),
+        d_normed_ref[...].reshape(total, width),
+    )
     out = result.astype(BF16)
     for j in range(images):
         out_ref[j] = out[j * rows : j * rows + length]
@@ -261,33 +397,26 @@
     a_vec[2] += fold(d_normed)
     a_vec[3] += fold(dz_f)
 
-    @pl.when(step == pl.num_programs(0) - 1)
+    @pl.when(pl.program_id(0) == pl.num_programs(0) - 1)
     def _():
-        columns = jnp.sum(a_bias[...], axis=0, keepdims=True)
-        vector_rows = [jnp.sum(a_vec[...], axis=1)]
-        vector_rows += [columns[:, c : c + width] for c in range(0, hidden_width, width)]
-        vector_rows += [jnp.zeros((VEC_ROWS - 4 - hidden_width // width, width), F32)]
-        vectors = jnp.concatenate(vector_rows, axis=0).astype(BF16)
-        deep, tall = a_drop.shape[0] // 4, width // 4
-        for dest, slot, half, core in quarters(index, keep_a, send_a):
-            first = pl.multiple_of((2 * half + core) * deep, 8)
-            dest[slot, 0:deep, :] = a_drop[pl.ds(first, deep), :].astype(BF16)
-            dest[slot, deep : deep + VEC_ROWS, :] = vectors
-        for dest, slot, half, core in quarters(index, keep_b, send_b):
-            rows_of = pl.ds(pl.multiple_of((2 * half + core) * tall, 8), tall)
-            blocks = hidden_width // width
-            for k in range(blocks):
-                dest[slot, k * tall : (k + 1) * tall, :] = a_lift[
-                    rows_of, k * width : (k + 1) * width
-                ].astype(BF16)
-            dest[slot, blocks * tall : (blocks + 1) * tall, :] = a_out[rows_of, :].astype(BF16)
-
-
-def back_kernel(length, *refs):
-    proj_ref, d_mixed_ref = refs[:2]
-    d_proj_ref = refs[-1]
+        vectors = jnp.sum(a_vec[...], axis=1)
+        emit_turn(index, here, there, a_drop, a_lift, a_bias, [vectors], a_out)
+
+
+def back_kernel(length, first, index, proj_ref, normed_ref, d_mixed_ref, *refs):
+    if first:
+        d_proj_ref, a_qkv, a_proj = refs
+    else:
+        old_qkv, old_proj, _, d_proj_ref, here, there, a_qkv, a_proj = refs
     images, rows, wide = d_proj_ref.shape
     width = wide // 3
+    total = images * rows
+
+    @pl.when(pl.program_id(0) == 0)
+    def _():
+        a_qkv[...] = jnp.zeros_like(a_qkv) if first else old_qkv[...]
+        a_proj[...] = jnp.zeros_like(a_proj) if first else old_proj[...]
+
     live = lax.broadcasted_iota(jnp.int32, (rows, 2 * rows), 0) < length
     for j in range(images):
         for c in range(0, width, PAIR):
@@ -308,31 +437,20 @@
             d_proj_ref[j, :, c : c + PAIR] = d_query.astype(BF16)
             d_proj_ref[j, :, width + c : width + c + PAIR] = d_key.astype(BF16)
             d_proj_ref[j, :, 2 * width + c : 2 * width + c + PAIR] = d_value.astype(BF16)
-
-
-def weight_kernel(index, normed_ref, d_proj_ref, keep, send, a_qkv, a_proj):
-    step = pl.program_id(0)
-    images, rows, wide = d_proj_ref.shape
-    width = wide // 3
-    total = images * rows
-
-    @pl.when(step == 0)
-    def _():
-        for acc in (a_qkv, a_proj):
-            acc[...] = jnp.zeros_like(acc)
-
     d_proj = d_proj_ref[...].reshape(total, wide)
     a_qkv[...] += tn(normed_ref[...].reshape(total, width), d_proj)
     a_proj[...] += fold(d_proj.astype(F32))
-
-    @pl.when(step == pl.num_programs(0) - 1)
+    if first:
+        return
+
+    @pl.when(pl.program_id(0) == pl.num_programs(0) - 1)
     def _():
         columns = jnp.sum(a_proj[...], axis=0, keepdims=True)
         vectors = jnp.concatenate(
             [columns[:, :width], columns[:, 2 * width :], jnp.zeros((VEC_ROWS - 2, width), F32)], axis=0
         ).astype(BF16)
         tall = width // 4
-        for dest, slot, half, core in quarters(index, keep, send):
+        for dest, slot, half, core in quarters(index, here, there):
             rows_of = pl.ds(pl.multiple_of((2 * half + core) * tall, 8), tall)
             for k in range(3):
                 dest[slot, k * tall : (k + 1) * tall, :] = a_qkv[
@@ -374,30 +492,26 @@
 
 
 def unpack_outer_kernel(index, *refs):
-    a_pieces, b_pieces = refs[0:4], refs[4:8]
     g_drop, g_lift, g_out, g_out_bias, g_gain, g_shift, g_drop_bias, g_lift_bias, a_s, b_s = refs[8:]
-    placed(a_s, index, a_pieces)
-    placed(b_s, index, b_pieces)
     width = g_out.shape[1]
-    deep, tall = g_drop.shape[0] // 2, g_out.shape[0] // 2
-    blocks = g_lift.shape[1] // width
+    deep, tall = width // 2, width // 4
+    for turn, (full, pieces) in enumerate(((a_s, refs[0:4]), (b_s, refs[4:8]))):
+        placed(full, index, pieces)
+        for core in range(2):
+            first = turn * width + core * deep
+            g_drop[first : first + deep, :] = full[core, 0:deep, :]
+            for k in range(2):
+                block = 2 * k + turn
+                g_lift[core * tall : (core + 1) * tall, block * width : (block + 1) * width] = full[
+                    core, deep + k * tall : deep + (k + 1) * tall, :
+                ]
+        low, high = full[0, 2 * deep : 2 * deep + 1, :], full[0, 2 * deep + 1 : 2 * deep + 2, :]
+        g_lift_bias[turn * width : (turn + 1) * width] = jnp.where(index[0] == 0, low, high)[0]
     for core in range(2):
-        g_drop[core * deep : (core + 1) * deep, :] = a_s[core, 0:deep, :]
-        for k in range(blocks):
-            g_lift[core * tall : (core + 1) * tall, k * width : (k + 1) * width] = b_s[
-                core, k * tall : (k + 1) * tall, :
-            ]
-        g_out[core * tall : (core + 1) * tall, :] = b_s[core, blocks * tall : (blocks + 1) * tall, :]
-    vectors = a_s[0, deep : deep + VEC_ROWS, :]
+        g_out[core * tall : (core + 1) * tall, :] = b_s[core, 2 * deep + VEC_ROWS :, :]
+    vectors = b_s[0, 2 * deep : 2 * deep + VEC_ROWS, :]
     for i, ref in enumerate((g_out_bias, g_gain, g_shift, g_drop_bias)):
-        ref[...] = own_half(index, vectors[i : i + 1, :])
-    for k in range(blocks // 2):
-        row = jnp.where(
-            index[0] == 0,
-            vectors[4 + k : 5 + k, :],
-            vectors[4 + blocks // 2 + k : 5 + blocks // 2 + k, :],
-        )
-        g_lift_bias[k * width : (k + 1) * width] = row[0]
+        ref[...] = own_half(index, vectors[2 + i : 3 + i, :])
 
 
 def unpack_inner_kernel(index, *refs):
@@ -476,7 +590,7 @@
 def forward_attention(index, tokens, ff, packed, pieces):
     images, length, width = tokens.shape
     rows = -(-length // 16) * 16
-    group = 2 if images % 2 == 0 else 1
+    group = 4 if images % 4 == 0 else 1
     return pl.pallas_call(
         functools.partial(attend_kernel, length),
         grid=(images // group,),
@@ -502,14 +616,13 @@
     )(index, tokens, packed, *pieces)
 
 
-def mlp_both_ways(index, tokens, cotangent, mixed, vectors, ff, pieces):
+def mlp_first(index, tokens, cotangent, mixed, vectors, ff, pieces):
     images, length, width = tokens.shape
     rows = mixed.shape[1]
     group = 2 if images % 2 == 0 else 1
-    a_rows = ff // 4 + VEC_ROWS
-    b_rows = (width // 4) * (ff // width + 1)
+    quarter = width + VEC_ROWS
     return pl.pallas_call(
-        functools.partial(mlp_kernel, length, 256),
+        functools.partial(mlp_first_kernel, length),
         grid=(images // group,),
         in_specs=[
             SCALARS,
@@ -518,84 +631,99 @@
             per_step(group, rows, width),
             *whole_like((vectors, *pieces)),
         ],
+        out_specs=[per_step(group, rows, width)] * 3 + [whole(2, quarter, width)] * 2,
+        out_shape=[shape_of(F32, images, rows, width)] * 3 + [shape_of(BF16, 2, quarter, width)] * 2,
+        scratch_shapes=[
+            pltpu.VMEM((group, rows, width), BF16),
+            pltpu.VMEM((group, rows, width), BF16),
+            pltpu.VMEM((width, width), BF16),
+            pltpu.VMEM((width, ff // 2), BF16),
+            pltpu.VMEM((ff // 2, width), BF16),
+            pltpu.VMEM((1, ff // 2), F32),
+            pltpu.VMEM((ff // 2, width), F32),
+            pltpu.VMEM((width, ff // 2), F32),
+            pltpu.VMEM((8, ff // 2), F32),
+        ],
+        compiler_params=PARAMS,
+        cost_estimate=cost(1),
+        name="mlp_first",
+    )(index, tokens, cotangent, mixed, vectors, *pieces)
+
+
+def mlp_second(index, cotangent, mixed, middle, result, d_normed, vectors, ff, pieces):
+    images, length, width = cotangent.shape
+    rows = mixed.shape[1]
+    group = 2 if images % 2 == 0 else 1
+    quarter = width + VEC_ROWS + width // 4
+    return pl.pallas_call(
+        functools.partial(mlp_second_kernel, length),
+        grid=(images // group,),
+        in_specs=[
+            SCALARS,
+            per_step(group, length, width),
+            *[per_step(group, rows, width)] * 4,
+            *whole_like((vectors, *pieces)),
+        ],
         out_specs=[
             per_step(group, length, width),
             per_step(group, rows, width),
             per_step(group, rows, width),
-            whole(2, a_rows, width),
-            whole(2, a_rows, width),
-            whole(2, b_rows, width),
-            whole(2, b_rows, width),
+            whole(2, quarter, width),
+            whole(2, quarter, width),
         ],
         out_shape=[
             shape_of(BF16, images, length, width),
             shape_of(F32, images, rows, width),
             shape_of(BF16, images, rows, width),
-            shape_of(BF16, 2, a_rows, width),
-            shape_of(BF16, 2, a_rows, width),
-            shape_of(BF16, 2, b_rows, width),
-            shape_of(BF16, 2, b_rows, width),
+            shape_of(BF16, 2, quarter, width),
+            shape_of(BF16, 2, quarter, width),
         ],
         scratch_shapes=[
             pltpu.VMEM((group, rows, width), BF16),
-            pltpu.VMEM((group, rows, width), BF16),
             pltpu.VMEM((width, width), BF16),
-            pltpu.VMEM((width, ff), BF16),
-            pltpu.VMEM((ff, width), BF16),
-            pltpu.VMEM((1, ff), F32),
-            pltpu.VMEM((ff, width), F32),
-            pltpu.VMEM((width, ff), F32),
+            pltpu.VMEM((width, ff // 2), BF16),
+            pltpu.VMEM((ff // 2, width), BF16),
+            pltpu.VMEM((1, ff // 2), F32),
+            pltpu.VMEM((ff // 2, width), F32),
+            pltpu.VMEM((width, ff // 2), F32),
             pltpu.VMEM((width, width), F32),
             pltpu.VMEM((4, 8, width), F32),
-            pltpu.VMEM((8, ff), F32),
+            pltpu.VMEM((8, ff // 2), F32),
         ],
         compiler_params=PARAMS,
         cost_estimate=cost(1),
-        name="mlp",
-    )(index, tokens, cotangent, mixed, vectors, *pieces)
-
-
-def attention_backward(projected, d_mixed, length, first, count, earlier):
+        name="mlp_second",
+    )(index, cotangent, mixed, middle, result, d_normed, vectors, *pieces)
+
+
+def attention_backward(index, projected, normed, d_mixed, length, start, count, earlier=None):
     images, rows, wide = projected.shape
+    width = wide // 3
     group = 2 if images % 2 == 0 else 1
-    start = first // group
+    offset = start // group
+    first = earlier is None
+    c_rows = 3 * width // 4 + VEC_ROWS
 
     def at(*shape):
-        return pl.BlockSpec(shape, lambda i: (i + start if start else i, 0, 0))
-
-    more = [] if earlier is None else [earlier]
+        return pl.BlockSpec(shape, lambda i: (i + offset if offset else i, 0, 0))
+
+    sums = [(width, wide), (8, wide)]
+    more = () if first else earlier
     return pl.pallas_call(
-        functools.partial(back_kernel, length),
+        functools.partial(back_kernel, length, first),
         grid=(count // group,),
-        in_specs=[at(group, rows, wide), at(group, rows, wide // 3)]
-        + [pl.BlockSpec(memory_space=pl.ANY)] * len(more),
-        out_specs=at(group, rows, wide),
-        out_shape=shape_of(BF16, images, rows, wide),
-        input_output_aliases={2: 0} if more else {},
-        compiler_params=PARAMS,
-        cost_estimate=cost(count / 2),
-        name="back",
-    )(projected, d_mixed, *more)
-
-
-def qkv_weight_gradient(index, normed, d_proj):
-    images, rows, width = normed.shape
-    group = 2 if images % 2 == 0 else 1
-    c_rows = 3 * width // 4 + VEC_ROWS
-    return pl.pallas_call(
-        weight_kernel,
-        grid=(images // group,),
-        in_specs=[SCALARS, per_step(group, rows, width), per_step(group, rows, 3 * width)],
-        out_specs=[whole(2, c_rows, width)] * 2,
-        out_shape=[shape_of(BF16, 2, c_rows, width)] * 2,
-        scratch_shapes=[
-            pltpu.VMEM((width, 3 * width), F32),
-            pltpu.VMEM((8, 3 * width), F32),
-        ],
+        in_specs=[SCALARS, at(group, rows, wide), at(group, rows, width), at(group, rows, width)]
+        + ([] if first else [whole(*d) for d in sums] + [pl.BlockSpec(memory_space=pl.ANY)]),
+        out_specs=[at(group, rows, wide)]
+        + ([whole(*d) for d in sums] if first else [whole(2, c_rows, width)] * 2),
+        out_shape=[shape_of(BF16, images, rows, wide)]
+        + ([shape_of(F32, *d) for d in sums] if first else [shape_of(BF16, 2, c_rows, width)] * 2),
+        scratch_shapes=[] if first else [pltpu.VMEM(d, F32) for d in sums],
+        input_output_aliases={} if first else {6: 0},
         compiler_params=PARAMS,
         cost_estimate=cost(1),
-        name="qkv_weight_gradient",
-    )(index, normed, d_proj)
+        name="back",
+    )(index, projected, normed, d_mixed, *more)
 
 
 def input_gradient(tokens, d_proj, d_middle, w_qkv, vectors):
@@ -735,17 +863,15 @@
     return lax.optimization_barrier(arrays)
 
 
-def assembled(keep, send, first, tall, blocks):
-    order = (keep[0], send[0], keep[1], send[1])
-    return jnp.concatenate(
-        [
-            jnp.concatenate(
-                [q[first + k * tall : first + (k + 1) * tall] for k in range(blocks)], axis=1
-            )
-            for q in order
-        ],
-        axis=0,
-    )
+def assembled(here, there, first, tall, blocks=1, x_first=False):
+    middle = (here[1], there[0]) if x_first else (there[0], here[1])
+    order = (here[0], *middle, there[1])
+    return [
+        jnp.concatenate(
+            [q[first + k * tall : first + (k + 1) * tall] for k in range(blocks)], axis=1
+        )
+        for q in order
+    ]
 
 
 def per_device(
@@ -801,86 +927,104 @@
         ]
     else:
         outer = [piece for w in rest for piece in plan.gather_weight(w)]
-    output, d_middle, d_mixed, keep_a, send_a, keep_b, send_b = mlp_both_ways(
+    middle, result, d_normed, here_a, there_a = mlp_first(
         index, tokens, cotangent, mixed, vectors, ff, outer
     )
+    second = functools.partial(
+        mlp_second, index, cotangent, mixed, middle, result, d_normed, vectors, ff, outer
+    )
+    backward = functools.partial(attention_backward, index, projected, normed)
     images = tokens.shape[0]
-    backward = functools.partial(attention_backward, projected, d_mixed, length)
+    some = images // 4 * 2 if images % 4 == 0 else images // 2
     if swaps:
-        got_a, got_b = plan.over_core(send_a), plan.over_core(send_b)
-        d_proj, got_a, got_b = after(backward(0, 2, None), got_a, got_b)
-        other_a = keep_a[1] + got_a[1]
-        sum_b = keep_b + got_b
-        d_proj, other_a, other_b, sum_b = after(d_proj, other_a, plan.to_send(sum_b), sum_b)
-        over_a, over_b = plan.over_x(other_a), plan.over_y(other_b)
-        d_proj, over_a, over_b = after(backward(2, images - 4, d_proj), over_a, over_b)
-        mine_a = keep_a[0] + got_a[0] + over_a
-        both_b = plan.to_keep(sum_b) + over_b
-        d_proj, other_a, other_b, mine_a, both_b = after(
-            d_proj, plan.to_send(mine_a), both_b[1], mine_a, both_b
+        over_a = plan.over_x(there_a)
+        output, d_middle, d_mixed, here_b, there_b = second()
+        over_a, here_b, there_b, d_mixed = after(over_a, here_b, there_b, d_mixed)
+        sum_a, send_a = here_a[0] + over_a[0], here_a[1] + over_a[1]
+        send_a, d_mixed = after(send_a, d_mixed)
+        got_a = plan.over_core(send_a)
+        got_b = plan.over_core(there_b)
+        earlier = backward(d_mixed, length, 0, some)
+        earlier, got_a, got_b = after(earlier, got_a, got_b)
+        mine_a, other_b = sum_a + got_a, here_b[1] + got_b[1]
+        earlier, other_a, mine_a, other_b = after(earlier, plan.to_send(mine_a), mine_a, other_b)
+        over_a, over_b = plan.over_y(other_a), plan.over_x(other_b)
+        d_proj, here_c, there_c = backward(
+            d_mixed, length, some, images - some, (earlier[1], earlier[2], earlier[0])
         )
-        over_a, over_b = plan.over_y(other_a), plan.over_x(other_b)
-        d_proj, over_a, over_b = after(backward(images - 2, 2, d_proj), over_a, over_b)
+        here_c, there_c, over_a = after(here_c, there_c, over_a)
+        got_c = plan.over_core(there_c)
         part_a = plan.to_keep(mine_a) + over_a
-        part_b = both_b[0] + over_b
-        d_proj, part_a, part_b = after(d_proj, part_a, part_b)
-        over_a, over_b = plan.over_z(part_a, 1), plan.over_z(part_b, 1)
-        keep_c, send_c = qkv_weight_gradient(index, normed, d_proj)
-        send_c, over_a = after(send_c, over_a)
-        got_c = plan.over_core(send_c)
-        over_b, got_c = after(over_b, got_c)
-        part_a, part_b, other_c = part_a + over_a, part_b + over_b, keep_c[1] + got_c[1]
-        d_proj, part_a, part_b, other_c = after(d_proj, part_a, part_b, other_c)
-        over_c, over_a, over_b = (
-            plan.over_x(other_c),
-            plan.over_z(part_a, 2),
-            plan.over_z(part_b, 2),
+        part_a, over_b, got_c = after(part_a, over_b, got_c)
+        other_c = here_c[1] + got_c[1]
+        mine_b = here_b[0] + got_b[0] + over_b
+        d_proj, part_a, other_b, mine_b, other_c = after(
+            d_proj, part_a, plan.to_send(mine_b), mine_b, other_c
+        )
+        over_c, over_a, over_b = plan.over_x(other_c), plan.over_z(part_a, 1), plan.over_y(other_b)
+        input_grad, late = input_gradient(tokens, d_proj, d_middle, full_qkv, vectors)
+        late, over_c, over_a, over_b = after(late, over_c, over_a, over_b)
+        mine_c = here_c[0] + got_c[0] + over_c
+        other_c, mine_c, late = after(plan.to_send(mine_c), mine_c, late)
+        over_c, more = plan.over_y(other_c), plan.over_core(late)
+        part_a, part_b = part_a + over_a, plan.to_keep(mine_b) + over_b
+        over_c, more, part_a, part_b = after(over_c, more, part_a, part_b)
+        over_a = plan.over_z(part_a, 2)
+        part_c, late = plan.to_keep(mine_c) + over_c, late + more
+        part_c, late = after(part_c, late)
+        over_c, more, over_b = plan.over_z(part_c, 1), plan.over_x(late), plan.over_z(part_b, 1)
+        over_c, more, over_a = after(over_c, more, over_a)
+        part_c, late, part_a = part_c + over_c, late + more, part_a + over_a
+        part_c, late, part_a = after(part_c, late, part_a)
+        over_c, more = plan.over_z(part_c, 2), plan.over_y(late)
+        across_a, beside_a = plan.over_y(part_a), plan.over_core(part_a)
+        part_b = part_b + over_b
+        over_c, more, part_b = after(over_c, more, part_b)
+        over_b = plan.over_z(part_b, 2)
+        part_c, late = part_c + over_c, late + more
+        part_c, late, across_a = after(part_c, late, across_a)
+        across_c, beside_c, more = plan.over_y(part_c), plan.over_core(part_c), plan.over_z(late, 1)
+        a_pieces = (part_a, across_a, beside_a, plan.over_core(across_a))
+        across_c, more, over_b = after(across_c, more, over_b)
+        part_b, late = part_b + over_b, late + more
+        part_b, late, across_c = after(part_b, late, across_c)
+        across_b, beside_b, more = plan.over_y(part_b), plan.over_core(part_b), plan.over_z(late, 2)
+        c_pieces = (part_c, across_c, beside_c, plan.over_core(across_c))
+        late = late + more
+        g_qkv, g_query, g_value, g_gain_one, g_shift_one = unpack_inner(index, c_pieces, late)
+        across_b, g_qkv = after(across_b, g_qkv)
+        b_pieces = (part_b, across_b, beside_b, plan.over_core(across_b))
+        g_drop, g_lift, g_out, g_out_bias, g_gain_two, g_shift_two, g_drop_bias, g_lift_bias = (
+            unpack_outer(index, a_pieces, b_pieces, width, ff)
+        )
+    else:
+        output, d_middle, d_mixed, here_b, there_b = second()
+        earlier = backward(d_mixed, length, 0, some)
+        d_proj, here_c, there_c = backward(
+            d_mixed, length, some, images - some, (earlier[1], earlier[2], earlier[0])
         )
         input_grad, late = input_gradient(tokens, d_proj, d_middle, full_qkv, vectors)
-        late, over_c = after(late, over_c)
-        mine_c = keep_c[0] + got_c[0] + over_c
-        other_c, mine_c, late = after(plan.to_send(mine_c), mine_c, late)
-        over_c, more = plan.over_y(other_c), plan.over_core(late)
-        over_c, more, over_a = after(over_c, more, over_a)
-        part_c, late, part_a = plan.to_keep(mine_c) + over_c, late + more, part_a + over_a
-        part_c, late, part_a = after(part_c, late, part_a)
-        over_c, more = plan.over_z(part_c, 1), plan.over_x(late)
-        across_a, beside_a = plan.over_y(part_a), plan.over_core(part_a)
-        over_c, more, over_b = after(over_c, more, over_b)
-        part_c, late, part_b = part_c + over_c, late + more, part_b + over_b
-        part_c, late, part_b = after(part_c, late, part_b)
-        over_c, more = plan.over_z(part_c, 2), plan.over_y(late)
-        across_b, beside_b = plan.over_y(part_b), plan.over_core(part_b)
-        over_c, more, across_a, across_b = after(over_c, more, across_a, across_b)
-        a_pieces = (part_a, across_a, beside_a, plan.over_core(across_a))
-        b_pieces = (part_b, across_b, beside_b, plan.over_core(across_b))
-        part_c, late = part_c + over_c, late + more
-        part_c, late, a_pieces, b_pieces = after(part_c, late, a_pieces, b_pieces)
-        across_c, beside_c, more = plan.over_y(part_c), plan.over_core(part_c), plan.over_z(late, 1)
-        outer_grads = unpack_outer(index, a_pieces, b_pieces, width, ff)
-        across_c, beside_c, more, outer_grads = after(across_c, beside_c, more, outer_grads)
-        late = late + more
-        c_pieces = (part_c, across_c, beside_c, plan.over_core(across_c))
-        late = late + plan.over_z(late, 2)
-        g_drop, g_lift, g_out, g_out_bias, g_gain_two, g_shift_two, g_drop_bias, g_lift_bias = (
-            outer_grads
+        deep, tall = width // 2, width // 4
+        drop_a, drop_b = assembled(here_a, there_a, 0, deep, 1, True), assembled(here_b, there_b, 0, deep)
+        g_drop = plan.reduce(
+            jnp.concatenate([*drop_a[:2], *drop_b[:2], *drop_a[2:], *drop_b[2:]])
         )
-        g_qkv, g_query, g_value, g_gain_one, g_shift_one = unpack_inner(index, c_pieces, late)
-    else:
-        d_proj = backward(0, images, None)
-        keep_c, send_c = qkv_weight_gradient(index, normed, d_proj)
-        input_grad, g_first = input_gradient(tokens, d_proj, d_middle, full_qkv, vectors)
-        tall = width // 4
-        g_drop = plan.reduce(assembled(keep_a, send_a, 0, ff // 4, 1))
-        g_lift = plan.reduce(assembled(keep_b, send_b, 0, tall, ff // width))
-        g_out = plan.reduce(assembled(keep_b, send_b, ff // width * tall, tall, 1))
-        g_qkv = plan.reduce(assembled(keep_c, send_c, 0, tall, 3))
-        rows_a = keep_a[0, ff // 4 :]
-        rows_c = keep_c[0, 3 * tall :]
-        g_out_bias, g_gain_two, g_shift_two, g_drop_bias = (plan.reduce(rows_a[i]) for i in range(4))
-        g_lift_bias = plan.reduce(rows_a[4 : 4 + ff // width].reshape(-1))
+        lift_a = jnp.concatenate(assembled(here_a, there_a, deep, tall, 2, True))
+        lift_b = jnp.concatenate(assembled(here_b, there_b, deep, tall, 2))
+        g_lift = plan.reduce(
+            jnp.stack(
+                [lift_a.reshape(width, 2, width), lift_b.reshape(width, 2, width)], axis=2
+            ).reshape(width, ff)
+        )
+        g_out = plan.reduce(jnp.concatenate(assembled(here_b, there_b, width + VEC_ROWS, tall)))
+        g_qkv = plan.reduce(jnp.concatenate(assembled(here_c, there_c, 0, tall, 3)))
+        rows_a, rows_b, rows_c = here_a[0, width:], here_b[0, width:], here_c[0, 3 * tall :]
+        g_out_bias, g_gain_two, g_shift_two, g_drop_bias = (
+            plan.reduce(rows_b[2 + i]) for i in range(4)
+        )
+        g_lift_bias = plan.reduce(jnp.concatenate([rows_a[0], rows_b[0], rows_a[1], rows_b[1]]))
         g_query, g_value = plan.reduce(rows_c[0]), plan.reduce(rows_c[1])
-        g_gain_one, g_shift_one = plan.reduce(g_first[0]), plan.reduce(g_first[1])
+        g_gain_one, g_shift_one = plan.reduce(late[0]), plan.reduce(late[1])
     return (
         output,
         input_grad,

time: 151 us -> 164 us (1.086)
  starting transfers between devices: 26.6 us -> 36.3 us
  local copies, waits for them, and re-layouts: 8.18 us -> 10.2 us
    ppermute x37, starting transfers between devices: 26.6 us -> 36.3 us  [swap(): return lax.ppermute(v, AXES, pairs)]
    pallas_call x5 -> x4, Pallas kernels: 53.5 us -> 55.6 us  [the longest x2 20.6 us: attention_backward(): pl.pallas_call(functools.partial(back_kernel, length, first), grid=(count...]
    unnamed x60, local copies, waits for them, and re-layouts: 8.06 us -> 10.1 us
  transfers between devices with their start and end apart: 37 -> 37, of which waited for: 15 -> 13; matrix products, arithmetic and copies ran while one was open for 4% -> 4% of each run, Pallas kernels for 32% -> 37%
where the time goes in v4:
time: 164 us
  Pallas kernels  82.3 us (50%)
  starting transfers between devices  36.3 us (22%)
  waiting for transfers between devices  30.7 us (19%)
  local copies, waits for them, and re-layouts  10.2 us (6%)
  other arithmetic  2.96 us (2%)
    ppermute x37, starting transfers between devices, swap(): return lax.ppermute(v, AXES, pairs)  36.3 us
    ppermute x37, waiting for transfers between devices, swap(): return lax.ppermute(v, AXES, pairs)  30.7 us
    pallas_call x2, Pallas kernels, attention_backward(): pl.pallas_call(functools.partial(back_kernel, length, first), grid=(count...  20.6 us
    pallas_call x1, Pallas kernels, mlp_second(): pl.pallas_call(functools.partial(mlp_second_kernel, length), grid=(images...  18.1 us
    pallas_call x1, Pallas kernels, mlp_first(): pl.pallas_call(functools.partial(mlp_first_kernel, length), grid=(images...  16.9 us
    unnamed x60, local copies, waits for them, and re-layouts  10.1 us
    pallas_call x1, Pallas kernels, forward_attention(): pl.pallas_call(functools.partial(attend_kernel, length), grid=(images //...  9.92 us
    pallas_call x1, Pallas kernels, input_gradient(): pl.pallas_call(functools.partial(input_kernel, length), grid=(images // g...  7.4 us
  transfers between devices with their start and end apart: 37, of which 13 were waited for; matrix products, arithmetic and copies ran while one was open for 4% of the time, Pallas kernels for 37%

profile of v4, /device:TPU:0, one launch (start us, length us, event | category | flops | bytes accessed | tf_op | source)
XLA Modules:
  0.0 163.8 jit_solution(18173058223439372922)
XLA Ops:
  0.7 0.6 pad_add_fusion.index
  1.3 1.9 %pack_first.1.packed = bf16[104,1152]{1,0:T(8,128)(2,1)} custom-call(s32[3]{0:T(128)} %pad_add_fusion.index, bf16[192]{0:T(256)(128)(2,1)} %refs_0_.1, bf16[192]{0:T(256)(128)(2,1)} %refs_1_.1, bf16[192]{0:T(256)(128)(2,1)} %refs_2_.1, bf16[192]{0:T(256)(128)(2,1)} %refs_3_.1, bf16[192]{0:T(256)(128)(2,1)} %refs_4_.1, bf16[192]{0:T(256)(128)(2,1)} %refs_5_.1, ...), custom_call_target="tpu_custom_call" | custom-call | flops 1000 | bytes 1 | tf_op jit(solution)/shard_map/pack_first/pallas_call | solution.py:565
  3.2 2.9 %collective-permute-start = (bf16[104,1152]{1,0:T(8,128)(2,1)}, bf16[104,1152]{1,0:T(8,128)(2,1)S(1)}, u32[]{:S(2)}, u32[]{:S(2)}) collective-permute-start(bf16[104,1152]{1,0:T(8,128)(2,1)} %pack_first.1.packed), channel_id=1, source_target_pairs={{0,1},{1,0},{2,3},{3,2},{4,5},{5,4},{6,7},{7,6},{8,9},{9,8},{10,11... | collective-permute-start | bytes 718856 | tf_op jit(solution)/shard_map/ppermute | solution.py:809
  6.1 2.2 %pack_rest.1 = (bf16[96,384]{1,0:T(8,128)(2,1)}, bf16[96,1536]{1,0:T(8,128)(2,1)}, bf16[384,384]{1,0:T(8,128)(2,1)}) custom-call(s32[3]{0:T(128)} %pad_add_fusion.index, bf16[192,384]{1,0:T(8,128)(2,1)} %out_own.3, bf16[192,1536]{1,0:T(8,128)(2,1)} %lift_own.3, bf16[768,384]{1,0:T(8,128)(2,1)} %drop_own.3), custom_call_target="tpu_custom_call" | custom-call | flops 1000 | bytes 1 | tf_op jit(solution)/shard_map/pack_rest/pallas_call | solution.py:578
  8.3 2.0 %collective-permute-start.4 = (bf16[384,384]{1,0:T(8,128)(2,1)}, bf16[384,384]{1,0:T(8,128)(2,1)S(1)}, u32[]{:S(2)}, u32[]{:S(2)}) collective-permute-start(bf16[384,384]{1,0:T(8,128)(2,1)} %get-tuple-element.130), channel_id=1, source_target_pairs={{0,1},{1,0},{2,3},{3,2},{4,5},{5,4},{6,7},{7,6},{8,9},{9,8},{10,11... | collective-permute-start | bytes 884744 | tf_op jit(solution)/shard_map/ppermute | solution.py:809
  10.3 2.6 %collective-permute-done.near = bf16[104,1152]{1,0:T(8,128)(2,1)S(1)} collective-permute-done((bf16[104,1152]{1,0:T(8,128)(2,1)}, bf16[104,1152]{1,0:T(8,128)(2,1)S(1)}, u32[]{:S(2)}, u32[]{:S(2)}) %collective-permute-start) | collective-permute-done | bytes 239648 | tf_op jit(solution)/shard_map/ppermute | solution.py:809
  13.0 2.1 %collective-permute-start.2 = (bf16[96,384]{1,0:T(8,128)(2,1)}, bf16[96,384]{1,0:T(8,128)(2,1)S(1)}, u32[]{:S(2)}, u32[]{:S(2)}) collective-permute-start(bf16[96,384]{1,0:T(8,128)(2,1)} %get-tuple-element.128), channel_id=1, source_target_pairs={{0,1},{1,0},{2,3},{3,2},{4,5},{5,4},{6,7},{7,6},{8,9},{9,8},{10,11... | collective-permute-start | bytes 221192 | tf_op jit(solution)/shard_map/ppermute | solution.py:809
  15.0 1.2 copy.31.tok_ref
  16.3 0.7 copy-done.17
  16.9 9.9 %attend.1 = (bf16[8,208,384]{2,1,0:T(8,128)(2,1)}, bf16[8,208,1152]{2,1,0:T(8,128)(2,1)}, bf16[8,208,384]{2,1,0:T(8,128)(2,1)}, bf16[384,1152]{1,0:T(8,128)(2,1)}, f32[12,384]{1,0:T(8,128)}) custom-call(s32[3]{0:T(128)} %pad_add_fusion.index, bf16[8,197,384]{2,1,0:T(8,128)(2,1)} %copy.31.tok_ref, bf16[104,1152]{1,0:T(8,128)(2,1)} %pack_first.1.packed, ...), custom_call_target="tpu_custom_call" | custom-call | flops 1000 | bytes 1 | tf_op jit(solution)/shard_map/attend/pallas_call | solution.py:594
  26.9 0.3 collective-permute-start.6
  27.2 0.3 collective-permute-start.7
  27.5 0.2 collective-permute-start.5
  27.7 1.2 copy.34.cot_ref
  29.2 0.6 copy-done.15
  29.8 0.1 copy-done.7
  30.0 16.9 %mlp_first.1 = (f32[8,208,384]{2,1,0:T(8,128)}, f32[8,208,384]{2,1,0:T(8,128)}, f32[8,208,384]{2,1,0:T(8,128)}, bf16[2,400,384]{2,1,0:T(8,128)(2,1)}, bf16[2,400,384]{2,1,0:T(8,128)(2,1)}) custom-call(s32[3]{0:T(128)} %pad_add_fusion.index, bf16[8,197,384]{2,1,0:T(8,128)(2,1)} %copy.31.tok_ref, bf16[8,197,384]{2,1,0:T(8,128)(2,1)} %copy.34.cot_ref, ...), custom_call_target="tpu_custom_call" | custom-call | flops 1000 | bytes 1 | tf_op jit(solution)/shard_map/mlp_first/pallas_call | solution.py:624
  46.9 1.3 collective-permute-start.8
  48.1 18.1 %mlp_second.1 = (bf16[8,197,384]{2,1,0:T(8,128)(2,1)}, f32[8,208,384]{2,1,0:T(8,128)}, bf16[8,208,384]{2,1,0:T(8,128)(2,1)}, bf16[2,496,384]{2,1,0:T(8,128)(2,1)}, bf16[2,496,384]{2,1,0:T(8,128)(2,1)}) custom-call(s32[3]{0:T(128)} %pad_add_fusion.index, bf16[8,197,384]{2,1,0:T(8,128)(2,1)} %copy.34.cot_ref, ...), custom_call_target="tpu_custom_call" | custom-call | flops 1000 | bytes 1 | tf_op jit(solution)/shard_map/mlp_second/pallas_call | solution.py:658
  66.4 0.6 collective-permute-start.9
  67.0 9.9 %back.2 = (bf16[8,208,1152]{2,1,0:T(8,128)(2,1)}, f32[384,1152]{1,0:T(8,128)}, f32[8,1152]{1,0:T(8,128)}) custom-call(s32[3]{0:T(128)} %pad_add_fusion.index, bf16[8,208,1152]{2,1,0:T(8,128)(2,1)} %get-tuple-element.140.proj_ref, bf16[8,208,384]{2,1,0:T(8,128)(2,1)} %get-tuple-element.141.normed_ref, bf16[8,208,384]{2,1,0:T(8,128)(2,1)} %get-tuple-element.149.d_mixed_ref), custom_call_target="tpu_custom_call" | custom-call | flops 1000 | bytes 1 | tf_op jit(solution)/shard_map/back/pallas_call | solution.py:712
  77.0 1.0 copy-done.8
  78.1 1.6 collective-permute-start.11
  79.7 10.7 %back.3 = (bf16[8,208,1152]{2,1,0:T(8,128)(2,1)}, bf16[2,304,384]{2,1,0:T(8,128)(2,1)}, bf16[2,304,384]{2,1,0:T(8,128)(2,1)}) custom-call(s32[3]{0:T(128)} %pad_add_fusion.index, bf16[8,208,1152]{2,1,0:T(8,128)(2,1)} %get-tuple-element.140.proj_ref, bf16[8,208,384]{2,1,0:T(8,128)(2,1)} %get-tuple-element.141.normed_ref, ...), custom_call_target="tpu_custom_call", output_to_operand_aliasing={{0}: (6, {})} | custom-call | flops 1000 | bytes 1 | tf_op jit(solution)/shard_map/back/pallas_call | solution.py:712
  90.5 0.9 collective-permute-start.12
  91.4 10.4 %collective-permute-done.12 = bf16[496,384]{1,0:T(8,128)(2,1)} collective-permute-done((bf16[496,384]{1,0:T(8,128)(2,1)S(1)}, bf16[496,384]{1,0:T(8,128)(2,1)}, u32[]{:S(2)}, u32[]{:S(2)}) %collective-permute-start.12) | collective-permute-done | bytes 380960 | tf_op jit(solution)/shard_map/ppermute | solution.py:809
  101.9 1.1 bitcast_add_fusion
  103.0 0.9 collective-permute-start.14
  103.9 0.5 collective-permute-start.16
  104.4 1.6 collective-permute-start.15
  106.0 7.4 %input_gradient.1 = (bf16[8,197,384]{2,1,0:T(8,128)(2,1)}, f32[8,384]{1,0:T(8,128)}) custom-call(bf16[8,197,384]{2,1,0:T(8,128)(2,1)} %copy.31.tok_ref, bf16[8,208,1152]{2,1,0:T(8,128)(2,1)} %get-tuple-element.176.d_proj_ref, f32[8,208,384]{2,1,0:T(8,128)} %get-tuple-element.177.d_middle_ref, bf16[384,1152]{1,0:T(8,128)(2,1)} %get-tuple-element.178.w_ref, ...), custom_call_target="tpu_custom_call" | custom-call | flops 1000 | bytes 1 | tf_op jit(solution)/shard_map/input_gradient/pallas_call | solution.py:733
  113.5 1.6 collective-permute-start.17
  115.2 1.3 collective-permute-done.18
  116.5 1.9 %collective-permute-done.17 = bf16[152,384]{1,0:T(8,128)(2,1)S(1)} collective-permute-done((bf16[152,384]{1,0:T(8,128)(2,1)S(1)}, bf16[152,384]{1,0:T(8,128)(2,1)S(1)}, u32[]{:S(2)}, u32[]{:S(2)}) %collective-permute-start.17) | collective-permute-done | bytes 116768 | tf_op jit(solution)/shard_map/ppermute | solution.py:809
  118.4 2.6 %collective-permute-start.21 = (bf16[200,384]{1,0:T(8,128)(2,1)S(1)}, bf16[200,384]{1,0:T(8,128)(2,1)S(1)}, u32[]{:S(2)}, u32[]{:S(2)}) collective-permute-start(bf16[200,384]{1,0:T(8,128)(2,1)S(1)} %add.126), channel_id=1, source_target_pairs={{0,16},{1,17},{2,18},{3,19},{4,20},{5,21},{6,22},{7,23},{8,24},{9,... | collective-permute-start | bytes 460808 | tf_op jit(solution)/shard_map/ppermute | solution.py:809
  121.1 0.5 collective-permute-start.19
  121.6 1.6 collective-permute-start.24
  123.2 1.2 collective-permute-start.20
  124.3 2.5 %collective-permute-done.20 = f32[8,384]{1,0:T(8,128)S(1)} collective-permute-done((f32[8,384]{1,0:T(8,128)S(1)}, f32[8,384]{1,0:T(8,128)S(1)}, u32[]{:S(2)}, u32[]{:S(2)}) %collective-permute-start.20) | collective-permute-done | bytes 12320 | tf_op jit(solution)/shard_map/ppermute | solution.py:809
  126.9 1.7 %collective-permute-done.19 = bf16[152,384]{1,0:T(8,128)(2,1)S(1)} collective-permute-done((bf16[152,384]{1,0:T(8,128)(2,1)S(1)}, bf16[152,384]{1,0:T(8,128)(2,1)S(1)}, u32[]{:S(2)}, u32[]{:S(2)}) %collective-permute-start.19) | collective-permute-done | bytes 116768 | tf_op jit(solution)/shard_map/ppermute | solution.py:809
  128.7 0.4 collective-permute-start.22
  129.0 1.6 collective-permute-start.25
  130.6 0.4 collective-permute-start.23
  131.0 1.7 %collective-permute-done.24 = bf16[248,384]{1,0:T(8,128)(2,1)S(1)} collective-permute-done((bf16[248,384]{1,0:T(8,128)(2,1)S(1)}, bf16[248,384]{1,0:T(8,128)(2,1)S(1)}, u32[]{:S(2)}, u32[]{:S(2)}) %collective-permute-start.24) | collective-permute-done | bytes 190496 | tf_op jit(solution)/shard_map/ppermute | solution.py:809
  132.8 1.6 collective-permute-done.23
  134.4 2.6 %collective-permute-start.28 = (bf16[248,384]{1,0:T(8,128)(2,1)S(1)}, bf16[248,384]{1,0:T(8,128)(2,1)S(1)}, u32[]{:S(2)}, u32[]{:S(2)}) collective-permute-start(bf16[248,384]{1,0:T(8,128)(2,1)S(1)} %add.134), channel_id=1, source_target_pairs={{0,16},{1,17},{2,18},{3,19},{4,20},{5,21},{6,22},{7,23},{8,24},{9,... | collective-permute-start | bytes 571400 | tf_op jit(solution)/shard_map/ppermute | solution.py:809
  137.1 2.0 %collective-permute-start.26 = (bf16[152,384]{1,0:T(8,128)(2,1)S(1)}, bf16[152,384]{1,0:T(8,128)(2,1)S(1)}, u32[]{:S(2)}, u32[]{:S(2)}) collective-permute-start(bf16[152,384]{1,0:T(8,128)(2,1)S(1)} %add.135.refs_0_), channel_id=1, source_target_pairs={{0,4},{1,5},{2,6},{3,7},{4,0},{5,1},{6,2},{7,3},{8,12},{9,13},{10,... | collective-permute-start | bytes 350216 | tf_op jit(solution)/shard_map/ppermute | solution.py:809
  139.1 2.5 %collective-permute-start.27 = (f32[8,384]{1,0:T(8,128)S(1)}, f32[8,384]{1,0:T(8,128)S(1)}, u32[]{:S(2)}, u32[]{:S(2)}) collective-permute-start(f32[8,384]{1,0:T(8,128)S(1)} %add.136), channel_id=1, source_target_pairs={{0,8},{1,9},{2,10},{3,11},{4,12},{5,13},{6,14},{7,15},{8,0},{9,1},... | collective-permute-start | bytes 36872 | tf_op jit(solution)/shard_map/ppermute | solution.py:809
  141.6 1.7 %collective-permute-done.27 = f32[8,384]{1,0:T(8,128)S(1)} collective-permute-done((f32[8,384]{1,0:T(8,128)S(1)}, f32[8,384]{1,0:T(8,128)S(1)}, u32[]{:S(2)}, u32[]{:S(2)}) %collective-permute-start.27) | collective-permute-done | bytes 12320 | tf_op jit(solution)/shard_map/ppermute | solution.py:809
  143.3 0.6 collective-permute-done.28
  144.0 2.8 %collective-permute-start.32 = (bf16[248,384]{1,0:T(8,128)(2,1)S(1)}, bf16[248,384]{1,0:T(8,128)(2,1)S(1)}, u32[]{:S(2)}, u32[]{:S(2)}) collective-permute-start(bf16[248,384]{1,0:T(8,128)(2,1)S(1)} %add.137.refs_4_), channel_id=1, source_target_pairs={{0,4},{1,5},{2,6},{3,7},{4,0},{5,1},{6,2},{7,3},{8,12},{9,13},{10,... | collective-permute-start | bytes 571400 | tf_op jit(solution)/shard_map/ppermute | solution.py:809
  146.8 0.5 collective-permute-start.30
  147.3 0.2 collective-permute-start.31
  147.5 4.4 %collective-permute-done.31 = f32[8,384]{1,0:T(8,128)S(1)} collective-permute-done((f32[8,384]{1,0:T(8,128)S(1)}, f32[8,384]{1,0:T(8,128)S(1)}, u32[]{:S(2)}, u32[]{:S(2)}) %collective-permute-start.31) | collective-permute-done | bytes 12320 | tf_op jit(solution)/shard_map/ppermute | solution.py:809
  151.9 0.6 add.139.refs_4_
  152.5 0.6 copy-done.25
  153.1 0.6 copy-done.26
  153.8 2.1 %unpack_inner.1 = (f32[192,1152]{1,0:T(8,128)}, f32[192]{0:T(256)}, f32[192]{0:T(256)}, f32[192]{0:T(256)}, f32[192]{0:T(256)}) custom-call(s32[3]{0:T(128)} %pad_add_fusion.index, bf16[152,384]{1,0:T(8,128)(2,1)} %copy-done.13, bf16[152,384]{1,0:T(8,128)(2,1)} %copy-done.24, bf16[152,384]{1,0:T(8,128)(2,1)} %copy-done.25, bf16[152,384]{1,0:T(8,128)(2,1)} %copy-done.26, ...), custom_call_target="tpu_custom_call" | custom-call | flops 2000 | bytes 1 | tf_op jit(solution)/shard_map/unpack_inner/pallas_call | solution.py:783
  156.0 0.5 collective-permute-start.33
  156.6 1.2 copy.36
  157.8 1.2 copy.37
  159.0 0.6 copy-done.22
  159.8 0.7 copy-done.20
  160.4 3.2 %unpack_outer.1 = (f32[768,384]{1,0:T(8,128)}, f32[192,1536]{1,0:T(8,128)}, f32[192,384]{1,0:T(8,128)}, f32[192]{0:T(256)}, f32[192]{0:T(256)}, /*index=5*/f32[192]{0:T(256)}, f32[192]{0:T(256)}, f32[768]{0:T(1024)}) custom-call(s32[3]{0:T(128)} %pad_add_fusion.index, bf16[200,384]{1,0:T(8,128)(2,1)} %copy-done.11, bf16[200,384]{1,0:T(8,128)(2,1)} %copy-done.21, ...), custom_call_target="tpu_custom_call" | custom-call | flops 3000 | bytes 1 | tf_op jit(solution)/shard_map/unpack_outer/pallas_call | solution.py:752
  (104 shorter events, 1.7 us)
Async XLA Ops:
  0.6 14.4 %copy-start.2 = (bf16[8,197,384]{2,0,1:T(8,128)(2,1)S(1)}, bf16[8,197,384]{2,0,1:T(8,128)(2,1)}, u32[]{:S(2)}) copy-start(bf16[8,197,384]{2,0,1:T(8,128)(2,1)} %param.15) | copy-start | bytes 3631108
  3.2 9.8 %collective-permute-start = (bf16[104,1152]{1,0:T(8,128)(2,1)}, bf16[104,1152]{1,0:T(8,128)(2,1)S(1)}, u32[]{:S(2)}, u32[]{:S(2)}) collective-permute-start(bf16[104,1152]{1,0:T(8,128)(2,1)} %pack_first.1.packed), channel_id=1, source_target_pairs={{0,1},{1,0},{2,3},{3,2},{4,5},{5,4},{6,7},{7,6},{8,9},{9,8},{10,11... | collective-permute-start | bytes 718856 | tf_op jit(solution)/shard_map/ppermute | solution.py:809
  8.3 18.6 %collective-permute-start.3 = (bf16[96,1536]{1,0:T(8,128)(2,1)}, bf16[96,1536]{1,0:T(8,128)(2,1)S(1)}, u32[]{:S(2)}, u32[]{:S(2)}) collective-permute-start(bf16[96,1536]{1,0:T(8,128)(2,1)} %get-tuple-element.129), channel_id=1, source_target_pairs={{0,1},{1,0},{2,3},{3,2},{4,5},{5,4},{6,7},{7,6},{8,9},{9,8},{10,11... | collective-permute-start | bytes 884744 | tf_op jit(solution)/shard_map/ppermute | solution.py:809
  8.3 18.6 %collective-permute-start.4 = (bf16[384,384]{1,0:T(8,128)(2,1)}, bf16[384,384]{1,0:T(8,128)(2,1)S(1)}, u32[]{:S(2)}, u32[]{:S(2)}) collective-permute-start(bf16[384,384]{1,0:T(8,128)(2,1)} %get-tuple-element.130), channel_id=1, source_target_pairs={{0,1},{1,0},{2,3},{3,2},{4,5},{5,4},{6,7},{7,6},{8,9},{9,8},{10,11... | collective-permute-start | bytes 884744 | tf_op jit(solution)/shard_map/ppermute | solution.py:809
  13.0 3.3 %copy-start.16 = (bf16[104,1152]{1,0:T(8,128)(2,1)}, bf16[104,1152]{1,0:T(8,128)(2,1)S(1)}, u32[]{:S(2)}) copy-start(bf16[104,1152]{1,0:T(8,128)(2,1)S(1)} %collective-permute-done.near) | copy-start | bytes 718852
  13.0 3.3 %collective-permute-start.1 = (bf16[104,1152]{1,0:T(8,128)(2,1)S(1)}, bf16[104,1152]{1,0:T(8,128)(2,1)S(1)}, u32[]{:S(2)}, u32[]{:S(2)}) collective-permute-start(bf16[104,1152]{1,0:T(8,128)(2,1)S(1)} %collective-permute-done.near), channel_id=1, source_target_pairs={{0,2},{1,3},{2,0},{3,1},{4,6},{5,7},{6,4},{7,5},{8,10},{9,11},{10,... | collective-permute-start | bytes 718856 | tf_op jit(solution)/shard_map/ppermute | solution.py:809
  13.0 13.9 %collective-permute-start.2 = (bf16[96,384]{1,0:T(8,128)(2,1)}, bf16[96,384]{1,0:T(8,128)(2,1)S(1)}, u32[]{:S(2)}, u32[]{:S(2)}) collective-permute-start(bf16[96,384]{1,0:T(8,128)(2,1)} %get-tuple-element.128), channel_id=1, source_target_pairs={{0,1},{1,0},{2,3},{3,2},{4,5},{5,4},{6,7},{7,6},{8,9},{9,8},{10,11... | collective-permute-start | bytes 221192 | tf_op jit(solution)/shard_map/ppermute | solution.py:809
  16.2 11.5 %copy-start.3 = (bf16[8,197,384]{2,0,1:T(8,128)(2,1)S(1)}, bf16[8,197,384]{2,0,1:T(8,128)(2,1)}, u32[]{:S(2)}) copy-start(bf16[8,197,384]{2,0,1:T(8,128)(2,1)} %param.29) | copy-start | bytes 3631108
  16.3 0.7 copy-start.17
  26.9 2.3 %copy-start.14 = (bf16[96,384]{1,0:T(8,128)(2,1)}, bf16[96,384]{1,0:T(8,128)(2,1)S(1)}, u32[]{:S(2)}) copy-start(bf16[96,384]{1,0:T(8,128)(2,1)S(1)} %collective-permute-done.2.out_near) | copy-start | bytes 221188
  26.9 2.2 %copy-start.4 = (bf16[96,1536]{1,0:T(8,128)(2,1)}, bf16[96,1536]{1,0:T(8,128)(2,1)S(1)}, u32[]{:S(2)}) copy-start(bf16[96,1536]{1,0:T(8,128)(2,1)S(1)} %collective-permute-done.3.lift_near) | copy-start | bytes 884740
  26.9 2.2 %copy-start.5 = (bf16[384,384]{1,0:T(8,128)(2,1)}, bf16[384,384]{1,0:T(8,128)(2,1)S(1)}, u32[]{:S(2)}) copy-start(bf16[384,384]{1,0:T(8,128)(2,1)S(1)} %collective-permute-done.4.drop_near) | copy-start | bytes 884740
  26.9 2.2 %collective-permute-start.6 = (bf16[96,1536]{1,0:T(8,128)(2,1)S(1)}, bf16[96,1536]{1,0:T(8,128)(2,1)S(1)}, u32[]{:S(2)}, u32[]{:S(2)}) collective-permute-start(bf16[96,1536]{1,0:T(8,128)(2,1)S(1)} %collective-permute-done.3.lift_near), channel_id=1, source_target_pairs={{0,2},{1,3},{2,0},{3,1},{4,6},{5,7},{6,4},{7,5},{8,10},{9,11},{10,... | collective-permute-start | bytes 884744 | tf_op jit(solution)/shard_map/ppermute | solution.py:809
  27.2 1.9 %collective-permute-start.7 = (bf16[384,384]{1,0:T(8,128)(2,1)S(1)}, bf16[384,384]{1,0:T(8,128)(2,1)S(1)}, u32[]{:S(2)}, u32[]{:S(2)}) collective-permute-start(bf16[384,384]{1,0:T(8,128)(2,1)S(1)} %collective-permute-done.4.drop_near), channel_id=1, source_target_pairs={{0,2},{1,3},{2,0},{3,1},{4,6},{5,7},{6,4},{7,5},{8,10},{9,11},{10,... | collective-permute-start | bytes 884744 | tf_op jit(solution)/shard_map/ppermute | solution.py:809
  27.5 1.6 collective-permute-start.5
  29.1 0.7 copy-start.6
  29.1 0.9 copy-start.7
  46.9 19.4 %collective-permute-start.8 = (bf16[2,400,384]{2,1,0:T(8,128)(2,1)}, bf16[2,400,384]{2,1,0:T(8,128)(2,1)S(1)}, u32[]{:S(2)}, u32[]{:S(2)}) collective-permute-start(bf16[2,400,384]{2,1,0:T(8,128)(2,1)} %get-tuple-element.143), channel_id=1, source_target_pairs={{0,1},{1,0},{2,3},{3,2},{4,5},{5,4},{6,7},{7,6},{8,9},{9,8},{10,11... | collective-permute-start | bytes 1843208 | tf_op jit(solution)/shard_map/ppermute | solution.py:809
  48.1 18.2 %copy-start.10 = (bf16[2,400,384]{2,1,0:T(8,128)(2,1)S(1)}, bf16[2,400,384]{2,1,0:T(8,128)(2,1)}, u32[]{:S(2)}) copy-start(bf16[2,400,384]{2,1,0:T(8,128)(2,1)} %get-tuple-element.142) | copy-start | bytes 1843204
  66.3 10.6 %collective-permute-start.10 = (bf16[2,496,384]{2,1,0:T(8,128)(2,1)}, bf16[2,496,384]{2,1,0:T(8,128)(2,1)S(1)}, u32[]{:S(2)}, u32[]{:S(2)}) collective-permute-start(bf16[2,496,384]{2,1,0:T(8,128)(2,1)} %get-tuple-element.154), channel_id=1, source_target_pairs={{0,2},{1,3},{2,0},{3,1},{4,6},{5,7},{6,4},{7,5},{8,10},{9,11},{10,... | collective-permute-start | bytes 2285576 | tf_op jit(solution)/shard_map/ppermute | solution.py:809
  66.4 10.5 %collective-permute-start.9 = (bf16[400,384]{1,0:T(8,128)(2,1)S(1)}, bf16[400,384]{1,0:T(8,128)(2,1)S(1)}, u32[]{:S(2)}, u32[]{:S(2)}) collective-permute-start(bf16[400,384]{1,0:T(8,128)(2,1)S(1)} %add_bitcast_fusion.1), channel_id=1, source_target_pairs={{0,2},{1,3},{2,0},{3,1},{4,6},{5,7},{6,4},{7,5},{8,10},{9,11},{10,... | collective-permute-start | bytes 921608 | tf_op jit(solution)/shard_map/ppermute | solution.py:809
  76.9 1.1 copy-start.8
  78.1 12.3 %collective-permute-start.11 = (bf16[200,384]{1,0:T(8,128)(2,1)S(1)}, bf16[200,384]{1,0:T(8,128)(2,1)S(1)}, u32[]{:S(2)}, u32[]{:S(2)}) collective-permute-start(bf16[200,384]{1,0:T(8,128)(2,1)S(1)} %constant_dynamic-slice_fusion.2), channel_id=1, source_target_pairs={{0,4},{1,5},{2,6},{3,7},{4,0},{5,1},{6,2},{7,3},{8,12},{9,13},{10,... | collective-permute-start | bytes 460808 | tf_op jit(solution)/shard_map/ppermute | solution.py:809
  90.4 12.6 %copy-start.12 = (bf16[2,304,384]{2,1,0:T(8,128)(2,1)S(1)}, bf16[2,304,384]{2,1,0:T(8,128)(2,1)}, u32[]{:S(2)}) copy-start(bf16[2,304,384]{2,1,0:T(8,128)(2,1)} %get-tuple-element.174) | copy-start | bytes 1400836
  90.4 11.5 %collective-permute-start.13 = (bf16[2,304,384]{2,1,0:T(8,128)(2,1)}, bf16[2,304,384]{2,1,0:T(8,128)(2,1)S(1)}, u32[]{:S(2)}, u32[]{:S(2)}) collective-permute-start(bf16[2,304,384]{2,1,0:T(8,128)(2,1)} %get-tuple-element.171), channel_id=1, source_target_pairs={{0,2},{1,3},{2,0},{3,1},{4,6},{5,7},{6,4},{7,5},{8,10},{9,11},{10,... | collective-permute-start | bytes 1400840 | tf_op jit(solution)/shard_map/ppermute | solution.py:809
  90.5 11.4 %collective-permute-start.12 = (bf16[496,384]{1,0:T(8,128)(2,1)S(1)}, bf16[496,384]{1,0:T(8,128)(2,1)}, u32[]{:S(2)}, u32[]{:S(2)}) collective-permute-start(bf16[496,384]{1,0:T(8,128)(2,1)S(1)} %add_bitcast_fusion), channel_id=1, source_target_pairs={{0,1},{1,0},{2,3},{3,2},{4,5},{5,4},{6,7},{7,6},{8,9},{9,8},{10,11... | collective-permute-start | bytes 1142792 | tf_op jit(solution)/shard_map/ppermute | solution.py:809
  103.0 10.4 %collective-permute-start.14 = (bf16[304,384]{1,0:T(8,128)(2,1)S(1)}, bf16[304,384]{1,0:T(8,128)(2,1)S(1)}, u32[]{:S(2)}, u32[]{:S(2)}) collective-permute-start(bf16[304,384]{1,0:T(8,128)(2,1)S(1)} %add_bitcast_fusion.2), channel_id=1, source_target_pairs={{0,1},{1,0},{2,3},{3,2},{4,5},{5,4},{6,7},{7,6},{8,9},{9,8},{10,11... | collective-permute-start | bytes 700424 | tf_op jit(solution)/shard_map/ppermute | solution.py:809
  103.9 9.5 %collective-permute-start.16 = (bf16[248,384]{1,0:T(8,128)(2,1)S(1)}, bf16[248,384]{1,0:T(8,128)(2,1)S(1)}, u32[]{:S(2)}, u32[]{:S(2)}) collective-permute-start(bf16[248,384]{1,0:T(8,128)(2,1)S(1)} %constant_dynamic-slice_fusion.1), channel_id=1, source_target_pairs={{0,4},{1,5},{2,6},{3,7},{4,0},{5,1},{6,2},{7,3},{8,12},{9,13},{10,... | collective-permute-start | bytes 571400 | tf_op jit(solution)/shard_map/ppermute | solution.py:809
  104.4 9.0 %collective-permute-start.15 = (bf16[200,384]{1,0:T(8,128)(2,1)S(1)}, bf16[200,384]{1,0:T(8,128)(2,1)S(1)}, u32[]{:S(2)}, u32[]{:S(2)}) collective-permute-start(bf16[200,384]{1,0:T(8,128)(2,1)S(1)} %dynamic-slice_add_fusion.1), channel_id=1, source_target_pairs={{0,8},{1,9},{2,10},{3,11},{4,12},{5,13},{6,14},{7,15},{8,0},{9,1},... | collective-permute-start | bytes 460808 | tf_op jit(solution)/shard_map/ppermute | solution.py:809
  113.4 7.6 %copy-start.27 = (f32[8,384]{1,0:T(8,128)S(1)}, f32[8,384]{1,0:T(8,128)}, u32[]{:S(2)}) copy-start(f32[8,384]{1,0:T(8,128)} %get-tuple-element.188) | copy-start | bytes 36868
  113.5 4.9 %collective-permute-start.17 = (bf16[152,384]{1,0:T(8,128)(2,1)S(1)}, bf16[152,384]{1,0:T(8,128)(2,1)S(1)}, u32[]{:S(2)}, u32[]{:S(2)}) collective-permute-start(bf16[152,384]{1,0:T(8,128)(2,1)S(1)} %constant_dynamic-slice_fusion), channel_id=1, source_target_pairs={{0,4},{1,5},{2,6},{3,7},{4,0},{5,1},{6,2},{7,3},{8,12},{9,13},{10,... | collective-permute-start | bytes 350216 | tf_op jit(solution)/shard_map/ppermute | solution.py:809
  115.1 1.4 collective-permute-start.18
  118.4 10.1 %collective-permute-start.21 = (bf16[200,384]{1,0:T(8,128)(2,1)S(1)}, bf16[200,384]{1,0:T(8,128)(2,1)S(1)}, u32[]{:S(2)}, u32[]{:S(2)}) collective-permute-start(bf16[200,384]{1,0:T(8,128)(2,1)S(1)} %add.126), channel_id=1, source_target_pairs={{0,16},{1,17},{2,18},{3,19},{4,20},{5,21},{6,22},{7,23},{8,24},{9,... | collective-permute-start | bytes 460808 | tf_op jit(solution)/shard_map/ppermute | solution.py:809
  121.1 7.5 %collective-permute-start.19 = (bf16[152,384]{1,0:T(8,128)(2,1)S(1)}, bf16[152,384]{1,0:T(8,128)(2,1)S(1)}, u32[]{:S(2)}, u32[]{:S(2)}) collective-permute-start(bf16[152,384]{1,0:T(8,128)(2,1)S(1)} %dynamic-slice_add_fusion.2), channel_id=1, source_target_pairs={{0,8},{1,9},{2,10},{3,11},{4,12},{5,13},{6,14},{7,15},{8,0},{9,1},... | collective-permute-start | bytes 350216 | tf_op jit(solution)/shard_map/ppermute | solution.py:809
  121.6 11.2 %collective-permute-start.24 = (bf16[248,384]{1,0:T(8,128)(2,1)S(1)}, bf16[248,384]{1,0:T(8,128)(2,1)S(1)}, u32[]{:S(2)}, u32[]{:S(2)}) collective-permute-start(bf16[248,384]{1,0:T(8,128)(2,1)S(1)} %dynamic-slice_add_fusion), channel_id=1, source_target_pairs={{0,8},{1,9},{2,10},{3,11},{4,12},{5,13},{6,14},{7,15},{8,0},{9,1},... | collective-permute-start | bytes 571400 | tf_op jit(solution)/shard_map/ppermute | solution.py:809
  123.2 3.7 %collective-permute-start.20 = (f32[8,384]{1,0:T(8,128)S(1)}, f32[8,384]{1,0:T(8,128)S(1)}, u32[]{:S(2)}, u32[]{:S(2)}) collective-permute-start(f32[8,384]{1,0:T(8,128)S(1)} %add.130), channel_id=1, source_target_pairs={{0,1},{1,0},{2,3},{3,2},{4,5},{5,4},{6,7},{7,6},{8,9},{9,8},{10,11... | collective-permute-start | bytes 36872 | tf_op jit(solution)/shard_map/ppermute | solution.py:809
  128.6 29.2 %copy-start.11 = (bf16[200,384]{1,0:T(8,128)(2,1)}, bf16[200,384]{1,0:T(8,128)(2,1)S(1)}, u32[]{:S(2)}) copy-start(bf16[200,384]{1,0:T(8,128)(2,1)S(1)} %add.133.refs_0_) | copy-start | bytes 460804
  128.6 28.0 %copy-start = (bf16[8,197,384]{2,1,0:T(8,128)(2,1)S(1)}, bf16[8,197,384]{2,1,0:T(8,128)(2,1)}, u32[]{:S(2)}) copy-start(bf16[8,197,384]{2,1,0:T(8,128)(2,1)} %get-tuple-element.231) | copy-start | bytes 3631108
  128.7 5.8 %collective-permute-start.22 = (bf16[152,384]{1,0:T(8,128)(2,1)S(1)}, bf16[152,384]{1,0:T(8,128)(2,1)S(1)}, u32[]{:S(2)}, u32[]{:S(2)}) collective-permute-start(bf16[152,384]{1,0:T(8,128)(2,1)S(1)} %add.131), channel_id=1, source_target_pairs={{0,16},{1,17},{2,18},{3,19},{4,20},{5,21},{6,22},{7,23},{8,24},{9,... | collective-permute-start | bytes 350216 | tf_op jit(solution)/shard_map/ppermute | solution.py:809
  129.0 8.0 %collective-permute-start.25 = (bf16[200,384]{1,0:T(8,128)(2,1)S(1)}, bf16[200,384]{1,0:T(8,128)(2,1)S(1)}, u32[]{:S(2)}, u32[]{:S(2)}) collective-permute-start(bf16[200,384]{1,0:T(8,128)(2,1)S(1)} %add.133.refs_0_), channel_id=1, source_target_pairs={{0,4},{1,5},{2,6},{3,7},{4,0},{5,1},{6,2},{7,3},{8,12},{9,13},{10,... | collective-permute-start | bytes 460808 | tf_op jit(solution)/shard_map/ppermute | solution.py:809
  130.6 3.7 %collective-permute-start.23 = (f32[8,384]{1,0:T(8,128)S(1)}, f32[8,384]{1,0:T(8,128)S(1)}, u32[]{:S(2)}, u32[]{:S(2)}) collective-permute-start(f32[8,384]{1,0:T(8,128)S(1)} %add.132), channel_id=1, source_target_pairs={{0,4},{1,5},{2,6},{3,7},{4,0},{5,1},{6,2},{7,3},{8,12},{9,13},{10,... | collective-permute-start | bytes 36872 | tf_op jit(solution)/shard_map/ppermute | solution.py:809
  134.4 9.5 %collective-permute-start.28 = (bf16[248,384]{1,0:T(8,128)(2,1)S(1)}, bf16[248,384]{1,0:T(8,128)(2,1)S(1)}, u32[]{:S(2)}, u32[]{:S(2)}) collective-permute-start(bf16[248,384]{1,0:T(8,128)(2,1)S(1)} %add.134), channel_id=1, source_target_pairs={{0,16},{1,17},{2,18},{3,19},{4,20},{5,21},{6,22},{7,23},{8,24},{9,... | collective-permute-start | bytes 571400 | tf_op jit(solution)/shard_map/ppermute | solution.py:809
  137.0 15.5 %copy-start.13 = (bf16[152,384]{1,0:T(8,128)(2,1)}, bf16[152,384]{1,0:T(8,128)(2,1)S(1)}, u32[]{:S(2)}) copy-start(bf16[152,384]{1,0:T(8,128)(2,1)S(1)} %add.135.refs_0_) | copy-start | bytes 350212
  137.1 20.7 %copy-start.21 = (bf16[200,384]{1,0:T(8,128)(2,1)}, bf16[200,384]{1,0:T(8,128)(2,1)S(1)}, u32[]{:S(2)}) copy-start(bf16[200,384]{1,0:T(8,128)(2,1)S(1)} %collective-permute-done.25.refs_1_) | copy-start | bytes 460804
  137.1 6.2 %collective-permute-start.26 = (bf16[152,384]{1,0:T(8,128)(2,1)S(1)}, bf16[152,384]{1,0:T(8,128)(2,1)S(1)}, u32[]{:S(2)}, u32[]{:S(2)}) collective-permute-start(bf16[152,384]{1,0:T(8,128)(2,1)S(1)} %add.135.refs_0_), channel_id=1, source_target_pairs={{0,4},{1,5},{2,6},{3,7},{4,0},{5,1},{6,2},{7,3},{8,12},{9,13},{10,... | collective-permute-start | bytes 350216 | tf_op jit(solution)/shard_map/ppermute | solution.py:809
  139.1 4.2 %collective-permute-start.27 = (f32[8,384]{1,0:T(8,128)S(1)}, f32[8,384]{1,0:T(8,128)S(1)}, u32[]{:S(2)}, u32[]{:S(2)}) collective-permute-start(f32[8,384]{1,0:T(8,128)S(1)} %add.136), channel_id=1, source_target_pairs={{0,8},{1,9},{2,10},{3,11},{4,12},{5,13},{6,14},{7,15},{8,0},{9,1},... | collective-permute-start | bytes 36872 | tf_op jit(solution)/shard_map/ppermute | solution.py:809
  143.3 9.2 %copy-start.24 = (bf16[152,384]{1,0:T(8,128)(2,1)}, bf16[152,384]{1,0:T(8,128)(2,1)S(1)}, u32[]{:S(2)}) copy-start(bf16[152,384]{1,0:T(8,128)(2,1)S(1)} %collective-permute-done.26.refs_1_) | copy-start | bytes 350212
  144.0 13.8 %copy-start.9 = (bf16[248,384]{1,0:T(8,128)(2,1)}, bf16[248,384]{1,0:T(8,128)(2,1)S(1)}, u32[]{:S(2)}) copy-start(bf16[248,384]{1,0:T(8,128)(2,1)S(1)} %add.137.refs_4_) | copy-start | bytes 571396
  144.0 11.9 %collective-permute-start.32 = (bf16[248,384]{1,0:T(8,128)(2,1)S(1)}, bf16[248,384]{1,0:T(8,128)(2,1)S(1)}, u32[]{:S(2)}, u32[]{:S(2)}) collective-permute-start(bf16[248,384]{1,0:T(8,128)(2,1)S(1)} %add.137.refs_4_), channel_id=1, source_target_pairs={{0,4},{1,5},{2,6},{3,7},{4,0},{5,1},{6,2},{7,3},{8,12},{9,13},{10,... | collective-permute-start | bytes 571400 | tf_op jit(solution)/shard_map/ppermute | solution.py:809
  146.8 5.7 %collective-permute-start.29 = (bf16[152,384]{1,0:T(8,128)(2,1)S(1)}, bf16[152,384]{1,0:T(8,128)(2,1)S(1)}, u32[]{:S(2)}, u32[]{:S(2)}) collective-permute-start(bf16[152,384]{1,0:T(8,128)(2,1)S(1)} %add.135.refs_0_), channel_id=1, source_target_pairs={{0,2},{1,3},{2,0},{3,1},{4,6},{5,7},{6,4},{7,5},{8,10},{9,11},{10,... | collective-permute-start | bytes 350216 | tf_op jit(solution)/shard_map/ppermute | solution.py:809
  146.8 5.7 %collective-permute-start.30 = (bf16[152,384]{1,0:T(8,128)(2,1)S(1)}, bf16[152,384]{1,0:T(8,128)(2,1)S(1)}, u32[]{:S(2)}, u32[]{:S(2)}) collective-permute-start(bf16[152,384]{1,0:T(8,128)(2,1)S(1)} %collective-permute-done.26.refs_1_), channel_id=1, source_target_pairs={{0,2},{1,3},{2,0},{3,1},{4,6},{5,7},{6,4},{7,5},{8,10},{9,11},{10,... | collective-permute-start | bytes 350216 | tf_op jit(solution)/shard_map/ppermute | solution.py:809
  147.3 4.6 %collective-permute-start.31 = (f32[8,384]{1,0:T(8,128)S(1)}, f32[8,384]{1,0:T(8,128)S(1)}, u32[]{:S(2)}, u32[]{:S(2)}) collective-permute-start(f32[8,384]{1,0:T(8,128)S(1)} %add.138), channel_id=1, source_target_pairs={{0,16},{1,17},{2,18},{3,19},{4,20},{5,21},{6,22},{7,23},{8,24},{9,... | collective-permute-start | bytes 36872 | tf_op jit(solution)/shard_map/ppermute | solution.py:809
  147.4 11.5 %collective-permute-start.35 = (bf16[248,384]{1,0:T(8,128)(2,1)S(1)}, bf16[248,384]{1,0:T(8,128)(2,1)S(1)}, u32[]{:S(2)}, u32[]{:S(2)}) collective-permute-start(bf16[248,384]{1,0:T(8,128)(2,1)S(1)} %add.137.refs_4_), channel_id=1, source_target_pairs={{0,2},{1,3},{2,0},{3,1},{4,6},{5,7},{6,4},{7,5},{8,10},{9,11},{10,... | collective-permute-start | bytes 571400 | tf_op jit(solution)/shard_map/ppermute | solution.py:809
  152.5 0.6 copy-start.25
  153.1 0.6 copy-start.26
  155.9 1.9 %copy-start.1 = (bf16[8,197,384]{2,1,0:T(8,128)(2,1)S(1)}, bf16[8,197,384]{2,1,0:T(8,128)(2,1)}, u32[]{:S(2)}) copy-start(bf16[8,197,384]{2,1,0:T(8,128)(2,1)} %get-tuple-element.232) | copy-start | bytes 3631108
  155.9 3.0 %copy-start.18 = (bf16[248,384]{1,0:T(8,128)(2,1)}, bf16[248,384]{1,0:T(8,128)(2,1)S(1)}, u32[]{:S(2)}) copy-start(bf16[248,384]{1,0:T(8,128)(2,1)S(1)} %collective-permute-done.32.refs_5_) | copy-start | bytes 571396
  155.9 3.1 %collective-permute-start.36 = (bf16[248,384]{1,0:T(8,128)(2,1)S(1)}, bf16[248,384]{1,0:T(8,128)(2,1)S(1)}, u32[]{:S(2)}, u32[]{:S(2)}) collective-permute-start(bf16[248,384]{1,0:T(8,128)(2,1)S(1)} %collective-permute-done.32.refs_5_), channel_id=1, source_target_pairs={{0,2},{1,3},{2,0},{3,1},{4,6},{5,7},{6,4},{7,5},{8,10},{9,11},{10,... | collective-permute-start | bytes 571400 | tf_op jit(solution)/shard_map/ppermute | solution.py:809
  156.0 3.0 %collective-permute-start.33 = (bf16[200,384]{1,0:T(8,128)(2,1)S(1)}, bf16[200,384]{1,0:T(8,128)(2,1)S(1)}, u32[]{:S(2)}, u32[]{:S(2)}) collective-permute-start(bf16[200,384]{1,0:T(8,128)(2,1)S(1)} %add.133.refs_0_), channel_id=1, source_target_pairs={{0,2},{1,3},{2,0},{3,1},{4,6},{5,7},{6,4},{7,5},{8,10},{9,11},{10,... | collective-permute-start | bytes 460808 | tf_op jit(solution)/shard_map/ppermute | solution.py:809
  156.5 2.5 %collective-permute-start.34 = (bf16[200,384]{1,0:T(8,128)(2,1)S(1)}, bf16[200,384]{1,0:T(8,128)(2,1)S(1)}, u32[]{:S(2)}, u32[]{:S(2)}) collective-permute-start(bf16[200,384]{1,0:T(8,128)(2,1)S(1)} %collective-permute-done.25.refs_1_), channel_id=1, source_target_pairs={{0,2},{1,3},{2,0},{3,1},{4,6},{5,7},{6,4},{7,5},{8,10},{9,11},{10,... | collective-permute-start | bytes 460808 | tf_op jit(solution)/shard_map/ppermute | solution.py:809
  159.0 0.7 copy-start.22
  159.0 0.7 copy-start.23
  159.0 0.8 copy-start.19
  159.8 0.7 copy-start.20
  (1 other events, 0.6 us)

commit v5 on v3

--- a/solution.py
+++ b/solution.py
@@ -87,10 +87,11 @@
 
 
 def quarters(index, keep, send):
-    x, core = index[0], index[1]
-    for slot, half in ((0, x), (1, 1 - x)):
-        yield keep, slot, half, core
-        yield send, slot, half, 1 - core
+    x, core, y = index[0], index[1], index[2]
+    for dest, owner in ((keep, core), (send, 1 - core)):
+        for slot, half in ((0, x), (1, 1 - x)):
+            for side in range(2):
+                yield dest.at[slot, jnp.where(y == side, 0, 1)], half, owner, side
 
 
 def pack_first_kernel(index, *refs):
@@ -190,10 +191,8 @@
     out_ref,
     d_middle_ref,
     d_mixed_ref,
-    keep_a,
-    send_a,
-    keep_b,
-    send_b,
+    keep,
+    send,
     x_s,
     z_s,
     w_out_ref,
@@ -264,30 +263,50 @@
     @pl.when(step == pl.num_programs(0) - 1)
     def _():
         columns = jnp.sum(a_bias[...], axis=0, keepdims=True)
-        vector_rows = [jnp.sum(a_vec[...], axis=1)]
-        vector_rows += [columns[:, c : c + width] for c in range(0, hidden_width, width)]
-        vector_rows += [jnp.zeros((VEC_ROWS - 4 - hidden_width // width, width), F32)]
-        vectors = jnp.concatenate(vector_rows, axis=0).astype(BF16)
-        deep, tall = a_drop.shape[0] // 4, width // 4
-        for dest, slot, half, core in quarters(index, keep_a, send_a):
-            first = pl.multiple_of((2 * half + core) * deep, 8)
-            dest[slot, 0:deep, :] = a_drop[pl.ds(first, deep), :].astype(BF16)
-            dest[slot, deep : deep + VEC_ROWS, :] = vectors
-        for dest, slot, half, core in quarters(index, keep_b, send_b):
-            rows_of = pl.ds(pl.multiple_of((2 * half + core) * tall, 8), tall)
-            blocks = hidden_width // width
-            for k in range(blocks):
-                dest[slot, k * tall : (k + 1) * tall, :] = a_lift[
-                    rows_of, k * width : (k + 1) * width
-                ].astype(BF16)
-            dest[slot, blocks * tall : (blocks + 1) * tall, :] = a_out[rows_of, :].astype(BF16)
-
-
-def back_kernel(length, *refs):
-    proj_ref, d_mixed_ref = refs[:2]
-    d_proj_ref = refs[-1]
-    images, rows, wide = d_proj_ref.shape
+        vectors = jnp.concatenate(
+            [jnp.sum(a_vec[...], axis=1)]
+            + [columns[:, c : c + width] for c in range(0, hidden_width, width)],
+            axis=0,
+        ).astype(BF16)
+        deep, tall, small = hidden_width // 4, width // 4, width // 8
+        for place, half, core, side in quarters(index, keep, send):
+            quarter = 2 * half + core
+            if side == 0:
+                first = pl.multiple_of(quarter * deep, 8)
+                place[0:deep, :] = a_drop[pl.ds(first, deep), :].astype(BF16)
+                place[deep + small :, :] = vectors
+            else:
+                rows_of = pl.ds(pl.multiple_of(quarter * tall, 8), tall)
+                for k in range(hidden_width // width):
+                    place[k * tall : (k + 1) * tall, :] = a_lift[
+                        rows_of, k * width : (k + 1) * width
+                    ].astype(BF16)
+                place[deep + small :, :] = jnp.zeros((8, width), BF16)
+            first = pl.multiple_of(quarter * tall + side * small, 8)
+            place[deep : deep + small, :] = a_out[pl.ds(first, small), :].astype(BF16)
+
+
+def back_kernel(
+    length, first, last, index, tok_ref, proj_ref, normed_ref, d_mixed_ref, d_middle_ref, w_ref, vec_ref, *refs
+):
+    if not first:
+        old, refs = refs[:3], refs[4:]
+    in_grad_ref = refs[0]
+    if last:
+        keep, send = refs[1:3]
+        sums, d_s = refs[3:6], refs[6]
+    else:
+        sums, d_s = refs[1:4], refs[4]
+    a_qkv, a_proj, a_vec = sums
+    images, rows, wide = d_s.shape
     width = wide // 3
+    total = images * rows
+
+    @pl.when(pl.program_id(0) == 0)
+    def _():
+        for i, acc in enumerate(sums):
+            acc[...] = jnp.zeros_like(acc) if first else old[i][...]
+
     live = lax.broadcasted_iota(jnp.int32, (rows, 2 * rows), 0) < length
     for j in range(images):
         for c in range(0, width, PAIR):
@@ -305,50 +324,13 @@
             d_value = nn(probs.astype(BF16), d_mixed)
             d_key = nn(d_scores, query)
             d_query = join_pair(tn(d_scores, key)) * SCALE
-            d_proj_ref[j, :, c : c + PAIR] = d_query.astype(BF16)
-            d_proj_ref[j, :, width + c : width + c + PAIR] = d_key.astype(BF16)
-            d_proj_ref[j, :, 2 * width + c : 2 * width + c + PAIR] = d_value.astype(BF16)
-
-
-def weight_kernel(index, normed_ref, d_proj_ref, keep, send, a_qkv, a_proj):
-    step = pl.program_id(0)
-    images, rows, wide = d_proj_ref.shape
-    width = wide // 3
-    total = images * rows
-
-    @pl.when(step == 0)
-    def _():
-        for acc in (a_qkv, a_proj):
-            acc[...] = jnp.zeros_like(acc)
-
-    d_proj = d_proj_ref[...].reshape(total, wide)
+            d_s[j, :, c : c + PAIR] = d_query.astype(BF16)
+            d_s[j, :, width + c : width + c + PAIR] = d_key.astype(BF16)
+            d_s[j, :, 2 * width + c : 2 * width + c + PAIR] = d_value.astype(BF16)
+    d_proj = d_s[...].reshape(total, wide)
     a_qkv[...] += tn(normed_ref[...].reshape(total, width), d_proj)
     a_proj[...] += fold(d_proj.astype(F32))
-
-    @pl.when(step == pl.num_programs(0) - 1)
-    def _():
-        columns = jnp.sum(a_proj[...], axis=0, keepdims=True)
-        vectors = jnp.concatenate(
-            [columns[:, :width], columns[:, 2 * width :], jnp.zeros((VEC_ROWS - 2, width), F32)], axis=0
-        ).astype(BF16)
-        tall = width // 4
-        for dest, slot, half, core in quarters(index, keep, send):
-            rows_of = pl.ds(pl.multiple_of((2 * half + core) * tall, 8), tall)
-            for k in range(3):
-                dest[slot, k * tall : (k + 1) * tall, :] = a_qkv[
-                    rows_of, k * width : (k + 1) * width
-                ].astype(BF16)
-            dest[slot, 3 * tall : 3 * tall + VEC_ROWS, :] = vectors
-
-
-def input_kernel(length, tok_ref, d_proj_ref, d_middle_ref, w_ref, vec_ref, in_grad_ref, g_vec_ref):
-    images, rows, wide = d_proj_ref.shape
-
-    @pl.when(pl.program_id(0) == 0)
-    def _():
-        g_vec_ref[...] = jnp.zeros_like(g_vec_ref)
-
-    d_normed = nt(d_proj_ref[...].reshape(images * rows, wide), w_ref[...])
+    d_normed = nt(d_proj, w_ref[...])
     gain = vec_ref[0:1, :]
     for j in range(images):
         normal, inverse = normalise(tok_ref[j].astype(F32))
@@ -356,16 +338,33 @@
         in_grad_ref[j] = (
             d_middle_ref[j, 0:length, :] + norm_back(grad, normal, inverse, gain)
         ).astype(BF16)
-        g_vec_ref[0:1, :] += jnp.sum(grad * normal, axis=0, keepdims=True)
-        g_vec_ref[1:2, :] += jnp.sum(grad, axis=0, keepdims=True)
+        a_vec[0:1, :] += jnp.sum(grad * normal, axis=0, keepdims=True)
+        a_vec[1:2, :] += jnp.sum(grad, axis=0, keepdims=True)
+    if not last:
+        return
+
+    @pl.when(pl.program_id(0) == pl.num_programs(0) - 1)
+    def _():
+        columns = jnp.sum(a_proj[...], axis=0, keepdims=True)
+        vectors = jnp.concatenate(
+            [columns[:, :width], columns[:, 2 * width :], a_vec[...], jnp.zeros((4, width), F32)],
+            axis=0,
+        ).astype(BF16)
+        small = width // 8
+        for place, half, core, side in quarters(index, keep, send):
+            first_row = pl.multiple_of((2 * half + core) * 2 * small + side * small, 8)
+            for k in range(3):
+                place[k * small : (k + 1) * small, :] = a_qkv[
+                    pl.ds(first_row, small), k * width : (k + 1) * width
+                ].astype(BF16)
+            place[3 * small :, :] = vectors
 
 
 def placed(full, index, pieces):
-    half = pieces[0].shape[0]
     core, y = index[1], index[2]
     spots = ((core, y), (core, 1 - y), (1 - core, y), (1 - core, 1 - y))
-    for (where, side), piece in zip(spots, pieces):
-        full[where, pl.ds(pl.multiple_of(side * half, 8), half), :] = piece[...].astype(F32)
+    for (owner, side), piece in zip(spots, pieces):
+        full[owner, side] = piece[...].astype(F32)
 
 
 def own_half(index, row):
@@ -374,21 +373,21 @@
 
 
 def unpack_outer_kernel(index, *refs):
-    a_pieces, b_pieces = refs[0:4], refs[4:8]
-    g_drop, g_lift, g_out, g_out_bias, g_gain, g_shift, g_drop_bias, g_lift_bias, a_s, b_s = refs[8:]
-    placed(a_s, index, a_pieces)
-    placed(b_s, index, b_pieces)
+    g_drop, g_lift, g_out, g_out_bias, g_gain, g_shift, g_drop_bias, g_lift_bias, full = refs[4:]
+    placed(full, index, refs[0:4])
     width = g_out.shape[1]
-    deep, tall = g_drop.shape[0] // 2, g_out.shape[0] // 2
+    deep, tall, small = g_drop.shape[0] // 2, width // 4, width // 8
     blocks = g_lift.shape[1] // width
     for core in range(2):
-        g_drop[core * deep : (core + 1) * deep, :] = a_s[core, 0:deep, :]
+        g_drop[core * deep : (core + 1) * deep, :] = full[core, 0, 0:deep, :]
         for k in range(blocks):
-            g_lift[core * tall : (core + 1) * tall, k * width : (k + 1) * width] = b_s[
-                core, k * tall : (k + 1) * tall, :
+            g_lift[core * tall : (core + 1) * tall, k * width : (k + 1) * width] = full[
+                core, 1, k * tall : (k + 1) * tall, :
             ]
-        g_out[core * tall : (core + 1) * tall, :] = b_s[core, blocks * tall : (blocks + 1) * tall, :]
-    vectors = a_s[0, deep : deep + VEC_ROWS, :]
+        for side in range(2):
+            first = core * tall + side * small
+            g_out[first : first + small, :] = full[core, side, deep : deep + small, :]
+    vectors = full[0, 0, deep + small :, :]
     for i, ref in enumerate((g_out_bias, g_gain, g_shift, g_drop_bias)):
         ref[...] = own_half(index, vectors[i : i + 1, :])
     for k in range(blocks // 2):
@@ -401,24 +400,20 @@
 
 
 def unpack_inner_kernel(index, *refs):
-    pieces, late = refs[0:4], refs[4]
-    g_qkv, g_query, g_value, g_gain, g_shift, c_s = refs[5:]
-    placed(c_s, index, pieces)
-    width = late.shape[1]
-    tall = g_qkv.shape[0] // 2
+    g_qkv, g_query, g_value, g_gain, g_shift, full = refs[4:]
+    placed(full, index, refs[0:4])
+    width = full.shape[3]
+    small = width // 8
     for core in range(2):
-        for k in range(3):
-            g_qkv[core * tall : (core + 1) * tall, k * width : (k + 1) * width] = c_s[
-                core, k * tall : (k + 1) * tall, :
-            ]
-    vectors = c_s[0, 3 * tall : 3 * tall + VEC_ROWS, :]
-    g_query[...] = own_half(index, vectors[0:1, :])
-    g_value[...] = own_half(index, vectors[1:2, :])
-    g_gain[...] = own_half(index, late[0:1, :])
-    g_shift[...] = own_half(index, late[1:2, :])
-
-
-VEC_ROWS = 16
+        for side in range(2):
+            first = (2 * core + side) * small
+            for k in range(3):
+                g_qkv[first : first + small, k * width : (k + 1) * width] = full[
+                    core, side, k * small : (k + 1) * small, :
+                ]
+    vectors = full[0, 0, 3 * small :, :]
+    for i, ref in enumerate((g_query, g_value, g_gain, g_shift)):
+        ref[...] = own_half(index, vectors[i : i + 1, :])
 
 
 VMEM_LIMIT = 60 * 1024 * 1024
@@ -476,7 +471,7 @@
 def forward_attention(index, tokens, ff, packed, pieces):
     images, length, width = tokens.shape
     rows = -(-length // 16) * 16
-    group = 2 if images % 2 == 0 else 1
+    group = 4 if images % 4 == 0 else 1
     return pl.pallas_call(
         functools.partial(attend_kernel, length),
         grid=(images // group,),
@@ -506,10 +501,9 @@
     images, length, width = tokens.shape
     rows = mixed.shape[1]
     group = 2 if images % 2 == 0 else 1
-    a_rows = ff // 4 + VEC_ROWS
-    b_rows = (width // 4) * (ff // width + 1)
+    eighth = (2, 2, ff // 4 + width // 8 + 8, width)
     return pl.pallas_call(
-        functools.partial(mlp_kernel, length, 256),
+        functools.partial(mlp_kernel, length, 512),
         grid=(images // group,),
         in_specs=[
             SCALARS,
@@ -522,19 +516,15 @@
             per_step(group, length, width),
             per_step(group, rows, width),
             per_step(group, rows, width),
-            whole(2, a_rows, width),
-            whole(2, a_rows, width),
-            whole(2, b_rows, width),
-            whole(2, b_rows, width),
+            whole(*eighth),
+            whole(*eighth),
         ],
         out_shape=[
             shape_of(BF16, images, length, width),
             shape_of(F32, images, rows, width),
             shape_of(BF16, images, rows, width),
-            shape_of(BF16, 2, a_rows, width),
-            shape_of(BF16, 2, a_rows, width),
-            shape_of(BF16, 2, b_rows, width),
-            shape_of(BF16, 2, b_rows, width),
+            shape_of(BF16, *eighth),
+            shape_of(BF16, *eighth),
         ],
         scratch_shapes=[
             pltpu.VMEM((group, rows, width), BF16),
@@ -555,114 +545,59 @@
     )(index, tokens, cotangent, mixed, vectors, *pieces)
 
 
-def attention_backward(projected, d_mixed, length, first, count, earlier):
-    images, rows, wide = projected.shape
+def attention_backward(
+    index, tokens, projected, normed, w_qkv, vectors, d_mixed, d_middle, start, stop, earlier=()
+):
+    images, length, width = tokens.shape
+    rows = normed.shape[1]
+    wide = 3 * width
     group = 2 if images % 2 == 0 else 1
-    start = first // group
+    offset = start // group
+    first, last = not earlier, stop == images
+    chunk = (2, 2, 3 * width // 8 + 8, width)
+    sums = [(width, wide), (8, wide), (2, width)]
 
     def at(*shape):
-        return pl.BlockSpec(shape, lambda i: (i + start if start else i, 0, 0))
-
-    more = [] if earlier is None else [earlier]
+        return pl.BlockSpec((group,) + shape, lambda i: (i + offset if offset else i, 0, 0))
+
     return pl.pallas_call(
-        functools.partial(back_kernel, length),
-        grid=(count // group,),
-        in_specs=[at(group, rows, wide), at(group, rows, wide // 3)]
-        + [pl.BlockSpec(memory_space=pl.ANY)] * len(more),
-        out_specs=at(group, rows, wide),
-        out_shape=shape_of(BF16, images, rows, wide),
-        input_output_aliases={2: 0} if more else {},
-        compiler_params=PARAMS,
-        cost_estimate=cost(count / 2),
-        name="back",
-    )(projected, d_mixed, *more)
-
-
-def qkv_weight_gradient(index, normed, d_proj):
-    images, rows, width = normed.shape
-    group = 2 if images % 2 == 0 else 1
-    c_rows = 3 * width // 4 + VEC_ROWS
-    return pl.pallas_call(
-        weight_kernel,
-        grid=(images // group,),
-        in_specs=[SCALARS, per_step(group, rows, width), per_step(group, rows, 3 * width)],
-        out_specs=[whole(2, c_rows, width)] * 2,
-        out_shape=[shape_of(BF16, 2, c_rows, width)] * 2,
-        scratch_shapes=[
-            pltpu.VMEM((width, 3 * width), F32),
-            pltpu.VMEM((8, 3 * width), F32),
-        ],
+        functools.partial(back_kernel, length, first, last),
+        grid=((stop - start) // group,),
+        in_specs=[
+            SCALARS,
+            at(length, width),
+            at(rows, wide),
+            at(rows, width),
+            at(rows, width),
+            at(rows, width),
+            *whole_like((w_qkv, vectors)),
+        ]
+        + ([] if first else [whole(*d) for d in sums] + [pl.BlockSpec(memory_space=pl.ANY)]),
+        out_specs=[at(length, width)]
+        + ([whole(*chunk)] * 2 if last else [whole(*d) for d in sums]),
+        out_shape=[shape_of(BF16, images, length, width)]
+        + ([shape_of(BF16, *chunk)] * 2 if last else [shape_of(F32, *d) for d in sums]),
+        scratch_shapes=([pltpu.VMEM(d, F32) for d in sums] if last else [])
+        + [pltpu.VMEM((group, rows, wide), BF16)],
+        input_output_aliases={} if first else {11: 0},
         compiler_params=PARAMS,
         cost_estimate=cost(1),
-        name="qkv_weight_gradient",
-    )(index, normed, d_proj)
-
-
-def input_gradient(tokens, d_proj, d_middle, w_qkv, vectors):
-    images, length, width = tokens.shape
-    rows = d_proj.shape[1]
-    group = 2 if images % 2 == 0 else 1
+        name="back",
+    )(index, tokens, projected, normed, d_mixed, d_middle, w_qkv, vectors, *earlier)
+
+
+def unpack(kernel, index, pieces, shapes, name):
     return pl.pallas_call(
-        functools.partial(input_kernel, length),
-        grid=(images // group,),
-        in_specs=[
-            per_step(group, length, width),
-            per_step(group, rows, 3 * width),
-            per_step(group, rows, width),
-            *whole_like((w_qkv, vectors)),
-        ],
-        out_specs=[per_step(group, length, width), whole(8, width)],
-        out_shape=[shape_of(BF16, images, length, width), shape_of(F32, 8, width)],
+        kernel,
+        grid=(1,),
+        in_specs=[SCALARS, *whole_like(pieces)],
+        out_specs=[whole(*d) for d in shapes],
+        out_shape=[shape_of(F32, *d) for d in shapes],
+        scratch_shapes=[pltpu.VMEM((2, 2) + pieces[0].shape, F32)],
         compiler_params=PARAMS,
         cost_estimate=cost(1),
-        name="input_gradient",
-    )(tokens, d_proj, d_middle, w_qkv, vectors)
-
-
-def unpack_outer(index, a_pieces, b_pieces, width, ff):
-    half = width // 2
-    return pl.pallas_call(
-        unpack_outer_kernel,
-        grid=(1,),
-        in_specs=[SCALARS, *whole_like((*a_pieces, *b_pieces))],
-        out_specs=[
-            whole(ff // 2, width),
-            whole(half, ff),
-            whole(half, width),
-            *[whole(half)] * 4,
-            whole(ff // 2),
-        ],
-        out_shape=[
-            shape_of(F32, ff // 2, width),
-            shape_of(F32, half, ff),
-            shape_of(F32, half, width),
-            *[shape_of(F32, half)] * 4,
-            shape_of(F32, ff // 2),
-        ],
-        scratch_shapes=[
-            pltpu.VMEM((2, 2 * a_pieces[0].shape[0], width), F32),
-            pltpu.VMEM((2, 2 * b_pieces[0].shape[0], width), F32),
-        ],
-        compiler_params=PARAMS,
-        cost_estimate=cost(3),
-        name="unpack_outer",
-    )(index, *a_pieces, *b_pieces)
-
-
-def unpack_inner(index, pieces, late):
-    width = late.shape[1]
-    half = width // 2
-    return pl.pallas_call(
-        unpack_inner_kernel,
-        grid=(1,),
-        in_specs=[SCALARS, *whole_like((*pieces, late))],
-        out_specs=[whole(half, 3 * width), *[whole(half)] * 4],
-        out_shape=[shape_of(F32, half, 3 * width), *[shape_of(F32, half)] * 4],
-        scratch_shapes=[pltpu.VMEM((2, 2 * pieces[0].shape[0], width), F32)],
-        compiler_params=PARAMS,
-        cost_estimate=cost(2),
-        name="unpack_inner",
-    )(index, *pieces, late)
+        name=name,
+    )(index, *pieces)
 
 
 AXES = ("rep", "fsdp")
@@ -692,15 +627,18 @@
     def over_z(self, v, mask):
         return self.swap(v, 4 * mask)
 
-    def half_of(self, v, which):
-        rows = v.shape[-2] // 2
-        return lax.dynamic_slice_in_dim(v, which * rows, rows, v.ndim - 2)
-
-    def to_send(self, v):
-        return self.half_of(v, 1 - self.y)
-
-    def to_keep(self, v):
-        return self.half_of(v, self.y)
+    def over_corner(self, v):
+        return self.swap(v, 2, 1)
+
+    def over_y_and_core(self, v):
+        return self.swap(v, 3)
+
+    def scatter(self, keep, got):
+        total = [[keep[i, j] + got[i, j] for j in range(2)] for i in range(2)]
+        return (total[1][0], total[0][1], total[1][1]), total[0][0]
+
+    def send(self, parts):
+        return self.over_x(parts[0]), self.over_y(parts[1]), self.over_corner(parts[2])
 
 
 class Collective:
@@ -735,17 +673,8 @@
     return lax.optimization_barrier(arrays)
 
 
-def assembled(keep, send, first, tall, blocks):
-    order = (keep[0], send[0], keep[1], send[1])
-    return jnp.concatenate(
-        [
-            jnp.concatenate(
-                [q[first + k * tall : first + (k + 1) * tall] for k in range(blocks)], axis=1
-            )
-            for q in order
-        ],
-        axis=0,
-    )
+def in_order(keep, send):
+    return [(q[0], q[1]) for q in (keep[0], send[0], keep[1], send[1])]
 
 
 def per_device(
@@ -801,86 +730,99 @@
         ]
     else:
         outer = [piece for w in rest for piece in plan.gather_weight(w)]
-    output, d_middle, d_mixed, keep_a, send_a, keep_b, send_b = mlp_both_ways(
+    output, d_middle, d_mixed, keep_a, send_a = mlp_both_ways(
         index, tokens, cotangent, mixed, vectors, ff, outer
     )
-    images = tokens.shape[0]
-    backward = functools.partial(attention_backward, projected, d_mixed, length)
+    backward = functools.partial(
+        attention_backward, index, tokens, projected, normed, full_qkv, vectors
+    )
+    images, half = tokens.shape[0], width // 2
     if swaps:
-        got_a, got_b = plan.over_core(send_a), plan.over_core(send_b)
-        d_proj, got_a, got_b = after(backward(0, 2, None), got_a, got_b)
-        other_a = keep_a[1] + got_a[1]
-        sum_b = keep_b + got_b
-        d_proj, other_a, other_b, sum_b = after(d_proj, other_a, plan.to_send(sum_b), sum_b)
-        over_a, over_b = plan.over_x(other_a), plan.over_y(other_b)
-        d_proj, over_a, over_b = after(backward(2, images - 4, d_proj), over_a, over_b)
-        mine_a = keep_a[0] + got_a[0] + over_a
-        both_b = plan.to_keep(sum_b) + over_b
-        d_proj, other_a, other_b, mine_a, both_b = after(
-            d_proj, plan.to_send(mine_a), both_b[1], mine_a, both_b
+        got_a = plan.over_core(send_a)
+        input_grad, *sums = backward(d_mixed, d_middle, 0, 2)
+        sums, got_a = after(sums, got_a)
+        parts_a, stay_a = plan.scatter(keep_a, got_a)
+        sums, parts_a = after(sums, parts_a)
+        more_a = plan.send(parts_a)
+        input_grad, keep_c, send_c = backward(
+            d_mixed, d_middle, 2, images, (*sums, input_grad)
         )
-        over_a, over_b = plan.over_y(other_a), plan.over_x(other_b)
-        d_proj, over_a, over_b = after(backward(images - 2, 2, d_proj), over_a, over_b)
-        part_a = plan.to_keep(mine_a) + over_a
-        part_b = both_b[0] + over_b
-        d_proj, part_a, part_b = after(d_proj, part_a, part_b)
-        over_a, over_b = plan.over_z(part_a, 1), plan.over_z(part_b, 1)
-        keep_c, send_c = qkv_weight_gradient(index, normed, d_proj)
-        send_c, over_a = after(send_c, over_a)
+        send_c, more_a = after(send_c, more_a)
         got_c = plan.over_core(send_c)
-        over_b, got_c = after(over_b, got_c)
-        part_a, part_b, other_c = part_a + over_a, part_b + over_b, keep_c[1] + got_c[1]
-        d_proj, part_a, part_b, other_c = after(d_proj, part_a, part_b, other_c)
-        over_c, over_a, over_b = (
-            plan.over_x(other_c),
-            plan.over_z(part_a, 2),
-            plan.over_z(part_b, 2),
+        sum_a = stay_a + more_a[0] + more_a[1] + more_a[2]
+        over_a = plan.over_z(sum_a, 1)
+        got_c, sum_a = after(got_c, sum_a)
+        parts_c, stay_c = plan.scatter(keep_c, got_c)
+        parts_c = after(*parts_c)
+        more_c = plan.send(parts_c)
+        more_c, over_a = after(more_c, over_a)
+        sum_c = stay_c + more_c[0] + more_c[1] + more_c[2]
+        sum_a = sum_a + over_a
+        sum_c, sum_a = after(sum_c, sum_a)
+        over_c, over_a = plan.over_z(sum_c, 1), plan.over_z(sum_a, 2)
+        sum_c = sum_c + over_c
+        over_c = plan.over_z(sum_c, 2)
+        over_c, over_a = after(over_c, over_a)
+        sum_c, sum_a = sum_c + over_c, sum_a + over_a
+        sum_c, sum_a = after(sum_c, sum_a)
+        pieces_c = (sum_c, plan.over_y(sum_c), plan.over_core(sum_c), plan.over_y_and_core(sum_c))
+        across_a, beside_a = plan.over_y(sum_a), plan.over_core(sum_a)
+        pieces_c, beside_a = after(pieces_c, beside_a)
+    else:
+        input_grad, *sums = backward(d_mixed, d_middle, 0, images - 2)
+        input_grad, keep_c, send_c = backward(
+            d_mixed, d_middle, images - 2, images, (*sums, input_grad)
         )
-        input_grad, late = input_gradient(tokens, d_proj, d_middle, full_qkv, vectors)
-        late, over_c = after(late, over_c)
-        mine_c = keep_c[0] + got_c[0] + over_c
-        other_c, mine_c, late = after(plan.to_send(mine_c), mine_c, late)
-        over_c, more = plan.over_y(other_c), plan.over_core(late)
-        over_c, more, over_a = after(over_c, more, over_a)
-        part_c, late, part_a = plan.to_keep(mine_c) + over_c, late + more, part_a + over_a
-        part_c, late, part_a = after(part_c, late, part_a)
-        over_c, more = plan.over_z(part_c, 1), plan.over_x(late)
-        across_a, beside_a = plan.over_y(part_a), plan.over_core(part_a)
-        over_c, more, over_b = after(over_c, more, over_b)
-        part_c, late, part_b = part_c + over_c, late + more, part_b + over_b
-        part_c, late, part_b = after(part_c, late, part_b)
-        over_c, more = plan.over_z(part_c, 2), plan.over_y(late)
-        across_b, beside_b = plan.over_y(part_b), plan.over_core(part_b)
-        over_c, more, across_a, across_b = after(over_c, more, across_a, across_b)
-        a_pieces = (part_a, across_a, beside_a, plan.over_core(across_a))
-        b_pieces = (part_b, across_b, beside_b, plan.over_core(across_b))
-        part_c, late = part_c + over_c, late + more
-        part_c, late, a_pieces, b_pieces = after(part_c, late, a_pieces, b_pieces)
-        across_c, beside_c, more = plan.over_y(part_c), plan.over_core(part_c), plan.over_z(late, 1)
-        outer_grads = unpack_outer(index, a_pieces, b_pieces, width, ff)
-        across_c, beside_c, more, outer_grads = after(across_c, beside_c, more, outer_grads)
-        late = late + more
-        c_pieces = (part_c, across_c, beside_c, plan.over_core(across_c))
-        late = late + plan.over_z(late, 2)
+        deep, tall, small = ff // 4, width // 4, width // 8
+        eighths = in_order(keep_a, send_a)
+        g_drop = plan.reduce(jnp.concatenate([q[0][:deep] for q in eighths]))
+        g_lift = plan.reduce(
+            jnp.concatenate(
+                [
+                    jnp.concatenate(
+                        [q[1][k * tall : (k + 1) * tall] for k in range(ff // width)], axis=1
+                    )
+                    for q in eighths
+                ]
+            )
+        )
+        g_out = plan.reduce(
+            jnp.concatenate([side[deep : deep + small] for q in eighths for side in q])
+        )
+        rows = eighths[0][0][deep + small :]
+        g_out_bias, g_gain_two, g_shift_two, g_drop_bias = (plan.reduce(rows[i]) for i in range(4))
+        g_lift_bias = plan.reduce(rows[4:].reshape(-1))
+        eighths = in_order(keep_c, send_c)
+        g_qkv = plan.reduce(
+            jnp.concatenate(
+                [
+                    jnp.concatenate([side[k * small : (k + 1) * small] for k in range(3)], axis=1)
+                    for q in eighths
+                    for side in q
+                ]
+            )
+        )
+        rows = eighths[0][0][3 * small :]
+        g_query, g_value, g_gain_one, g_shift_one = (plan.reduce(rows[i]) for i in range(4))
+    if swaps:
+        g_qkv, g_query, g_value, g_gain_one, g_shift_one = unpack(
+            unpack_inner_kernel,
+            index,
+            pieces_c,
+            [(half, 3 * width)] + [(half,)] * 4,
+            "unpack_inner",
+        )
+        across_a, g_qkv = after(across_a, g_qkv)
+        pieces_a = (sum_a, across_a, beside_a, plan.over_core(across_a))
         g_drop, g_lift, g_out, g_out_bias, g_gain_two, g_shift_two, g_drop_bias, g_lift_bias = (
-            outer_grads
+            unpack(
+                unpack_outer_kernel,
+                index,
+                pieces_a,
+                [(ff // 2, width), (half, ff), (half, width)] + [(half,)] * 4 + [(ff // 2,)],
+                "unpack_outer",
+            )
         )
-        g_qkv, g_query, g_value, g_gain_one, g_shift_one = unpack_inner(index, c_pieces, late)
-    else:
-        d_proj = backward(0, images, None)
-        keep_c, send_c = qkv_weight_gradient(index, normed, d_proj)
-        input_grad, g_first = input_gradient(tokens, d_proj, d_middle, full_qkv, vectors)
-        tall = width // 4
-        g_drop = plan.reduce(assembled(keep_a, send_a, 0, ff // 4, 1))
-        g_lift = plan.reduce(assembled(keep_b, send_b, 0, tall, ff // width))
-        g_out = plan.reduce(assembled(keep_b, send_b, ff // width * tall, tall, 1))
-        g_qkv = plan.reduce(assembled(keep_c, send_c, 0, tall, 3))
-        rows_a = keep_a[0, ff // 4 :]
-        rows_c = keep_c[0, 3 * tall :]
-        g_out_bias, g_gain_two, g_shift_two, g_drop_bias = (plan.reduce(rows_a[i]) for i in range(4))
-        g_lift_bias = plan.reduce(rows_a[4 : 4 + ff // width].reshape(-1))
-        g_query, g_value = plan.reduce(rows_c[0]), plan.reduce(rows_c[1])
-        g_gain_one, g_shift_one = plan.reduce(g_first[0]), plan.reduce(g_first[1])
     return (
         output,
         input_grad,

time: 151 us -> 146 us (0.967)
  Pallas kernels: 80.7 us -> 70.9 us
  waiting for transfers between devices: 31.2 us -> 35.7 us
    pallas_call x8 -> x5, Pallas kernels: 66.2 us -> 56.9 us  [the longest x1 27.5 us: mlp_both_ways(): pl.pallas_call(functools.partial(mlp_kernel, length, 512), grid=(images /...]
    ppermute x37 -> x26, waiting for transfers between devices: 31.2 us -> 35.7 us  [swap(): return lax.ppermute(v, AXES, pairs)]
    ppermute x37 -> x26, starting transfers between devices: 26.6 us -> 27.4 us  [swap(): return lax.ppermute(v, AXES, pairs)]
    unnamed x60 -> x48, local copies, waits for them, and re-layouts: 8.06 us -> 8.18 us
  transfers between devices with their start and end apart: 37 -> 26, of which waited for: 15 -> 9; matrix products, arithmetic and copies ran while one was open for 4% -> 3% of each run, Pallas kernels for 32% -> 26%
where the time goes in v5:
time: 146 us; the launch traced here: 145 us
  Pallas kernels  70.9 us (49%)
  waiting for transfers between devices  35.7 us (24%)
  starting transfers between devices  27.4 us (19%)
  local copies, waits for them, and re-layouts  8.18 us (6%)
  other arithmetic  2.13 us (1%)
    ppermute x26, waiting for transfers between devices, swap(): return lax.ppermute(v, AXES, pairs)  35.7 us
    pallas_call x1, Pallas kernels, mlp_both_ways(): pl.pallas_call(functools.partial(mlp_kernel, length, 512), grid=(images /...  27.5 us
    ppermute x26, starting transfers between devices, swap(): return lax.ppermute(v, AXES, pairs)  27.4 us
    pallas_call x2, Pallas kernels, attention_backward(): pl.pallas_call(functools.partial(back_kernel, length, first, last), grid=...  24.1 us
    pallas_call x1, Pallas kernels, forward_attention(): pl.pallas_call(functools.partial(attend_kernel, length), grid=(images //...  9.9 us
    unnamed x48, local copies, waits for them, and re-layouts  8.18 us
    pallas_call x2, Pallas kernels, unpack(): pl.pallas_call(kernel, grid=(1,), in_specs=[SCALARS, *whole_like(pieces)]...  5.3 us
  transfers between devices with their start and end apart: 26, of which 9 were waited for; matrix products, arithmetic and copies ran while one was open for 3% of the time, Pallas kernels for 26%

profile of v5, /device:TPU:0, one launch (start us, length us, event | category | flops | bytes accessed | tf_op | source)
XLA Modules:
  0.0 145.3 jit_solution(4116912831418520208)
XLA Ops:
  0.7 0.6 pad_add_fusion.index
  1.3 1.9 %pack_first.1.packed = bf16[104,1152]{1,0:T(8,128)(2,1)} custom-call(s32[3]{0:T(128)} %pad_add_fusion.index, bf16[192]{0:T(256)(128)(2,1)} %refs_0_.1, bf16[192]{0:T(256)(128)(2,1)} %refs_1_.1, bf16[192]{0:T(256)(128)(2,1)} %refs_2_.1, bf16[192]{0:T(256)(128)(2,1)} %refs_3_.1, bf16[192]{0:T(256)(128)(2,1)} %refs_4_.1, bf16[192]{0:T(256)(128)(2,1)} %refs_5_.1, ...), custom_call_target="tpu_custom_call" | custom-call | flops 1000 | bytes 1 | tf_op jit(solution)/shard_map/pack_first/pallas_call | solution.py:446
  3.1 2.9 %collective-permute-start = (bf16[104,1152]{1,0:T(8,128)(2,1)}, bf16[104,1152]{1,0:T(8,128)(2,1)S(1)}, u32[]{:S(2)}, u32[]{:S(2)}) collective-permute-start(bf16[104,1152]{1,0:T(8,128)(2,1)} %pack_first.1.packed), channel_id=1, source_target_pairs={{0,1},{1,0},{2,3},{3,2},{4,5},{5,4},{6,7},{7,6},{8,9},{9,8},{10,11... | collective-permute-start | bytes 718856 | tf_op jit(solution)/shard_map/ppermute | solution.py:616
  6.1 2.2 %pack_rest.1 = (bf16[96,384]{1,0:T(8,128)(2,1)}, bf16[96,1536]{1,0:T(8,128)(2,1)}, bf16[384,384]{1,0:T(8,128)(2,1)}) custom-call(s32[3]{0:T(128)} %pad_add_fusion.index, bf16[192,384]{1,0:T(8,128)(2,1)} %out_own.1, bf16[192,1536]{1,0:T(8,128)(2,1)} %lift_own.1, bf16[768,384]{1,0:T(8,128)(2,1)} %drop_own.1), custom_call_target="tpu_custom_call" | custom-call | flops 1000 | bytes 1 | tf_op jit(solution)/shard_map/pack_rest/pallas_call | solution.py:459
  8.3 2.0 %collective-permute-start.4 = (bf16[384,384]{1,0:T(8,128)(2,1)}, bf16[384,384]{1,0:T(8,128)(2,1)S(1)}, u32[]{:S(2)}, u32[]{:S(2)}) collective-permute-start(bf16[384,384]{1,0:T(8,128)(2,1)} %get-tuple-element.99), channel_id=1, source_target_pairs={{0,1},{1,0},{2,3},{3,2},{4,5},{5,4},{6,7},{7,6},{8,9},{9,8},{10,11... | collective-permute-start | bytes 884744 | tf_op jit(solution)/shard_map/ppermute | solution.py:616
  10.3 2.6 %collective-permute-done.near = bf16[104,1152]{1,0:T(8,128)(2,1)S(1)} collective-permute-done((bf16[104,1152]{1,0:T(8,128)(2,1)}, bf16[104,1152]{1,0:T(8,128)(2,1)S(1)}, u32[]{:S(2)}, u32[]{:S(2)}) %collective-permute-start) | collective-permute-done | bytes 239648 | tf_op jit(solution)/shard_map/ppermute | solution.py:616
  13.0 2.1 %collective-permute-start.2 = (bf16[96,384]{1,0:T(8,128)(2,1)}, bf16[96,384]{1,0:T(8,128)(2,1)S(1)}, u32[]{:S(2)}, u32[]{:S(2)}) collective-permute-start(bf16[96,384]{1,0:T(8,128)(2,1)} %get-tuple-element.97), channel_id=1, source_target_pairs={{0,1},{1,0},{2,3},{3,2},{4,5},{5,4},{6,7},{7,6},{8,9},{9,8},{10,11... | collective-permute-start | bytes 221192 | tf_op jit(solution)/shard_map/ppermute | solution.py:616
  15.0 1.2 copy.32.tok_ref
  16.2 0.7 copy-done.16
  16.9 9.9 %attend.1 = (bf16[8,208,384]{2,1,0:T(8,128)(2,1)}, bf16[8,208,1152]{2,1,0:T(8,128)(2,1)}, bf16[8,208,384]{2,1,0:T(8,128)(2,1)}, bf16[384,1152]{1,0:T(8,128)(2,1)}, f32[12,384]{1,0:T(8,128)}) custom-call(s32[3]{0:T(128)} %pad_add_fusion.index, bf16[8,197,384]{2,1,0:T(8,128)(2,1)} %copy.32.tok_ref, bf16[104,1152]{1,0:T(8,128)(2,1)} %pack_first.1.packed, ...), custom_call_target="tpu_custom_call" | custom-call | flops 1000 | bytes 1 | tf_op jit(solution)/shard_map/attend/pallas_call | solution.py:475
  26.8 0.0 copy-start.20
  26.8 0.0 copy-start.11
  26.8 0.0 copy-start.12
  26.9 0.3 collective-permute-start.6
  27.1 0.3 collective-permute-start.7
  27.4 0.2 collective-permute-start.5
  27.7 1.2 copy.33.cot_ref
  28.8 0.2 collective-permute-done.5.out_far
  29.0 0.0 copy-start.14
  29.1 0.6 copy-done.21
  29.7 0.1 copy-done.13
  29.8 0.1 copy-done.14
  29.9 27.5 %mlp.1 = (bf16[8,197,384]{2,1,0:T(8,128)(2,1)}, f32[8,208,384]{2,1,0:T(8,128)}, bf16[8,208,384]{2,1,0:T(8,128)(2,1)}, bf16[2,2,440,384]{3,2,1,0:T(8,128)(2,1)}, bf16[2,2,440,384]{3,2,1,0:T(8,128)(2,1)}) custom-call(s32[3]{0:T(128)} %pad_add_fusion.index, bf16[8,197,384]{2,1,0:T(8,128)(2,1)} %copy.32.tok_ref, bf16[8,197,384]{2,1,0:T(8,128)(2,1)} %copy.33.cot_ref, ...), custom_call_target="tpu_custom_call" | custom-call | flops 1000 | bytes 1 | tf_op jit(solution)/shard_map/mlp/pallas_call | solution.py:505
  57.3 0.3 collective-permute-start.8
  57.6 7.0 %back.2 = (bf16[8,197,384]{2,1,0:T(8,128)(2,1)}, f32[384,1152]{1,0:T(8,128)}, f32[8,1152]{1,0:T(8,128)}, f32[2,384]{1,0:T(2,128)}) custom-call(s32[3]{0:T(128)} %pad_add_fusion.index, bf16[8,197,384]{2,1,0:T(8,128)(2,1)} %copy.32.tok_ref, bf16[8,208,1152]{2,1,0:T(8,128)(2,1)} %get-tuple-element.106.proj_ref, ...), custom_call_target="tpu_custom_call" | custom-call | flops 1000 | bytes 1 | tf_op jit(solution)/shard_map/back/pallas_call | solution.py:563
  64.6 1.0 add_bitcast_fusion
  65.7 1.2 collective-permute-start.9
  66.8 1.5 %collective-permute-start.10 = (bf16[440,384]{1,0:T(8,128)(2,1)}, bf16[440,384]{1,0:T(8,128)(2,1)S(1)}, u32[]{:S(2)}, u32[]{:S(2)}) collective-permute-start(bf16[440,384]{1,0:T(8,128)(2,1)} %get-tuple-element.128), channel_id=1, source_target_pairs={{0,4},{1,5},{2,6},{3,7},{4,0},{5,1},{6,2},{7,3},{8,12},{9,13},{10,... | collective-permute-start | bytes 1013768 | tf_op jit(solution)/shard_map/ppermute | solution.py:616
  68.4 0.8 collective-permute-start.11
  69.2 17.1 %back.3 = (bf16[8,197,384]{2,1,0:T(8,128)(2,1)}, bf16[2,2,152,384]{3,2,1,0:T(8,128)(2,1)}, bf16[2,2,152,384]{3,2,1,0:T(8,128)(2,1)}) custom-call(s32[3]{0:T(128)} %pad_add_fusion.index, bf16[8,197,384]{2,1,0:T(8,128)(2,1)} %copy.32.tok_ref, bf16[8,208,1152]{2,1,0:T(8,128)(2,1)} %get-tuple-element.106.proj_ref, ...), custom_call_target="tpu_custom_call", output_to_operand_aliasing={{0}: (11, {})} | custom-call | flops 1000 | bytes 1 | tf_op jit(solution)/shard_map/back/pallas_call | solution.py:563
  86.3 0.1 collective-permute-start.12
  86.4 0.2 fusion.1
  86.6 1.6 %collective-permute-start.16 = (bf16[440,384]{1,0:T(8,128)(2,1)S(1)}, bf16[440,384]{1,0:T(8,128)(2,1)S(1)}, u32[]{:S(2)}, u32[]{:S(2)}) collective-permute-start(bf16[440,384]{1,0:T(8,128)(2,1)S(1)} %fusion.1), channel_id=1, source_target_pairs={{0,8},{1,9},{2,10},{3,11},{4,12},{5,13},{6,14},{7,15},{8,0},{9,1},... | collective-permute-start | bytes 1013768 | tf_op jit(solution)/shard_map/ppermute | solution.py:616
  88.2 0.2 collective-permute-done.12
  88.4 0.1 add_bitcast_fusion.3
  88.5 1.2 collective-permute-start.13
  89.7 1.5 %collective-permute-start.14 = (bf16[152,384]{1,0:T(8,128)(2,1)S(1)}, bf16[152,384]{1,0:T(8,128)(2,1)S(1)}, u32[]{:S(2)}, u32[]{:S(2)}) collective-permute-start(bf16[152,384]{1,0:T(8,128)(2,1)S(1)} %get-tuple-element.136), channel_id=1, source_target_pairs={{0,4},{1,5},{2,6},{3,7},{4,0},{5,1},{6,2},{7,3},{8,12},{9,13},{10,... | collective-permute-start | bytes 350216 | tf_op jit(solution)/shard_map/ppermute | solution.py:616
  91.2 0.8 collective-permute-start.15
  92.0 4.9 %collective-permute-done.16 = bf16[440,384]{1,0:T(8,128)(2,1)S(1)} collective-permute-done((bf16[440,384]{1,0:T(8,128)(2,1)S(1)}, bf16[440,384]{1,0:T(8,128)(2,1)S(1)}, u32[]{:S(2)}, u32[]{:S(2)}) %collective-permute-start.16) | collective-permute-done | bytes 337952 | tf_op jit(solution)/shard_map/ppermute | solution.py:616
  97.0 0.3 collective-permute-done.15
  97.2 0.1 add.100
  97.3 0.1 fusion.3
  97.4 2.7 %collective-permute-start.19 = (bf16[440,384]{1,0:T(8,128)(2,1)S(1)}, bf16[440,384]{1,0:T(8,128)(2,1)S(1)}, u32[]{:S(2)}, u32[]{:S(2)}) collective-permute-start(bf16[440,384]{1,0:T(8,128)(2,1)S(1)} %add.100), channel_id=1, source_target_pairs={{0,16},{1,17},{2,18},{3,19},{4,20},{5,21},{6,22},{7,23},{8,24},{9,... | collective-permute-start | bytes 1013768 | tf_op jit(solution)/shard_map/ppermute | solution.py:616
  100.1 1.6 %collective-permute-start.17 = (bf16[152,384]{1,0:T(8,128)(2,1)S(1)}, bf16[152,384]{1,0:T(8,128)(2,1)S(1)}, u32[]{:S(2)}, u32[]{:S(2)}) collective-permute-start(bf16[152,384]{1,0:T(8,128)(2,1)S(1)} %fusion.3), channel_id=1, source_target_pairs={{0,8},{1,9},{2,10},{3,11},{4,12},{5,13},{6,14},{7,15},{8,0},{9,1},... | collective-permute-start | bytes 350216 | tf_op jit(solution)/shard_map/ppermute | solution.py:616
  101.6 7.8 %collective-permute-done.17 = bf16[152,384]{1,0:T(8,128)(2,1)S(1)} collective-permute-done((bf16[152,384]{1,0:T(8,128)(2,1)S(1)}, bf16[152,384]{1,0:T(8,128)(2,1)S(1)}, u32[]{:S(2)}, u32[]{:S(2)}) %collective-permute-start.17) | collective-permute-done | bytes 116768 | tf_op jit(solution)/shard_map/ppermute | solution.py:616
  109.4 2.4 %collective-permute-start.18 = (bf16[152,384]{1,0:T(8,128)(2,1)S(1)}, bf16[152,384]{1,0:T(8,128)(2,1)S(1)}, u32[]{:S(2)}, u32[]{:S(2)}) collective-permute-start(bf16[152,384]{1,0:T(8,128)(2,1)S(1)} %add.101), channel_id=1, source_target_pairs={{0,16},{1,17},{2,18},{3,19},{4,20},{5,21},{6,22},{7,23},{8,24},{9,... | collective-permute-start | bytes 350216 | tf_op jit(solution)/shard_map/ppermute | solution.py:616
  111.9 8.0 %collective-permute-done.18 = bf16[152,384]{1,0:T(8,128)(2,1)S(1)} collective-permute-done((bf16[152,384]{1,0:T(8,128)(2,1)S(1)}, bf16[152,384]{1,0:T(8,128)(2,1)S(1)}, u32[]{:S(2)}, u32[]{:S(2)}) %collective-permute-start.18) | collective-permute-done | bytes 116768 | tf_op jit(solution)/shard_map/ppermute | solution.py:616
  119.9 0.0 copy-start.7
  119.9 0.1 add.103.refs_0_
  120.0 0.1 collective-permute-start.23
  120.1 1.6 %collective-permute-start.24 = (bf16[440,384]{1,0:T(8,128)(2,1)S(1)}, bf16[440,384]{1,0:T(8,128)(2,1)S(1)}, u32[]{:S(2)}, u32[]{:S(2)}) collective-permute-start(bf16[440,384]{1,0:T(8,128)(2,1)S(1)} %add.103.refs_0_), channel_id=1, source_target_pairs={{0,4},{1,5},{2,6},{3,7},{4,0},{5,1},{6,2},{7,3},{8,12},{9,13},{10,... | collective-permute-start | bytes 1013768 | tf_op jit(solution)/shard_map/ppermute | solution.py:616
  121.7 0.3 collective-permute-start.22
  122.0 0.3 collective-permute-start.21
  122.3 1.5 %collective-permute-start.20 = (bf16[152,384]{1,0:T(8,128)(2,1)S(1)}, bf16[152,384]{1,0:T(8,128)(2,1)S(1)}, u32[]{:S(2)}, u32[]{:S(2)}) collective-permute-start(bf16[152,384]{1,0:T(8,128)(2,1)S(1)} %add.102.refs_0_), channel_id=1, source_target_pairs={{0,4},{1,5},{2,6},{3,7},{4,0},{5,1},{6,2},{7,3},{8,12},{9,13},{10,... | collective-permute-start | bytes 350216 | tf_op jit(solution)/shard_map/ppermute | solution.py:616
  123.9 8.7 %collective-permute-done.22.refs_3_ = bf16[152,384]{1,0:T(8,128)(2,1)S(1)} collective-permute-done((bf16[152,384]{1,0:T(8,128)(2,1)S(1)}, bf16[152,384]{1,0:T(8,128)(2,1)S(1)}, u32[]{:S(2)}, u32[]{:S(2)}) %collective-permute-start.22) | collective-permute-done | bytes 116768 | tf_op jit(solution)/shard_map/ppermute | solution.py:616
  132.5 2.9 %collective-permute-done.20.refs_1_ = bf16[152,384]{1,0:T(8,128)(2,1)S(1)} collective-permute-done((bf16[152,384]{1,0:T(8,128)(2,1)S(1)}, bf16[152,384]{1,0:T(8,128)(2,1)S(1)}, u32[]{:S(2)}, u32[]{:S(2)}) %collective-permute-start.20) | collective-permute-done | bytes 116768 | tf_op jit(solution)/shard_map/ppermute | solution.py:616
  135.5 0.6 copy-done.19
  136.1 2.2 %unpack_inner.1 = (f32[192,1152]{1,0:T(8,128)}, f32[192]{0:T(256)}, f32[192]{0:T(256)}, f32[192]{0:T(256)}, f32[192]{0:T(256)}) custom-call(s32[3]{0:T(128)} %pad_add_fusion.index, bf16[152,384]{1,0:T(8,128)(2,1)} %copy-done.7, bf16[152,384]{1,0:T(8,128)(2,1)} %copy-done.19, bf16[152,384]{1,0:T(8,128)(2,1)} %copy-done.18, bf16[152,384]{1,0:T(8,128)(2,1)} %copy-done.17), custom_call_target="tpu_custom_call" | custom-call | flops 1000 | bytes 1 | tf_op jit(solution)/shard_map/unpack_inner/pallas_call | solution.py:590
  138.4 0.1 collective-permute-start.25
  138.5 1.2 copy.36
  139.7 0.6 copy-done
  140.2 1.2 copy.37
  141.4 0.7 copy-done.10
  142.1 3.1 %unpack_outer.1 = (f32[768,384]{1,0:T(8,128)}, f32[192,1536]{1,0:T(8,128)}, f32[192,384]{1,0:T(8,128)}, f32[192]{0:T(256)}, f32[192]{0:T(256)}, /*index=5*/f32[192]{0:T(256)}, f32[192]{0:T(256)}, f32[768]{0:T(1024)}) custom-call(s32[3]{0:T(128)} %pad_add_fusion.index, bf16[440,384]{1,0:T(8,128)(2,1)} %copy-done.2, bf16[440,384]{1,0:T(8,128)(2,1)} %copy-done.9, ...), custom_call_target="tpu_custom_call" | custom-call | flops 1000 | bytes 1 | tf_op jit(solution)/shard_map/unpack_outer/pallas_call | solution.py:590
  (53 shorter events, 0.2 us)
Async XLA Ops:
  0.6 14.4 %copy-start.4 = (bf16[8,197,384]{2,0,1:T(8,128)(2,1)S(1)}, bf16[8,197,384]{2,0,1:T(8,128)(2,1)}, u32[]{:S(2)}) copy-start(bf16[8,197,384]{2,0,1:T(8,128)(2,1)} %param.15) | copy-start | bytes 3631108
  3.1 9.8 %collective-permute-start = (bf16[104,1152]{1,0:T(8,128)(2,1)}, bf16[104,1152]{1,0:T(8,128)(2,1)S(1)}, u32[]{:S(2)}, u32[]{:S(2)}) collective-permute-start(bf16[104,1152]{1,0:T(8,128)(2,1)} %pack_first.1.packed), channel_id=1, source_target_pairs={{0,1},{1,0},{2,3},{3,2},{4,5},{5,4},{6,7},{7,6},{8,9},{9,8},{10,11... | collective-permute-start | bytes 718856 | tf_op jit(solution)/shard_map/ppermute | solution.py:616
  8.3 18.5 %collective-permute-start.3 = (bf16[96,1536]{1,0:T(8,128)(2,1)}, bf16[96,1536]{1,0:T(8,128)(2,1)S(1)}, u32[]{:S(2)}, u32[]{:S(2)}) collective-permute-start(bf16[96,1536]{1,0:T(8,128)(2,1)} %get-tuple-element.98), channel_id=1, source_target_pairs={{0,1},{1,0},{2,3},{3,2},{4,5},{5,4},{6,7},{7,6},{8,9},{9,8},{10,11... | collective-permute-start | bytes 884744 | tf_op jit(solution)/shard_map/ppermute | solution.py:616
  8.3 18.6 %collective-permute-start.4 = (bf16[384,384]{1,0:T(8,128)(2,1)}, bf16[384,384]{1,0:T(8,128)(2,1)S(1)}, u32[]{:S(2)}, u32[]{:S(2)}) collective-permute-start(bf16[384,384]{1,0:T(8,128)(2,1)} %get-tuple-element.99), channel_id=1, source_target_pairs={{0,1},{1,0},{2,3},{3,2},{4,5},{5,4},{6,7},{7,6},{8,9},{9,8},{10,11... | collective-permute-start | bytes 884744 | tf_op jit(solution)/shard_map/ppermute | solution.py:616
  12.9 3.3 %copy-start.15 = (bf16[104,1152]{1,0:T(8,128)(2,1)}, bf16[104,1152]{1,0:T(8,128)(2,1)S(1)}, u32[]{:S(2)}) copy-start(bf16[104,1152]{1,0:T(8,128)(2,1)S(1)} %collective-permute-done.near) | copy-start | bytes 718852
  12.9 3.2 %collective-permute-start.1 = (bf16[104,1152]{1,0:T(8,128)(2,1)S(1)}, bf16[104,1152]{1,0:T(8,128)(2,1)S(1)}, u32[]{:S(2)}, u32[]{:S(2)}) collective-permute-start(bf16[104,1152]{1,0:T(8,128)(2,1)S(1)} %collective-permute-done.near), channel_id=1, source_target_pairs={{0,2},{1,3},{2,0},{3,1},{4,6},{5,7},{6,4},{7,5},{8,10},{9,11},{10,... | collective-permute-start | bytes 718856 | tf_op jit(solution)/shard_map/ppermute | solution.py:616
  13.0 13.8 %collective-permute-start.2 = (bf16[96,384]{1,0:T(8,128)(2,1)}, bf16[96,384]{1,0:T(8,128)(2,1)S(1)}, u32[]{:S(2)}, u32[]{:S(2)}) collective-permute-start(bf16[96,384]{1,0:T(8,128)(2,1)} %get-tuple-element.97), channel_id=1, source_target_pairs={{0,1},{1,0},{2,3},{3,2},{4,5},{5,4},{6,7},{7,6},{8,9},{9,8},{10,11... | collective-permute-start | bytes 221192 | tf_op jit(solution)/shard_map/ppermute | solution.py:616
  16.2 11.5 %copy-start.5 = (bf16[8,197,384]{2,0,1:T(8,128)(2,1)S(1)}, bf16[8,197,384]{2,0,1:T(8,128)(2,1)}, u32[]{:S(2)}) copy-start(bf16[8,197,384]{2,0,1:T(8,128)(2,1)} %param.29) | copy-start | bytes 3631108
  16.2 0.7 copy-start.16
  26.8 2.3 %copy-start.20 = (bf16[96,384]{1,0:T(8,128)(2,1)}, bf16[96,384]{1,0:T(8,128)(2,1)S(1)}, u32[]{:S(2)}) copy-start(bf16[96,384]{1,0:T(8,128)(2,1)S(1)} %collective-permute-done.2.out_near) | copy-start | bytes 221188
  26.8 2.2 %copy-start.11 = (bf16[96,1536]{1,0:T(8,128)(2,1)}, bf16[96,1536]{1,0:T(8,128)(2,1)S(1)}, u32[]{:S(2)}) copy-start(bf16[96,1536]{1,0:T(8,128)(2,1)S(1)} %collective-permute-done.3.lift_near) | copy-start | bytes 884740
  26.8 2.2 %copy-start.12 = (bf16[384,384]{1,0:T(8,128)(2,1)}, bf16[384,384]{1,0:T(8,128)(2,1)S(1)}, u32[]{:S(2)}) copy-start(bf16[384,384]{1,0:T(8,128)(2,1)S(1)} %collective-permute-done.4.drop_near) | copy-start | bytes 884740
  26.9 2.2 %collective-permute-start.6 = (bf16[96,1536]{1,0:T(8,128)(2,1)S(1)}, bf16[96,1536]{1,0:T(8,128)(2,1)S(1)}, u32[]{:S(2)}, u32[]{:S(2)}) collective-permute-start(bf16[96,1536]{1,0:T(8,128)(2,1)S(1)} %collective-permute-done.3.lift_near), channel_id=1, source_target_pairs={{0,2},{1,3},{2,0},{3,1},{4,6},{5,7},{6,4},{7,5},{8,10},{9,11},{10,... | collective-permute-start | bytes 884744 | tf_op jit(solution)/shard_map/ppermute | solution.py:616
  27.1 1.9 %collective-permute-start.7 = (bf16[384,384]{1,0:T(8,128)(2,1)S(1)}, bf16[384,384]{1,0:T(8,128)(2,1)S(1)}, u32[]{:S(2)}, u32[]{:S(2)}) collective-permute-start(bf16[384,384]{1,0:T(8,128)(2,1)S(1)} %collective-permute-done.4.drop_near), channel_id=1, source_target_pairs={{0,2},{1,3},{2,0},{3,1},{4,6},{5,7},{6,4},{7,5},{8,10},{9,11},{10,... | collective-permute-start | bytes 884744 | tf_op jit(solution)/shard_map/ppermute | solution.py:616
  27.4 1.6 %collective-permute-start.5 = (bf16[96,384]{1,0:T(8,128)(2,1)S(1)}, bf16[96,384]{1,0:T(8,128)(2,1)S(1)}, u32[]{:S(2)}, u32[]{:S(2)}) collective-permute-start(bf16[96,384]{1,0:T(8,128)(2,1)S(1)} %collective-permute-done.2.out_near), channel_id=1, source_target_pairs={{0,2},{1,3},{2,0},{3,1},{4,6},{5,7},{6,4},{7,5},{8,10},{9,11},{10,... | collective-permute-start | bytes 221192 | tf_op jit(solution)/shard_map/ppermute | solution.py:616
  29.0 0.6 copy-start.21
  29.0 0.7 copy-start.13
  29.0 0.8 copy-start.14
  57.3 7.3 %collective-permute-start.8 = (bf16[2,2,440,384]{3,2,1,0:T(8,128)(2,1)}, bf16[2,2,440,384]{3,2,1,0:T(8,128)(2,1)S(1)}, u32[]{:S(2)}, u32[]{:S(2)}) collective-permute-start(bf16[2,2,440,384]{3,2,1,0:T(8,128)(2,1)} %get-tuple-element.114), channel_id=1, source_target_pairs={{0,2},{1,3},{2,0},{3,1},{4,6},{5,7},{6,4},{7,5},{8,10},{9,11},{10,... | collective-permute-start | bytes 4055048 | tf_op jit(solution)/shard_map/ppermute | solution.py:616
  57.6 7.0 %copy-start.1 = (bf16[2,2,440,384]{3,2,1,0:T(8,128)(2,1)S(1)}, bf16[2,2,440,384]{3,2,1,0:T(8,128)(2,1)}, u32[]{:S(2)}) copy-start(bf16[2,2,440,384]{3,2,1,0:T(8,128)(2,1)} %get-tuple-element.118) | copy-start | bytes 4055044
  65.7 20.6 %collective-permute-start.9 = (bf16[440,384]{1,0:T(8,128)(2,1)}, bf16[440,384]{1,0:T(8,128)(2,1)S(1)}, u32[]{:S(2)}, u32[]{:S(2)}) collective-permute-start(bf16[440,384]{1,0:T(8,128)(2,1)} %get-tuple-element.127), channel_id=1, source_target_pairs={{0,1},{1,0},{2,3},{3,2},{4,5},{5,4},{6,7},{7,6},{8,9},{9,8},{10,11... | collective-permute-start | bytes 1013768 | tf_op jit(solution)/shard_map/ppermute | solution.py:616
  66.8 19.5 %collective-permute-start.10 = (bf16[440,384]{1,0:T(8,128)(2,1)}, bf16[440,384]{1,0:T(8,128)(2,1)S(1)}, u32[]{:S(2)}, u32[]{:S(2)}) collective-permute-start(bf16[440,384]{1,0:T(8,128)(2,1)} %get-tuple-element.128), channel_id=1, source_target_pairs={{0,4},{1,5},{2,6},{3,7},{4,0},{5,1},{6,2},{7,3},{8,12},{9,13},{10,... | collective-permute-start | bytes 1013768 | tf_op jit(solution)/shard_map/ppermute | solution.py:616
  68.4 17.9 %collective-permute-start.11 = (bf16[440,384]{1,0:T(8,128)(2,1)S(1)}, bf16[440,384]{1,0:T(8,128)(2,1)S(1)}, u32[]{:S(2)}, u32[]{:S(2)}) collective-permute-start(bf16[440,384]{1,0:T(8,128)(2,1)S(1)} %get-tuple-element.129), channel_id=1, source_target_pairs={{0,5},{1,4},{2,7},{3,6},{4,1},{5,0},{6,3},{7,2},{8,13},{9,12},{10,... | collective-permute-start | bytes 1013768 | tf_op jit(solution)/shard_map/ppermute | solution.py:616
  86.3 2.2 %copy-start.6 = (bf16[2,2,152,384]{3,2,1,0:T(8,128)(2,1)S(1)}, bf16[2,2,152,384]{3,2,1,0:T(8,128)(2,1)}, u32[]{:S(2)}) copy-start(bf16[2,2,152,384]{3,2,1,0:T(8,128)(2,1)} %get-tuple-element.125) | copy-start | bytes 1400836
  86.3 2.1 %collective-permute-start.12 = (bf16[2,2,152,384]{3,2,1,0:T(8,128)(2,1)}, bf16[2,2,152,384]{3,2,1,0:T(8,128)(2,1)S(1)}, u32[]{:S(2)}, u32[]{:S(2)}) collective-permute-start(bf16[2,2,152,384]{3,2,1,0:T(8,128)(2,1)} %get-tuple-element.130), channel_id=1, source_target_pairs={{0,2},{1,3},{2,0},{3,1},{4,6},{5,7},{6,4},{7,5},{8,10},{9,11},{10,... | collective-permute-start | bytes 1400840 | tf_op jit(solution)/shard_map/ppermute | solution.py:616
  86.6 10.4 %collective-permute-start.16 = (bf16[440,384]{1,0:T(8,128)(2,1)S(1)}, bf16[440,384]{1,0:T(8,128)(2,1)S(1)}, u32[]{:S(2)}, u32[]{:S(2)}) collective-permute-start(bf16[440,384]{1,0:T(8,128)(2,1)S(1)} %fusion.1), channel_id=1, source_target_pairs={{0,8},{1,9},{2,10},{3,11},{4,12},{5,13},{6,14},{7,15},{8,0},{9,1},... | collective-permute-start | bytes 1013768 | tf_op jit(solution)/shard_map/ppermute | solution.py:616
  88.5 8.5 %collective-permute-start.13 = (bf16[152,384]{1,0:T(8,128)(2,1)S(1)}, bf16[152,384]{1,0:T(8,128)(2,1)S(1)}, u32[]{:S(2)}, u32[]{:S(2)}) collective-permute-start(bf16[152,384]{1,0:T(8,128)(2,1)S(1)} %get-tuple-element.135), channel_id=1, source_target_pairs={{0,1},{1,0},{2,3},{3,2},{4,5},{5,4},{6,7},{7,6},{8,9},{9,8},{10,11... | collective-permute-start | bytes 350216 | tf_op jit(solution)/shard_map/ppermute | solution.py:616
  89.7 7.2 %collective-permute-start.14 = (bf16[152,384]{1,0:T(8,128)(2,1)S(1)}, bf16[152,384]{1,0:T(8,128)(2,1)S(1)}, u32[]{:S(2)}, u32[]{:S(2)}) collective-permute-start(bf16[152,384]{1,0:T(8,128)(2,1)S(1)} %get-tuple-element.136), channel_id=1, source_target_pairs={{0,4},{1,5},{2,6},{3,7},{4,0},{5,1},{6,2},{7,3},{8,12},{9,13},{10,... | collective-permute-start | bytes 350216 | tf_op jit(solution)/shard_map/ppermute | solution.py:616
  91.2 6.0 %collective-permute-start.15 = (bf16[152,384]{1,0:T(8,128)(2,1)S(1)}, bf16[152,384]{1,0:T(8,128)(2,1)S(1)}, u32[]{:S(2)}, u32[]{:S(2)}) collective-permute-start(bf16[152,384]{1,0:T(8,128)(2,1)S(1)} %get-tuple-element.137), channel_id=1, source_target_pairs={{0,5},{1,4},{2,7},{3,6},{4,1},{5,0},{6,3},{7,2},{8,13},{9,12},{10,... | collective-permute-start | bytes 350216 | tf_op jit(solution)/shard_map/ppermute | solution.py:616
  97.3 41.1 %copy-start.3 = (bf16[8,197,384]{2,1,0:T(8,128)(2,1)S(1)}, bf16[8,197,384]{2,1,0:T(8,128)(2,1)}, u32[]{:S(2)}) copy-start(bf16[8,197,384]{2,1,0:T(8,128)(2,1)} %get-tuple-element.169) | copy-start | bytes 3631108
  97.4 22.5 %collective-permute-start.19 = (bf16[440,384]{1,0:T(8,128)(2,1)S(1)}, bf16[440,384]{1,0:T(8,128)(2,1)S(1)}, u32[]{:S(2)}, u32[]{:S(2)}) collective-permute-start(bf16[440,384]{1,0:T(8,128)(2,1)S(1)} %add.100), channel_id=1, source_target_pairs={{0,16},{1,17},{2,18},{3,19},{4,20},{5,21},{6,22},{7,23},{8,24},{9,... | collective-permute-start | bytes 1013768 | tf_op jit(solution)/shard_map/ppermute | solution.py:616
  100.1 9.3 %collective-permute-start.17 = (bf16[152,384]{1,0:T(8,128)(2,1)S(1)}, bf16[152,384]{1,0:T(8,128)(2,1)S(1)}, u32[]{:S(2)}, u32[]{:S(2)}) collective-permute-start(bf16[152,384]{1,0:T(8,128)(2,1)S(1)} %fusion.3), channel_id=1, source_target_pairs={{0,8},{1,9},{2,10},{3,11},{4,12},{5,13},{6,14},{7,15},{8,0},{9,1},... | collective-permute-start | bytes 350216 | tf_op jit(solution)/shard_map/ppermute | solution.py:616
  109.4 10.5 %collective-permute-start.18 = (bf16[152,384]{1,0:T(8,128)(2,1)S(1)}, bf16[152,384]{1,0:T(8,128)(2,1)S(1)}, u32[]{:S(2)}, u32[]{:S(2)}) collective-permute-start(bf16[152,384]{1,0:T(8,128)(2,1)S(1)} %add.101), channel_id=1, source_target_pairs={{0,16},{1,17},{2,18},{3,19},{4,20},{5,21},{6,22},{7,23},{8,24},{9,... | collective-permute-start | bytes 350216 | tf_op jit(solution)/shard_map/ppermute | solution.py:616
  119.9 15.6 %copy-start.7 = (bf16[152,384]{1,0:T(8,128)(2,1)}, bf16[152,384]{1,0:T(8,128)(2,1)S(1)}, u32[]{:S(2)}) copy-start(bf16[152,384]{1,0:T(8,128)(2,1)S(1)} %add.102.refs_0_) | copy-start | bytes 350212
  120.0 19.6 %copy-start.2 = (bf16[440,384]{1,0:T(8,128)(2,1)}, bf16[440,384]{1,0:T(8,128)(2,1)S(1)}, u32[]{:S(2)}) copy-start(bf16[440,384]{1,0:T(8,128)(2,1)S(1)} %add.103.refs_0_) | copy-start | bytes 1013764
  120.0 15.4 %collective-permute-start.23 = (bf16[440,384]{1,0:T(8,128)(2,1)S(1)}, bf16[440,384]{1,0:T(8,128)(2,1)S(1)}, u32[]{:S(2)}, u32[]{:S(2)}) collective-permute-start(bf16[440,384]{1,0:T(8,128)(2,1)S(1)} %add.103.refs_0_), channel_id=1, source_target_pairs={{0,2},{1,3},{2,0},{3,1},{4,6},{5,7},{6,4},{7,5},{8,10},{9,11},{10,... | collective-permute-start | bytes 1013768 | tf_op jit(solution)/shard_map/ppermute | solution.py:616
  120.1 18.2 %collective-permute-start.24 = (bf16[440,384]{1,0:T(8,128)(2,1)S(1)}, bf16[440,384]{1,0:T(8,128)(2,1)S(1)}, u32[]{:S(2)}, u32[]{:S(2)}) collective-permute-start(bf16[440,384]{1,0:T(8,128)(2,1)S(1)} %add.103.refs_0_), channel_id=1, source_target_pairs={{0,4},{1,5},{2,6},{3,7},{4,0},{5,1},{6,2},{7,3},{8,12},{9,13},{10,... | collective-permute-start | bytes 1013768 | tf_op jit(solution)/shard_map/ppermute | solution.py:616
  121.7 10.8 %collective-permute-start.22 = (bf16[152,384]{1,0:T(8,128)(2,1)S(1)}, bf16[152,384]{1,0:T(8,128)(2,1)S(1)}, u32[]{:S(2)}, u32[]{:S(2)}) collective-permute-start(bf16[152,384]{1,0:T(8,128)(2,1)S(1)} %add.102.refs_0_), channel_id=1, source_target_pairs={{0,6},{1,7},{2,4},{3,5},{4,2},{5,3},{6,0},{7,1},{8,14},{9,15},{10,... | collective-permute-start | bytes 350216 | tf_op jit(solution)/shard_map/ppermute | solution.py:616
  122.0 10.5 %collective-permute-start.21 = (bf16[152,384]{1,0:T(8,128)(2,1)S(1)}, bf16[152,384]{1,0:T(8,128)(2,1)S(1)}, u32[]{:S(2)}, u32[]{:S(2)}) collective-permute-start(bf16[152,384]{1,0:T(8,128)(2,1)S(1)} %add.102.refs_0_), channel_id=1, source_target_pairs={{0,2},{1,3},{2,0},{3,1},{4,6},{5,7},{6,4},{7,5},{8,10},{9,11},{10,... | collective-permute-start | bytes 350216 | tf_op jit(solution)/shard_map/ppermute | solution.py:616
  122.3 13.1 %collective-permute-start.20 = (bf16[152,384]{1,0:T(8,128)(2,1)S(1)}, bf16[152,384]{1,0:T(8,128)(2,1)S(1)}, u32[]{:S(2)}, u32[]{:S(2)}) collective-permute-start(bf16[152,384]{1,0:T(8,128)(2,1)S(1)} %add.102.refs_0_), channel_id=1, source_target_pairs={{0,4},{1,5},{2,6},{3,7},{4,0},{5,1},{6,2},{7,3},{8,12},{9,13},{10,... | collective-permute-start | bytes 350216 | tf_op jit(solution)/shard_map/ppermute | solution.py:616
  132.5 3.0 %copy-start.17 = (bf16[152,384]{1,0:T(8,128)(2,1)}, bf16[152,384]{1,0:T(8,128)(2,1)S(1)}, u32[]{:S(2)}) copy-start(bf16[152,384]{1,0:T(8,128)(2,1)S(1)} %collective-permute-done.22.refs_3_) | copy-start | bytes 350212
  132.5 3.0 %copy-start.18 = (bf16[152,384]{1,0:T(8,128)(2,1)}, bf16[152,384]{1,0:T(8,128)(2,1)S(1)}, u32[]{:S(2)}) copy-start(bf16[152,384]{1,0:T(8,128)(2,1)S(1)} %collective-permute-done.21.refs_2_) | copy-start | bytes 350212
  135.5 0.6 copy-start.19
  136.1 3.5 %copy-start.8 = (bf16[440,384]{1,0:T(8,128)(2,1)}, bf16[440,384]{1,0:T(8,128)(2,1)S(1)}, u32[]{:S(2)}) copy-start(bf16[440,384]{1,0:T(8,128)(2,1)S(1)} %collective-permute-done.23.refs_2_) | copy-start | bytes 1013764
  138.4 1.9 %copy-start = (bf16[8,197,384]{2,1,0:T(8,128)(2,1)S(1)}, bf16[8,197,384]{2,1,0:T(8,128)(2,1)}, u32[]{:S(2)}) copy-start(bf16[8,197,384]{2,1,0:T(8,128)(2,1)} %get-tuple-element.170) | copy-start | bytes 3631108
  138.4 3.0 %copy-start.9 = (bf16[440,384]{1,0:T(8,128)(2,1)}, bf16[440,384]{1,0:T(8,128)(2,1)S(1)}, u32[]{:S(2)}) copy-start(bf16[440,384]{1,0:T(8,128)(2,1)S(1)} %collective-permute-done.24.refs_1_) | copy-start | bytes 1013764
  138.4 3.0 %collective-permute-start.25 = (bf16[440,384]{1,0:T(8,128)(2,1)S(1)}, bf16[440,384]{1,0:T(8,128)(2,1)S(1)}, u32[]{:S(2)}, u32[]{:S(2)}) collective-permute-start(bf16[440,384]{1,0:T(8,128)(2,1)S(1)} %collective-permute-done.24.refs_1_), channel_id=1, source_target_pairs={{0,2},{1,3},{2,0},{3,1},{4,6},{5,7},{6,4},{7,5},{8,10},{9,11},{10,... | collective-permute-start | bytes 1013768 | tf_op jit(solution)/shard_map/ppermute | solution.py:616
  141.4 0.7 copy-start.10

commit v6 on v5

--- a/solution.py
+++ b/solution.py
@@ -4,6 +4,7 @@
 import jax.numpy as jnp
 from jax import lax
 from jax.experimental import pallas as pl
+from jax.experimental.layout import Layout, with_layout_constraint
 from jax.experimental.pallas import tpu as pltpu
 from jax.sharding import PartitionSpec as P
 
@@ -274,14 +275,15 @@
             if side == 0:
                 first = pl.multiple_of(quarter * deep, 8)
                 place[0:deep, :] = a_drop[pl.ds(first, deep), :].astype(BF16)
-                place[deep + small :, :] = vectors
+                place[deep + small : deep + small + 8, :] = vectors
+                place[deep + small + 8 :, :] = jnp.zeros((8, width), BF16)
             else:
                 rows_of = pl.ds(pl.multiple_of(quarter * tall, 8), tall)
                 for k in range(hidden_width // width):
                     place[k * tall : (k + 1) * tall, :] = a_lift[
                         rows_of, k * width : (k + 1) * width
                     ].astype(BF16)
-                place[deep + small :, :] = jnp.zeros((8, width), BF16)
+                place[deep + small :, :] = jnp.zeros((16, width), BF16)
             first = pl.multiple_of(quarter * tall + side * small, 8)
             place[deep : deep + small, :] = a_out[pl.ds(first, small), :].astype(BF16)
 
@@ -360,11 +362,19 @@
             place[3 * small :, :] = vectors
 
 
-def placed(full, index, pieces):
+def placed(full, index, pieces, by_z=False):
     core, y = index[1], index[2]
     spots = ((core, y), (core, 1 - y), (1 - core, y), (1 - core, 1 - y))
+    rows = pieces[0].shape[0]
     for (owner, side), piece in zip(spots, pieces):
-        full[owner, side] = piece[...].astype(F32)
+        if by_z:
+            half = rows // 2
+            for k, z in ((0, index[3]), (1, 1 - index[3])):
+                full[owner, side, pl.ds(pl.multiple_of(z * half, 8), half), :] = piece[
+                    k * half : (k + 1) * half, :
+                ].astype(F32)
+        else:
+            full[owner, side] = piece[...].astype(F32)
 
 
 def own_half(index, row):
@@ -372,9 +382,14 @@
     return jnp.where(index[0] == 0, row[:, :half], row[:, half:])[0]
 
 
-def unpack_outer_kernel(index, *refs):
-    g_drop, g_lift, g_out, g_out_bias, g_gain, g_shift, g_drop_bias, g_lift_bias, full = refs[4:]
-    placed(full, index, refs[0:4])
+def unpack_kernel(index, *refs):
+    unpack_outer(index, refs[0:4], refs[8:16], refs[21])
+    unpack_inner(index, refs[4:8], refs[16:21], refs[22])
+
+
+def unpack_outer(index, pieces, outs, full):
+    g_drop, g_lift, g_out, g_out_bias, g_gain, g_shift, g_drop_bias, g_lift_bias = outs
+    placed(full, index, pieces, by_z=True)
     width = g_out.shape[1]
     deep, tall, small = g_drop.shape[0] // 2, width // 4, width // 8
     blocks = g_lift.shape[1] // width
@@ -399,9 +414,9 @@
         g_lift_bias[k * width : (k + 1) * width] = row[0]
 
 
-def unpack_inner_kernel(index, *refs):
-    g_qkv, g_query, g_value, g_gain, g_shift, full = refs[4:]
-    placed(full, index, refs[0:4])
+def unpack_inner(index, pieces, outs, full):
+    g_qkv, g_query, g_value, g_gain, g_shift = outs
+    placed(full, index, pieces)
     width = full.shape[3]
     small = width // 8
     for core in range(2):
@@ -501,7 +516,7 @@
     images, length, width = tokens.shape
     rows = mixed.shape[1]
     group = 2 if images % 2 == 0 else 1
-    eighth = (2, 2, ff // 4 + width // 8 + 8, width)
+    eighth = (2, 2, ff // 4 + width // 8 + 16, width)
     return pl.pallas_call(
         functools.partial(mlp_kernel, length, 512),
         grid=(images // group,),
@@ -586,18 +601,21 @@
     )(index, tokens, projected, normed, d_mixed, d_middle, w_qkv, vectors, *earlier)
 
 
-def unpack(kernel, index, pieces, shapes, name):
+def unpack(index, outer, inner, shapes):
     return pl.pallas_call(
-        kernel,
+        unpack_kernel,
         grid=(1,),
-        in_specs=[SCALARS, *whole_like(pieces)],
+        in_specs=[SCALARS, *whole_like((*outer, *inner))],
         out_specs=[whole(*d) for d in shapes],
         out_shape=[shape_of(F32, *d) for d in shapes],
-        scratch_shapes=[pltpu.VMEM((2, 2) + pieces[0].shape, F32)],
+        scratch_shapes=[
+            pltpu.VMEM((2, 2) + outer[0].shape, F32),
+            pltpu.VMEM((2, 2) + inner[0].shape, F32),
+        ],
         compiler_params=PARAMS,
         cost_estimate=cost(1),
-        name=name,
-    )(index, *pieces)
+        name="unpack",
+    )(index, *outer, *inner)
 
 
 AXES = ("rep", "fsdp")
@@ -606,8 +624,8 @@
 class Butterfly:
     def __init__(self):
         rep, x = lax.axis_index("rep"), lax.axis_index("fsdp")
-        self.x, self.core, self.y = x, rep & 1, (rep >> 1) & 1
-        self.index = jnp.stack([self.x, self.core, self.y]).astype(jnp.int32)
+        self.z = (rep >> 2) & 1
+        self.index = jnp.stack([x, rep & 1, (rep >> 1) & 1, self.z]).astype(jnp.int32)
 
     def swap(self, v, rep_mask, x_mask=0):
         pairs = [
@@ -633,6 +651,10 @@
     def over_y_and_core(self, v):
         return self.swap(v, 3)
 
+    def half(self, v, which):
+        rows = v.shape[0] // 2
+        return lax.dynamic_slice_in_dim(v, which * rows, rows, 0)
+
     def scatter(self, keep, got):
         total = [[keep[i, j] + got[i, j] for j in range(2)] for i in range(2)]
         return (total[1][0], total[0][1], total[1][1]), total[0][0]
@@ -643,7 +665,7 @@
 
 class Collective:
     def __init__(self):
-        self.index = jnp.zeros((3,), jnp.int32)
+        self.index = jnp.zeros((4,), jnp.int32)
 
     def gather_weight(self, own):
         full = lax.all_gather(own, "fsdp", axis=0, tiled=True)
@@ -671,6 +693,14 @@
 
 def after(*arrays):
     return lax.optimization_barrier(arrays)
+
+
+def behind(arrays, *others):
+    return lax.optimization_barrier((arrays, others))[0]
+
+
+def settled(v):
+    return with_layout_constraint(v.transpose(1, 0, 2), Layout(major_to_minor=(0, 1, 2)))
 
 
 def in_order(keep, send):
@@ -750,24 +780,56 @@
         send_c, more_a = after(send_c, more_a)
         got_c = plan.over_core(send_c)
         sum_a = stay_a + more_a[0] + more_a[1] + more_a[2]
-        over_a = plan.over_z(sum_a, 1)
-        got_c, sum_a = after(got_c, sum_a)
+        low_a, high_a = plan.half(sum_a, plan.z), plan.half(sum_a, 1 - plan.z)
+        over_a = plan.over_z(high_a, 1)
+        got_c = behind(got_c, low_a, high_a)
         parts_c, stay_c = plan.scatter(keep_c, got_c)
-        parts_c = after(*parts_c)
+        over_a = behind(over_a, parts_c)
         more_c = plan.send(parts_c)
-        more_c, over_a = after(more_c, over_a)
+        low_a = low_a + over_a
+        over_a = plan.over_z(low_a, 2)
+        more_c = behind(more_c, low_a)
         sum_c = stay_c + more_c[0] + more_c[1] + more_c[2]
-        sum_a = sum_a + over_a
-        sum_c, sum_a = after(sum_c, sum_a)
-        over_c, over_a = plan.over_z(sum_c, 1), plan.over_z(sum_a, 2)
+        over_a = behind(over_a, sum_c)
+        over_c = plan.over_z(sum_c, 1)
+        low_a = low_a + over_a
+        over_a = plan.over_z(low_a, 1)
+        over_c = behind(over_c, low_a)
         sum_c = sum_c + over_c
+        over_a = behind(over_a, sum_c)
         over_c = plan.over_z(sum_c, 2)
-        over_c, over_a = after(over_c, over_a)
-        sum_c, sum_a = sum_c + over_c, sum_a + over_a
-        sum_c, sum_a = after(sum_c, sum_a)
+        sum_a = jnp.concatenate([low_a, over_a])
+        across_a, beside_a = plan.over_y(sum_a), plan.over_core(sum_a)
+        output, input_grad = settled(output), settled(input_grad)
+        over_c, output, input_grad = behind((over_c, output, input_grad), sum_a)
+        output, input_grad = output.transpose(1, 0, 2), input_grad.transpose(1, 0, 2)
+        sum_c = sum_c + over_c
+        across_a = behind(across_a, sum_c)
         pieces_c = (sum_c, plan.over_y(sum_c), plan.over_core(sum_c), plan.over_y_and_core(sum_c))
-        across_a, beside_a = plan.over_y(sum_a), plan.over_core(sum_a)
-        pieces_c, beside_a = after(pieces_c, beside_a)
+        pieces_a = (sum_a, across_a, beside_a, plan.over_core(across_a))
+        (
+            g_drop,
+            g_lift,
+            g_out,
+            g_out_bias,
+            g_gain_two,
+            g_shift_two,
+            g_drop_bias,
+            g_lift_bias,
+            g_qkv,
+            g_query,
+            g_value,
+            g_gain_one,
+            g_shift_one,
+        ) = unpack(
+            index,
+            pieces_a,
+            pieces_c,
+            [(ff // 2, width), (half, ff), (half, width)]
+            + [(half,)] * 4
+            + [(ff // 2,), (half, 3 * width)]
+            + [(half,)] * 4,
+        )
     else:
         input_grad, *sums = backward(d_mixed, d_middle, 0, images - 2)
         input_grad, keep_c, send_c = backward(
@@ -789,7 +851,7 @@
         g_out = plan.reduce(
             jnp.concatenate([side[deep : deep + small] for q in eighths for side in q])
         )
-        rows = eighths[0][0][deep + small :]
+        rows = eighths[0][0][deep + small : deep + small + 8]
         g_out_bias, g_gain_two, g_shift_two, g_drop_bias = (plan.reduce(rows[i]) for i in range(4))
         g_lift_bias = plan.reduce(rows[4:].reshape(-1))
         eighths = in_order(keep_c, send_c)
@@ -804,25 +866,6 @@
         )
         rows = eighths[0][0][3 * small :]
         g_query, g_value, g_gain_one, g_shift_one = (plan.reduce(rows[i]) for i in range(4))
-    if swaps:
-        g_qkv, g_query, g_value, g_gain_one, g_shift_one = unpack(
-            unpack_inner_kernel,
-            index,
-            pieces_c,
-            [(half, 3 * width)] + [(half,)] * 4,
-            "unpack_inner",
-        )
-        across_a, g_qkv = after(across_a, g_qkv)
-        pieces_a = (sum_a, across_a, beside_a, plan.over_core(across_a))
-        g_drop, g_lift, g_out, g_out_bias, g_gain_two, g_shift_two, g_drop_bias, g_lift_bias = (
-            unpack(
-                unpack_outer_kernel,
-                index,
-                pieces_a,
-                [(ff // 2, width), (half, ff), (half, width)] + [(half,)] * 4 + [(ff // 2,)],
-                "unpack_outer",
-            )
-        )
     return (
         output,
         input_grad,

time: 146 us -> 136 us (0.932)
  waiting for transfers between devices: 35.7 us -> 26.6 us
  Pallas kernels: 70.9 us -> 69.1 us
  starting transfers between devices: 27.4 us -> 28.9 us
    ppermute x26 -> x27, waiting for transfers between devices: 35.7 us -> 26.6 us  [swap(): return lax.ppermute(v, AXES, pairs)]
    unnamed x48 -> x46, local copies, waits for them, and re-layouts: 8.18 us -> 5.4 us
    pallas_call x0 -> x2, local copies, waits for them, and re-layouts: none -> 2.36 us  [the longest x1 1.18 us: attention_backward(): pl.pallas_call(functools.partial(back_kernel, length, first, last), grid=...]
    pallas_call x2 -> x1, Pallas kernels: 5.3 us -> 3.6 us  [unpack(): pl.pallas_call(unpack_kernel, grid=(1,), in_specs=[SCALARS, *whole_like((...]
    ppermute x26 -> x27, starting transfers between devices: 27.4 us -> 28.9 us  [swap(): return lax.ppermute(v, AXES, pairs)]
  transfers between devices with their start and end apart: 26 -> 27, of which waited for: 9 -> 10; matrix products, arithmetic and copies ran while one was open for 3% -> 5% of each run, Pallas kernels for 26% -> 27%
where the time goes in v6:
time: 136 us
  Pallas kernels  69.1 us (51%)
  starting transfers between devices  28.9 us (21%)
  waiting for transfers between devices  26.6 us (20%)
  local copies, waits for them, and re-layouts  7.82 us (6%)
  other arithmetic  2.4 us (2%)
    ppermute x27, starting transfers between devices, swap(): return lax.ppermute(v, AXES, pairs)  28.9 us
    pallas_call x1, Pallas kernels, mlp_both_ways(): pl.pallas_call(functools.partial(mlp_kernel, length, 512), grid=(images /...  27.4 us
    ppermute x27, waiting for transfers between devices, swap(): return lax.ppermute(v, AXES, pairs)  26.6 us
    pallas_call x2, Pallas kernels, attention_backward(): pl.pallas_call(functools.partial(back_kernel, length, first, last), grid=...  24.1 us
    pallas_call x1, Pallas kernels, forward_attention(): pl.pallas_call(functools.partial(attend_kernel, length), grid=(images //...  9.88 us
    unnamed x46, local copies, waits for them, and re-layouts  5.4 us
    pallas_call x1, Pallas kernels, unpack(): pl.pallas_call(unpack_kernel, grid=(1,), in_specs=[SCALARS, *whole_like((...  3.6 us
  transfers between devices with their start and end apart: 27, of which 10 were waited for; matrix products, arithmetic and copies ran while one was open for 5% of the time, Pallas kernels for 27%

profile of v6, /device:TPU:0, one launch (start us, length us, event | category | flops | bytes accessed | tf_op | source)
XLA Modules:
  0.0 135.9 jit_solution(18437286021632267354)
XLA Ops:
  0.7 0.7 pad_add_fusion.index
  1.3 1.9 %pack_first.1.packed = bf16[104,1152]{1,0:T(8,128)(2,1)} custom-call(s32[4]{0:T(128)} %pad_add_fusion.index, bf16[192]{0:T(256)(128)(2,1)} %refs_0_.1, bf16[192]{0:T(256)(128)(2,1)} %refs_1_.1, bf16[192]{0:T(256)(128)(2,1)} %refs_2_.1, bf16[192]{0:T(256)(128)(2,1)} %refs_3_.1, bf16[192]{0:T(256)(128)(2,1)} %refs_4_.1, bf16[192]{0:T(256)(128)(2,1)} %refs_5_.1, ...), custom_call_target="tpu_custom_call" | custom-call | flops 1000 | bytes 1 | tf_op jit(solution)/shard_map/pack_first/pallas_call | solution.py:461
  3.2 2.9 %collective-permute-start = (bf16[104,1152]{1,0:T(8,128)(2,1)}, bf16[104,1152]{1,0:T(8,128)(2,1)S(1)}, u32[]{:S(2)}, u32[]{:S(2)}) collective-permute-start(bf16[104,1152]{1,0:T(8,128)(2,1)} %pack_first.1.packed), channel_id=1, source_target_pairs={{0,1},{1,0},{2,3},{3,2},{4,5},{5,4},{6,7},{7,6},{8,9},{9,8},{10,11... | collective-permute-start | bytes 718856 | tf_op jit(solution)/shard_map/ppermute | solution.py:634
  6.1 2.2 %pack_rest.1 = (bf16[96,384]{1,0:T(8,128)(2,1)}, bf16[96,1536]{1,0:T(8,128)(2,1)}, bf16[384,384]{1,0:T(8,128)(2,1)}) custom-call(s32[4]{0:T(128)} %pad_add_fusion.index, bf16[192,384]{1,0:T(8,128)(2,1)} %out_own.1, bf16[192,1536]{1,0:T(8,128)(2,1)} %lift_own.1, bf16[768,384]{1,0:T(8,128)(2,1)} %drop_own.1), custom_call_target="tpu_custom_call" | custom-call | flops 1000 | bytes 1 | tf_op jit(solution)/shard_map/pack_rest/pallas_call | solution.py:474
  8.3 0.0 collective-permute-start.3
  8.3 2.0 %collective-permute-start.4 = (bf16[384,384]{1,0:T(8,128)(2,1)}, bf16[384,384]{1,0:T(8,128)(2,1)S(1)}, u32[]{:S(2)}, u32[]{:S(2)}) collective-permute-start(bf16[384,384]{1,0:T(8,128)(2,1)} %get-tuple-element.91), channel_id=1, source_target_pairs={{0,1},{1,0},{2,3},{3,2},{4,5},{5,4},{6,7},{7,6},{8,9},{9,8},{10,11... | collective-permute-start | bytes 884744 | tf_op jit(solution)/shard_map/ppermute | solution.py:634
  10.4 2.6 %collective-permute-done.near = bf16[104,1152]{1,0:T(8,128)(2,1)S(1)} collective-permute-done((bf16[104,1152]{1,0:T(8,128)(2,1)}, bf16[104,1152]{1,0:T(8,128)(2,1)S(1)}, u32[]{:S(2)}, u32[]{:S(2)}) %collective-permute-start) | collective-permute-done | bytes 239648 | tf_op jit(solution)/shard_map/ppermute | solution.py:634
  13.0 2.1 %collective-permute-start.2 = (bf16[96,384]{1,0:T(8,128)(2,1)}, bf16[96,384]{1,0:T(8,128)(2,1)S(1)}, u32[]{:S(2)}, u32[]{:S(2)}) collective-permute-start(bf16[96,384]{1,0:T(8,128)(2,1)} %get-tuple-element.89), channel_id=1, source_target_pairs={{0,1},{1,0},{2,3},{3,2},{4,5},{5,4},{6,7},{7,6},{8,9},{9,8},{10,11... | collective-permute-start | bytes 221192 | tf_op jit(solution)/shard_map/ppermute | solution.py:634
  15.1 1.2 copy.35.tok_ref
  16.3 0.7 copy-done.16
  17.0 9.9 %attend.1 = (bf16[8,208,384]{2,1,0:T(8,128)(2,1)}, bf16[8,208,1152]{2,1,0:T(8,128)(2,1)}, bf16[8,208,384]{2,1,0:T(8,128)(2,1)}, bf16[384,1152]{1,0:T(8,128)(2,1)}, f32[12,384]{1,0:T(8,128)}) custom-call(s32[4]{0:T(128)} %pad_add_fusion.index, bf16[8,197,384]{2,1,0:T(8,128)(2,1)} %copy.35.tok_ref, bf16[104,1152]{1,0:T(8,128)(2,1)} %pack_first.1.packed, ...), custom_call_target="tpu_custom_call" | custom-call | flops 1000 | bytes 1 | tf_op jit(solution)/shard_map/attend/pallas_call | solution.py:490
  26.8 0.0 copy-start.20
  26.9 0.0 copy-start.11
  26.9 0.0 copy-start.12
  26.9 0.3 collective-permute-start.6
  27.2 0.3 collective-permute-start.7
  27.5 0.2 collective-permute-start.5
  27.7 1.2 copy.33.cot_ref
  28.9 0.2 collective-permute-done.5.out_far
  29.1 0.0 copy-start.14
  29.1 0.6 copy-done.21
  29.7 0.1 copy-done.13
  29.8 0.1 copy-done.14
  29.9 27.4 %mlp.1 = (bf16[8,197,384]{2,1,0:T(8,128)(2,1)}, f32[8,208,384]{2,1,0:T(8,128)}, bf16[8,208,384]{2,1,0:T(8,128)(2,1)}, bf16[2,2,448,384]{3,2,1,0:T(8,128)(2,1)}, bf16[2,2,448,384]{3,2,1,0:T(8,128)(2,1)}) custom-call(s32[4]{0:T(128)} %pad_add_fusion.index, bf16[8,197,384]{2,1,0:T(8,128)(2,1)} %copy.35.tok_ref, bf16[8,197,384]{2,1,0:T(8,128)(2,1)} %copy.33.cot_ref, ...), custom_call_target="tpu_custom_call" | custom-call | flops 1000 | bytes 1 | tf_op jit(solution)/shard_map/mlp/pallas_call | solution.py:520
  57.3 0.3 collective-permute-start.8
  57.6 7.0 %back.2 = (bf16[8,197,384]{2,1,0:T(8,128)(2,1)}, f32[384,1152]{1,0:T(8,128)}, f32[8,1152]{1,0:T(8,128)}, f32[2,384]{1,0:T(2,128)}) custom-call(s32[4]{0:T(128)} %pad_add_fusion.index, bf16[8,197,384]{2,1,0:T(8,128)(2,1)} %copy.35.tok_ref, bf16[8,208,1152]{2,1,0:T(8,128)(2,1)} %get-tuple-element.83.proj_ref, ...), custom_call_target="tpu_custom_call" | custom-call | flops 1000 | bytes 1 | tf_op jit(solution)/shard_map/back/pallas_call | solution.py:578
  64.7 0.1 add_bitcast_fusion
  64.8 1.2 collective-permute-start.9
  66.0 1.5 %collective-permute-start.10 = (bf16[448,384]{1,0:T(8,128)(2,1)S(1)}, bf16[448,384]{1,0:T(8,128)(2,1)}, u32[]{:S(2)}, u32[]{:S(2)}) collective-permute-start(bf16[448,384]{1,0:T(8,128)(2,1)S(1)} %get-tuple-element.116), channel_id=1, source_target_pairs={{0,4},{1,5},{2,6},{3,7},{4,0},{5,1},{6,2},{7,3},{8,12},{9,13},{10,... | collective-permute-start | bytes 1032200 | tf_op jit(solution)/shard_map/ppermute | solution.py:634
  67.5 0.8 collective-permute-start.11
  68.3 17.1 %back.3 = (bf16[8,197,384]{2,1,0:T(8,128)(2,1)}, bf16[2,2,152,384]{3,2,1,0:T(8,128)(2,1)}, bf16[2,2,152,384]{3,2,1,0:T(8,128)(2,1)}) custom-call(s32[4]{0:T(128)} %pad_add_fusion.index, bf16[8,197,384]{2,1,0:T(8,128)(2,1)} %copy.35.tok_ref, bf16[8,208,1152]{2,1,0:T(8,128)(2,1)} %get-tuple-element.83.proj_ref, ...), custom_call_target="tpu_custom_call", output_to_operand_aliasing={{0}: (11, {})} | custom-call | flops 1000 | bytes 1 | tf_op jit(solution)/shard_map/back/pallas_call | solution.py:578
  85.5 0.1 collective-permute-start.12
  85.6 0.0 copy-start.6
  85.6 1.3 fusion.1
  86.9 0.1 constant_dynamic-slice_fusion
  87.0 1.6 %collective-permute-start.16 = (bf16[224,384]{1,0:T(8,128)(2,1)S(1)}, bf16[224,384]{1,0:T(8,128)(2,1)S(1)}, u32[]{:S(2)}, u32[]{:S(2)}) collective-permute-start(bf16[224,384]{1,0:T(8,128)(2,1)S(1)} %get-tuple-element.155), channel_id=1, source_target_pairs={{0,8},{1,9},{2,10},{3,11},{4,12},{5,13},{6,14},{7,15},{8,0},{9,1},... | collective-permute-start | bytes 516104 | tf_op jit(solution)/shard_map/ppermute | solution.py:634
  88.6 0.1 add_bitcast_fusion.3
  88.7 2.2 %collective-permute-start.15 = (bf16[152,384]{1,0:T(8,128)(2,1)S(1)}, bf16[152,384]{1,0:T(8,128)(2,1)S(1)}, u32[]{:S(2)}, u32[]{:S(2)}) collective-permute-start(bf16[152,384]{1,0:T(8,128)(2,1)S(1)} %get-tuple-element.152), channel_id=1, source_target_pairs={{0,5},{1,4},{2,7},{3,6},{4,1},{5,0},{6,3},{7,2},{8,13},{9,12},{10,... | collective-permute-start | bytes 350216 | tf_op jit(solution)/shard_map/ppermute | solution.py:634
  90.9 0.5 collective-permute-start.14
  91.4 0.8 collective-permute-start.13
  92.2 1.6 %collective-permute-done.16 = bf16[224,384]{1,0:T(8,128)(2,1)S(1)} collective-permute-done((bf16[224,384]{1,0:T(8,128)(2,1)S(1)}, bf16[224,384]{1,0:T(8,128)(2,1)S(1)}, u32[]{:S(2)}, u32[]{:S(2)}) %collective-permute-start.16) | collective-permute-done | bytes 172064 | tf_op jit(solution)/shard_map/ppermute | solution.py:634
  93.9 2.7 %collective-permute-start.18 = (bf16[224,384]{1,0:T(8,128)(2,1)S(1)}, bf16[224,384]{1,0:T(8,128)(2,1)S(1)}, u32[]{:S(2)}, u32[]{:S(2)}) collective-permute-start(bf16[224,384]{1,0:T(8,128)(2,1)S(1)} %add.105), channel_id=1, source_target_pairs={{0,16},{1,17},{2,18},{3,19},{4,20},{5,21},{6,22},{7,23},{8,24},{9,... | collective-permute-start | bytes 516104 | tf_op jit(solution)/shard_map/ppermute | solution.py:634
  96.5 0.9 collective-permute-done.14
  97.4 0.1 collective-permute-done.13
  97.5 0.1 fusion.3
  97.6 6.9 %collective-permute-done.18 = bf16[224,384]{1,0:T(8,128)(2,1)S(1)} collective-permute-done((bf16[224,384]{1,0:T(8,128)(2,1)S(1)}, bf16[224,384]{1,0:T(8,128)(2,1)S(1)}, u32[]{:S(2)}, u32[]{:S(2)}) %collective-permute-start.18) | collective-permute-done | bytes 172064 | tf_op jit(solution)/shard_map/ppermute | solution.py:634
  104.5 0.7 collective-permute-start.20
  105.3 1.3 collective-permute-start.17
  106.6 5.7 %collective-permute-done.17 = bf16[152,384]{1,0:T(8,128)(2,1)S(1)} collective-permute-done((bf16[152,384]{1,0:T(8,128)(2,1)S(1)}, bf16[152,384]{1,0:T(8,128)(2,1)S(1)}, u32[]{:S(2)}, u32[]{:S(2)}) %collective-permute-start.17) | collective-permute-done | bytes 116768 | tf_op jit(solution)/shard_map/ppermute | solution.py:634
  112.4 1.6 %collective-permute-start.21 = (bf16[448,384]{1,0:T(8,128)(2,1)S(1)}, bf16[448,384]{1,0:T(8,128)(2,1)S(1)}, u32[]{:S(2)}, u32[]{:S(2)}) collective-permute-start(bf16[448,384]{1,0:T(8,128)(2,1)S(1)} %pad_maximum_fusion.refs_0_), channel_id=1, source_target_pairs={{0,4},{1,5},{2,6},{3,7},{4,0},{5,1},{6,2},{7,3},{8,12},{9,13},{10,... | collective-permute-start | bytes 1032200 | tf_op jit(solution)/shard_map/ppermute | solution.py:634
  114.0 3.4 %collective-permute-start.19 = (bf16[152,384]{1,0:T(8,128)(2,1)S(1)}, bf16[152,384]{1,0:T(8,128)(2,1)S(1)}, u32[]{:S(2)}, u32[]{:S(2)}) collective-permute-start(bf16[152,384]{1,0:T(8,128)(2,1)S(1)} %add.110), channel_id=1, source_target_pairs={{0,16},{1,17},{2,18},{3,19},{4,20},{5,21},{6,22},{7,23},{8,24},{9,... | collective-permute-start | bytes 350216 | tf_op jit(solution)/shard_map/ppermute | solution.py:634
  117.4 1.2 copy.41
  118.6 1.2 copy.40
  119.8 2.7 %collective-permute-done.19 = bf16[152,384]{1,0:T(8,128)(2,1)S(1)} collective-permute-done((bf16[152,384]{1,0:T(8,128)(2,1)S(1)}, bf16[152,384]{1,0:T(8,128)(2,1)S(1)}, u32[]{:S(2)}, u32[]{:S(2)}) %collective-permute-start.19) | collective-permute-done | bytes 116768 | tf_op jit(solution)/shard_map/ppermute | solution.py:634
  122.5 0.1 collective-permute-start.23
  122.6 0.6 collective-permute-start.26
  123.2 0.1 collective-permute-start.25
  123.3 1.5 %collective-permute-start.24 = (bf16[152,384]{1,0:T(8,128)(2,1)S(1)}, bf16[152,384]{1,0:T(8,128)(2,1)S(1)}, u32[]{:S(2)}, u32[]{:S(2)}) collective-permute-start(bf16[152,384]{1,0:T(8,128)(2,1)S(1)} %add.111.refs_4_), channel_id=1, source_target_pairs={{0,4},{1,5},{2,6},{3,7},{4,0},{5,1},{6,2},{7,3},{8,12},{9,13},{10,... | collective-permute-start | bytes 350216 | tf_op jit(solution)/shard_map/ppermute | solution.py:634
  124.8 2.8 %collective-permute-done.26.refs_7_ = bf16[152,384]{1,0:T(8,128)(2,1)S(1)} collective-permute-done((bf16[152,384]{1,0:T(8,128)(2,1)S(1)}, bf16[152,384]{1,0:T(8,128)(2,1)S(1)}, u32[]{:S(2)}, u32[]{:S(2)}) %collective-permute-start.26) | collective-permute-done | bytes 116768 | tf_op jit(solution)/shard_map/ppermute | solution.py:634
  127.6 3.1 %collective-permute-done.24.refs_5_ = bf16[152,384]{1,0:T(8,128)(2,1)S(1)} collective-permute-done((bf16[152,384]{1,0:T(8,128)(2,1)S(1)}, bf16[152,384]{1,0:T(8,128)(2,1)S(1)}, u32[]{:S(2)}, u32[]{:S(2)}) %collective-permute-start.24) | collective-permute-done | bytes 116768 | tf_op jit(solution)/shard_map/ppermute | solution.py:634
  130.7 0.6 copy-done.19
  131.3 0.1 copy-done.9
  131.4 0.7 copy-done.10
  132.2 3.6 %unpack.1 = (f32[768,384]{1,0:T(8,128)}, f32[192,1536]{1,0:T(8,128)}, f32[192,384]{1,0:T(8,128)}, f32[192]{0:T(256)}, f32[192]{0:T(256)}, /*index=5*/f32[192]{0:...) custom-call(s32[4]{0:T(128)} %pad_add_fusion.index, ...), custom_call_target="tpu_custom_call" | custom-call | flops 1000 | bytes 1 | tf_op jit(solution)/shard_map/unpack/pallas_call | solution.py:605
  (56 shorter events, 0.3 us)
Async XLA Ops:
  0.6 14.4 %copy-start.4 = (bf16[8,197,384]{2,0,1:T(8,128)(2,1)S(1)}, bf16[8,197,384]{2,0,1:T(8,128)(2,1)}, u32[]{:S(2)}) copy-start(bf16[8,197,384]{2,0,1:T(8,128)(2,1)} %param.15) | copy-start | bytes 3631108
  3.2 9.8 %collective-permute-start = (bf16[104,1152]{1,0:T(8,128)(2,1)}, bf16[104,1152]{1,0:T(8,128)(2,1)S(1)}, u32[]{:S(2)}, u32[]{:S(2)}) collective-permute-start(bf16[104,1152]{1,0:T(8,128)(2,1)} %pack_first.1.packed), channel_id=1, source_target_pairs={{0,1},{1,0},{2,3},{3,2},{4,5},{5,4},{6,7},{7,6},{8,9},{9,8},{10,11... | collective-permute-start | bytes 718856 | tf_op jit(solution)/shard_map/ppermute | solution.py:634
  8.3 18.5 %collective-permute-start.3 = (bf16[96,1536]{1,0:T(8,128)(2,1)}, bf16[96,1536]{1,0:T(8,128)(2,1)S(1)}, u32[]{:S(2)}, u32[]{:S(2)}) collective-permute-start(bf16[96,1536]{1,0:T(8,128)(2,1)} %get-tuple-element.90), channel_id=1, source_target_pairs={{0,1},{1,0},{2,3},{3,2},{4,5},{5,4},{6,7},{7,6},{8,9},{9,8},{10,11... | collective-permute-start | bytes 884744 | tf_op jit(solution)/shard_map/ppermute | solution.py:634
  8.3 18.5 %collective-permute-start.4 = (bf16[384,384]{1,0:T(8,128)(2,1)}, bf16[384,384]{1,0:T(8,128)(2,1)S(1)}, u32[]{:S(2)}, u32[]{:S(2)}) collective-permute-start(bf16[384,384]{1,0:T(8,128)(2,1)} %get-tuple-element.91), channel_id=1, source_target_pairs={{0,1},{1,0},{2,3},{3,2},{4,5},{5,4},{6,7},{7,6},{8,9},{9,8},{10,11... | collective-permute-start | bytes 884744 | tf_op jit(solution)/shard_map/ppermute | solution.py:634
  13.0 3.3 %copy-start.15 = (bf16[104,1152]{1,0:T(8,128)(2,1)}, bf16[104,1152]{1,0:T(8,128)(2,1)S(1)}, u32[]{:S(2)}) copy-start(bf16[104,1152]{1,0:T(8,128)(2,1)S(1)} %collective-permute-done.near) | copy-start | bytes 718852
  13.0 3.3 %collective-permute-start.1 = (bf16[104,1152]{1,0:T(8,128)(2,1)S(1)}, bf16[104,1152]{1,0:T(8,128)(2,1)S(1)}, u32[]{:S(2)}, u32[]{:S(2)}) collective-permute-start(bf16[104,1152]{1,0:T(8,128)(2,1)S(1)} %collective-permute-done.near), channel_id=1, source_target_pairs={{0,2},{1,3},{2,0},{3,1},{4,6},{5,7},{6,4},{7,5},{8,10},{9,11},{10,... | collective-permute-start | bytes 718856 | tf_op jit(solution)/shard_map/ppermute | solution.py:634
  13.0 13.8 %collective-permute-start.2 = (bf16[96,384]{1,0:T(8,128)(2,1)}, bf16[96,384]{1,0:T(8,128)(2,1)S(1)}, u32[]{:S(2)}, u32[]{:S(2)}) collective-permute-start(bf16[96,384]{1,0:T(8,128)(2,1)} %get-tuple-element.89), channel_id=1, source_target_pairs={{0,1},{1,0},{2,3},{3,2},{4,5},{5,4},{6,7},{7,6},{8,9},{9,8},{10,11... | collective-permute-start | bytes 221192 | tf_op jit(solution)/shard_map/ppermute | solution.py:634
  16.3 11.5 %copy-start.5 = (bf16[8,197,384]{2,0,1:T(8,128)(2,1)S(1)}, bf16[8,197,384]{2,0,1:T(8,128)(2,1)}, u32[]{:S(2)}) copy-start(bf16[8,197,384]{2,0,1:T(8,128)(2,1)} %param.29) | copy-start | bytes 3631108
  16.3 0.7 copy-start.16
  26.8 2.3 %copy-start.20 = (bf16[96,384]{1,0:T(8,128)(2,1)}, bf16[96,384]{1,0:T(8,128)(2,1)S(1)}, u32[]{:S(2)}) copy-start(bf16[96,384]{1,0:T(8,128)(2,1)S(1)} %collective-permute-done.2.out_near) | copy-start | bytes 221188
  26.9 2.2 %copy-start.11 = (bf16[96,1536]{1,0:T(8,128)(2,1)}, bf16[96,1536]{1,0:T(8,128)(2,1)S(1)}, u32[]{:S(2)}) copy-start(bf16[96,1536]{1,0:T(8,128)(2,1)S(1)} %collective-permute-done.3.lift_near) | copy-start | bytes 884740
  26.9 2.2 %copy-start.12 = (bf16[384,384]{1,0:T(8,128)(2,1)}, bf16[384,384]{1,0:T(8,128)(2,1)S(1)}, u32[]{:S(2)}) copy-start(bf16[384,384]{1,0:T(8,128)(2,1)S(1)} %collective-permute-done.4.drop_near) | copy-start | bytes 884740
  26.9 2.2 %collective-permute-start.6 = (bf16[96,1536]{1,0:T(8,128)(2,1)S(1)}, bf16[96,1536]{1,0:T(8,128)(2,1)S(1)}, u32[]{:S(2)}, u32[]{:S(2)}) collective-permute-start(bf16[96,1536]{1,0:T(8,128)(2,1)S(1)} %collective-permute-done.3.lift_near), channel_id=1, source_target_pairs={{0,2},{1,3},{2,0},{3,1},{4,6},{5,7},{6,4},{7,5},{8,10},{9,11},{10,... | collective-permute-start | bytes 884744 | tf_op jit(solution)/shard_map/ppermute | solution.py:634
  27.2 1.9 %collective-permute-start.7 = (bf16[384,384]{1,0:T(8,128)(2,1)S(1)}, bf16[384,384]{1,0:T(8,128)(2,1)S(1)}, u32[]{:S(2)}, u32[]{:S(2)}) collective-permute-start(bf16[384,384]{1,0:T(8,128)(2,1)S(1)} %collective-permute-done.4.drop_near), channel_id=1, source_target_pairs={{0,2},{1,3},{2,0},{3,1},{4,6},{5,7},{6,4},{7,5},{8,10},{9,11},{10,... | collective-permute-start | bytes 884744 | tf_op jit(solution)/shard_map/ppermute | solution.py:634
  27.5 1.6 %collective-permute-start.5 = (bf16[96,384]{1,0:T(8,128)(2,1)S(1)}, bf16[96,384]{1,0:T(8,128)(2,1)S(1)}, u32[]{:S(2)}, u32[]{:S(2)}) collective-permute-start(bf16[96,384]{1,0:T(8,128)(2,1)S(1)} %collective-permute-done.2.out_near), channel_id=1, source_target_pairs={{0,2},{1,3},{2,0},{3,1},{4,6},{5,7},{6,4},{7,5},{8,10},{9,11},{10,... | collective-permute-start | bytes 221192 | tf_op jit(solution)/shard_map/ppermute | solution.py:634
  29.1 0.6 copy-start.21
  29.1 0.7 copy-start.13
  29.1 0.8 copy-start.14
  57.3 7.3 %collective-permute-start.8 = (bf16[2,2,448,384]{3,2,1,0:T(8,128)(2,1)}, bf16[2,2,448,384]{3,2,1,0:T(8,128)(2,1)S(1)}, u32[]{:S(2)}, u32[]{:S(2)}) collective-permute-start(bf16[2,2,448,384]{3,2,1,0:T(8,128)(2,1)} %get-tuple-element.103), channel_id=1, source_target_pairs={{0,2},{1,3},{2,0},{3,1},{4,6},{5,7},{6,4},{7,5},{8,10},{9,11},{10,... | collective-permute-start | bytes 4128776 | tf_op jit(solution)/shard_map/ppermute | solution.py:634
  57.6 7.0 %copy-start.1 = (bf16[2,2,448,384]{3,2,1,0:T(8,128)(2,1)S(1)}, bf16[2,2,448,384]{3,2,1,0:T(8,128)(2,1)}, u32[]{:S(2)}) copy-start(bf16[2,2,448,384]{3,2,1,0:T(8,128)(2,1)} %get-tuple-element.107) | copy-start | bytes 4128772
  64.8 20.7 %collective-permute-start.9 = (bf16[448,384]{1,0:T(8,128)(2,1)S(1)}, bf16[448,384]{1,0:T(8,128)(2,1)}, u32[]{:S(2)}, u32[]{:S(2)}) collective-permute-start(bf16[448,384]{1,0:T(8,128)(2,1)S(1)} %get-tuple-element.115), channel_id=1, source_target_pairs={{0,1},{1,0},{2,3},{3,2},{4,5},{5,4},{6,7},{7,6},{8,9},{9,8},{10,11... | collective-permute-start | bytes 1032200 | tf_op jit(solution)/shard_map/ppermute | solution.py:634
  66.0 19.4 %collective-permute-start.10 = (bf16[448,384]{1,0:T(8,128)(2,1)S(1)}, bf16[448,384]{1,0:T(8,128)(2,1)}, u32[]{:S(2)}, u32[]{:S(2)}) collective-permute-start(bf16[448,384]{1,0:T(8,128)(2,1)S(1)} %get-tuple-element.116), channel_id=1, source_target_pairs={{0,4},{1,5},{2,6},{3,7},{4,0},{5,1},{6,2},{7,3},{8,12},{9,13},{10,... | collective-permute-start | bytes 1032200 | tf_op jit(solution)/shard_map/ppermute | solution.py:634
  67.5 17.9 %collective-permute-start.11 = (bf16[448,384]{1,0:T(8,128)(2,1)S(1)}, bf16[448,384]{1,0:T(8,128)(2,1)}, u32[]{:S(2)}, u32[]{:S(2)}) collective-permute-start(bf16[448,384]{1,0:T(8,128)(2,1)S(1)} %get-tuple-element.117), channel_id=1, source_target_pairs={{0,5},{1,4},{2,7},{3,6},{4,1},{5,0},{6,3},{7,2},{8,13},{9,12},{10,... | collective-permute-start | bytes 1032200 | tf_op jit(solution)/shard_map/ppermute | solution.py:634
  85.5 3.1 %collective-permute-start.12 = (bf16[2,2,152,384]{3,2,1,0:T(8,128)(2,1)}, bf16[2,2,152,384]{3,2,1,0:T(8,128)(2,1)S(1)}, u32[]{:S(2)}, u32[]{:S(2)}) collective-permute-start(bf16[2,2,152,384]{3,2,1,0:T(8,128)(2,1)} %get-tuple-element.118), channel_id=1, source_target_pairs={{0,2},{1,3},{2,0},{3,1},{4,6},{5,7},{6,4},{7,5},{8,10},{9,11},{10,... | collective-permute-start | bytes 1400840 | tf_op jit(solution)/shard_map/ppermute | solution.py:634
  85.6 3.1 %copy-start.6 = (bf16[2,2,152,384]{3,2,1,0:T(8,128)(2,1)S(1)}, bf16[2,2,152,384]{3,2,1,0:T(8,128)(2,1)}, u32[]{:S(2)}) copy-start(bf16[2,2,152,384]{3,2,1,0:T(8,128)(2,1)} %get-tuple-element.113) | copy-start | bytes 1400836
  87.0 6.8 %collective-permute-start.16 = (bf16[224,384]{1,0:T(8,128)(2,1)S(1)}, bf16[224,384]{1,0:T(8,128)(2,1)S(1)}, u32[]{:S(2)}, u32[]{:S(2)}) collective-permute-start(bf16[224,384]{1,0:T(8,128)(2,1)S(1)} %get-tuple-element.155), channel_id=1, source_target_pairs={{0,8},{1,9},{2,10},{3,11},{4,12},{5,13},{6,14},{7,15},{8,0},{9,1},... | collective-permute-start | bytes 516104 | tf_op jit(solution)/shard_map/ppermute | solution.py:634
  88.7 7.8 %collective-permute-start.15 = (bf16[152,384]{1,0:T(8,128)(2,1)S(1)}, bf16[152,384]{1,0:T(8,128)(2,1)S(1)}, u32[]{:S(2)}, u32[]{:S(2)}) collective-permute-start(bf16[152,384]{1,0:T(8,128)(2,1)S(1)} %get-tuple-element.152), channel_id=1, source_target_pairs={{0,5},{1,4},{2,7},{3,6},{4,1},{5,0},{6,3},{7,2},{8,13},{9,12},{10,... | collective-permute-start | bytes 350216 | tf_op jit(solution)/shard_map/ppermute | solution.py:634
  90.9 6.6 %collective-permute-start.14 = (bf16[152,384]{1,0:T(8,128)(2,1)S(1)}, bf16[152,384]{1,0:T(8,128)(2,1)S(1)}, u32[]{:S(2)}, u32[]{:S(2)}) collective-permute-start(bf16[152,384]{1,0:T(8,128)(2,1)S(1)} %get-tuple-element.153), channel_id=1, source_target_pairs={{0,4},{1,5},{2,6},{3,7},{4,0},{5,1},{6,2},{7,3},{8,12},{9,13},{10,... | collective-permute-start | bytes 350216 | tf_op jit(solution)/shard_map/ppermute | solution.py:634
  91.4 26.0 %copy-start.3 = (bf16[8,197,384]{2,1,0:T(8,128)(2,1)S(1)}, bf16[8,197,384]{2,1,0:T(8,128)(2,1)}, u32[]{:S(2)}) copy-start(bf16[8,197,384]{2,1,0:T(8,128)(2,1)} %get-tuple-element.129) | copy-start | bytes 3631108
  91.4 6.1 %collective-permute-start.13 = (bf16[152,384]{1,0:T(8,128)(2,1)S(1)}, bf16[152,384]{1,0:T(8,128)(2,1)S(1)}, u32[]{:S(2)}, u32[]{:S(2)}) collective-permute-start(bf16[152,384]{1,0:T(8,128)(2,1)S(1)} %get-tuple-element.154), channel_id=1, source_target_pairs={{0,1},{1,0},{2,3},{3,2},{4,5},{5,4},{6,7},{7,6},{8,9},{9,8},{10,11... | collective-permute-start | bytes 350216 | tf_op jit(solution)/shard_map/ppermute | solution.py:634
  93.9 10.6 %collective-permute-start.18 = (bf16[224,384]{1,0:T(8,128)(2,1)S(1)}, bf16[224,384]{1,0:T(8,128)(2,1)S(1)}, u32[]{:S(2)}, u32[]{:S(2)}) collective-permute-start(bf16[224,384]{1,0:T(8,128)(2,1)S(1)} %add.105), channel_id=1, source_target_pairs={{0,16},{1,17},{2,18},{3,19},{4,20},{5,21},{6,22},{7,23},{8,24},{9,... | collective-permute-start | bytes 516104 | tf_op jit(solution)/shard_map/ppermute | solution.py:634
  104.5 7.8 %collective-permute-start.20 = (bf16[224,384]{1,0:T(8,128)(2,1)S(1)}, bf16[224,384]{1,0:T(8,128)(2,1)S(1)}, u32[]{:S(2)}, u32[]{:S(2)}) collective-permute-start(bf16[224,384]{1,0:T(8,128)(2,1)S(1)} %add.109), channel_id=1, source_target_pairs={{0,8},{1,9},{2,10},{3,11},{4,12},{5,13},{6,14},{7,15},{8,0},{9,1},... | collective-permute-start | bytes 516104 | tf_op jit(solution)/shard_map/ppermute | solution.py:634
  105.3 7.1 %collective-permute-start.17 = (bf16[152,384]{1,0:T(8,128)(2,1)S(1)}, bf16[152,384]{1,0:T(8,128)(2,1)S(1)}, u32[]{:S(2)}, u32[]{:S(2)}) collective-permute-start(bf16[152,384]{1,0:T(8,128)(2,1)S(1)} %fusion.3), channel_id=1, source_target_pairs={{0,8},{1,9},{2,10},{3,11},{4,12},{5,13},{6,14},{7,15},{8,0},{9,1},... | collective-permute-start | bytes 350216 | tf_op jit(solution)/shard_map/ppermute | solution.py:634
  112.4 7.3 %copy-start.2 = (bf16[448,384]{1,0:T(8,128)(2,1)}, bf16[448,384]{1,0:T(8,128)(2,1)S(1)}, u32[]{:S(2)}) copy-start(bf16[448,384]{1,0:T(8,128)(2,1)S(1)} %pad_maximum_fusion.refs_0_) | copy-start | bytes 1032196
  112.4 6.1 %copy-start = (bf16[8,197,384]{2,1,0:T(8,128)(2,1)S(1)}, bf16[8,197,384]{2,1,0:T(8,128)(2,1)}, u32[]{:S(2)}) copy-start(bf16[8,197,384]{2,1,0:T(8,128)(2,1)} %get-tuple-element.130) | copy-start | bytes 3631108
  112.4 10.1 %collective-permute-start.21 = (bf16[448,384]{1,0:T(8,128)(2,1)S(1)}, bf16[448,384]{1,0:T(8,128)(2,1)S(1)}, u32[]{:S(2)}, u32[]{:S(2)}) collective-permute-start(bf16[448,384]{1,0:T(8,128)(2,1)S(1)} %pad_maximum_fusion.refs_0_), channel_id=1, source_target_pairs={{0,4},{1,5},{2,6},{3,7},{4,0},{5,1},{6,2},{7,3},{8,12},{9,13},{10,... | collective-permute-start | bytes 1032200 | tf_op jit(solution)/shard_map/ppermute | solution.py:634
  114.0 8.4 %collective-permute-start.19 = (bf16[152,384]{1,0:T(8,128)(2,1)S(1)}, bf16[152,384]{1,0:T(8,128)(2,1)S(1)}, u32[]{:S(2)}, u32[]{:S(2)}) collective-permute-start(bf16[152,384]{1,0:T(8,128)(2,1)S(1)} %add.110), channel_id=1, source_target_pairs={{0,16},{1,17},{2,18},{3,19},{4,20},{5,21},{6,22},{7,23},{8,24},{9,... | collective-permute-start | bytes 350216 | tf_op jit(solution)/shard_map/ppermute | solution.py:634
  119.8 10.9 %collective-permute-start.22 = (bf16[448,384]{1,0:T(8,128)(2,1)S(1)}, bf16[448,384]{1,0:T(8,128)(2,1)S(1)}, u32[]{:S(2)}, u32[]{:S(2)}) collective-permute-start(bf16[448,384]{1,0:T(8,128)(2,1)S(1)} %pad_maximum_fusion.refs_0_), channel_id=1, source_target_pairs={{0,2},{1,3},{2,0},{3,1},{4,6},{5,7},{6,4},{7,5},{8,10},{9,11},{10,... | collective-permute-start | bytes 1032200 | tf_op jit(solution)/shard_map/ppermute | solution.py:634
  122.5 8.2 %copy-start.7 = (bf16[152,384]{1,0:T(8,128)(2,1)}, bf16[152,384]{1,0:T(8,128)(2,1)S(1)}, u32[]{:S(2)}) copy-start(bf16[152,384]{1,0:T(8,128)(2,1)S(1)} %add.111.refs_4_) | copy-start | bytes 350212
  122.5 8.2 %copy-start.8 = (bf16[448,384]{1,0:T(8,128)(2,1)}, bf16[448,384]{1,0:T(8,128)(2,1)S(1)}, u32[]{:S(2)}) copy-start(bf16[448,384]{1,0:T(8,128)(2,1)S(1)} %collective-permute-done.21.refs_1_) | copy-start | bytes 1032196
  122.5 8.1 %collective-permute-start.23 = (bf16[448,384]{1,0:T(8,128)(2,1)S(1)}, bf16[448,384]{1,0:T(8,128)(2,1)S(1)}, u32[]{:S(2)}, u32[]{:S(2)}) collective-permute-start(bf16[448,384]{1,0:T(8,128)(2,1)S(1)} %collective-permute-done.21.refs_1_), channel_id=1, source_target_pairs={{0,2},{1,3},{2,0},{3,1},{4,6},{5,7},{6,4},{7,5},{8,10},{9,11},{10,... | collective-permute-start | bytes 1032200 | tf_op jit(solution)/shard_map/ppermute | solution.py:634
  122.6 5.0 %collective-permute-start.26 = (bf16[152,384]{1,0:T(8,128)(2,1)S(1)}, bf16[152,384]{1,0:T(8,128)(2,1)S(1)}, u32[]{:S(2)}, u32[]{:S(2)}) collective-permute-start(bf16[152,384]{1,0:T(8,128)(2,1)S(1)} %add.111.refs_4_), channel_id=1, source_target_pairs={{0,6},{1,7},{2,4},{3,5},{4,2},{5,3},{6,0},{7,1},{8,14},{9,15},{10,... | collective-permute-start | bytes 350216 | tf_op jit(solution)/shard_map/ppermute | solution.py:634
  123.2 4.4 %collective-permute-start.25 = (bf16[152,384]{1,0:T(8,128)(2,1)S(1)}, bf16[152,384]{1,0:T(8,128)(2,1)S(1)}, u32[]{:S(2)}, u32[]{:S(2)}) collective-permute-start(bf16[152,384]{1,0:T(8,128)(2,1)S(1)} %add.111.refs_4_), channel_id=1, source_target_pairs={{0,2},{1,3},{2,0},{3,1},{4,6},{5,7},{6,4},{7,5},{8,10},{9,11},{10,... | collective-permute-start | bytes 350216 | tf_op jit(solution)/shard_map/ppermute | solution.py:634
  123.3 7.4 %collective-permute-start.24 = (bf16[152,384]{1,0:T(8,128)(2,1)S(1)}, bf16[152,384]{1,0:T(8,128)(2,1)S(1)}, u32[]{:S(2)}, u32[]{:S(2)}) collective-permute-start(bf16[152,384]{1,0:T(8,128)(2,1)S(1)} %add.111.refs_4_), channel_id=1, source_target_pairs={{0,4},{1,5},{2,6},{3,7},{4,0},{5,1},{6,2},{7,3},{8,12},{9,13},{10,... | collective-permute-start | bytes 350216 | tf_op jit(solution)/shard_map/ppermute | solution.py:634
  127.6 3.1 %copy-start.17 = (bf16[152,384]{1,0:T(8,128)(2,1)}, bf16[152,384]{1,0:T(8,128)(2,1)S(1)}, u32[]{:S(2)}) copy-start(bf16[152,384]{1,0:T(8,128)(2,1)S(1)} %collective-permute-done.26.refs_7_) | copy-start | bytes 350212
  127.6 3.1 %copy-start.18 = (bf16[152,384]{1,0:T(8,128)(2,1)}, bf16[152,384]{1,0:T(8,128)(2,1)S(1)}, u32[]{:S(2)}) copy-start(bf16[152,384]{1,0:T(8,128)(2,1)S(1)} %collective-permute-done.25.refs_6_) | copy-start | bytes 350212
  130.7 0.6 copy-start.19
  130.7 0.8 copy-start.9
  131.4 0.7 copy-start.10

commit v7 on v6

--- a/solution.py
+++ b/solution.py
@@ -77,14 +77,14 @@
     return jnp.where(first, v[:rows], v[rows:])
 
 
-def join_pieces(full, own, near, far, index):
+def join_pieces(full, own, near, far, index, first=0):
     block = own.shape[0]
     half = block // 2
     x, core = index[0], index[1]
     other = (1 - x) * block
     full[pl.ds(pl.multiple_of(x * block, 16), block), :] = own[...]
-    full[pl.ds(pl.multiple_of(other + core * half, 16), half), :] = near[0:half, :]
-    full[pl.ds(pl.multiple_of(other + (1 - core) * half, 16), half), :] = far[0:half, :]
+    full[pl.ds(pl.multiple_of(other + core * half, 16), half), :] = near[first : first + half, :]
+    full[pl.ds(pl.multiple_of(other + (1 - core) * half, 16), half), :] = far[first : first + half, :]
 
 
 def quarters(index, keep, send):
@@ -109,10 +109,12 @@
         packed[half + k : half + k + 1, width : 2 * width] = bias[:, k * width : (k + 1) * width]
 
 
-def pack_rest_kernel(index, *refs):
-    for weight, half_out in zip(refs[:3], refs[3:]):
-        half = half_out.shape[0]
-        half_out[...] = weight[pl.ds(pl.multiple_of(index[1] * half, 16), half), :]
+def pack_rest_kernel(index, out_own, lift_own, drop_own, lift_half, both_half):
+    tall, deep = lift_half.shape[0], drop_own.shape[0] // 2
+    rows_of = pl.ds(pl.multiple_of(index[1] * tall, 16), tall)
+    lift_half[...] = lift_own[rows_of, :]
+    both_half[0:deep, :] = drop_own[pl.ds(pl.multiple_of(index[1] * deep, 16), deep), :]
+    both_half[deep:, :] = out_own[rows_of, :]
 
 
 def join_vectors(vec_ref, own, other, index):
@@ -181,14 +183,12 @@
     mixed_ref,
     vec_ref,
     out_own,
-    out_near,
-    out_far,
     lift_own,
+    drop_own,
     lift_near,
     lift_far,
-    drop_own,
-    drop_near,
-    drop_far,
+    both_near,
+    both_far,
     out_ref,
     d_middle_ref,
     d_mixed_ref,
@@ -215,9 +215,10 @@
     def _():
         zero_tail(x_s, length)
         zero_tail(z_s, length)
-        join_pieces(w_out_ref, out_own, out_near, out_far, index)
+        deep = drop_own.shape[0] // 2
+        join_pieces(w_out_ref, out_own, both_near, both_far, index, deep)
         join_pieces(w_lift_ref, lift_own, lift_near, lift_far, index)
-        join_pieces(w_drop_ref, drop_own, drop_near, drop_far, index)
+        join_pieces(w_drop_ref, drop_own, both_near, both_far, index)
         for k in range(hidden_width // width):
             lift_bias_ref[:, k * width : (k + 1) * width] = vec_ref[8 + k : 9 + k, :]
         for acc in (a_drop, a_lift, a_out, a_vec, a_bias):
@@ -382,14 +383,9 @@
     return jnp.where(index[0] == 0, row[:, :half], row[:, half:])[0]
 
 
-def unpack_kernel(index, *refs):
-    unpack_outer(index, refs[0:4], refs[8:16], refs[21])
-    unpack_inner(index, refs[4:8], refs[16:21], refs[22])
-
-
-def unpack_outer(index, pieces, outs, full):
-    g_drop, g_lift, g_out, g_out_bias, g_gain, g_shift, g_drop_bias, g_lift_bias = outs
-    placed(full, index, pieces, by_z=True)
+def unpack_outer_kernel(index, *refs):
+    g_drop, g_lift, g_out, g_out_bias, g_gain, g_shift, g_drop_bias, g_lift_bias, full = refs[4:]
+    placed(full, index, refs[:4], by_z=True)
     width = g_out.shape[1]
     deep, tall, small = g_drop.shape[0] // 2, width // 4, width // 8
     blocks = g_lift.shape[1] // width
@@ -414,9 +410,9 @@
         g_lift_bias[k * width : (k + 1) * width] = row[0]
 
 
-def unpack_inner(index, pieces, outs, full):
-    g_qkv, g_query, g_value, g_gain, g_shift = outs
-    placed(full, index, pieces)
+def unpack_inner_kernel(index, *refs):
+    g_qkv, g_query, g_value, g_gain, g_shift, full = refs[4:]
+    placed(full, index, refs[:4])
     width = full.shape[3]
     small = width // 8
     for core in range(2):
@@ -471,12 +467,15 @@
 
 
 def pack_rest(index, weights):
+    out_weight, lift_weight, drop_weight = weights
+    tall, width = out_weight.shape[0] // 2, out_weight.shape[1]
+    shapes = [(tall, lift_weight.shape[1]), (drop_weight.shape[0] // 2 + tall, width)]
     return pl.pallas_call(
         pack_rest_kernel,
         grid=(1,),
         in_specs=[SCALARS, *whole_like(weights)],
-        out_specs=[whole(w.shape[0] // 2, w.shape[1]) for w in weights],
-        out_shape=[shape_of(BF16, w.shape[0] // 2, w.shape[1]) for w in weights],
+        out_specs=[whole(*d) for d in shapes],
+        out_shape=[shape_of(BF16, *d) for d in shapes],
         compiler_params=PARAMS,
         cost_estimate=cost(1),
         name="pack_rest",
@@ -601,21 +600,18 @@
     )(index, tokens, projected, normed, d_mixed, d_middle, w_qkv, vectors, *earlier)
 
 
-def unpack(index, outer, inner, shapes):
+def unpack(kernel, name, index, pieces, shapes):
     return pl.pallas_call(
-        unpack_kernel,
+        kernel,
         grid=(1,),
-        in_specs=[SCALARS, *whole_like((*outer, *inner))],
+        in_specs=[SCALARS, *whole_like(pieces)],
         out_specs=[whole(*d) for d in shapes],
         out_shape=[shape_of(F32, *d) for d in shapes],
-        scratch_shapes=[
-            pltpu.VMEM((2, 2) + outer[0].shape, F32),
-            pltpu.VMEM((2, 2) + inner[0].shape, F32),
-        ],
+        scratch_shapes=[pltpu.VMEM((2, 2) + pieces[0].shape, F32)],
         compiler_params=PARAMS,
         cost_estimate=cost(1),
-        name="unpack",
-    )(index, *outer, *inner)
+        name=name,
+    )(index, *pieces)
 
 
 AXES = ("rep", "fsdp")
@@ -755,11 +751,12 @@
     )
     if swaps:
         mixed, nears = after(mixed, nears)
-        outer = [
-            piece for w, near in zip(rest, nears) for piece in (w, near, plan.over_core(near))
-        ]
+        pieces = [piece for near in nears for piece in (near, plan.over_core(near))]
     else:
-        outer = [piece for w in rest for piece in plan.gather_weight(w)]
+        (out_own, *outs), (lift_own, *lifts), (drop_own, *drops) = map(plan.gather_weight, rest)
+        rest = (out_own, lift_own, drop_own)
+        pieces = [*lifts, *(jnp.concatenate(both) for both in zip(drops, outs))]
+    outer = (*rest, *pieces)
     output, d_middle, d_mixed, keep_a, send_a = mlp_both_ways(
         index, tokens, cotangent, mixed, vectors, ff, outer
     )
@@ -807,28 +804,23 @@
         across_a = behind(across_a, sum_c)
         pieces_c = (sum_c, plan.over_y(sum_c), plan.over_core(sum_c), plan.over_y_and_core(sum_c))
         pieces_a = (sum_a, across_a, beside_a, plan.over_core(across_a))
-        (
-            g_drop,
-            g_lift,
-            g_out,
-            g_out_bias,
-            g_gain_two,
-            g_shift_two,
-            g_drop_bias,
-            g_lift_bias,
-            g_qkv,
-            g_query,
-            g_value,
-            g_gain_one,
-            g_shift_one,
-        ) = unpack(
+        outer_grads = unpack(
+            unpack_outer_kernel,
+            "unpack_outer",
             index,
             pieces_a,
+            [(ff // 2, width), (half, ff), (half, width)] + [(half,)] * 4 + [(ff // 2,)],
+        )
+        g_drop, g_lift, g_out, g_out_bias, g_gain_two, g_shift_two, g_drop_bias, g_lift_bias = (
+            outer_grads
+        )
+        pieces_c = behind(pieces_c, g_drop)
+        g_qkv, g_query, g_value, g_gain_one, g_shift_one = unpack(
+            unpack_inner_kernel,
+            "unpack_inner",
+            index,
             pieces_c,
-            [(ff // 2, width), (half, ff), (half, width)]
-            + [(half,)] * 4
-            + [(ff // 2,), (half, 3 * width)]
-            + [(half,)] * 4,
+            [(half, 3 * width)] + [(half,)] * 4,
         )
     else:
         input_grad, *sums = backward(d_mixed, d_middle, 0, images - 2)

time: 136 us -> 133 us (0.978)
  waiting for transfers between devices: 26.6 us -> 23.6 us
  starting transfers between devices: 28.9 us -> 27 us
  Pallas kernels: 69.1 us -> 70.8 us
    ppermute x27 -> x25, waiting for transfers between devices: 26.6 us -> 23.6 us  [swap(): return lax.ppermute(v, AXES, pairs)]
    ppermute x27 -> x25, starting transfers between devices: 28.9 us -> 27 us  [swap(): return lax.ppermute(v, AXES, pairs)]
    pallas_call x1 -> x2, Pallas kernels: 3.6 us -> 5.19 us  [unpack(): pl.pallas_call(kernel, grid=(1,), in_specs=[SCALARS, *whole_like(pieces)]...]
    unnamed x46 -> x42, local copies, waits for them, and re-layouts: 5.4 us -> 6.06 us
  transfers between devices with their start and end apart: 27 -> 25, of which waited for: 10 -> 11; matrix products, arithmetic and copies ran while one was open for 5% -> 5% of each run, Pallas kernels for 27% -> 30%
where the time goes in v7:
time: 133 us
  Pallas kernels  70.8 us (53%)
  starting transfers between devices  27 us (20%)
  waiting for transfers between devices  23.6 us (18%)
  local copies, waits for them, and re-layouts  8.47 us (6%)
  other arithmetic  2.35 us (2%)
    pallas_call x1, Pallas kernels, mlp_both_ways(): pl.pallas_call(functools.partial(mlp_kernel, length, 512), grid=(images /...  27.5 us
    ppermute x25, starting transfers between devices, swap(): return lax.ppermute(v, AXES, pairs)  27 us
    pallas_call x2, Pallas kernels, attention_backward(): pl.pallas_call(functools.partial(back_kernel, length, first, last), grid=...  24.1 us
    ppermute x25, waiting for transfers between devices, swap(): return lax.ppermute(v, AXES, pairs)  23.6 us
    pallas_call x1, Pallas kernels, forward_attention(): pl.pallas_call(functools.partial(attend_kernel, length), grid=(images //...  9.9 us
    unnamed x42, local copies, waits for them, and re-layouts  6.06 us
    pallas_call x2, Pallas kernels, unpack(): pl.pallas_call(kernel, grid=(1,), in_specs=[SCALARS, *whole_like(pieces)]...  5.19 us
  transfers between devices with their start and end apart: 25, of which 11 were waited for; matrix products, arithmetic and copies ran while one was open for 5% of the time, Pallas kernels for 30%

profile of v7, /device:TPU:0, one launch (start us, length us, event | category | flops | bytes accessed | tf_op | source)
XLA Modules:
  0.0 133.1 jit_solution(3838977718133541426)
XLA Ops:
  0.7 0.6 pad_add_fusion.index
  1.3 1.9 %pack_first.1.packed = bf16[104,1152]{1,0:T(8,128)(2,1)} custom-call(s32[4]{0:T(128)} %pad_add_fusion.index, bf16[192]{0:T(256)(128)(2,1)} %refs_0_.1, bf16[192]{0:T(256)(128)(2,1)} %refs_1_.1, bf16[192]{0:T(256)(128)(2,1)} %refs_2_.1, bf16[192]{0:T(256)(128)(2,1)} %refs_3_.1, bf16[192]{0:T(256)(128)(2,1)} %refs_4_.1, bf16[192]{0:T(256)(128)(2,1)} %refs_5_.1, ...), custom_call_target="tpu_custom_call" | custom-call | flops 1000 | bytes 1 | tf_op jit(solution)/shard_map/pack_first/pallas_call | solution.py:457
  3.2 2.9 %collective-permute-start = (bf16[104,1152]{1,0:T(8,128)(2,1)}, bf16[104,1152]{1,0:T(8,128)(2,1)S(1)}, u32[]{:S(2)}, u32[]{:S(2)}) collective-permute-start(bf16[104,1152]{1,0:T(8,128)(2,1)} %pack_first.1.packed), channel_id=1, source_target_pairs={{0,1},{1,0},{2,3},{3,2},{4,5},{5,4},{6,7},{7,6},{8,9},{9,8},{10,11... | collective-permute-start | bytes 718856 | tf_op jit(solution)/shard_map/ppermute | solution.py:630
  6.1 2.2 %pack_rest.1 = (bf16[96,1536]{1,0:T(8,128)(2,1)}, bf16[480,384]{1,0:T(8,128)(2,1)}) custom-call(s32[4]{0:T(128)} %pad_add_fusion.index, bf16[192,384]{1,0:T(8,128)(2,1)} %out_own.2, bf16[192,1536]{1,0:T(8,128)(2,1)} %lift_own.2, bf16[768,384]{1,0:T(8,128)(2,1)} %drop_own.2), custom_call_target="tpu_custom_call" | custom-call | flops 1000 | bytes 1 | tf_op jit(solution)/shard_map/pack_rest/pallas_call | solution.py:473
  8.3 0.0 collective-permute-start.3
  8.3 2.0 %collective-permute-start.2 = (bf16[96,1536]{1,0:T(8,128)(2,1)}, bf16[96,1536]{1,0:T(8,128)(2,1)S(1)}, u32[]{:S(2)}, u32[]{:S(2)}) collective-permute-start(bf16[96,1536]{1,0:T(8,128)(2,1)} %get-tuple-element.91), channel_id=1, source_target_pairs={{0,1},{1,0},{2,3},{3,2},{4,5},{5,4},{6,7},{7,6},{8,9},{9,8},{10,11... | collective-permute-start | bytes 884744 | tf_op jit(solution)/shard_map/ppermute | solution.py:630
  10.3 2.6 %collective-permute-done.near = bf16[104,1152]{1,0:T(8,128)(2,1)S(1)} collective-permute-done((bf16[104,1152]{1,0:T(8,128)(2,1)}, bf16[104,1152]{1,0:T(8,128)(2,1)S(1)}, u32[]{:S(2)}, u32[]{:S(2)}) %collective-permute-start) | collective-permute-done | bytes 239648 | tf_op jit(solution)/shard_map/ppermute | solution.py:630
  13.0 0.0 collective-permute-start.1
  13.0 1.2 copy.35.tok_ref
  14.2 0.3 collective-permute-done.1.far
  14.5 0.7 copy-done.16
  15.1 9.9 %attend.1 = (bf16[8,208,384]{2,1,0:T(8,128)(2,1)}, bf16[8,208,1152]{2,1,0:T(8,128)(2,1)}, bf16[8,208,384]{2,1,0:T(8,128)(2,1)}, bf16[384,1152]{1,0:T(8,128)(2,1)}, f32[12,384]{1,0:T(8,128)}) custom-call(s32[4]{0:T(128)} %pad_add_fusion.index, bf16[8,197,384]{2,1,0:T(8,128)(2,1)} %copy.35.tok_ref, bf16[104,1152]{1,0:T(8,128)(2,1)} %pack_first.1.packed, ...), custom_call_target="tpu_custom_call" | custom-call | flops 1000 | bytes 1 | tf_op jit(solution)/shard_map/attend/pallas_call | solution.py:489
  25.0 1.3 collective-permute-done.2.lift_near
  26.3 0.0 collective-permute-done.3.both_near
  26.3 0.1 collective-permute-start.5
  26.4 0.5 collective-permute-start.4
  26.9 1.2 copy.33.cot_ref
  28.1 0.4 collective-permute-done.4.lift_far
  28.5 0.0 collective-permute-done.5.both_far
  28.5 0.7 copy-done.14
  29.2 0.1 copy-done.9
  29.4 27.5 %mlp.1 = (bf16[8,197,384]{2,1,0:T(8,128)(2,1)}, f32[8,208,384]{2,1,0:T(8,128)}, bf16[8,208,384]{2,1,0:T(8,128)(2,1)}, bf16[2,2,448,384]{3,2,1,0:T(8,128)(2,1)}, bf16[2,2,448,384]{3,2,1,0:T(8,128)(2,1)}) custom-call(s32[4]{0:T(128)} %pad_add_fusion.index, bf16[8,197,384]{2,1,0:T(8,128)(2,1)} %copy.35.tok_ref, bf16[8,197,384]{2,1,0:T(8,128)(2,1)} %copy.33.cot_ref, ...), custom_call_target="tpu_custom_call" | custom-call | flops 1000 | bytes 1 | tf_op jit(solution)/shard_map/mlp/pallas_call | solution.py:519
  56.9 0.2 collective-permute-start.6
  57.1 7.0 %back.2 = (bf16[8,197,384]{2,1,0:T(8,128)(2,1)}, f32[384,1152]{1,0:T(8,128)}, f32[8,1152]{1,0:T(8,128)}, f32[2,384]{1,0:T(2,128)}) custom-call(s32[4]{0:T(128)} %pad_add_fusion.index, bf16[8,197,384]{2,1,0:T(8,128)(2,1)} %copy.35.tok_ref, bf16[8,208,1152]{2,1,0:T(8,128)(2,1)} %get-tuple-element.85.proj_ref, ...), custom_call_target="tpu_custom_call" | custom-call | flops 1000 | bytes 1 | tf_op jit(solution)/shard_map/back/pallas_call | solution.py:577
  64.1 0.1 add_bitcast_fusion
  64.2 1.8 %collective-permute-start.7 = (bf16[448,384]{1,0:T(8,128)(2,1)S(1)}, bf16[448,384]{1,0:T(8,128)(2,1)}, u32[]{:S(2)}, u32[]{:S(2)}) collective-permute-start(bf16[448,384]{1,0:T(8,128)(2,1)S(1)} %get-tuple-element.115), channel_id=1, source_target_pairs={{0,1},{1,0},{2,3},{3,2},{4,5},{5,4},{6,7},{7,6},{8,9},{9,8},{10,11... | collective-permute-start | bytes 1032200 | tf_op jit(solution)/shard_map/ppermute | solution.py:630
  66.0 1.5 %collective-permute-start.8 = (bf16[448,384]{1,0:T(8,128)(2,1)S(1)}, bf16[448,384]{1,0:T(8,128)(2,1)}, u32[]{:S(2)}, u32[]{:S(2)}) collective-permute-start(bf16[448,384]{1,0:T(8,128)(2,1)S(1)} %get-tuple-element.116), channel_id=1, source_target_pairs={{0,4},{1,5},{2,6},{3,7},{4,0},{5,1},{6,2},{7,3},{8,12},{9,13},{10,... | collective-permute-start | bytes 1032200 | tf_op jit(solution)/shard_map/ppermute | solution.py:630
  67.6 0.2 collective-permute-start.9
  67.8 17.1 %back.3 = (bf16[8,197,384]{2,1,0:T(8,128)(2,1)}, bf16[2,2,152,384]{3,2,1,0:T(8,128)(2,1)}, bf16[2,2,152,384]{3,2,1,0:T(8,128)(2,1)}) custom-call(s32[4]{0:T(128)} %pad_add_fusion.index, bf16[8,197,384]{2,1,0:T(8,128)(2,1)} %copy.35.tok_ref, bf16[8,208,1152]{2,1,0:T(8,128)(2,1)} %get-tuple-element.85.proj_ref, ...), custom_call_target="tpu_custom_call", output_to_operand_aliasing={{0}: (11, {})} | custom-call | flops 1000 | bytes 1 | tf_op jit(solution)/shard_map/back/pallas_call | solution.py:577
  84.9 0.0 collective-permute-done.7
  84.9 0.1 collective-permute-start.10
  85.0 0.0 copy-start.6
  85.0 1.3 fusion.1
  86.4 0.1 constant_dynamic-slice_fusion
  86.4 1.9 %collective-permute-start.14 = (bf16[224,384]{1,0:T(8,128)(2,1)S(1)}, bf16[224,384]{1,0:T(8,128)(2,1)S(1)}, u32[]{:S(2)}, u32[]{:S(2)}) collective-permute-start(bf16[224,384]{1,0:T(8,128)(2,1)S(1)} %get-tuple-element.159), channel_id=1, source_target_pairs={{0,8},{1,9},{2,10},{3,11},{4,12},{5,13},{6,14},{7,15},{8,0},{9,1},... | collective-permute-start | bytes 516104 | tf_op jit(solution)/shard_map/ppermute | solution.py:630
  88.3 0.1 add_bitcast_fusion.3
  88.4 2.5 %collective-permute-start.13 = (bf16[152,384]{1,0:T(8,128)(2,1)S(1)}, bf16[152,384]{1,0:T(8,128)(2,1)S(1)}, u32[]{:S(2)}, u32[]{:S(2)}) collective-permute-start(bf16[152,384]{1,0:T(8,128)(2,1)S(1)} %get-tuple-element.156), channel_id=1, source_target_pairs={{0,5},{1,4},{2,7},{3,6},{4,1},{5,0},{6,3},{7,2},{8,13},{9,12},{10,... | collective-permute-start | bytes 350216 | tf_op jit(solution)/shard_map/ppermute | solution.py:630
  90.9 0.5 collective-permute-start.12
  91.4 0.5 collective-permute-start.11
  91.9 1.4 %collective-permute-done.14 = bf16[224,384]{1,0:T(8,128)(2,1)S(1)} collective-permute-done((bf16[224,384]{1,0:T(8,128)(2,1)S(1)}, bf16[224,384]{1,0:T(8,128)(2,1)S(1)}, u32[]{:S(2)}, u32[]{:S(2)}) %collective-permute-start.14) | collective-permute-done | bytes 172064 | tf_op jit(solution)/shard_map/ppermute | solution.py:630
  93.4 2.8 %collective-permute-start.16 = (bf16[224,384]{1,0:T(8,128)(2,1)S(1)}, bf16[224,384]{1,0:T(8,128)(2,1)S(1)}, u32[]{:S(2)}, u32[]{:S(2)}) collective-permute-start(bf16[224,384]{1,0:T(8,128)(2,1)S(1)} %add.105), channel_id=1, source_target_pairs={{0,16},{1,17},{2,18},{3,19},{4,20},{5,21},{6,22},{7,23},{8,24},{9,... | collective-permute-start | bytes 516104 | tf_op jit(solution)/shard_map/ppermute | solution.py:630
  96.2 0.9 collective-permute-done.12
  97.2 0.1 collective-permute-done.11
  97.2 0.1 fusion.3
  97.3 6.9 %collective-permute-done.16 = bf16[224,384]{1,0:T(8,128)(2,1)S(1)} collective-permute-done((bf16[224,384]{1,0:T(8,128)(2,1)S(1)}, bf16[224,384]{1,0:T(8,128)(2,1)S(1)}, u32[]{:S(2)}, u32[]{:S(2)}) %collective-permute-start.16) | collective-permute-done | bytes 172064 | tf_op jit(solution)/shard_map/ppermute | solution.py:630
  104.2 0.8 collective-permute-start.18
  105.0 1.3 collective-permute-start.15
  106.3 5.8 %collective-permute-done.15 = bf16[152,384]{1,0:T(8,128)(2,1)S(1)} collective-permute-done((bf16[152,384]{1,0:T(8,128)(2,1)S(1)}, bf16[152,384]{1,0:T(8,128)(2,1)S(1)}, u32[]{:S(2)}, u32[]{:S(2)}) %collective-permute-start.15) | collective-permute-done | bytes 116768 | tf_op jit(solution)/shard_map/ppermute | solution.py:630
  112.1 0.0 copy-start.2
  112.1 1.6 %collective-permute-start.22 = (bf16[448,384]{1,0:T(8,128)(2,1)S(1)}, bf16[448,384]{1,0:T(8,128)(2,1)S(1)}, u32[]{:S(2)}, u32[]{:S(2)}) collective-permute-start(bf16[448,384]{1,0:T(8,128)(2,1)S(1)} %pad_maximum_fusion.refs_0_), channel_id=1, source_target_pairs={{0,4},{1,5},{2,6},{3,7},{4,0},{5,1},{6,2},{7,3},{8,12},{9,13},{10,... | collective-permute-start | bytes 1032200 | tf_op jit(solution)/shard_map/ppermute | solution.py:630
  113.7 3.4 %collective-permute-start.17 = (bf16[152,384]{1,0:T(8,128)(2,1)S(1)}, bf16[152,384]{1,0:T(8,128)(2,1)S(1)}, u32[]{:S(2)}, u32[]{:S(2)}) collective-permute-start(bf16[152,384]{1,0:T(8,128)(2,1)S(1)} %add.110), channel_id=1, source_target_pairs={{0,16},{1,17},{2,18},{3,19},{4,20},{5,21},{6,22},{7,23},{8,24},{9,... | collective-permute-start | bytes 350216 | tf_op jit(solution)/shard_map/ppermute | solution.py:630
  117.1 1.2 copy.41
  118.3 1.2 copy.40
  119.5 2.7 %collective-permute-done.17 = bf16[152,384]{1,0:T(8,128)(2,1)S(1)} collective-permute-done((bf16[152,384]{1,0:T(8,128)(2,1)S(1)}, bf16[152,384]{1,0:T(8,128)(2,1)S(1)}, u32[]{:S(2)}, u32[]{:S(2)}) %collective-permute-start.17) | collective-permute-done | bytes 116768 | tf_op jit(solution)/shard_map/ppermute | solution.py:630
  122.2 0.1 collective-permute-start.24
  122.3 0.6 collective-permute-start.21
  122.9 0.1 collective-permute-start.20
  123.0 1.5 %collective-permute-start.19 = (bf16[152,384]{1,0:T(8,128)(2,1)S(1)}, bf16[152,384]{1,0:T(8,128)(2,1)S(1)}, u32[]{:S(2)}, u32[]{:S(2)}) collective-permute-start(bf16[152,384]{1,0:T(8,128)(2,1)S(1)} %add.111.refs_0_), channel_id=1, source_target_pairs={{0,4},{1,5},{2,6},{3,7},{4,0},{5,1},{6,2},{7,3},{8,12},{9,13},{10,... | collective-permute-start | bytes 350216 | tf_op jit(solution)/shard_map/ppermute | solution.py:630
  124.5 0.7 copy-done.11
  125.3 0.7 copy-done.12
  126.0 3.1 %unpack_outer.1 = (f32[768,384]{1,0:T(8,128)}, f32[192,1536]{1,0:T(8,128)}, f32[192,384]{1,0:T(8,128)}, f32[192]{0:T(256)}, f32[192]{0:T(256)}, /*index=5*/f32[192]{0:T(256)}, f32[192]{0:T(256)}, f32[768]{0:T(1024)}) custom-call(s32[4]{0:T(128)} %pad_add_fusion.index, bf16[448,384]{1,0:T(8,128)(2,1)} %copy-done.2, bf16[448,384]{1,0:T(8,128)(2,1)} %copy-done.10, ...), custom_call_target="tpu_custom_call" | custom-call | flops 1000 | bytes 1 | tf_op jit(solution)/shard_map/unpack_outer/pallas_call | solution.py:604
  129.1 1.3 collective-permute-done.19.refs_1_
  130.4 0.6 copy-done.19
  131.0 2.1 %unpack_inner.1 = (f32[192,1152]{1,0:T(8,128)}, f32[192]{0:T(256)}, f32[192]{0:T(256)}, f32[192]{0:T(256)}, f32[192]{0:T(256)}) custom-call(s32[4]{0:T(128)} %pad_add_fusion.index, bf16[152,384]{1,0:T(8,128)(2,1)} %copy-done.7, bf16[152,384]{1,0:T(8,128)(2,1)} %copy-done.19, bf16[152,384]{1,0:T(8,128)(2,1)} %copy-done.18, bf16[152,384]{1,0:T(8,128)(2,1)} %copy-done.17), custom_call_target="tpu_custom_call" | custom-call | flops 1000 | bytes 1 | tf_op jit(solution)/shard_map/unpack_inner/pallas_call | solution.py:604
  (49 shorter events, 0.3 us)
Async XLA Ops:
  0.6 12.3 %copy-start.4 = (bf16[8,197,384]{2,0,1:T(8,128)(2,1)S(1)}, bf16[8,197,384]{2,0,1:T(8,128)(2,1)}, u32[]{:S(2)}) copy-start(bf16[8,197,384]{2,0,1:T(8,128)(2,1)} %param.15) | copy-start | bytes 3631108
  3.2 9.8 %collective-permute-start = (bf16[104,1152]{1,0:T(8,128)(2,1)}, bf16[104,1152]{1,0:T(8,128)(2,1)S(1)}, u32[]{:S(2)}, u32[]{:S(2)}) collective-permute-start(bf16[104,1152]{1,0:T(8,128)(2,1)} %pack_first.1.packed), channel_id=1, source_target_pairs={{0,1},{1,0},{2,3},{3,2},{4,5},{5,4},{6,7},{7,6},{8,9},{9,8},{10,11... | collective-permute-start | bytes 718856 | tf_op jit(solution)/shard_map/ppermute | solution.py:630
  8.3 18.1 %collective-permute-start.3 = (bf16[480,384]{1,0:T(8,128)(2,1)}, bf16[480,384]{1,0:T(8,128)(2,1)S(1)}, u32[]{:S(2)}, u32[]{:S(2)}) collective-permute-start(bf16[480,384]{1,0:T(8,128)(2,1)} %get-tuple-element.92), channel_id=1, source_target_pairs={{0,1},{1,0},{2,3},{3,2},{4,5},{5,4},{6,7},{7,6},{8,9},{9,8},{10,11... | collective-permute-start | bytes 1105928 | tf_op jit(solution)/shard_map/ppermute | solution.py:630
  8.3 18.1 %collective-permute-start.2 = (bf16[96,1536]{1,0:T(8,128)(2,1)}, bf16[96,1536]{1,0:T(8,128)(2,1)S(1)}, u32[]{:S(2)}, u32[]{:S(2)}) collective-permute-start(bf16[96,1536]{1,0:T(8,128)(2,1)} %get-tuple-element.91), channel_id=1, source_target_pairs={{0,1},{1,0},{2,3},{3,2},{4,5},{5,4},{6,7},{7,6},{8,9},{9,8},{10,11... | collective-permute-start | bytes 884744 | tf_op jit(solution)/shard_map/ppermute | solution.py:630
  12.9 1.5 %copy-start.15 = (bf16[104,1152]{1,0:T(8,128)(2,1)}, bf16[104,1152]{1,0:T(8,128)(2,1)S(1)}, u32[]{:S(2)}) copy-start(bf16[104,1152]{1,0:T(8,128)(2,1)S(1)} %collective-permute-done.near) | copy-start | bytes 718852
  13.0 1.5 %collective-permute-start.1 = (bf16[104,1152]{1,0:T(8,128)(2,1)S(1)}, bf16[104,1152]{1,0:T(8,128)(2,1)S(1)}, u32[]{:S(2)}, u32[]{:S(2)}) collective-permute-start(bf16[104,1152]{1,0:T(8,128)(2,1)S(1)} %collective-permute-done.near), channel_id=1, source_target_pairs={{0,2},{1,3},{2,0},{3,1},{4,6},{5,7},{6,4},{7,5},{8,10},{9,11},{10,... | collective-permute-start | bytes 718856 | tf_op jit(solution)/shard_map/ppermute | solution.py:630
  14.2 12.8 %copy-start.5 = (bf16[8,197,384]{2,0,1:T(8,128)(2,1)S(1)}, bf16[8,197,384]{2,0,1:T(8,128)(2,1)}, u32[]{:S(2)}) copy-start(bf16[8,197,384]{2,0,1:T(8,128)(2,1)} %param.29) | copy-start | bytes 3631108
  14.5 0.7 copy-start.16
  26.3 2.2 %copy-start.13 = (bf16[96,1536]{1,0:T(8,128)(2,1)}, bf16[96,1536]{1,0:T(8,128)(2,1)S(1)}, u32[]{:S(2)}) copy-start(bf16[96,1536]{1,0:T(8,128)(2,1)S(1)} %collective-permute-done.2.lift_near) | copy-start | bytes 884740
  26.3 2.2 %copy-start.8 = (bf16[480,384]{1,0:T(8,128)(2,1)}, bf16[480,384]{1,0:T(8,128)(2,1)S(1)}, u32[]{:S(2)}) copy-start(bf16[480,384]{1,0:T(8,128)(2,1)S(1)} %collective-permute-done.3.both_near) | copy-start | bytes 1105924
  26.3 2.2 %collective-permute-start.5 = (bf16[480,384]{1,0:T(8,128)(2,1)S(1)}, bf16[480,384]{1,0:T(8,128)(2,1)S(1)}, u32[]{:S(2)}, u32[]{:S(2)}) collective-permute-start(bf16[480,384]{1,0:T(8,128)(2,1)S(1)} %collective-permute-done.3.both_near), channel_id=1, source_target_pairs={{0,2},{1,3},{2,0},{3,1},{4,6},{5,7},{6,4},{7,5},{8,10},{9,11},{10,... | collective-permute-start | bytes 1105928 | tf_op jit(solution)/shard_map/ppermute | solution.py:630
  26.4 2.1 %collective-permute-start.4 = (bf16[96,1536]{1,0:T(8,128)(2,1)S(1)}, bf16[96,1536]{1,0:T(8,128)(2,1)S(1)}, u32[]{:S(2)}, u32[]{:S(2)}) collective-permute-start(bf16[96,1536]{1,0:T(8,128)(2,1)S(1)} %collective-permute-done.2.lift_near), channel_id=1, source_target_pairs={{0,2},{1,3},{2,0},{3,1},{4,6},{5,7},{6,4},{7,5},{8,10},{9,11},{10,... | collective-permute-start | bytes 884744 | tf_op jit(solution)/shard_map/ppermute | solution.py:630
  28.5 0.7 copy-start.14
  28.5 0.8 copy-start.9
  56.9 7.2 %collective-permute-start.6 = (bf16[2,2,448,384]{3,2,1,0:T(8,128)(2,1)}, bf16[2,2,448,384]{3,2,1,0:T(8,128)(2,1)S(1)}, u32[]{:S(2)}, u32[]{:S(2)}) collective-permute-start(bf16[2,2,448,384]{3,2,1,0:T(8,128)(2,1)} %get-tuple-element.103), channel_id=1, source_target_pairs={{0,2},{1,3},{2,0},{3,1},{4,6},{5,7},{6,4},{7,5},{8,10},{9,11},{10,... | collective-permute-start | bytes 4128776 | tf_op jit(solution)/shard_map/ppermute | solution.py:630
  57.1 7.0 %copy-start.1 = (bf16[2,2,448,384]{3,2,1,0:T(8,128)(2,1)S(1)}, bf16[2,2,448,384]{3,2,1,0:T(8,128)(2,1)}, u32[]{:S(2)}) copy-start(bf16[2,2,448,384]{3,2,1,0:T(8,128)(2,1)} %get-tuple-element.107) | copy-start | bytes 4128772
  64.2 20.7 %collective-permute-start.7 = (bf16[448,384]{1,0:T(8,128)(2,1)S(1)}, bf16[448,384]{1,0:T(8,128)(2,1)}, u32[]{:S(2)}, u32[]{:S(2)}) collective-permute-start(bf16[448,384]{1,0:T(8,128)(2,1)S(1)} %get-tuple-element.115), channel_id=1, source_target_pairs={{0,1},{1,0},{2,3},{3,2},{4,5},{5,4},{6,7},{7,6},{8,9},{9,8},{10,11... | collective-permute-start | bytes 1032200 | tf_op jit(solution)/shard_map/ppermute | solution.py:630
  66.0 18.9 %collective-permute-start.8 = (bf16[448,384]{1,0:T(8,128)(2,1)S(1)}, bf16[448,384]{1,0:T(8,128)(2,1)}, u32[]{:S(2)}, u32[]{:S(2)}) collective-permute-start(bf16[448,384]{1,0:T(8,128)(2,1)S(1)} %get-tuple-element.116), channel_id=1, source_target_pairs={{0,4},{1,5},{2,6},{3,7},{4,0},{5,1},{6,2},{7,3},{8,12},{9,13},{10,... | collective-permute-start | bytes 1032200 | tf_op jit(solution)/shard_map/ppermute | solution.py:630
  67.6 17.4 %collective-permute-start.9 = (bf16[448,384]{1,0:T(8,128)(2,1)S(1)}, bf16[448,384]{1,0:T(8,128)(2,1)}, u32[]{:S(2)}, u32[]{:S(2)}) collective-permute-start(bf16[448,384]{1,0:T(8,128)(2,1)S(1)} %get-tuple-element.117), channel_id=1, source_target_pairs={{0,5},{1,4},{2,7},{3,6},{4,1},{5,0},{6,3},{7,2},{8,13},{9,12},{10,... | collective-permute-start | bytes 1032200 | tf_op jit(solution)/shard_map/ppermute | solution.py:630
  84.9 3.4 %collective-permute-start.10 = (bf16[2,2,152,384]{3,2,1,0:T(8,128)(2,1)}, bf16[2,2,152,384]{3,2,1,0:T(8,128)(2,1)S(1)}, u32[]{:S(2)}, u32[]{:S(2)}) collective-permute-start(bf16[2,2,152,384]{3,2,1,0:T(8,128)(2,1)} %get-tuple-element.118), channel_id=1, source_target_pairs={{0,2},{1,3},{2,0},{3,1},{4,6},{5,7},{6,4},{7,5},{8,10},{9,11},{10,... | collective-permute-start | bytes 1400840 | tf_op jit(solution)/shard_map/ppermute | solution.py:630
  85.0 3.3 %copy-start.6 = (bf16[2,2,152,384]{3,2,1,0:T(8,128)(2,1)S(1)}, bf16[2,2,152,384]{3,2,1,0:T(8,128)(2,1)}, u32[]{:S(2)}) copy-start(bf16[2,2,152,384]{3,2,1,0:T(8,128)(2,1)} %get-tuple-element.113) | copy-start | bytes 1400836
  86.4 6.9 %collective-permute-start.14 = (bf16[224,384]{1,0:T(8,128)(2,1)S(1)}, bf16[224,384]{1,0:T(8,128)(2,1)S(1)}, u32[]{:S(2)}, u32[]{:S(2)}) collective-permute-start(bf16[224,384]{1,0:T(8,128)(2,1)S(1)} %get-tuple-element.159), channel_id=1, source_target_pairs={{0,8},{1,9},{2,10},{3,11},{4,12},{5,13},{6,14},{7,15},{8,0},{9,1},... | collective-permute-start | bytes 516104 | tf_op jit(solution)/shard_map/ppermute | solution.py:630
  88.4 7.8 %collective-permute-start.13 = (bf16[152,384]{1,0:T(8,128)(2,1)S(1)}, bf16[152,384]{1,0:T(8,128)(2,1)S(1)}, u32[]{:S(2)}, u32[]{:S(2)}) collective-permute-start(bf16[152,384]{1,0:T(8,128)(2,1)S(1)} %get-tuple-element.156), channel_id=1, source_target_pairs={{0,5},{1,4},{2,7},{3,6},{4,1},{5,0},{6,3},{7,2},{8,13},{9,12},{10,... | collective-permute-start | bytes 350216 | tf_op jit(solution)/shard_map/ppermute | solution.py:630
  90.9 6.3 %collective-permute-start.12 = (bf16[152,384]{1,0:T(8,128)(2,1)S(1)}, bf16[152,384]{1,0:T(8,128)(2,1)S(1)}, u32[]{:S(2)}, u32[]{:S(2)}) collective-permute-start(bf16[152,384]{1,0:T(8,128)(2,1)S(1)} %get-tuple-element.157), channel_id=1, source_target_pairs={{0,4},{1,5},{2,6},{3,7},{4,0},{5,1},{6,2},{7,3},{8,12},{9,13},{10,... | collective-permute-start | bytes 350216 | tf_op jit(solution)/shard_map/ppermute | solution.py:630
  91.4 25.7 %copy-start.3 = (bf16[8,197,384]{2,1,0:T(8,128)(2,1)S(1)}, bf16[8,197,384]{2,1,0:T(8,128)(2,1)}, u32[]{:S(2)}) copy-start(bf16[8,197,384]{2,1,0:T(8,128)(2,1)} %get-tuple-element.129) | copy-start | bytes 3631108
  91.4 5.8 %collective-permute-start.11 = (bf16[152,384]{1,0:T(8,128)(2,1)S(1)}, bf16[152,384]{1,0:T(8,128)(2,1)S(1)}, u32[]{:S(2)}, u32[]{:S(2)}) collective-permute-start(bf16[152,384]{1,0:T(8,128)(2,1)S(1)} %get-tuple-element.158), channel_id=1, source_target_pairs={{0,1},{1,0},{2,3},{3,2},{4,5},{5,4},{6,7},{7,6},{8,9},{9,8},{10,11... | collective-permute-start | bytes 350216 | tf_op jit(solution)/shard_map/ppermute | solution.py:630
  93.4 10.7 %collective-permute-start.16 = (bf16[224,384]{1,0:T(8,128)(2,1)S(1)}, bf16[224,384]{1,0:T(8,128)(2,1)S(1)}, u32[]{:S(2)}, u32[]{:S(2)}) collective-permute-start(bf16[224,384]{1,0:T(8,128)(2,1)S(1)} %add.105), channel_id=1, source_target_pairs={{0,16},{1,17},{2,18},{3,19},{4,20},{5,21},{6,22},{7,23},{8,24},{9,... | collective-permute-start | bytes 516104 | tf_op jit(solution)/shard_map/ppermute | solution.py:630
  104.2 7.9 %collective-permute-start.18 = (bf16[224,384]{1,0:T(8,128)(2,1)S(1)}, bf16[224,384]{1,0:T(8,128)(2,1)S(1)}, u32[]{:S(2)}, u32[]{:S(2)}) collective-permute-start(bf16[224,384]{1,0:T(8,128)(2,1)S(1)} %add.109), channel_id=1, source_target_pairs={{0,8},{1,9},{2,10},{3,11},{4,12},{5,13},{6,14},{7,15},{8,0},{9,1},... | collective-permute-start | bytes 516104 | tf_op jit(solution)/shard_map/ppermute | solution.py:630
  105.0 7.1 %collective-permute-start.15 = (bf16[152,384]{1,0:T(8,128)(2,1)S(1)}, bf16[152,384]{1,0:T(8,128)(2,1)S(1)}, u32[]{:S(2)}, u32[]{:S(2)}) collective-permute-start(bf16[152,384]{1,0:T(8,128)(2,1)S(1)} %fusion.3), channel_id=1, source_target_pairs={{0,8},{1,9},{2,10},{3,11},{4,12},{5,13},{6,14},{7,15},{8,0},{9,1},... | collective-permute-start | bytes 350216 | tf_op jit(solution)/shard_map/ppermute | solution.py:630
  112.1 7.4 %copy-start.2 = (bf16[448,384]{1,0:T(8,128)(2,1)}, bf16[448,384]{1,0:T(8,128)(2,1)S(1)}, u32[]{:S(2)}) copy-start(bf16[448,384]{1,0:T(8,128)(2,1)S(1)} %pad_maximum_fusion.refs_0_) | copy-start | bytes 1032196
  112.1 6.2 %copy-start = (bf16[8,197,384]{2,1,0:T(8,128)(2,1)S(1)}, bf16[8,197,384]{2,1,0:T(8,128)(2,1)}, u32[]{:S(2)}) copy-start(bf16[8,197,384]{2,1,0:T(8,128)(2,1)} %get-tuple-element.130) | copy-start | bytes 3631108
  112.1 10.1 %collective-permute-start.22 = (bf16[448,384]{1,0:T(8,128)(2,1)S(1)}, bf16[448,384]{1,0:T(8,128)(2,1)S(1)}, u32[]{:S(2)}, u32[]{:S(2)}) collective-permute-start(bf16[448,384]{1,0:T(8,128)(2,1)S(1)} %pad_maximum_fusion.refs_0_), channel_id=1, source_target_pairs={{0,4},{1,5},{2,6},{3,7},{4,0},{5,1},{6,2},{7,3},{8,12},{9,13},{10,... | collective-permute-start | bytes 1032200 | tf_op jit(solution)/shard_map/ppermute | solution.py:630
  113.7 8.4 %collective-permute-start.17 = (bf16[152,384]{1,0:T(8,128)(2,1)S(1)}, bf16[152,384]{1,0:T(8,128)(2,1)S(1)}, u32[]{:S(2)}, u32[]{:S(2)}) collective-permute-start(bf16[152,384]{1,0:T(8,128)(2,1)S(1)} %add.110), channel_id=1, source_target_pairs={{0,16},{1,17},{2,18},{3,19},{4,20},{5,21},{6,22},{7,23},{8,24},{9,... | collective-permute-start | bytes 350216 | tf_op jit(solution)/shard_map/ppermute | solution.py:630
  119.5 5.1 %collective-permute-start.23 = (bf16[448,384]{1,0:T(8,128)(2,1)S(1)}, bf16[448,384]{1,0:T(8,128)(2,1)S(1)}, u32[]{:S(2)}, u32[]{:S(2)}) collective-permute-start(bf16[448,384]{1,0:T(8,128)(2,1)S(1)} %pad_maximum_fusion.refs_0_), channel_id=1, source_target_pairs={{0,2},{1,3},{2,0},{3,1},{4,6},{5,7},{6,4},{7,5},{8,10},{9,11},{10,... | collective-permute-start | bytes 1032200 | tf_op jit(solution)/shard_map/ppermute | solution.py:630
  122.2 8.2 %copy-start.7 = (bf16[152,384]{1,0:T(8,128)(2,1)}, bf16[152,384]{1,0:T(8,128)(2,1)S(1)}, u32[]{:S(2)}) copy-start(bf16[152,384]{1,0:T(8,128)(2,1)S(1)} %add.111.refs_0_) | copy-start | bytes 350212
  122.2 2.3 %copy-start.10 = (bf16[448,384]{1,0:T(8,128)(2,1)}, bf16[448,384]{1,0:T(8,128)(2,1)S(1)}, u32[]{:S(2)}) copy-start(bf16[448,384]{1,0:T(8,128)(2,1)S(1)} %collective-permute-done.22.refs_1_) | copy-start | bytes 1032196
  122.2 2.3 %collective-permute-start.24 = (bf16[448,384]{1,0:T(8,128)(2,1)S(1)}, bf16[448,384]{1,0:T(8,128)(2,1)S(1)}, u32[]{:S(2)}, u32[]{:S(2)}) collective-permute-start(bf16[448,384]{1,0:T(8,128)(2,1)S(1)} %collective-permute-done.22.refs_1_), channel_id=1, source_target_pairs={{0,2},{1,3},{2,0},{3,1},{4,6},{5,7},{6,4},{7,5},{8,10},{9,11},{10,... | collective-permute-start | bytes 1032200 | tf_op jit(solution)/shard_map/ppermute | solution.py:630
  122.3 6.8 %collective-permute-start.21 = (bf16[152,384]{1,0:T(8,128)(2,1)S(1)}, bf16[152,384]{1,0:T(8,128)(2,1)S(1)}, u32[]{:S(2)}, u32[]{:S(2)}) collective-permute-start(bf16[152,384]{1,0:T(8,128)(2,1)S(1)} %add.111.refs_0_), channel_id=1, source_target_pairs={{0,6},{1,7},{2,4},{3,5},{4,2},{5,3},{6,0},{7,1},{8,14},{9,15},{10,... | collective-permute-start | bytes 350216 | tf_op jit(solution)/shard_map/ppermute | solution.py:630
  122.9 6.2 %collective-permute-start.20 = (bf16[152,384]{1,0:T(8,128)(2,1)S(1)}, bf16[152,384]{1,0:T(8,128)(2,1)S(1)}, u32[]{:S(2)}, u32[]{:S(2)}) collective-permute-start(bf16[152,384]{1,0:T(8,128)(2,1)S(1)} %add.111.refs_0_), channel_id=1, source_target_pairs={{0,2},{1,3},{2,0},{3,1},{4,6},{5,7},{6,4},{7,5},{8,10},{9,11},{10,... | collective-permute-start | bytes 350216 | tf_op jit(solution)/shard_map/ppermute | solution.py:630
  123.0 7.4 %collective-permute-start.19 = (bf16[152,384]{1,0:T(8,128)(2,1)S(1)}, bf16[152,384]{1,0:T(8,128)(2,1)S(1)}, u32[]{:S(2)}, u32[]{:S(2)}) collective-permute-start(bf16[152,384]{1,0:T(8,128)(2,1)S(1)} %add.111.refs_0_), channel_id=1, source_target_pairs={{0,4},{1,5},{2,6},{3,7},{4,0},{5,1},{6,2},{7,3},{8,12},{9,13},{10,... | collective-permute-start | bytes 350216 | tf_op jit(solution)/shard_map/ppermute | solution.py:630
  124.5 0.8 copy-start.11
  125.3 0.7 copy-start.12
  129.1 1.3 copy-start.17
  129.1 1.3 copy-start.18
  130.4 0.6 copy-start.19

commit v8 on v7

--- a/solution.py
+++ b/solution.py
@@ -289,27 +289,9 @@
             place[deep : deep + small, :] = a_out[pl.ds(first, small), :].astype(BF16)
 
 
-def back_kernel(
-    length, first, last, index, tok_ref, proj_ref, normed_ref, d_mixed_ref, d_middle_ref, w_ref, vec_ref, *refs
-):
-    if not first:
-        old, refs = refs[:3], refs[4:]
-    in_grad_ref = refs[0]
-    if last:
-        keep, send = refs[1:3]
-        sums, d_s = refs[3:6], refs[6]
-    else:
-        sums, d_s = refs[1:4], refs[4]
-    a_qkv, a_proj, a_vec = sums
+def attention_back(length, proj_ref, d_mixed_ref, d_s):
     images, rows, wide = d_s.shape
     width = wide // 3
-    total = images * rows
-
-    @pl.when(pl.program_id(0) == 0)
-    def _():
-        for i, acc in enumerate(sums):
-            acc[...] = jnp.zeros_like(acc) if first else old[i][...]
-
     live = lax.broadcasted_iota(jnp.int32, (rows, 2 * rows), 0) < length
     for j in range(images):
         for c in range(0, width, PAIR):
@@ -330,6 +312,42 @@
             d_s[j, :, c : c + PAIR] = d_query.astype(BF16)
             d_s[j, :, width + c : width + c + PAIR] = d_key.astype(BF16)
             d_s[j, :, 2 * width + c : 2 * width + c + PAIR] = d_value.astype(BF16)
+
+
+def back_kernel(
+    length,
+    index,
+    tok_ref,
+    proj_ref,
+    normed_ref,
+    d_mixed_ref,
+    d_middle_ref,
+    w_ref,
+    vec_ref,
+    head_ref,
+    in_grad_ref,
+    keep,
+    send,
+    a_qkv,
+    a_proj,
+    a_vec,
+    d_s,
+):
+    step = pl.program_id(0)
+    images, rows, wide = d_s.shape
+    width = wide // 3
+    total = images * rows
+
+    @pl.when(step == 0)
+    def _():
+        for acc in (a_qkv, a_proj, a_vec):
+            acc[...] = jnp.zeros_like(acc)
+        d_s[...] = head_ref[...]
+
+    @pl.when(step > 0)
+    def _():
+        attention_back(length, proj_ref, d_mixed_ref, d_s)
+
     d_proj = d_s[...].reshape(total, wide)
     a_qkv[...] += tn(normed_ref[...].reshape(total, width), d_proj)
     a_proj[...] += fold(d_proj.astype(F32))
@@ -343,10 +361,8 @@
         ).astype(BF16)
         a_vec[0:1, :] += jnp.sum(grad * normal, axis=0, keepdims=True)
         a_vec[1:2, :] += jnp.sum(grad, axis=0, keepdims=True)
-    if not last:
-        return
-
-    @pl.when(pl.program_id(0) == pl.num_programs(0) - 1)
+
+    @pl.when(step == pl.num_programs(0) - 1)
     def _():
         columns = jnp.sum(a_proj[...], axis=0, keepdims=True)
         vectors = jnp.concatenate(
@@ -427,7 +443,7 @@
         ref[...] = own_half(index, vectors[i : i + 1, :])
 
 
-VMEM_LIMIT = 60 * 1024 * 1024
+VMEM_LIMIT = 67043328
 PARAMS = pltpu.CompilerParams(vmem_limit_bytes=VMEM_LIMIT)
 SCALARS = pl.BlockSpec(memory_space=pltpu.SMEM)
 
@@ -559,45 +575,49 @@
     )(index, tokens, cotangent, mixed, vectors, *pieces)
 
 
-def attention_backward(
-    index, tokens, projected, normed, w_qkv, vectors, d_mixed, d_middle, start, stop, earlier=()
-):
+def backward_head(projected, d_mixed, length):
+    images, rows, wide = projected.shape
+    group = 2 if images % 2 == 0 else 1
+    return pl.pallas_call(
+        functools.partial(attention_back, length),
+        grid=(1,),
+        in_specs=[per_step(group, rows, wide), per_step(group, rows, wide // 3)],
+        out_specs=per_step(group, rows, wide),
+        out_shape=shape_of(BF16, group, rows, wide),
+        compiler_params=PARAMS,
+        cost_estimate=cost(1),
+        name="back_head",
+    )(projected, d_mixed)
+
+
+def backward(index, tokens, projected, normed, w_qkv, vectors, d_mixed, d_middle, head):
     images, length, width = tokens.shape
-    rows = normed.shape[1]
-    wide = 3 * width
-    group = 2 if images % 2 == 0 else 1
-    offset = start // group
-    first, last = not earlier, stop == images
+    group, rows, wide = head.shape
     chunk = (2, 2, 3 * width // 8 + 8, width)
-    sums = [(width, wide), (8, wide), (2, width)]
-
-    def at(*shape):
-        return pl.BlockSpec((group,) + shape, lambda i: (i + offset if offset else i, 0, 0))
-
     return pl.pallas_call(
-        functools.partial(back_kernel, length, first, last),
-        grid=((stop - start) // group,),
+        functools.partial(back_kernel, length),
+        grid=(images // group,),
         in_specs=[
             SCALARS,
-            at(length, width),
-            at(rows, wide),
-            at(rows, width),
-            at(rows, width),
-            at(rows, width),
-            *whole_like((w_qkv, vectors)),
-        ]
-        + ([] if first else [whole(*d) for d in sums] + [pl.BlockSpec(memory_space=pl.ANY)]),
-        out_specs=[at(length, width)]
-        + ([whole(*chunk)] * 2 if last else [whole(*d) for d in sums]),
-        out_shape=[shape_of(BF16, images, length, width)]
-        + ([shape_of(BF16, *chunk)] * 2 if last else [shape_of(F32, *d) for d in sums]),
-        scratch_shapes=([pltpu.VMEM(d, F32) for d in sums] if last else [])
-        + [pltpu.VMEM((group, rows, wide), BF16)],
-        input_output_aliases={} if first else {11: 0},
+            per_step(group, length, width),
+            per_step(group, rows, wide),
+            per_step(group, rows, width),
+            per_step(group, rows, width),
+            per_step(group, rows, width),
+            *whole_like((w_qkv, vectors, head)),
+        ],
+        out_specs=[per_step(group, length, width)] + [whole(*chunk)] * 2,
+        out_shape=[shape_of(BF16, images, length, width)] + [shape_of(BF16, *chunk)] * 2,
+        scratch_shapes=[
+            pltpu.VMEM((width, wide), F32),
+            pltpu.VMEM((8, wide), F32),
+            pltpu.VMEM((2, width), F32),
+            pltpu.VMEM((group, rows, wide), BF16),
+        ],
         compiler_params=PARAMS,
         cost_estimate=cost(1),
         name="back",
-    )(index, tokens, projected, normed, d_mixed, d_middle, w_qkv, vectors, *earlier)
+    )(index, tokens, projected, normed, d_mixed, d_middle, w_qkv, vectors, head)
 
 
 def unpack(kernel, name, index, pieces, shapes):
@@ -738,7 +758,8 @@
     rest = (out_weight, lift_weight, drop_weight)
     if swaps:
         packed = pack_first(index, small, lift_bias, qkv_weight)
-        near = plan.over_x(packed)
+        tokens = with_layout_constraint(tokens, Layout(major_to_minor=(0, 1, 2)))
+        near = behind(plan.over_x(packed), tokens)
         qkv = (qkv_weight, near, plan.over_core(near))
         rest_then, packed = after(rest, packed)
         nears = [plan.over_x(half) for half in pack_rest(index, rest_then)]
@@ -760,20 +781,18 @@
     output, d_middle, d_mixed, keep_a, send_a = mlp_both_ways(
         index, tokens, cotangent, mixed, vectors, ff, outer
     )
-    backward = functools.partial(
-        attention_backward, index, tokens, projected, normed, full_qkv, vectors
+    head = backward_head(projected, d_mixed, length)
+    rest_of_backward = functools.partial(
+        backward, index, tokens, projected, normed, full_qkv, vectors, d_mixed, d_middle
     )
-    images, half = tokens.shape[0], width // 2
+    half = width // 2
     if swaps:
         got_a = plan.over_core(send_a)
-        input_grad, *sums = backward(d_mixed, d_middle, 0, 2)
-        sums, got_a = after(sums, got_a)
+        head, got_a = after(head, got_a)
         parts_a, stay_a = plan.scatter(keep_a, got_a)
-        sums, parts_a = after(sums, parts_a)
+        head, parts_a = after(head, parts_a)
         more_a = plan.send(parts_a)
-        input_grad, keep_c, send_c = backward(
-            d_mixed, d_middle, 2, images, (*sums, input_grad)
-        )
+        input_grad, keep_c, send_c = rest_of_backward(head)
         send_c, more_a = after(send_c, more_a)
         got_c = plan.over_core(send_c)
         sum_a = stay_a + more_a[0] + more_a[1] + more_a[2]
@@ -823,10 +842,7 @@
             [(half, 3 * width)] + [(half,)] * 4,
         )
     else:
-        input_grad, *sums = backward(d_mixed, d_middle, 0, images - 2)
-        input_grad, keep_c, send_c = backward(
-            d_mixed, d_middle, images - 2, images, (*sums, input_grad)
-        )
+        input_grad, keep_c, send_c = rest_of_backward(head)
         deep, tall, small = ff // 4, width // 4, width // 8
         eighths = in_order(keep_a, send_a)
         g_drop = plan.reduce(jnp.concatenate([q[0][:deep] for q in eighths]))

time: 133 us -> 136 us (1.023)
  other arithmetic: 2.35 us -> 5.58 us
    add x2, other arithmetic: 0.17 us -> 2.56 us  [scatter(): total = [[keep[i, j] + got[i, j] for j in range(2)] for i in range(2)]]
    unnamed x42 -> x14, local copies, waits for them, and re-layouts: 6.06 us -> 5.73 us
  transfers between devices with their start and end apart: 25 -> 25, of which waited for: 11 -> 9; matrix products, arithmetic and copies ran while one was open for 5% -> 7% of each run, Pallas kernels for 30% -> 29%
where the time goes in v8:
time: 136 us
  Pallas kernels  70.6 us (52%)
  starting transfers between devices  26.7 us (20%)
  waiting for transfers between devices  23.9 us (18%)
  local copies, waits for them, and re-layouts  8.14 us (6%)
  other arithmetic  5.58 us (4%)
    pallas_call x1, Pallas kernels, mlp_both_ways(): pl.pallas_call(functools.partial(mlp_kernel, length, 512), grid=(images /...  27.6 us
    ppermute x25, starting transfers between devices, swap(): return lax.ppermute(v, AXES, pairs)  26.7 us
    ppermute x25, waiting for transfers between devices, swap(): return lax.ppermute(v, AXES, pairs)  23.9 us
    pallas_call x1, Pallas kernels, backward(): pl.pallas_call(functools.partial(back_kernel, length), grid=(images // gr...  18.8 us
    pallas_call x1, Pallas kernels, forward_attention(): pl.pallas_call(functools.partial(attend_kernel, length), grid=(images //...  9.83 us
    unnamed x14, local copies, waits for them, and re-layouts  5.73 us
    pallas_call x2, Pallas kernels, unpack(): pl.pallas_call(kernel, grid=(1,), in_specs=[SCALARS, *whole_like(pieces)]...  5.19 us
    pallas_call x1, Pallas kernels, backward_head(): pl.pallas_call(functools.partial(attention_back, length), grid=(1,), in_s...  5.13 us
  transfers between devices with their start and end apart: 25, of which 9 were waited for; matrix products, arithmetic and copies ran while one was open for 7% of the time, Pallas kernels for 29%

profile of v8, /device:TPU:0, one launch (start us, length us, event | category | flops | bytes accessed | tf_op | source)
XLA Modules:
  0.0 135.7 jit_solution(11840098799726177697)
XLA Ops:
  0.7 0.6 pad_add_fusion.index
  1.3 1.9 %pack_first.1.packed = bf16[104,1152]{1,0:T(8,128)(2,1)} custom-call(s32[4]{0:T(128)} %pad_add_fusion.index, bf16[192]{0:T(256)(128)(2,1)} %refs_0_.1, bf16[192]{0:T(256)(128)(2,1)} %refs_1_.1, bf16[192]{0:T(256)(128)(2,1)} %refs_2_.1, bf16[192]{0:T(256)(128)(2,1)} %refs_3_.1, bf16[192]{0:T(256)(128)(2,1)} %refs_4_.1, bf16[192]{0:T(256)(128)(2,1)} %refs_5_.1, ...), custom_call_target="tpu_custom_call" | custom-call | flops 1000 | bytes 1 | tf_op jit(solution)/shard_map/pack_first/pallas_call | solution.py:473
  3.1 2.9 %collective-permute-start = (bf16[104,1152]{1,0:T(8,128)(2,1)}, bf16[104,1152]{1,0:T(8,128)(2,1)}, u32[]{:S(2)}, u32[]{:S(2)}) collective-permute-start(bf16[104,1152]{1,0:T(8,128)(2,1)} %pack_first.1.packed), channel_id=1, source_target_pairs={{0,1},{1,0},{2,3},{3,2},{4,5},{5,4},{6,7},{7,6},{8,9},{9,8},{10,11... | collective-permute-start | bytes 718856 | tf_op jit(solution)/shard_map/ppermute | solution.py:650
  6.1 2.2 %pack_rest.1 = (bf16[96,1536]{1,0:T(8,128)(2,1)}, bf16[480,384]{1,0:T(8,128)(2,1)}) custom-call(s32[4]{0:T(128)} %pad_add_fusion.index, bf16[192,384]{1,0:T(8,128)(2,1)} %out_own.2, bf16[192,1536]{1,0:T(8,128)(2,1)} %lift_own.2, bf16[768,384]{1,0:T(8,128)(2,1)} %drop_own.2), custom_call_target="tpu_custom_call" | custom-call | flops 1000 | bytes 1 | tf_op jit(solution)/shard_map/pack_rest/pallas_call | solution.py:489
  8.3 0.0 collective-permute-start.3
  8.3 2.0 %collective-permute-start.2 = (bf16[96,1536]{1,0:T(8,128)(2,1)}, bf16[96,1536]{1,0:T(8,128)(2,1)}, u32[]{:S(2)}, u32[]{:S(2)}) collective-permute-start(bf16[96,1536]{1,0:T(8,128)(2,1)} %get-tuple-element.85), channel_id=1, source_target_pairs={{0,1},{1,0},{2,3},{3,2},{4,5},{5,4},{6,7},{7,6},{8,9},{9,8},{10,11... | collective-permute-start | bytes 884744 | tf_op jit(solution)/shard_map/ppermute | solution.py:650
  10.3 2.5 %copy.30.tok_ref = bf16[8,197,384]{2,1,0:T(8,128)(2,1)} copy(bf16[8,197,384]{2,0,1:T(8,128)(2,1)} %param.15) | data formatting | bytes 2420736 | tf_op args[0]
  12.8 0.3 collective-permute-done.near
  13.0 1.8 %collective-permute-done.1.far = bf16[104,1152]{1,0:T(8,128)(2,1)} collective-permute-done((bf16[104,1152]{1,0:T(8,128)(2,1)}, bf16[104,1152]{1,0:T(8,128)(2,1)}, u32[]{:S(2)}, u32[]{:S(2)}) %collective-permute-start.1) | collective-permute-done | bytes 239648 | tf_op jit(solution)/shard_map/ppermute | solution.py:650
  14.9 9.8 %attend.1 = (bf16[8,208,384]{2,1,0:T(8,128)(2,1)}, bf16[8,208,1152]{2,1,0:T(8,128)(2,1)}, bf16[8,208,384]{2,1,0:T(8,128)(2,1)}, bf16[384,1152]{1,0:T(8,128)(2,1)}, f32[12,384]{1,0:T(8,128)}) custom-call(s32[4]{0:T(128)} %pad_add_fusion.index, bf16[8,197,384]{2,1,0:T(8,128)(2,1)} %copy.30.tok_ref, bf16[104,1152]{1,0:T(8,128)(2,1)} %pack_first.1.packed, ...), custom_call_target="tpu_custom_call" | custom-call | flops 1000 | bytes 1 | tf_op jit(solution)/shard_map/attend/pallas_call | solution.py:505
  24.7 1.7 %collective-permute-done.2.lift_near = bf16[96,1536]{1,0:T(8,128)(2,1)} collective-permute-done((bf16[96,1536]{1,0:T(8,128)(2,1)}, bf16[96,1536]{1,0:T(8,128)(2,1)}, u32[]{:S(2)}, u32[]{:S(2)}) %collective-permute-start.2) | collective-permute-done | bytes 294944 | tf_op jit(solution)/shard_map/ppermute | solution.py:650
  26.4 0.0 collective-permute-done.3.both_near
  26.4 0.0 collective-permute-start.5
  26.4 0.5 collective-permute-start.4
  26.9 2.5 %copy.31.cot_ref = bf16[8,197,384]{2,1,0:T(8,128)(2,1)} copy(bf16[8,197,384]{2,0,1:T(8,128)(2,1)} %param.29) | data formatting | bytes 2420736 | tf_op args[14]
  29.4 0.0 collective-permute-done.4.lift_far
  29.4 0.0 collective-permute-done.5.both_far
  29.4 27.6 %mlp.1 = (bf16[8,197,384]{2,1,0:T(8,128)(2,1)}, f32[8,208,384]{2,1,0:T(8,128)}, bf16[8,208,384]{2,1,0:T(8,128)(2,1)}, bf16[2,2,448,384]{3,2,1,0:T(8,128)(2,1)}, bf16[2,2,448,384]{3,2,1,0:T(8,128)(2,1)}) custom-call(s32[4]{0:T(128)} %pad_add_fusion.index, bf16[8,197,384]{2,1,0:T(8,128)(2,1)} %copy.30.tok_ref, bf16[8,197,384]{2,1,0:T(8,128)(2,1)} %copy.31.cot_ref, ...), custom_call_target="tpu_custom_call" | custom-call | flops 1000 | bytes 1 | tf_op jit(solution)/shard_map/mlp/pallas_call | solution.py:535
  57.0 0.1 collective-permute-start.6
  57.1 5.1 %back_head.1.head_ref = bf16[2,208,1152]{2,1,0:T(8,128)(2,1)} custom-call(bf16[8,208,1152]{2,1,0:T(8,128)(2,1)} %get-tuple-element.79.proj_ref, bf16[8,208,384]{2,1,0:T(8,128)(2,1)} %get-tuple-element.91.d_mixed_ref), custom_call_target="tpu_custom_call" | custom-call | flops 1000 | bytes 1 | tf_op jit(solution)/shard_map/back_head/pallas_call | solution.py:581
  62.2 0.0 collective-permute-done.6
  62.2 2.5 %add_bitcast_fusion = (bf16[448,384]{1,0:T(8,128)(2,1)}, bf16[448,384]{1,0:T(8,128)(2,1)}, bf16[448,384]{1,0:T(8,128)(2,1)}) fusion(bf16[2,2,448,384]{3,2,1,0:T(8,128)(2,1)} %collective-permute-done.6, bf16[2,2,448,384]{3,2,1,0:T(8,128)(2,1)} %get-tuple-element.96), kind=kLoop, calls=%fused_computation.6 | loop fusion | flops 516096 | bytes 3096576 | tf_op jit(solution)/shard_map/add | solution.py:675
  64.7 1.7 %collective-permute-start.7 = (bf16[448,384]{1,0:T(8,128)(2,1)}, bf16[448,384]{1,0:T(8,128)(2,1)}, u32[]{:S(2)}, u32[]{:S(2)}) collective-permute-start(bf16[448,384]{1,0:T(8,128)(2,1)} %get-tuple-element.101), channel_id=1, source_target_pairs={{0,1},{1,0},{2,3},{3,2},{4,5},{5,4},{6,7},{7,6},{8,9},{9,8},{10,11... | collective-permute-start | bytes 1032200 | tf_op jit(solution)/shard_map/ppermute | solution.py:650
  66.5 1.5 %collective-permute-start.8 = (bf16[448,384]{1,0:T(8,128)(2,1)}, bf16[448,384]{1,0:T(8,128)(2,1)}, u32[]{:S(2)}, u32[]{:S(2)}) collective-permute-start(bf16[448,384]{1,0:T(8,128)(2,1)} %get-tuple-element.102), channel_id=1, source_target_pairs={{0,4},{1,5},{2,6},{3,7},{4,0},{5,1},{6,2},{7,3},{8,12},{9,13},{10,... | collective-permute-start | bytes 1032200 | tf_op jit(solution)/shard_map/ppermute | solution.py:650
  68.0 0.2 collective-permute-start.9
  68.2 18.8 %back.1 = (bf16[8,197,384]{2,1,0:T(8,128)(2,1)}, bf16[2,2,152,384]{3,2,1,0:T(8,128)(2,1)}, bf16[2,2,152,384]{3,2,1,0:T(8,128)(2,1)}) custom-call(s32[4]{0:T(128)} %pad_add_fusion.index, bf16[8,197,384]{2,1,0:T(8,128)(2,1)} %copy.30.tok_ref, bf16[8,208,1152]{2,1,0:T(8,128)(2,1)} %get-tuple-element.79.proj_ref, ...), custom_call_target="tpu_custom_call" | custom-call | flops 1000 | bytes 1 | tf_op jit(solution)/shard_map/back/pallas_call | solution.py:597
  87.0 0.0 collective-permute-done.7
  87.0 0.0 collective-permute-done.8
  87.0 0.1 collective-permute-start.10
  87.1 0.0 copy-start.3
  87.1 1.5 %fusion.1 = bf16[448,384]{1,0:T(8,128)(2,1)S(1)} fusion(bf16[448,384]{1,0:T(8,128)(2,1)} %collective-permute-done.9, bf16[448,384]{1,0:T(8,128)(2,1)} %collective-permute-done.8, bf16[448,384]{1,0:T(8,128)(2,1)} %collective-permute-done.7, bf16[2,2,448,384]{3,2,1,0:T(8,128)(2,1)} %collective-permute-done.6, bf16[2,2,448,384]{3,2,1,0:T(8,128)(2,1)} %get-tuple-element.96), kind=kLoop, calls=%fused_computation.5 | loop fusion | flops 688128 | bytes 2064384 | tf_op jit(solution)/shard_map/add | solution.py:798
  88.7 0.1 constant_dynamic-slice_fusion
  88.7 1.9 %collective-permute-start.14 = (bf16[224,384]{1,0:T(8,128)(2,1)S(1)}, bf16[224,384]{1,0:T(8,128)(2,1)S(1)}, u32[]{:S(2)}, u32[]{:S(2)}) collective-permute-start(bf16[224,384]{1,0:T(8,128)(2,1)S(1)} %get-tuple-element.145), channel_id=1, source_target_pairs={{0,8},{1,9},{2,10},{3,11},{4,12},{5,13},{6,14},{7,15},{8,0},{9,1},... | collective-permute-start | bytes 516104 | tf_op jit(solution)/shard_map/ppermute | solution.py:650
  90.7 0.1 add_bitcast_fusion.3
  90.7 2.5 %collective-permute-start.13 = (bf16[152,384]{1,0:T(8,128)(2,1)S(1)}, bf16[152,384]{1,0:T(8,128)(2,1)S(1)}, u32[]{:S(2)}, u32[]{:S(2)}) collective-permute-start(bf16[152,384]{1,0:T(8,128)(2,1)S(1)} %get-tuple-element.142), channel_id=1, source_target_pairs={{0,5},{1,4},{2,7},{3,6},{4,1},{5,0},{6,3},{7,2},{8,13},{9,12},{10,... | collective-permute-start | bytes 350216 | tf_op jit(solution)/shard_map/ppermute | solution.py:650
  93.2 0.5 collective-permute-start.12
  93.7 0.6 collective-permute-start.11
  94.3 1.4 %collective-permute-done.14 = bf16[224,384]{1,0:T(8,128)(2,1)S(1)} collective-permute-done((bf16[224,384]{1,0:T(8,128)(2,1)S(1)}, bf16[224,384]{1,0:T(8,128)(2,1)S(1)}, u32[]{:S(2)}, u32[]{:S(2)}) %collective-permute-start.14) | collective-permute-done | bytes 172064 | tf_op jit(solution)/shard_map/ppermute | solution.py:650
  95.7 2.8 %collective-permute-start.16 = (bf16[224,384]{1,0:T(8,128)(2,1)S(1)}, bf16[224,384]{1,0:T(8,128)(2,1)S(1)}, u32[]{:S(2)}, u32[]{:S(2)}) collective-permute-start(bf16[224,384]{1,0:T(8,128)(2,1)S(1)} %add.105), channel_id=1, source_target_pairs={{0,16},{1,17},{2,18},{3,19},{4,20},{5,21},{6,22},{7,23},{8,24},{9,... | collective-permute-start | bytes 516104 | tf_op jit(solution)/shard_map/ppermute | solution.py:650
  98.5 0.0 collective-permute-done.13
  98.5 1.0 collective-permute-done.12
  99.5 0.0 collective-permute-done.11
  99.5 0.1 fusion.3
  99.6 6.9 %collective-permute-done.16 = bf16[224,384]{1,0:T(8,128)(2,1)S(1)} collective-permute-done((bf16[224,384]{1,0:T(8,128)(2,1)S(1)}, bf16[224,384]{1,0:T(8,128)(2,1)S(1)}, u32[]{:S(2)}, u32[]{:S(2)}) %collective-permute-start.16) | collective-permute-done | bytes 172064 | tf_op jit(solution)/shard_map/ppermute | solution.py:650
  106.5 0.7 collective-permute-start.18
  107.3 1.3 collective-permute-start.15
  108.6 5.7 %collective-permute-done.15 = bf16[152,384]{1,0:T(8,128)(2,1)S(1)} collective-permute-done((bf16[152,384]{1,0:T(8,128)(2,1)S(1)}, bf16[152,384]{1,0:T(8,128)(2,1)S(1)}, u32[]{:S(2)}, u32[]{:S(2)}) %collective-permute-start.15) | collective-permute-done | bytes 116768 | tf_op jit(solution)/shard_map/ppermute | solution.py:650
  114.4 0.0 collective-permute-done.18
  114.4 0.0 copy-start
  114.4 1.6 %collective-permute-start.22 = (bf16[448,384]{1,0:T(8,128)(2,1)S(1)}, bf16[448,384]{1,0:T(8,128)(2,1)S(1)}, u32[]{:S(2)}, u32[]{:S(2)}) collective-permute-start(bf16[448,384]{1,0:T(8,128)(2,1)S(1)} %pad_maximum_fusion.refs_0_), channel_id=1, source_target_pairs={{0,4},{1,5},{2,6},{3,7},{4,0},{5,1},{6,2},{7,3},{8,12},{9,13},{10,... | collective-permute-start | bytes 1032200 | tf_op jit(solution)/shard_map/ppermute | solution.py:650
  116.1 3.4 %collective-permute-start.17 = (bf16[152,384]{1,0:T(8,128)(2,1)S(1)}, bf16[152,384]{1,0:T(8,128)(2,1)S(1)}, u32[]{:S(2)}, u32[]{:S(2)}) collective-permute-start(bf16[152,384]{1,0:T(8,128)(2,1)S(1)} %add.110), channel_id=1, source_target_pairs={{0,16},{1,17},{2,18},{3,19},{4,20},{5,21},{6,22},{7,23},{8,24},{9,... | collective-permute-start | bytes 350216 | tf_op jit(solution)/shard_map/ppermute | solution.py:650
  119.4 1.2 copy.37
  120.6 1.2 copy.36
  121.8 0.0 collective-permute-start.23
  121.8 2.7 %collective-permute-done.17 = bf16[152,384]{1,0:T(8,128)(2,1)S(1)} collective-permute-done((bf16[152,384]{1,0:T(8,128)(2,1)S(1)}, bf16[152,384]{1,0:T(8,128)(2,1)S(1)}, u32[]{:S(2)}, u32[]{:S(2)}) %collective-permute-start.17) | collective-permute-done | bytes 116768 | tf_op jit(solution)/shard_map/ppermute | solution.py:650
  124.5 0.7 add.111.refs_0_
  125.2 0.0 collective-permute-start.24
  125.2 0.6 collective-permute-start.21
  125.8 0.1 collective-permute-start.20
  125.8 1.5 %collective-permute-start.19 = (bf16[152,384]{1,0:T(8,128)(2,1)}, bf16[152,384]{1,0:T(8,128)(2,1)}, u32[]{:S(2)}, u32[]{:S(2)}) collective-permute-start(bf16[152,384]{1,0:T(8,128)(2,1)} %add.111.refs_0_), channel_id=1, source_target_pairs={{0,4},{1,5},{2,6},{3,7},{4,0},{5,1},{6,2},{7,3},{8,12},{9,13},{10,... | collective-permute-start | bytes 350216 | tf_op jit(solution)/shard_map/ppermute | solution.py:650
  127.4 0.7 copy-done.5
  128.1 3.1 %unpack_outer.1 = (f32[768,384]{1,0:T(8,128)}, f32[192,1536]{1,0:T(8,128)}, f32[192,384]{1,0:T(8,128)}, f32[192]{0:T(256)}, f32[192]{0:T(256)}, /*index=5*/f32[192]{0:T(256)}, f32[192]{0:T(256)}, f32[768]{0:T(1024)}) custom-call(s32[4]{0:T(128)} %pad_add_fusion.index, bf16[448,384]{1,0:T(8,128)(2,1)} %copy-done, bf16[448,384]{1,0:T(8,128)(2,1)} %copy-done.4, ...), custom_call_target="tpu_custom_call" | custom-call | flops 1000 | bytes 1 | tf_op jit(solution)/shard_map/unpack_outer/pallas_call | solution.py:624
  131.2 2.3 %collective-permute-done.19.refs_1_ = bf16[152,384]{1,0:T(8,128)(2,1)} collective-permute-done((bf16[152,384]{1,0:T(8,128)(2,1)}, bf16[152,384]{1,0:T(8,128)(2,1)}, u32[]{:S(2)}, u32[]{:S(2)}) %collective-permute-start.19) | collective-permute-done | bytes 116768 | tf_op jit(solution)/shard_map/ppermute | solution.py:650
  133.6 2.1 %unpack_inner.1 = (f32[192,1152]{1,0:T(8,128)}, f32[192]{0:T(256)}, f32[192]{0:T(256)}, f32[192]{0:T(256)}, f32[192]{0:T(256)}) custom-call(s32[4]{0:T(128)} %pad_add_fusion.index, bf16[152,384]{1,0:T(8,128)(2,1)} %add.111.refs_0_, bf16[152,384]{1,0:T(8,128)(2,1)} %collective-permute-done.19.refs_1_, bf16[152,384]{1,0:T(8,128)(2,1)} %collective-permute-done.20.refs_2_, ...), custom_call_target="tpu_custom_call" | custom-call | flops 1000 | bytes 1 | tf_op jit(solution)/shard_map/unpack_inner/pallas_call | solution.py:624
  (21 shorter events, 0.2 us)
Async XLA Ops:
  3.1 9.9 %collective-permute-start = (bf16[104,1152]{1,0:T(8,128)(2,1)}, bf16[104,1152]{1,0:T(8,128)(2,1)}, u32[]{:S(2)}, u32[]{:S(2)}) collective-permute-start(bf16[104,1152]{1,0:T(8,128)(2,1)} %pack_first.1.packed), channel_id=1, source_target_pairs={{0,1},{1,0},{2,3},{3,2},{4,5},{5,4},{6,7},{7,6},{8,9},{9,8},{10,11... | collective-permute-start | bytes 718856 | tf_op jit(solution)/shard_map/ppermute | solution.py:650
  8.3 18.2 %collective-permute-start.3 = (bf16[480,384]{1,0:T(8,128)(2,1)}, bf16[480,384]{1,0:T(8,128)(2,1)}, u32[]{:S(2)}, u32[]{:S(2)}) collective-permute-start(bf16[480,384]{1,0:T(8,128)(2,1)} %get-tuple-element.86), channel_id=1, source_target_pairs={{0,1},{1,0},{2,3},{3,2},{4,5},{5,4},{6,7},{7,6},{8,9},{9,8},{10,11... | collective-permute-start | bytes 1105928 | tf_op jit(solution)/shard_map/ppermute | solution.py:650
  8.3 18.2 %collective-permute-start.2 = (bf16[96,1536]{1,0:T(8,128)(2,1)}, bf16[96,1536]{1,0:T(8,128)(2,1)}, u32[]{:S(2)}, u32[]{:S(2)}) collective-permute-start(bf16[96,1536]{1,0:T(8,128)(2,1)} %get-tuple-element.85), channel_id=1, source_target_pairs={{0,1},{1,0},{2,3},{3,2},{4,5},{5,4},{6,7},{7,6},{8,9},{9,8},{10,11... | collective-permute-start | bytes 884744 | tf_op jit(solution)/shard_map/ppermute | solution.py:650
  13.0 1.8 %collective-permute-start.1 = (bf16[104,1152]{1,0:T(8,128)(2,1)}, bf16[104,1152]{1,0:T(8,128)(2,1)}, u32[]{:S(2)}, u32[]{:S(2)}) collective-permute-start(bf16[104,1152]{1,0:T(8,128)(2,1)} %collective-permute-done.near), channel_id=1, source_target_pairs={{0,2},{1,3},{2,0},{3,1},{4,6},{5,7},{6,4},{7,5},{8,10},{9,11},{10,... | collective-permute-start | bytes 718856 | tf_op jit(solution)/shard_map/ppermute | solution.py:650
  26.4 3.0 %collective-permute-start.5 = (bf16[480,384]{1,0:T(8,128)(2,1)}, bf16[480,384]{1,0:T(8,128)(2,1)}, u32[]{:S(2)}, u32[]{:S(2)}) collective-permute-start(bf16[480,384]{1,0:T(8,128)(2,1)} %collective-permute-done.3.both_near), channel_id=1, source_target_pairs={{0,2},{1,3},{2,0},{3,1},{4,6},{5,7},{6,4},{7,5},{8,10},{9,11},{10,... | collective-permute-start | bytes 1105928 | tf_op jit(solution)/shard_map/ppermute | solution.py:650
  26.4 3.0 %collective-permute-start.4 = (bf16[96,1536]{1,0:T(8,128)(2,1)}, bf16[96,1536]{1,0:T(8,128)(2,1)}, u32[]{:S(2)}, u32[]{:S(2)}) collective-permute-start(bf16[96,1536]{1,0:T(8,128)(2,1)} %collective-permute-done.2.lift_near), channel_id=1, source_target_pairs={{0,2},{1,3},{2,0},{3,1},{4,6},{5,7},{6,4},{7,5},{8,10},{9,11},{10,... | collective-permute-start | bytes 884744 | tf_op jit(solution)/shard_map/ppermute | solution.py:650
  57.0 5.2 %collective-permute-start.6 = (bf16[2,2,448,384]{3,2,1,0:T(8,128)(2,1)}, bf16[2,2,448,384]{3,2,1,0:T(8,128)(2,1)}, u32[]{:S(2)}, u32[]{:S(2)}) collective-permute-start(bf16[2,2,448,384]{3,2,1,0:T(8,128)(2,1)} %get-tuple-element.94), channel_id=1, source_target_pairs={{0,2},{1,3},{2,0},{3,1},{4,6},{5,7},{6,4},{7,5},{8,10},{9,11},{10,... | collective-permute-start | bytes 4128776 | tf_op jit(solution)/shard_map/ppermute | solution.py:650
  64.7 22.3 %collective-permute-start.7 = (bf16[448,384]{1,0:T(8,128)(2,1)}, bf16[448,384]{1,0:T(8,128)(2,1)}, u32[]{:S(2)}, u32[]{:S(2)}) collective-permute-start(bf16[448,384]{1,0:T(8,128)(2,1)} %get-tuple-element.101), channel_id=1, source_target_pairs={{0,1},{1,0},{2,3},{3,2},{4,5},{5,4},{6,7},{7,6},{8,9},{9,8},{10,11... | collective-permute-start | bytes 1032200 | tf_op jit(solution)/shard_map/ppermute | solution.py:650
  66.5 20.6 %collective-permute-start.8 = (bf16[448,384]{1,0:T(8,128)(2,1)}, bf16[448,384]{1,0:T(8,128)(2,1)}, u32[]{:S(2)}, u32[]{:S(2)}) collective-permute-start(bf16[448,384]{1,0:T(8,128)(2,1)} %get-tuple-element.102), channel_id=1, source_target_pairs={{0,4},{1,5},{2,6},{3,7},{4,0},{5,1},{6,2},{7,3},{8,12},{9,13},{10,... | collective-permute-start | bytes 1032200 | tf_op jit(solution)/shard_map/ppermute | solution.py:650
  68.0 19.1 %collective-permute-start.9 = (bf16[448,384]{1,0:T(8,128)(2,1)}, bf16[448,384]{1,0:T(8,128)(2,1)}, u32[]{:S(2)}, u32[]{:S(2)}) collective-permute-start(bf16[448,384]{1,0:T(8,128)(2,1)} %get-tuple-element.103), channel_id=1, source_target_pairs={{0,5},{1,4},{2,7},{3,6},{4,1},{5,0},{6,3},{7,2},{8,13},{9,12},{10,... | collective-permute-start | bytes 1032200 | tf_op jit(solution)/shard_map/ppermute | solution.py:650
  87.0 3.6 %collective-permute-start.10 = (bf16[2,2,152,384]{3,2,1,0:T(8,128)(2,1)}, bf16[2,2,152,384]{3,2,1,0:T(8,128)(2,1)S(1)}, u32[]{:S(2)}, u32[]{:S(2)}) collective-permute-start(bf16[2,2,152,384]{3,2,1,0:T(8,128)(2,1)} %get-tuple-element.104), channel_id=1, source_target_pairs={{0,2},{1,3},{2,0},{3,1},{4,6},{5,7},{6,4},{7,5},{8,10},{9,11},{10,... | collective-permute-start | bytes 1400840 | tf_op jit(solution)/shard_map/ppermute | solution.py:650
  87.1 3.5 %copy-start.3 = (bf16[2,2,152,384]{3,2,1,0:T(8,128)(2,1)S(1)}, bf16[2,2,152,384]{3,2,1,0:T(8,128)(2,1)}, u32[]{:S(2)}) copy-start(bf16[2,2,152,384]{3,2,1,0:T(8,128)(2,1)} %get-tuple-element.99) | copy-start | bytes 1400836
  88.7 6.9 %collective-permute-start.14 = (bf16[224,384]{1,0:T(8,128)(2,1)S(1)}, bf16[224,384]{1,0:T(8,128)(2,1)S(1)}, u32[]{:S(2)}, u32[]{:S(2)}) collective-permute-start(bf16[224,384]{1,0:T(8,128)(2,1)S(1)} %get-tuple-element.145), channel_id=1, source_target_pairs={{0,8},{1,9},{2,10},{3,11},{4,12},{5,13},{6,14},{7,15},{8,0},{9,1},... | collective-permute-start | bytes 516104 | tf_op jit(solution)/shard_map/ppermute | solution.py:650
  90.7 7.8 %collective-permute-start.13 = (bf16[152,384]{1,0:T(8,128)(2,1)S(1)}, bf16[152,384]{1,0:T(8,128)(2,1)S(1)}, u32[]{:S(2)}, u32[]{:S(2)}) collective-permute-start(bf16[152,384]{1,0:T(8,128)(2,1)S(1)} %get-tuple-element.142), channel_id=1, source_target_pairs={{0,5},{1,4},{2,7},{3,6},{4,1},{5,0},{6,3},{7,2},{8,13},{9,12},{10,... | collective-permute-start | bytes 350216 | tf_op jit(solution)/shard_map/ppermute | solution.py:650
  93.2 6.3 %collective-permute-start.12 = (bf16[152,384]{1,0:T(8,128)(2,1)S(1)}, bf16[152,384]{1,0:T(8,128)(2,1)S(1)}, u32[]{:S(2)}, u32[]{:S(2)}) collective-permute-start(bf16[152,384]{1,0:T(8,128)(2,1)S(1)} %get-tuple-element.143), channel_id=1, source_target_pairs={{0,4},{1,5},{2,6},{3,7},{4,0},{5,1},{6,2},{7,3},{8,12},{9,13},{10,... | collective-permute-start | bytes 350216 | tf_op jit(solution)/shard_map/ppermute | solution.py:650
  93.7 25.7 %copy-start.1 = (bf16[8,197,384]{2,1,0:T(8,128)(2,1)S(1)}, bf16[8,197,384]{2,1,0:T(8,128)(2,1)}, u32[]{:S(2)}) copy-start(bf16[8,197,384]{2,1,0:T(8,128)(2,1)} %get-tuple-element.115) | copy-start | bytes 3631108
  93.7 5.8 %collective-permute-start.11 = (bf16[152,384]{1,0:T(8,128)(2,1)S(1)}, bf16[152,384]{1,0:T(8,128)(2,1)S(1)}, u32[]{:S(2)}, u32[]{:S(2)}) collective-permute-start(bf16[152,384]{1,0:T(8,128)(2,1)S(1)} %get-tuple-element.144), channel_id=1, source_target_pairs={{0,1},{1,0},{2,3},{3,2},{4,5},{5,4},{6,7},{7,6},{8,9},{9,8},{10,11... | collective-permute-start | bytes 350216 | tf_op jit(solution)/shard_map/ppermute | solution.py:650
  95.7 10.8 %collective-permute-start.16 = (bf16[224,384]{1,0:T(8,128)(2,1)S(1)}, bf16[224,384]{1,0:T(8,128)(2,1)S(1)}, u32[]{:S(2)}, u32[]{:S(2)}) collective-permute-start(bf16[224,384]{1,0:T(8,128)(2,1)S(1)} %add.105), channel_id=1, source_target_pairs={{0,16},{1,17},{2,18},{3,19},{4,20},{5,21},{6,22},{7,23},{8,24},{9,... | collective-permute-start | bytes 516104 | tf_op jit(solution)/shard_map/ppermute | solution.py:650
  106.5 7.8 %collective-permute-start.18 = (bf16[224,384]{1,0:T(8,128)(2,1)S(1)}, bf16[224,384]{1,0:T(8,128)(2,1)S(1)}, u32[]{:S(2)}, u32[]{:S(2)}) collective-permute-start(bf16[224,384]{1,0:T(8,128)(2,1)S(1)} %add.109), channel_id=1, source_target_pairs={{0,8},{1,9},{2,10},{3,11},{4,12},{5,13},{6,14},{7,15},{8,0},{9,1},... | collective-permute-start | bytes 516104 | tf_op jit(solution)/shard_map/ppermute | solution.py:650
  107.3 7.1 %collective-permute-start.15 = (bf16[152,384]{1,0:T(8,128)(2,1)S(1)}, bf16[152,384]{1,0:T(8,128)(2,1)S(1)}, u32[]{:S(2)}, u32[]{:S(2)}) collective-permute-start(bf16[152,384]{1,0:T(8,128)(2,1)S(1)} %fusion.3), channel_id=1, source_target_pairs={{0,8},{1,9},{2,10},{3,11},{4,12},{5,13},{6,14},{7,15},{8,0},{9,1},... | collective-permute-start | bytes 350216 | tf_op jit(solution)/shard_map/ppermute | solution.py:650
  114.4 7.4 %copy-start = (bf16[448,384]{1,0:T(8,128)(2,1)}, bf16[448,384]{1,0:T(8,128)(2,1)S(1)}, u32[]{:S(2)}) copy-start(bf16[448,384]{1,0:T(8,128)(2,1)S(1)} %pad_maximum_fusion.refs_0_) | copy-start | bytes 1032196
  114.4 6.2 %copy-start.2 = (bf16[8,197,384]{2,1,0:T(8,128)(2,1)S(1)}, bf16[8,197,384]{2,1,0:T(8,128)(2,1)}, u32[]{:S(2)}) copy-start(bf16[8,197,384]{2,1,0:T(8,128)(2,1)} %get-tuple-element.116) | copy-start | bytes 3631108
  114.4 10.7 %collective-permute-start.22 = (bf16[448,384]{1,0:T(8,128)(2,1)S(1)}, bf16[448,384]{1,0:T(8,128)(2,1)S(1)}, u32[]{:S(2)}, u32[]{:S(2)}) collective-permute-start(bf16[448,384]{1,0:T(8,128)(2,1)S(1)} %pad_maximum_fusion.refs_0_), channel_id=1, source_target_pairs={{0,4},{1,5},{2,6},{3,7},{4,0},{5,1},{6,2},{7,3},{8,12},{9,13},{10,... | collective-permute-start | bytes 1032200 | tf_op jit(solution)/shard_map/ppermute | solution.py:650
  116.1 8.4 %collective-permute-start.17 = (bf16[152,384]{1,0:T(8,128)(2,1)S(1)}, bf16[152,384]{1,0:T(8,128)(2,1)S(1)}, u32[]{:S(2)}, u32[]{:S(2)}) collective-permute-start(bf16[152,384]{1,0:T(8,128)(2,1)S(1)} %add.110), channel_id=1, source_target_pairs={{0,16},{1,17},{2,18},{3,19},{4,20},{5,21},{6,22},{7,23},{8,24},{9,... | collective-permute-start | bytes 350216 | tf_op jit(solution)/shard_map/ppermute | solution.py:650
  121.8 5.6 %collective-permute-start.23 = (bf16[448,384]{1,0:T(8,128)(2,1)S(1)}, bf16[448,384]{1,0:T(8,128)(2,1)S(1)}, u32[]{:S(2)}, u32[]{:S(2)}) collective-permute-start(bf16[448,384]{1,0:T(8,128)(2,1)S(1)} %pad_maximum_fusion.refs_0_), channel_id=1, source_target_pairs={{0,2},{1,3},{2,0},{3,1},{4,6},{5,7},{6,4},{7,5},{8,10},{9,11},{10,... | collective-permute-start | bytes 1032200 | tf_op jit(solution)/shard_map/ppermute | solution.py:650
  125.2 2.2 %copy-start.4 = (bf16[448,384]{1,0:T(8,128)(2,1)}, bf16[448,384]{1,0:T(8,128)(2,1)S(1)}, u32[]{:S(2)}) copy-start(bf16[448,384]{1,0:T(8,128)(2,1)S(1)} %collective-permute-done.22.refs_1_) | copy-start | bytes 1032196
  125.2 3.0 %collective-permute-start.24 = (bf16[448,384]{1,0:T(8,128)(2,1)S(1)}, bf16[448,384]{1,0:T(8,128)(2,1)}, u32[]{:S(2)}, u32[]{:S(2)}) collective-permute-start(bf16[448,384]{1,0:T(8,128)(2,1)S(1)} %collective-permute-done.22.refs_1_), channel_id=1, source_target_pairs={{0,2},{1,3},{2,0},{3,1},{4,6},{5,7},{6,4},{7,5},{8,10},{9,11},{10,... | collective-permute-start | bytes 1032200 | tf_op jit(solution)/shard_map/ppermute | solution.py:650
  125.2 6.0 %collective-permute-start.21 = (bf16[152,384]{1,0:T(8,128)(2,1)}, bf16[152,384]{1,0:T(8,128)(2,1)}, u32[]{:S(2)}, u32[]{:S(2)}) collective-permute-start(bf16[152,384]{1,0:T(8,128)(2,1)} %add.111.refs_0_), channel_id=1, source_target_pairs={{0,6},{1,7},{2,4},{3,5},{4,2},{5,3},{6,0},{7,1},{8,14},{9,15},{10,... | collective-permute-start | bytes 350216 | tf_op jit(solution)/shard_map/ppermute | solution.py:650
  125.8 5.4 %collective-permute-start.20 = (bf16[152,384]{1,0:T(8,128)(2,1)}, bf16[152,384]{1,0:T(8,128)(2,1)}, u32[]{:S(2)}, u32[]{:S(2)}) collective-permute-start(bf16[152,384]{1,0:T(8,128)(2,1)} %add.111.refs_0_), channel_id=1, source_target_pairs={{0,2},{1,3},{2,0},{3,1},{4,6},{5,7},{6,4},{7,5},{8,10},{9,11},{10,... | collective-permute-start | bytes 350216 | tf_op jit(solution)/shard_map/ppermute | solution.py:650
  125.8 7.7 %collective-permute-start.19 = (bf16[152,384]{1,0:T(8,128)(2,1)}, bf16[152,384]{1,0:T(8,128)(2,1)}, u32[]{:S(2)}, u32[]{:S(2)}) collective-permute-start(bf16[152,384]{1,0:T(8,128)(2,1)} %add.111.refs_0_), channel_id=1, source_target_pairs={{0,4},{1,5},{2,6},{3,7},{4,0},{5,1},{6,2},{7,3},{8,12},{9,13},{10,... | collective-permute-start | bytes 350216 | tf_op jit(solution)/shard_map/ppermute | solution.py:650
  127.4 0.7 copy-start.5

commit v9 on v6

--- a/solution.py
+++ b/solution.py
@@ -77,14 +77,14 @@
     return jnp.where(first, v[:rows], v[rows:])
 
 
-def join_pieces(full, own, near, far, index):
+def join_pieces(full, own, near, far, index, first=0):
     block = own.shape[0]
     half = block // 2
     x, core = index[0], index[1]
     other = (1 - x) * block
     full[pl.ds(pl.multiple_of(x * block, 16), block), :] = own[...]
-    full[pl.ds(pl.multiple_of(other + core * half, 16), half), :] = near[0:half, :]
-    full[pl.ds(pl.multiple_of(other + (1 - core) * half, 16), half), :] = far[0:half, :]
+    full[pl.ds(pl.multiple_of(other + core * half, 16), half), :] = near[first : first + half, :]
+    full[pl.ds(pl.multiple_of(other + (1 - core) * half, 16), half), :] = far[first : first + half, :]
 
 
 def quarters(index, keep, send):
@@ -109,10 +109,12 @@
         packed[half + k : half + k + 1, width : 2 * width] = bias[:, k * width : (k + 1) * width]
 
 
-def pack_rest_kernel(index, *refs):
-    for weight, half_out in zip(refs[:3], refs[3:]):
-        half = half_out.shape[0]
-        half_out[...] = weight[pl.ds(pl.multiple_of(index[1] * half, 16), half), :]
+def pack_rest_kernel(index, out_own, lift_own, drop_own, lift_half, both_half):
+    tall, deep = lift_half.shape[0], drop_own.shape[0] // 2
+    rows_of = pl.ds(pl.multiple_of(index[1] * tall, 16), tall)
+    lift_half[...] = lift_own[rows_of, :]
+    both_half[0:deep, :] = drop_own[pl.ds(pl.multiple_of(index[1] * deep, 16), deep), :]
+    both_half[deep:, :] = out_own[rows_of, :]
 
 
 def join_vectors(vec_ref, own, other, index):
@@ -181,14 +183,12 @@
     mixed_ref,
     vec_ref,
     out_own,
-    out_near,
-    out_far,
     lift_own,
+    drop_own,
     lift_near,
     lift_far,
-    drop_own,
-    drop_near,
-    drop_far,
+    both_near,
+    both_far,
     out_ref,
     d_middle_ref,
     d_mixed_ref,
@@ -215,9 +215,10 @@
     def _():
         zero_tail(x_s, length)
         zero_tail(z_s, length)
-        join_pieces(w_out_ref, out_own, out_near, out_far, index)
+        deep = drop_own.shape[0] // 2
+        join_pieces(w_out_ref, out_own, both_near, both_far, index, deep)
         join_pieces(w_lift_ref, lift_own, lift_near, lift_far, index)
-        join_pieces(w_drop_ref, drop_own, drop_near, drop_far, index)
+        join_pieces(w_drop_ref, drop_own, both_near, both_far, index)
         for k in range(hidden_width // width):
             lift_bias_ref[:, k * width : (k + 1) * width] = vec_ref[8 + k : 9 + k, :]
         for acc in (a_drop, a_lift, a_out, a_vec, a_bias):
@@ -362,19 +363,18 @@
             place[3 * small :, :] = vectors
 
 
-def placed(full, index, pieces, by_z=False):
-    core, y = index[1], index[2]
+def placed(full, index, pieces):
+    core, y, z = index[1], index[2], index[3]
+    rows = pieces[0].shape[0]
     spots = ((core, y), (core, 1 - y), (1 - core, y), (1 - core, 1 - y))
-    rows = pieces[0].shape[0]
-    for (owner, side), piece in zip(spots, pieces):
-        if by_z:
-            half = rows // 2
-            for k, z in ((0, index[3]), (1, 1 - index[3])):
-                full[owner, side, pl.ds(pl.multiple_of(z * half, 8), half), :] = piece[
-                    k * half : (k + 1) * half, :
-                ].astype(F32)
-        else:
+    if len(pieces) == 4:
+        for (owner, side), piece in zip(spots, pieces):
             full[owner, side] = piece[...].astype(F32)
+        return
+    for i, (owner, side) in enumerate(spots):
+        for piece, part in ((pieces[2 * i], z), (pieces[2 * i + 1], 1 - z)):
+            place = pl.ds(pl.multiple_of(part * rows, 8), rows)
+            full[owner, side, place, :] = piece[...].astype(F32)
 
 
 def own_half(index, row):
@@ -383,13 +383,13 @@
 
 
 def unpack_kernel(index, *refs):
-    unpack_outer(index, refs[0:4], refs[8:16], refs[21])
-    unpack_inner(index, refs[4:8], refs[16:21], refs[22])
+    unpack_outer(index, refs[0:8], refs[12:20], refs[25])
+    unpack_inner(index, refs[8:12], refs[20:25], refs[26])
 
 
 def unpack_outer(index, pieces, outs, full):
     g_drop, g_lift, g_out, g_out_bias, g_gain, g_shift, g_drop_bias, g_lift_bias = outs
-    placed(full, index, pieces, by_z=True)
+    placed(full, index, pieces)
     width = g_out.shape[1]
     deep, tall, small = g_drop.shape[0] // 2, width // 4, width // 8
     blocks = g_lift.shape[1] // width
@@ -471,12 +471,15 @@
 
 
 def pack_rest(index, weights):
+    out_weight, lift_weight, drop_weight = weights
+    tall, width = out_weight.shape[0] // 2, out_weight.shape[1]
+    shapes = [(tall, lift_weight.shape[1]), (drop_weight.shape[0] // 2 + tall, width)]
     return pl.pallas_call(
         pack_rest_kernel,
         grid=(1,),
         in_specs=[SCALARS, *whole_like(weights)],
-        out_specs=[whole(w.shape[0] // 2, w.shape[1]) for w in weights],
-        out_shape=[shape_of(BF16, w.shape[0] // 2, w.shape[1]) for w in weights],
+        out_specs=[whole(*d) for d in shapes],
+        out_shape=[shape_of(BF16, *d) for d in shapes],
         compiler_params=PARAMS,
         cost_estimate=cost(1),
         name="pack_rest",
@@ -602,6 +605,7 @@
 
 
 def unpack(index, outer, inner, shapes):
+    rows, width = outer[0].shape
     return pl.pallas_call(
         unpack_kernel,
         grid=(1,),
@@ -609,7 +613,7 @@
         out_specs=[whole(*d) for d in shapes],
         out_shape=[shape_of(F32, *d) for d in shapes],
         scratch_shapes=[
-            pltpu.VMEM((2, 2) + outer[0].shape, F32),
+            pltpu.VMEM((2, 2, 2 * rows, width), F32),
             pltpu.VMEM((2, 2) + inner[0].shape, F32),
         ],
         compiler_params=PARAMS,
@@ -647,9 +651,6 @@
 
     def over_corner(self, v):
         return self.swap(v, 2, 1)
-
-    def over_y_and_core(self, v):
-        return self.swap(v, 3)
 
     def half(self, v, which):
         rows = v.shape[0] // 2
@@ -742,7 +743,8 @@
     rest = (out_weight, lift_weight, drop_weight)
     if swaps:
         packed = pack_first(index, small, lift_bias, qkv_weight)
-        near = plan.over_x(packed)
+        tokens = with_layout_constraint(tokens, Layout(major_to_minor=(0, 1, 2)))
+        near = behind(plan.over_x(packed), tokens)
         qkv = (qkv_weight, near, plan.over_core(near))
         rest_then, packed = after(rest, packed)
         nears = [plan.over_x(half) for half in pack_rest(index, rest_then)]
@@ -755,11 +757,12 @@
     )
     if swaps:
         mixed, nears = after(mixed, nears)
-        outer = [
-            piece for w, near in zip(rest, nears) for piece in (w, near, plan.over_core(near))
-        ]
+        pieces = [piece for near in nears for piece in (near, plan.over_core(near))]
     else:
-        outer = [piece for w in rest for piece in plan.gather_weight(w)]
+        (out_own, *outs), (lift_own, *lifts), (drop_own, *drops) = map(plan.gather_weight, rest)
+        rest = (out_own, lift_own, drop_own)
+        pieces = [*lifts, *(jnp.concatenate(both) for both in zip(drops, outs))]
+    outer = (*rest, *pieces)
     output, d_middle, d_mixed, keep_a, send_a = mlp_both_ways(
         index, tokens, cotangent, mixed, vectors, ff, outer
     )
@@ -790,23 +793,33 @@
         over_a = plan.over_z(low_a, 2)
         more_c = behind(more_c, low_a)
         sum_c = stay_c + more_c[0] + more_c[1] + more_c[2]
-        over_a = behind(over_a, sum_c)
         over_c = plan.over_z(sum_c, 1)
-        low_a = low_a + over_a
-        over_a = plan.over_z(low_a, 1)
-        over_c = behind(over_c, low_a)
+        over_a, over_c = after(over_a, over_c)
+        low_a, sum_c = after(low_a + over_a, sum_c + over_c)
+        high_a, over_c = plan.over_z(low_a, 1), plan.over_z(sum_c, 2)
+        across_low, beside_low = plan.over_y(low_a), plan.over_core(low_a)
+        output, input_grad = settled(output), settled(input_grad)
+        high_a, over_c, across_low, beside_low, output, input_grad = after(
+            high_a, over_c, across_low, beside_low, output, input_grad
+        )
+        output, input_grad = output.transpose(1, 0, 2), input_grad.transpose(1, 0, 2)
+        across_high, beside_high = plan.over_y(high_a), plan.over_core(high_a)
+        corner_low = plan.over_core(across_low)
         sum_c = sum_c + over_c
-        over_a = behind(over_a, sum_c)
-        over_c = plan.over_z(sum_c, 2)
-        sum_a = jnp.concatenate([low_a, over_a])
-        across_a, beside_a = plan.over_y(sum_a), plan.over_core(sum_a)
-        output, input_grad = settled(output), settled(input_grad)
-        over_c, output, input_grad = behind((over_c, output, input_grad), sum_a)
-        output, input_grad = output.transpose(1, 0, 2), input_grad.transpose(1, 0, 2)
-        sum_c = sum_c + over_c
-        across_a = behind(across_a, sum_c)
-        pieces_c = (sum_c, plan.over_y(sum_c), plan.over_core(sum_c), plan.over_y_and_core(sum_c))
-        pieces_a = (sum_a, across_a, beside_a, plan.over_core(across_a))
+        across_c, beside_c = plan.over_y(sum_c), plan.over_core(sum_c)
+        across_high, across_c, beside_c = after(across_high, across_c, beside_c)
+        pieces_c = (sum_c, across_c, beside_c, plan.over_core(across_c))
+        pieces_a = (
+            low_a,
+            high_a,
+            across_low,
+            across_high,
+            beside_low,
+            beside_high,
+            corner_low,
+            plan.over_core(across_high),
+        )
+        pieces_a, pieces_c = after(pieces_a, pieces_c)
         (
             g_drop,
             g_lift,

time: 136 us -> 131 us (0.963)
  waiting for transfers between devices: 26.6 us -> 23 us
  starting transfers between devices: 28.9 us -> 27.3 us
    ppermute x27 -> x28, waiting for transfers between devices: 26.6 us -> 23 us  [swap(): return lax.ppermute(v, AXES, pairs)]
    ppermute x27 -> x28, starting transfers between devices: 28.9 us -> 27.3 us  [swap(): return lax.ppermute(v, AXES, pairs)]
    unnamed x46 -> x50, local copies, waits for them, and re-layouts: 5.4 us -> 5.2 us
  transfers between devices with their start and end apart: 27 -> 28, of which waited for: 10 -> 13; matrix products, arithmetic and copies ran while one was open for 5% -> 5% of each run, Pallas kernels for 27% -> 28%
where the time goes in v9:
time: 131 us
  Pallas kernels  69.2 us (53%)
  starting transfers between devices  27.3 us (21%)
  waiting for transfers between devices  23 us (18%)
  local copies, waits for them, and re-layouts  7.62 us (6%)
  other arithmetic  2.36 us (2%)
    pallas_call x1, Pallas kernels, mlp_both_ways(): pl.pallas_call(functools.partial(mlp_kernel, length, 512), grid=(images /...  27.4 us
    ppermute x28, starting transfers between devices, swap(): return lax.ppermute(v, AXES, pairs)  27.3 us
    pallas_call x2, Pallas kernels, attention_backward(): pl.pallas_call(functools.partial(back_kernel, length, first, last), grid=...  24.1 us
    ppermute x28, waiting for transfers between devices, swap(): return lax.ppermute(v, AXES, pairs)  23 us
    pallas_call x1, Pallas kernels, forward_attention(): pl.pallas_call(functools.partial(attend_kernel, length), grid=(images //...  9.91 us
    unnamed x50, local copies, waits for them, and re-layouts  5.2 us
    pallas_call x1, Pallas kernels, unpack(): pl.pallas_call(unpack_kernel, grid=(1,), in_specs=[SCALARS, *whole_like((...  3.7 us
  transfers between devices with their start and end apart: 28, of which 13 were waited for; matrix products, arithmetic and copies ran while one was open for 5% of the time, Pallas kernels for 28%

profile of v9, /device:TPU:0, one launch (start us, length us, event | category | flops | bytes accessed | tf_op | source)
XLA Modules:
  0.0 130.6 jit_solution(13617085016240704887)
XLA Ops:
  0.7 0.7 pad_add_fusion.index
  1.3 1.9 %pack_first.1.packed = bf16[104,1152]{1,0:T(8,128)(2,1)} custom-call(s32[4]{0:T(128)} %pad_add_fusion.index, bf16[192]{0:T(256)(128)(2,1)} %refs_0_.1, bf16[192]{0:T(256)(128)(2,1)} %refs_1_.1, bf16[192]{0:T(256)(128)(2,1)} %refs_2_.1, bf16[192]{0:T(256)(128)(2,1)} %refs_3_.1, bf16[192]{0:T(256)(128)(2,1)} %refs_4_.1, bf16[192]{0:T(256)(128)(2,1)} %refs_5_.1, ...), custom_call_target="tpu_custom_call" | custom-call | flops 1000 | bytes 1 | tf_op jit(solution)/shard_map/pack_first/pallas_call | solution.py:461
  3.2 2.9 %collective-permute-start = (bf16[104,1152]{1,0:T(8,128)(2,1)}, bf16[104,1152]{1,0:T(8,128)(2,1)S(1)}, u32[]{:S(2)}, u32[]{:S(2)}) collective-permute-start(bf16[104,1152]{1,0:T(8,128)(2,1)} %pack_first.1.packed), channel_id=1, source_target_pairs={{0,1},{1,0},{2,3},{3,2},{4,5},{5,4},{6,7},{7,6},{8,9},{9,8},{10,11... | collective-permute-start | bytes 718856 | tf_op jit(solution)/shard_map/ppermute | solution.py:638
  6.1 2.2 %pack_rest.1 = (bf16[96,1536]{1,0:T(8,128)(2,1)}, bf16[480,384]{1,0:T(8,128)(2,1)}) custom-call(s32[4]{0:T(128)} %pad_add_fusion.index, bf16[192,384]{1,0:T(8,128)(2,1)} %out_own.2, bf16[192,1536]{1,0:T(8,128)(2,1)} %lift_own.2, bf16[768,384]{1,0:T(8,128)(2,1)} %drop_own.2), custom_call_target="tpu_custom_call" | custom-call | flops 1000 | bytes 1 | tf_op jit(solution)/shard_map/pack_rest/pallas_call | solution.py:477
  8.3 0.0 collective-permute-start.3
  8.3 2.0 %collective-permute-start.2 = (bf16[96,1536]{1,0:T(8,128)(2,1)}, bf16[96,1536]{1,0:T(8,128)(2,1)S(1)}, u32[]{:S(2)}, u32[]{:S(2)}) collective-permute-start(bf16[96,1536]{1,0:T(8,128)(2,1)} %get-tuple-element.105), channel_id=1, source_target_pairs={{0,1},{1,0},{2,3},{3,2},{4,5},{5,4},{6,7},{7,6},{8,9},{9,8},{10,11... | collective-permute-start | bytes 884744 | tf_op jit(solution)/shard_map/ppermute | solution.py:638
  10.4 1.2 copy.31.tok_ref
  11.5 1.5 %collective-permute-done.near = bf16[104,1152]{1,0:T(8,128)(2,1)S(1)} collective-permute-done((bf16[104,1152]{1,0:T(8,128)(2,1)}, bf16[104,1152]{1,0:T(8,128)(2,1)S(1)}, u32[]{:S(2)}, u32[]{:S(2)}) %collective-permute-start) | collective-permute-done | bytes 239648 | tf_op jit(solution)/shard_map/ppermute | solution.py:638
  13.0 1.5 %collective-permute-done.1.far = bf16[104,1152]{1,0:T(8,128)(2,1)S(1)} collective-permute-done((bf16[104,1152]{1,0:T(8,128)(2,1)S(1)}, bf16[104,1152]{1,0:T(8,128)(2,1)S(1)}, u32[]{:S(2)}, u32[]{:S(2)}) %collective-permute-start.1) | collective-permute-done | bytes 239648 | tf_op jit(solution)/shard_map/ppermute | solution.py:638
  14.5 0.7 copy-done.13
  15.2 9.9 %attend.1 = (bf16[8,208,384]{2,1,0:T(8,128)(2,1)}, bf16[8,208,1152]{2,1,0:T(8,128)(2,1)}, bf16[8,208,384]{2,1,0:T(8,128)(2,1)}, bf16[384,1152]{1,0:T(8,128)(2,1)}, f32[12,384]{1,0:T(8,128)}) custom-call(s32[4]{0:T(128)} %pad_add_fusion.index, bf16[8,197,384]{2,1,0:T(8,128)(2,1)} %copy.31.tok_ref, bf16[104,1152]{1,0:T(8,128)(2,1)} %pack_first.1.packed, ...), custom_call_target="tpu_custom_call" | custom-call | flops 1000 | bytes 1 | tf_op jit(solution)/shard_map/attend/pallas_call | solution.py:493
  25.1 1.3 collective-permute-done.2.lift_near
  26.4 0.0 collective-permute-done.3.both_near
  26.4 0.1 collective-permute-start.5
  26.5 0.5 collective-permute-start.4
  27.0 1.2 copy.32.cot_ref
  28.2 0.4 collective-permute-done.4.lift_far
  28.6 0.0 collective-permute-done.5.both_far
  28.6 0.7 copy-done.11
  29.3 0.1 copy-done.9
  29.4 27.4 %mlp.1 = (bf16[8,197,384]{2,1,0:T(8,128)(2,1)}, f32[8,208,384]{2,1,0:T(8,128)}, bf16[8,208,384]{2,1,0:T(8,128)(2,1)}, bf16[2,2,448,384]{3,2,1,0:T(8,128)(2,1)}, bf16[2,2,448,384]{3,2,1,0:T(8,128)(2,1)}) custom-call(s32[4]{0:T(128)} %pad_add_fusion.index, bf16[8,197,384]{2,1,0:T(8,128)(2,1)} %copy.31.tok_ref, bf16[8,197,384]{2,1,0:T(8,128)(2,1)} %copy.32.cot_ref, ...), custom_call_target="tpu_custom_call" | custom-call | flops 1000 | bytes 1 | tf_op jit(solution)/shard_map/mlp/pallas_call | solution.py:523
  56.8 0.2 collective-permute-start.6
  57.0 7.0 %back.2 = (bf16[8,197,384]{2,1,0:T(8,128)(2,1)}, f32[384,1152]{1,0:T(8,128)}, f32[8,1152]{1,0:T(8,128)}, f32[2,384]{1,0:T(2,128)}) custom-call(s32[4]{0:T(128)} %pad_add_fusion.index, bf16[8,197,384]{2,1,0:T(8,128)(2,1)} %copy.31.tok_ref, bf16[8,208,1152]{2,1,0:T(8,128)(2,1)} %get-tuple-element.112.proj_ref, ...), custom_call_target="tpu_custom_call" | custom-call | flops 1000 | bytes 1 | tf_op jit(solution)/shard_map/back/pallas_call | solution.py:581
  64.0 0.1 add_bitcast_fusion
  64.2 1.8 %collective-permute-start.7 = (bf16[448,384]{1,0:T(8,128)(2,1)S(1)}, bf16[448,384]{1,0:T(8,128)(2,1)}, u32[]{:S(2)}, u32[]{:S(2)}) collective-permute-start(bf16[448,384]{1,0:T(8,128)(2,1)S(1)} %get-tuple-element.130), channel_id=1, source_target_pairs={{0,1},{1,0},{2,3},{3,2},{4,5},{5,4},{6,7},{7,6},{8,9},{9,8},{10,11... | collective-permute-start | bytes 1032200 | tf_op jit(solution)/shard_map/ppermute | solution.py:638
  66.0 1.5 %collective-permute-start.8 = (bf16[448,384]{1,0:T(8,128)(2,1)S(1)}, bf16[448,384]{1,0:T(8,128)(2,1)}, u32[]{:S(2)}, u32[]{:S(2)}) collective-permute-start(bf16[448,384]{1,0:T(8,128)(2,1)S(1)} %get-tuple-element.131), channel_id=1, source_target_pairs={{0,4},{1,5},{2,6},{3,7},{4,0},{5,1},{6,2},{7,3},{8,12},{9,13},{10,... | collective-permute-start | bytes 1032200 | tf_op jit(solution)/shard_map/ppermute | solution.py:638
  67.5 0.2 collective-permute-start.9
  67.7 17.1 %back.3 = (bf16[8,197,384]{2,1,0:T(8,128)(2,1)}, bf16[2,2,152,384]{3,2,1,0:T(8,128)(2,1)}, bf16[2,2,152,384]{3,2,1,0:T(8,128)(2,1)}) custom-call(s32[4]{0:T(128)} %pad_add_fusion.index, bf16[8,197,384]{2,1,0:T(8,128)(2,1)} %copy.31.tok_ref, bf16[8,208,1152]{2,1,0:T(8,128)(2,1)} %get-tuple-element.112.proj_ref, ...), custom_call_target="tpu_custom_call", output_to_operand_aliasing={{0}: (11, {})} | custom-call | flops 1000 | bytes 1 | tf_op jit(solution)/shard_map/back/pallas_call | solution.py:581
  84.9 0.1 collective-permute-start.11
  85.0 0.0 copy-start.6
  85.0 1.3 %fusion.1 = bf16[448,384]{1,0:T(8,128)(2,1)S(1)} fusion(bf16[448,384]{1,0:T(8,128)(2,1)} %collective-permute-done.9, bf16[448,384]{1,0:T(8,128)(2,1)} %collective-permute-done.8, bf16[448,384]{1,0:T(8,128)(2,1)} %collective-permute-done.7, bf16[2,2,448,384]{3,2,1,0:T(8,128)(2,1)S(1)} %collective-permute-done.6, bf16[2,2,448,384]{3,2,1,0:T(8,128)(2,1)S(1)} %copy-done.1), kind=kLoop, calls=%fused_computation.4 | loop fusion | flops 688128 | bytes 2064384 | tf_op jit(solution)/shard_map/add | solution.py:785
  86.3 0.1 constant_dynamic-slice_fusion
  86.4 1.9 %collective-permute-start.10 = (bf16[224,384]{1,0:T(8,128)(2,1)S(1)}, bf16[224,384]{1,0:T(8,128)(2,1)S(1)}, u32[]{:S(2)}, u32[]{:S(2)}) collective-permute-start(bf16[224,384]{1,0:T(8,128)(2,1)S(1)} %get-tuple-element.189), channel_id=1, source_target_pairs={{0,8},{1,9},{2,10},{3,11},{4,12},{5,13},{6,14},{7,15},{8,0},{9,1},... | collective-permute-start | bytes 516104 | tf_op jit(solution)/shard_map/ppermute | solution.py:638
  88.3 0.1 add_bitcast_fusion.3
  88.3 2.5 %collective-permute-start.15 = (bf16[152,384]{1,0:T(8,128)(2,1)S(1)}, bf16[152,384]{1,0:T(8,128)(2,1)S(1)}, u32[]{:S(2)}, u32[]{:S(2)}) collective-permute-start(bf16[152,384]{1,0:T(8,128)(2,1)S(1)} %get-tuple-element.186), channel_id=1, source_target_pairs={{0,5},{1,4},{2,7},{3,6},{4,1},{5,0},{6,3},{7,2},{8,13},{9,12},{10,... | collective-permute-start | bytes 350216 | tf_op jit(solution)/shard_map/ppermute | solution.py:638
  90.9 0.5 collective-permute-start.14
  91.4 0.5 collective-permute-start.13
  91.9 1.4 %collective-permute-done.10 = bf16[224,384]{1,0:T(8,128)(2,1)S(1)} collective-permute-done((bf16[224,384]{1,0:T(8,128)(2,1)S(1)}, bf16[224,384]{1,0:T(8,128)(2,1)S(1)}, u32[]{:S(2)}, u32[]{:S(2)}) %collective-permute-start.10) | collective-permute-done | bytes 172064 | tf_op jit(solution)/shard_map/ppermute | solution.py:638
  93.3 2.8 %collective-permute-start.12 = (bf16[224,384]{1,0:T(8,128)(2,1)S(1)}, bf16[224,384]{1,0:T(8,128)(2,1)S(1)}, u32[]{:S(2)}, u32[]{:S(2)}) collective-permute-start(bf16[224,384]{1,0:T(8,128)(2,1)S(1)} %add.103), channel_id=1, source_target_pairs={{0,16},{1,17},{2,18},{3,19},{4,20},{5,21},{6,22},{7,23},{8,24},{9,... | collective-permute-start | bytes 516104 | tf_op jit(solution)/shard_map/ppermute | solution.py:638
  96.2 0.9 collective-permute-done.14
  97.1 0.1 collective-permute-done.13
  97.2 0.1 fusion.3
  97.2 0.6 collective-permute-start.16
  97.9 6.3 %collective-permute-done.12 = bf16[224,384]{1,0:T(8,128)(2,1)S(1)} collective-permute-done((bf16[224,384]{1,0:T(8,128)(2,1)S(1)}, bf16[224,384]{1,0:T(8,128)(2,1)S(1)}, u32[]{:S(2)}, u32[]{:S(2)}) %collective-permute-start.12) | collective-permute-done | bytes 172064 | tf_op jit(solution)/shard_map/ppermute | solution.py:638
  104.2 0.7 collective-permute-done.16
  105.0 0.1 collective-permute-start.20
  105.1 1.6 %collective-permute-start.19 = (bf16[224,384]{1,0:T(8,128)(2,1)S(1)}, bf16[224,384]{1,0:T(8,128)(2,1)S(1)}, u32[]{:S(2)}, u32[]{:S(2)}) collective-permute-start(bf16[224,384]{1,0:T(8,128)(2,1)S(1)} %add.109.refs_0_), channel_id=1, source_target_pairs={{0,4},{1,5},{2,6},{3,7},{4,0},{5,1},{6,2},{7,3},{8,12},{9,13},{10,... | collective-permute-start | bytes 516104 | tf_op jit(solution)/shard_map/ppermute | solution.py:638
  106.7 4.1 %collective-permute-start.18 = (bf16[152,384]{1,0:T(8,128)(2,1)S(1)}, bf16[152,384]{1,0:T(8,128)(2,1)S(1)}, u32[]{:S(2)}, u32[]{:S(2)}) collective-permute-start(bf16[152,384]{1,0:T(8,128)(2,1)S(1)} %add.110), channel_id=1, source_target_pairs={{0,16},{1,17},{2,18},{3,19},{4,20},{5,21},{6,22},{7,23},{8,24},{9,... | collective-permute-start | bytes 350216 | tf_op jit(solution)/shard_map/ppermute | solution.py:638
  110.8 1.2 copy.38
  112.0 1.2 copy.37
  113.1 1.0 collective-permute-done.18
  114.1 1.5 %collective-permute-done.17.refs_1_ = bf16[224,384]{1,0:T(8,128)(2,1)S(1)} collective-permute-done((bf16[224,384]{1,0:T(8,128)(2,1)S(1)}, bf16[224,384]{1,0:T(8,128)(2,1)S(1)}, u32[]{:S(2)}, u32[]{:S(2)}) %collective-permute-start.17) | collective-permute-done | bytes 172064 | tf_op jit(solution)/shard_map/ppermute | solution.py:638
  115.6 0.5 collective-permute-start.21
  116.1 0.1 collective-permute-start.23
  116.2 1.6 %collective-permute-start.22 = (bf16[152,384]{1,0:T(8,128)(2,1)S(1)}, bf16[152,384]{1,0:T(8,128)(2,1)S(1)}, u32[]{:S(2)}, u32[]{:S(2)}) collective-permute-start(bf16[152,384]{1,0:T(8,128)(2,1)S(1)} %add.111.refs_8_), channel_id=1, source_target_pairs={{0,4},{1,5},{2,6},{3,7},{4,0},{5,1},{6,2},{7,3},{8,12},{9,13},{10,... | collective-permute-start | bytes 350216 | tf_op jit(solution)/shard_map/ppermute | solution.py:638
  117.9 0.2 collective-permute-start.24
  118.0 0.3 collective-permute-start.25
  118.4 5.4 %collective-permute-done.22.refs_9_ = bf16[152,384]{1,0:T(8,128)(2,1)S(1)} collective-permute-done((bf16[152,384]{1,0:T(8,128)(2,1)S(1)}, bf16[152,384]{1,0:T(8,128)(2,1)S(1)}, u32[]{:S(2)}, u32[]{:S(2)}) %collective-permute-start.22) | collective-permute-done | bytes 116768 | tf_op jit(solution)/shard_map/ppermute | solution.py:638
  123.8 0.1 collective-permute-start.26
  123.8 0.5 collective-permute-start.27
  124.4 1.0 collective-permute-done.27.refs_11_
  125.5 0.6 copy-done.23
  126.0 0.7 copy-done.20
  126.7 3.7 %unpack.1 = (f32[768,384]{1,0:T(8,128)}, f32[192,1536]{1,0:T(8,128)}, f32[192,384]{1,0:T(8,128)}, f32[192]{0:T(256)}, f32[192]{0:T(256)}, /*index=5*/f32[192]{0:...) custom-call(s32[4]{0:T(128)} %pad_add_fusion.index, ...), custom_call_target="tpu_custom_call" | custom-call | flops 1000 | bytes 1 | tf_op jit(solution)/shard_map/unpack/pallas_call | solution.py:609
  (61 shorter events, 0.3 us)
Async XLA Ops:
  0.6 9.7 %copy-start.3 = (bf16[8,197,384]{2,0,1:T(8,128)(2,1)S(1)}, bf16[8,197,384]{2,0,1:T(8,128)(2,1)}, u32[]{:S(2)}) copy-start(bf16[8,197,384]{2,0,1:T(8,128)(2,1)} %param.15) | copy-start | bytes 3631108
  3.2 9.8 %collective-permute-start = (bf16[104,1152]{1,0:T(8,128)(2,1)}, bf16[104,1152]{1,0:T(8,128)(2,1)S(1)}, u32[]{:S(2)}, u32[]{:S(2)}) collective-permute-start(bf16[104,1152]{1,0:T(8,128)(2,1)} %pack_first.1.packed), channel_id=1, source_target_pairs={{0,1},{1,0},{2,3},{3,2},{4,5},{5,4},{6,7},{7,6},{8,9},{9,8},{10,11... | collective-permute-start | bytes 718856 | tf_op jit(solution)/shard_map/ppermute | solution.py:638
  8.3 18.1 %collective-permute-start.3 = (bf16[480,384]{1,0:T(8,128)(2,1)}, bf16[480,384]{1,0:T(8,128)(2,1)S(1)}, u32[]{:S(2)}, u32[]{:S(2)}) collective-permute-start(bf16[480,384]{1,0:T(8,128)(2,1)} %get-tuple-element.106), channel_id=1, source_target_pairs={{0,1},{1,0},{2,3},{3,2},{4,5},{5,4},{6,7},{7,6},{8,9},{9,8},{10,11... | collective-permute-start | bytes 1105928 | tf_op jit(solution)/shard_map/ppermute | solution.py:638
  8.3 18.1 %collective-permute-start.2 = (bf16[96,1536]{1,0:T(8,128)(2,1)}, bf16[96,1536]{1,0:T(8,128)(2,1)S(1)}, u32[]{:S(2)}, u32[]{:S(2)}) collective-permute-start(bf16[96,1536]{1,0:T(8,128)(2,1)} %get-tuple-element.105), channel_id=1, source_target_pairs={{0,1},{1,0},{2,3},{3,2},{4,5},{5,4},{6,7},{7,6},{8,9},{9,8},{10,11... | collective-permute-start | bytes 884744 | tf_op jit(solution)/shard_map/ppermute | solution.py:638
  11.5 15.4 %copy-start.4 = (bf16[8,197,384]{2,0,1:T(8,128)(2,1)S(1)}, bf16[8,197,384]{2,0,1:T(8,128)(2,1)}, u32[]{:S(2)}) copy-start(bf16[8,197,384]{2,0,1:T(8,128)(2,1)} %param.29) | copy-start | bytes 3631108
  13.0 1.5 %copy-start.12 = (bf16[104,1152]{1,0:T(8,128)(2,1)}, bf16[104,1152]{1,0:T(8,128)(2,1)S(1)}, u32[]{:S(2)}) copy-start(bf16[104,1152]{1,0:T(8,128)(2,1)S(1)} %collective-permute-done.near) | copy-start | bytes 718852
  13.0 1.5 %collective-permute-start.1 = (bf16[104,1152]{1,0:T(8,128)(2,1)S(1)}, bf16[104,1152]{1,0:T(8,128)(2,1)S(1)}, u32[]{:S(2)}, u32[]{:S(2)}) collective-permute-start(bf16[104,1152]{1,0:T(8,128)(2,1)S(1)} %collective-permute-done.near), channel_id=1, source_target_pairs={{0,2},{1,3},{2,0},{3,1},{4,6},{5,7},{6,4},{7,5},{8,10},{9,11},{10,... | collective-permute-start | bytes 718856 | tf_op jit(solution)/shard_map/ppermute | solution.py:638
  14.5 0.7 copy-start.13
  26.4 2.2 %copy-start.10 = (bf16[96,1536]{1,0:T(8,128)(2,1)}, bf16[96,1536]{1,0:T(8,128)(2,1)S(1)}, u32[]{:S(2)}) copy-start(bf16[96,1536]{1,0:T(8,128)(2,1)S(1)} %collective-permute-done.2.lift_near) | copy-start | bytes 884740
  26.4 2.2 %copy-start.8 = (bf16[480,384]{1,0:T(8,128)(2,1)}, bf16[480,384]{1,0:T(8,128)(2,1)S(1)}, u32[]{:S(2)}) copy-start(bf16[480,384]{1,0:T(8,128)(2,1)S(1)} %collective-permute-done.3.both_near) | copy-start | bytes 1105924
  26.4 2.2 %collective-permute-start.5 = (bf16[480,384]{1,0:T(8,128)(2,1)S(1)}, bf16[480,384]{1,0:T(8,128)(2,1)S(1)}, u32[]{:S(2)}, u32[]{:S(2)}) collective-permute-start(bf16[480,384]{1,0:T(8,128)(2,1)S(1)} %collective-permute-done.3.both_near), channel_id=1, source_target_pairs={{0,2},{1,3},{2,0},{3,1},{4,6},{5,7},{6,4},{7,5},{8,10},{9,11},{10,... | collective-permute-start | bytes 1105928 | tf_op jit(solution)/shard_map/ppermute | solution.py:638
  26.5 2.1 %collective-permute-start.4 = (bf16[96,1536]{1,0:T(8,128)(2,1)S(1)}, bf16[96,1536]{1,0:T(8,128)(2,1)S(1)}, u32[]{:S(2)}, u32[]{:S(2)}) collective-permute-start(bf16[96,1536]{1,0:T(8,128)(2,1)S(1)} %collective-permute-done.2.lift_near), channel_id=1, source_target_pairs={{0,2},{1,3},{2,0},{3,1},{4,6},{5,7},{6,4},{7,5},{8,10},{9,11},{10,... | collective-permute-start | bytes 884744 | tf_op jit(solution)/shard_map/ppermute | solution.py:638
  28.6 0.7 copy-start.11
  28.6 0.8 copy-start.9
  56.8 7.2 %collective-permute-start.6 = (bf16[2,2,448,384]{3,2,1,0:T(8,128)(2,1)}, bf16[2,2,448,384]{3,2,1,0:T(8,128)(2,1)S(1)}, u32[]{:S(2)}, u32[]{:S(2)}) collective-permute-start(bf16[2,2,448,384]{3,2,1,0:T(8,128)(2,1)} %get-tuple-element.120), channel_id=1, source_target_pairs={{0,2},{1,3},{2,0},{3,1},{4,6},{5,7},{6,4},{7,5},{8,10},{9,11},{10,... | collective-permute-start | bytes 4128776 | tf_op jit(solution)/shard_map/ppermute | solution.py:638
  57.0 7.0 %copy-start.1 = (bf16[2,2,448,384]{3,2,1,0:T(8,128)(2,1)S(1)}, bf16[2,2,448,384]{3,2,1,0:T(8,128)(2,1)}, u32[]{:S(2)}) copy-start(bf16[2,2,448,384]{3,2,1,0:T(8,128)(2,1)} %get-tuple-element.111) | copy-start | bytes 4128772
  64.2 20.7 %collective-permute-start.7 = (bf16[448,384]{1,0:T(8,128)(2,1)S(1)}, bf16[448,384]{1,0:T(8,128)(2,1)}, u32[]{:S(2)}, u32[]{:S(2)}) collective-permute-start(bf16[448,384]{1,0:T(8,128)(2,1)S(1)} %get-tuple-element.130), channel_id=1, source_target_pairs={{0,1},{1,0},{2,3},{3,2},{4,5},{5,4},{6,7},{7,6},{8,9},{9,8},{10,11... | collective-permute-start | bytes 1032200 | tf_op jit(solution)/shard_map/ppermute | solution.py:638
  66.0 18.9 %collective-permute-start.8 = (bf16[448,384]{1,0:T(8,128)(2,1)S(1)}, bf16[448,384]{1,0:T(8,128)(2,1)}, u32[]{:S(2)}, u32[]{:S(2)}) collective-permute-start(bf16[448,384]{1,0:T(8,128)(2,1)S(1)} %get-tuple-element.131), channel_id=1, source_target_pairs={{0,4},{1,5},{2,6},{3,7},{4,0},{5,1},{6,2},{7,3},{8,12},{9,13},{10,... | collective-permute-start | bytes 1032200 | tf_op jit(solution)/shard_map/ppermute | solution.py:638
  67.5 17.4 %collective-permute-start.9 = (bf16[448,384]{1,0:T(8,128)(2,1)S(1)}, bf16[448,384]{1,0:T(8,128)(2,1)}, u32[]{:S(2)}, u32[]{:S(2)}) collective-permute-start(bf16[448,384]{1,0:T(8,128)(2,1)S(1)} %get-tuple-element.132), channel_id=1, source_target_pairs={{0,5},{1,4},{2,7},{3,6},{4,1},{5,0},{6,3},{7,2},{8,13},{9,12},{10,... | collective-permute-start | bytes 1032200 | tf_op jit(solution)/shard_map/ppermute | solution.py:638
  84.9 3.4 %collective-permute-start.11 = (bf16[2,2,152,384]{3,2,1,0:T(8,128)(2,1)}, bf16[2,2,152,384]{3,2,1,0:T(8,128)(2,1)S(1)}, u32[]{:S(2)}, u32[]{:S(2)}) collective-permute-start(bf16[2,2,152,384]{3,2,1,0:T(8,128)(2,1)} %get-tuple-element.137), channel_id=1, source_target_pairs={{0,2},{1,3},{2,0},{3,1},{4,6},{5,7},{6,4},{7,5},{8,10},{9,11},{10,... | collective-permute-start | bytes 1400840 | tf_op jit(solution)/shard_map/ppermute | solution.py:638
  85.0 3.3 %copy-start.6 = (bf16[2,2,152,384]{3,2,1,0:T(8,128)(2,1)S(1)}, bf16[2,2,152,384]{3,2,1,0:T(8,128)(2,1)}, u32[]{:S(2)}) copy-start(bf16[2,2,152,384]{3,2,1,0:T(8,128)(2,1)} %get-tuple-element.136) | copy-start | bytes 1400836
  86.4 6.9 %collective-permute-start.10 = (bf16[224,384]{1,0:T(8,128)(2,1)S(1)}, bf16[224,384]{1,0:T(8,128)(2,1)S(1)}, u32[]{:S(2)}, u32[]{:S(2)}) collective-permute-start(bf16[224,384]{1,0:T(8,128)(2,1)S(1)} %get-tuple-element.189), channel_id=1, source_target_pairs={{0,8},{1,9},{2,10},{3,11},{4,12},{5,13},{6,14},{7,15},{8,0},{9,1},... | collective-permute-start | bytes 516104 | tf_op jit(solution)/shard_map/ppermute | solution.py:638
  88.3 22.4 %copy-start.2 = (bf16[8,197,384]{2,1,0:T(8,128)(2,1)S(1)}, bf16[8,197,384]{2,1,0:T(8,128)(2,1)}, u32[]{:S(2)}) copy-start(bf16[8,197,384]{2,1,0:T(8,128)(2,1)} %get-tuple-element.147) | copy-start | bytes 3631108
  88.3 7.8 %collective-permute-start.15 = (bf16[152,384]{1,0:T(8,128)(2,1)S(1)}, bf16[152,384]{1,0:T(8,128)(2,1)S(1)}, u32[]{:S(2)}, u32[]{:S(2)}) collective-permute-start(bf16[152,384]{1,0:T(8,128)(2,1)S(1)} %get-tuple-element.186), channel_id=1, source_target_pairs={{0,5},{1,4},{2,7},{3,6},{4,1},{5,0},{6,3},{7,2},{8,13},{9,12},{10,... | collective-permute-start | bytes 350216 | tf_op jit(solution)/shard_map/ppermute | solution.py:638
  90.9 6.3 %collective-permute-start.14 = (bf16[152,384]{1,0:T(8,128)(2,1)S(1)}, bf16[152,384]{1,0:T(8,128)(2,1)S(1)}, u32[]{:S(2)}, u32[]{:S(2)}) collective-permute-start(bf16[152,384]{1,0:T(8,128)(2,1)S(1)} %get-tuple-element.187), channel_id=1, source_target_pairs={{0,4},{1,5},{2,6},{3,7},{4,0},{5,1},{6,2},{7,3},{8,12},{9,13},{10,... | collective-permute-start | bytes 350216 | tf_op jit(solution)/shard_map/ppermute | solution.py:638
  91.4 5.8 %collective-permute-start.13 = (bf16[152,384]{1,0:T(8,128)(2,1)S(1)}, bf16[152,384]{1,0:T(8,128)(2,1)S(1)}, u32[]{:S(2)}, u32[]{:S(2)}) collective-permute-start(bf16[152,384]{1,0:T(8,128)(2,1)S(1)} %get-tuple-element.188), channel_id=1, source_target_pairs={{0,1},{1,0},{2,3},{3,2},{4,5},{5,4},{6,7},{7,6},{8,9},{9,8},{10,11... | collective-permute-start | bytes 350216 | tf_op jit(solution)/shard_map/ppermute | solution.py:638
  93.3 10.8 %collective-permute-start.12 = (bf16[224,384]{1,0:T(8,128)(2,1)S(1)}, bf16[224,384]{1,0:T(8,128)(2,1)S(1)}, u32[]{:S(2)}, u32[]{:S(2)}) collective-permute-start(bf16[224,384]{1,0:T(8,128)(2,1)S(1)} %add.103), channel_id=1, source_target_pairs={{0,16},{1,17},{2,18},{3,19},{4,20},{5,21},{6,22},{7,23},{8,24},{9,... | collective-permute-start | bytes 516104 | tf_op jit(solution)/shard_map/ppermute | solution.py:638
  97.2 7.6 %collective-permute-start.16 = (bf16[152,384]{1,0:T(8,128)(2,1)S(1)}, bf16[152,384]{1,0:T(8,128)(2,1)S(1)}, u32[]{:S(2)}, u32[]{:S(2)}) collective-permute-start(bf16[152,384]{1,0:T(8,128)(2,1)S(1)} %fusion.3), channel_id=1, source_target_pairs={{0,8},{1,9},{2,10},{3,11},{4,12},{5,13},{6,14},{7,15},{8,0},{9,1},... | collective-permute-start | bytes 350216 | tf_op jit(solution)/shard_map/ppermute | solution.py:638
  104.9 7.0 %copy-start.5 = (bf16[224,384]{1,0:T(8,128)(2,1)}, bf16[224,384]{1,0:T(8,128)(2,1)S(1)}, u32[]{:S(2)}) copy-start(bf16[224,384]{1,0:T(8,128)(2,1)S(1)} %add.109.refs_0_) | copy-start | bytes 516100
  105.0 7.0 %copy-start = (bf16[8,197,384]{2,1,0:T(8,128)(2,1)S(1)}, bf16[8,197,384]{2,1,0:T(8,128)(2,1)}, u32[]{:S(2)}) copy-start(bf16[8,197,384]{2,1,0:T(8,128)(2,1)} %get-tuple-element.148) | copy-start | bytes 3631108
  105.0 9.1 %collective-permute-start.20 = (bf16[224,384]{1,0:T(8,128)(2,1)S(1)}, bf16[224,384]{1,0:T(8,128)(2,1)S(1)}, u32[]{:S(2)}, u32[]{:S(2)}) collective-permute-start(bf16[224,384]{1,0:T(8,128)(2,1)S(1)} %add.109.refs_0_), channel_id=1, source_target_pairs={{0,2},{1,3},{2,0},{3,1},{4,6},{5,7},{6,4},{7,5},{8,10},{9,11},{10,... | collective-permute-start | bytes 516104 | tf_op jit(solution)/shard_map/ppermute | solution.py:638
  105.1 9.1 %collective-permute-start.19 = (bf16[224,384]{1,0:T(8,128)(2,1)S(1)}, bf16[224,384]{1,0:T(8,128)(2,1)S(1)}, u32[]{:S(2)}, u32[]{:S(2)}) collective-permute-start(bf16[224,384]{1,0:T(8,128)(2,1)S(1)} %add.109.refs_0_), channel_id=1, source_target_pairs={{0,4},{1,5},{2,6},{3,7},{4,0},{5,1},{6,2},{7,3},{8,12},{9,13},{10,... | collective-permute-start | bytes 516104 | tf_op jit(solution)/shard_map/ppermute | solution.py:638
  106.7 8.9 %collective-permute-start.17 = (bf16[224,384]{1,0:T(8,128)(2,1)S(1)}, bf16[224,384]{1,0:T(8,128)(2,1)S(1)}, u32[]{:S(2)}, u32[]{:S(2)}) collective-permute-start(bf16[224,384]{1,0:T(8,128)(2,1)S(1)} %add.109.refs_0_), channel_id=1, source_target_pairs={{0,8},{1,9},{2,10},{3,11},{4,12},{5,13},{6,14},{7,15},{8,0},{9,1},... | collective-permute-start | bytes 516104 | tf_op jit(solution)/shard_map/ppermute | solution.py:638
  106.7 7.4 %collective-permute-start.18 = (bf16[152,384]{1,0:T(8,128)(2,1)S(1)}, bf16[152,384]{1,0:T(8,128)(2,1)S(1)}, u32[]{:S(2)}, u32[]{:S(2)}) collective-permute-start(bf16[152,384]{1,0:T(8,128)(2,1)S(1)} %add.110), channel_id=1, source_target_pairs={{0,16},{1,17},{2,18},{3,19},{4,20},{5,21},{6,22},{7,23},{8,24},{9,... | collective-permute-start | bytes 350216 | tf_op jit(solution)/shard_map/ppermute | solution.py:638
  114.1 11.3 %copy-start.14 = (bf16[224,384]{1,0:T(8,128)(2,1)}, bf16[224,384]{1,0:T(8,128)(2,1)S(1)}, u32[]{:S(2)}) copy-start(bf16[224,384]{1,0:T(8,128)(2,1)S(1)} %collective-permute-done.20.refs_4_) | copy-start | bytes 516100
  114.1 11.3 %copy-start.15 = (bf16[224,384]{1,0:T(8,128)(2,1)}, bf16[224,384]{1,0:T(8,128)(2,1)S(1)}, u32[]{:S(2)}) copy-start(bf16[224,384]{1,0:T(8,128)(2,1)S(1)} %collective-permute-done.19.refs_2_) | copy-start | bytes 516100
  115.6 9.8 %copy-start.16 = (bf16[224,384]{1,0:T(8,128)(2,1)}, bf16[224,384]{1,0:T(8,128)(2,1)S(1)}, u32[]{:S(2)}) copy-start(bf16[224,384]{1,0:T(8,128)(2,1)S(1)} %collective-permute-done.17.refs_1_) | copy-start | bytes 516100
  115.6 8.1 %collective-permute-start.21 = (bf16[224,384]{1,0:T(8,128)(2,1)S(1)}, bf16[224,384]{1,0:T(8,128)(2,1)S(1)}, u32[]{:S(2)}, u32[]{:S(2)}) collective-permute-start(bf16[224,384]{1,0:T(8,128)(2,1)S(1)} %collective-permute-done.17.refs_1_), channel_id=1, source_target_pairs={{0,4},{1,5},{2,6},{3,7},{4,0},{5,1},{6,2},{7,3},{8,12},{9,13},{10,... | collective-permute-start | bytes 516104 | tf_op jit(solution)/shard_map/ppermute | solution.py:638
  116.1 9.3 %copy-start.7 = (bf16[152,384]{1,0:T(8,128)(2,1)}, bf16[152,384]{1,0:T(8,128)(2,1)S(1)}, u32[]{:S(2)}) copy-start(bf16[152,384]{1,0:T(8,128)(2,1)S(1)} %add.111.refs_8_) | copy-start | bytes 350212
  116.1 2.2 %collective-permute-start.23 = (bf16[152,384]{1,0:T(8,128)(2,1)S(1)}, bf16[152,384]{1,0:T(8,128)(2,1)S(1)}, u32[]{:S(2)}, u32[]{:S(2)}) collective-permute-start(bf16[152,384]{1,0:T(8,128)(2,1)S(1)} %add.111.refs_8_), channel_id=1, source_target_pairs={{0,2},{1,3},{2,0},{3,1},{4,6},{5,7},{6,4},{7,5},{8,10},{9,11},{10,... | collective-permute-start | bytes 350216 | tf_op jit(solution)/shard_map/ppermute | solution.py:638
  116.2 7.5 %collective-permute-start.22 = (bf16[152,384]{1,0:T(8,128)(2,1)S(1)}, bf16[152,384]{1,0:T(8,128)(2,1)S(1)}, u32[]{:S(2)}, u32[]{:S(2)}) collective-permute-start(bf16[152,384]{1,0:T(8,128)(2,1)S(1)} %add.111.refs_8_), channel_id=1, source_target_pairs={{0,4},{1,5},{2,6},{3,7},{4,0},{5,1},{6,2},{7,3},{8,12},{9,13},{10,... | collective-permute-start | bytes 350216 | tf_op jit(solution)/shard_map/ppermute | solution.py:638
  117.9 6.5 %collective-permute-start.24 = (bf16[224,384]{1,0:T(8,128)(2,1)S(1)}, bf16[224,384]{1,0:T(8,128)(2,1)S(1)}, u32[]{:S(2)}, u32[]{:S(2)}) collective-permute-start(bf16[224,384]{1,0:T(8,128)(2,1)S(1)} %collective-permute-done.17.refs_1_), channel_id=1, source_target_pairs={{0,2},{1,3},{2,0},{3,1},{4,6},{5,7},{6,4},{7,5},{8,10},{9,11},{10,... | collective-permute-start | bytes 516104 | tf_op jit(solution)/shard_map/ppermute | solution.py:638
  118.0 6.3 %collective-permute-start.25 = (bf16[224,384]{1,0:T(8,128)(2,1)S(1)}, bf16[224,384]{1,0:T(8,128)(2,1)S(1)}, u32[]{:S(2)}, u32[]{:S(2)}) collective-permute-start(bf16[224,384]{1,0:T(8,128)(2,1)S(1)} %collective-permute-done.19.refs_2_), channel_id=1, source_target_pairs={{0,2},{1,3},{2,0},{3,1},{4,6},{5,7},{6,4},{7,5},{8,10},{9,11},{10,... | collective-permute-start | bytes 516104 | tf_op jit(solution)/shard_map/ppermute | solution.py:638
  118.4 7.1 %copy-start.21 = (bf16[152,384]{1,0:T(8,128)(2,1)}, bf16[152,384]{1,0:T(8,128)(2,1)S(1)}, u32[]{:S(2)}) copy-start(bf16[152,384]{1,0:T(8,128)(2,1)S(1)} %collective-permute-done.23.refs_10_) | copy-start | bytes 350212
  123.8 1.7 %copy-start.22 = (bf16[152,384]{1,0:T(8,128)(2,1)}, bf16[152,384]{1,0:T(8,128)(2,1)S(1)}, u32[]{:S(2)}) copy-start(bf16[152,384]{1,0:T(8,128)(2,1)S(1)} %collective-permute-done.22.refs_9_) | copy-start | bytes 350212
  123.8 1.7 %copy-start.17 = (bf16[224,384]{1,0:T(8,128)(2,1)}, bf16[224,384]{1,0:T(8,128)(2,1)S(1)}, u32[]{:S(2)}) copy-start(bf16[224,384]{1,0:T(8,128)(2,1)S(1)} %collective-permute-done.21.refs_3_) | copy-start | bytes 516100
  123.8 1.6 %collective-permute-start.26 = (bf16[224,384]{1,0:T(8,128)(2,1)S(1)}, bf16[224,384]{1,0:T(8,128)(2,1)S(1)}, u32[]{:S(2)}, u32[]{:S(2)}) collective-permute-start(bf16[224,384]{1,0:T(8,128)(2,1)S(1)} %collective-permute-done.21.refs_3_), channel_id=1, source_target_pairs={{0,2},{1,3},{2,0},{3,1},{4,6},{5,7},{6,4},{7,5},{8,10},{9,11},{10,... | collective-permute-start | bytes 516104 | tf_op jit(solution)/shard_map/ppermute | solution.py:638
  123.8 1.6 %collective-permute-start.27 = (bf16[152,384]{1,0:T(8,128)(2,1)S(1)}, bf16[152,384]{1,0:T(8,128)(2,1)S(1)}, u32[]{:S(2)}, u32[]{:S(2)}) collective-permute-start(bf16[152,384]{1,0:T(8,128)(2,1)S(1)} %collective-permute-done.22.refs_9_), channel_id=1, source_target_pairs={{0,2},{1,3},{2,0},{3,1},{4,6},{5,7},{6,4},{7,5},{8,10},{9,11},{10,... | collective-permute-start | bytes 350216 | tf_op jit(solution)/shard_map/ppermute | solution.py:638
  124.3 1.1 copy-start.19
  124.4 1.1 copy-start.18
  125.4 0.6 copy-start.23
  126.0 0.7 copy-start.20

commit v10 on v9

--- a/solution.py
+++ b/solution.py
@@ -171,7 +171,7 @@
             top = jnp.max(scores, axis=-1, keepdims=True)
             weights = jnp.exp(scores - top).astype(BF16)
             both = nn(weights, jnp.concatenate([value, ones], axis=1))
-            mixed_ref[j, :, c : c + PAIR] = join_pair(both[:, :PAIR] / both[:, PAIR:]).astype(BF16)
+            mixed_ref[j, :, c : c + PAIR] = (join_pair(both[:, :PAIR]) / join_pair(both[:, PAIR:])).astype(BF16)
 
 
 def mlp_kernel(
@@ -782,14 +782,14 @@
         )
         send_c, more_a = after(send_c, more_a)
         got_c = plan.over_core(send_c)
-        sum_a = stay_a + more_a[0] + more_a[1] + more_a[2]
-        low_a, high_a = plan.half(sum_a, plan.z), plan.half(sum_a, 1 - plan.z)
+        terms = (stay_a, *more_a)
+        high_a = sum(plan.half(v, 1 - plan.z) for v in terms)
         over_a = plan.over_z(high_a, 1)
-        got_c = behind(got_c, low_a, high_a)
+        got_c = behind(got_c, high_a)
         parts_c, stay_c = plan.scatter(keep_c, got_c)
         over_a = behind(over_a, parts_c)
         more_c = plan.send(parts_c)
-        low_a = low_a + over_a
+        low_a = sum(plan.half(v, plan.z) for v in terms) + over_a
         over_a = plan.over_z(low_a, 2)
         more_c = behind(more_c, low_a)
         sum_c = stay_c + more_c[0] + more_c[1] + more_c[2]

time: 131 us -> 132 us (level)
  other arithmetic: 2.36 us -> 3.89 us
    add x2, other arithmetic: 0.18 us -> 1.95 us  [scatter(): total = [[keep[i, j] + got[i, j] for j in range(2)] for i in range(2)]]
    unnamed x50 -> x48, local copies, waits for them, and re-layouts: 5.2 us -> 5.19 us
  transfers between devices with their start and end apart: 28 -> 28, of which waited for: 13 -> 13; matrix products, arithmetic and copies ran while one was open for 5% -> 5% of each run, Pallas kernels for 28% -> 27%
where the time goes in v10:
time: 132 us
  Pallas kernels  69.2 us (52%)
  starting transfers between devices  28.2 us (21%)
  waiting for transfers between devices  21.9 us (17%)
  local copies, waits for them, and re-layouts  7.54 us (6%)
  other arithmetic  3.89 us (3%)
    ppermute x28, starting transfers between devices, swap(): return lax.ppermute(v, AXES, pairs)  28.2 us
    pallas_call x1, Pallas kernels, mlp_both_ways(): pl.pallas_call(functools.partial(mlp_kernel, length, 512), grid=(images /...  27.4 us
    pallas_call x2, Pallas kernels, attention_backward(): pl.pallas_call(functools.partial(back_kernel, length, first, last), grid=...  24.1 us
    ppermute x28, waiting for transfers between devices, swap(): return lax.ppermute(v, AXES, pairs)  21.9 us
    pallas_call x1, Pallas kernels, forward_attention(): pl.pallas_call(functools.partial(attend_kernel, length), grid=(images //...  9.88 us
    unnamed x48, local copies, waits for them, and re-layouts  5.19 us
    pallas_call x1, Pallas kernels, unpack(): pl.pallas_call(unpack_kernel, grid=(1,), in_specs=[SCALARS, *whole_like((...  3.7 us
  transfers between devices with their start and end apart: 28, of which 13 were waited for; matrix products, arithmetic and copies ran while one was open for 5% of the time, Pallas kernels for 27%

profile of v10, /device:TPU:0, one launch (start us, length us, event | category | flops | bytes accessed | tf_op | source)
XLA Modules:
  0.0 131.8 jit_solution(16326274175852326953)
XLA Ops:
  0.7 0.7 pad_add_fusion.index
  1.3 1.9 %pack_first.1.packed = bf16[104,1152]{1,0:T(8,128)(2,1)} custom-call(s32[4]{0:T(128)} %pad_add_fusion.index, bf16[192]{0:T(256)(128)(2,1)} %refs_0_.1, bf16[192]{0:T(256)(128)(2,1)} %refs_1_.1, bf16[192]{0:T(256)(128)(2,1)} %refs_2_.1, bf16[192]{0:T(256)(128)(2,1)} %refs_3_.1, bf16[192]{0:T(256)(128)(2,1)} %refs_4_.1, bf16[192]{0:T(256)(128)(2,1)} %refs_5_.1, ...), custom_call_target="tpu_custom_call" | custom-call | flops 1000 | bytes 1 | tf_op jit(solution)/shard_map/pack_first/pallas_call | solution.py:461
  3.2 2.9 %collective-permute-start = (bf16[104,1152]{1,0:T(8,128)(2,1)}, bf16[104,1152]{1,0:T(8,128)(2,1)S(1)}, u32[]{:S(2)}, u32[]{:S(2)}) collective-permute-start(bf16[104,1152]{1,0:T(8,128)(2,1)} %pack_first.1.packed), channel_id=1, source_target_pairs={{0,1},{1,0},{2,3},{3,2},{4,5},{5,4},{6,7},{7,6},{8,9},{9,8},{10,11... | collective-permute-start | bytes 718856 | tf_op jit(solution)/shard_map/ppermute | solution.py:638
  6.1 2.2 %pack_rest.1 = (bf16[96,1536]{1,0:T(8,128)(2,1)}, bf16[480,384]{1,0:T(8,128)(2,1)}) custom-call(s32[4]{0:T(128)} %pad_add_fusion.index, bf16[192,384]{1,0:T(8,128)(2,1)} %out_own.2, bf16[192,1536]{1,0:T(8,128)(2,1)} %lift_own.2, bf16[768,384]{1,0:T(8,128)(2,1)} %drop_own.2), custom_call_target="tpu_custom_call" | custom-call | flops 1000 | bytes 1 | tf_op jit(solution)/shard_map/pack_rest/pallas_call | solution.py:477
  8.3 0.0 collective-permute-start.3
  8.3 2.0 %collective-permute-start.2 = (bf16[96,1536]{1,0:T(8,128)(2,1)}, bf16[96,1536]{1,0:T(8,128)(2,1)S(1)}, u32[]{:S(2)}, u32[]{:S(2)}) collective-permute-start(bf16[96,1536]{1,0:T(8,128)(2,1)} %get-tuple-element.105), channel_id=1, source_target_pairs={{0,1},{1,0},{2,3},{3,2},{4,5},{5,4},{6,7},{7,6},{8,9},{9,8},{10,11... | collective-permute-start | bytes 884744 | tf_op jit(solution)/shard_map/ppermute | solution.py:638
  10.4 1.2 copy.31.tok_ref
  11.5 1.5 %collective-permute-done.near = bf16[104,1152]{1,0:T(8,128)(2,1)S(1)} collective-permute-done((bf16[104,1152]{1,0:T(8,128)(2,1)}, bf16[104,1152]{1,0:T(8,128)(2,1)S(1)}, u32[]{:S(2)}, u32[]{:S(2)}) %collective-permute-start) | collective-permute-done | bytes 239648 | tf_op jit(solution)/shard_map/ppermute | solution.py:638
  13.0 0.0 collective-permute-start.1
  13.0 1.5 %collective-permute-done.1.far = bf16[104,1152]{1,0:T(8,128)(2,1)S(1)} collective-permute-done((bf16[104,1152]{1,0:T(8,128)(2,1)S(1)}, bf16[104,1152]{1,0:T(8,128)(2,1)S(1)}, u32[]{:S(2)}, u32[]{:S(2)}) %collective-permute-start.1) | collective-permute-done | bytes 239648 | tf_op jit(solution)/shard_map/ppermute | solution.py:638
  14.5 0.7 copy-done.12
  15.2 9.9 %attend.1 = (bf16[8,208,384]{2,1,0:T(8,128)(2,1)}, bf16[8,208,1152]{2,1,0:T(8,128)(2,1)}, bf16[8,208,384]{2,1,0:T(8,128)(2,1)}, bf16[384,1152]{1,0:T(8,128)(2,1)}, f32[12,384]{1,0:T(8,128)}) custom-call(s32[4]{0:T(128)} %pad_add_fusion.index, bf16[8,197,384]{2,1,0:T(8,128)(2,1)} %copy.31.tok_ref, bf16[104,1152]{1,0:T(8,128)(2,1)} %pack_first.1.packed, ...), custom_call_target="tpu_custom_call" | custom-call | flops 1000 | bytes 1 | tf_op jit(solution)/shard_map/attend/pallas_call | solution.py:493
  25.1 1.3 collective-permute-done.2.lift_near
  26.4 0.0 collective-permute-done.3.both_near
  26.4 0.1 collective-permute-start.5
  26.5 0.5 collective-permute-start.4
  27.0 1.2 copy.32.cot_ref
  28.2 0.4 collective-permute-done.4.lift_far
  28.6 0.7 copy-done.10
  29.3 0.1 copy-done.8
  29.4 27.4 %mlp.1 = (bf16[8,197,384]{2,1,0:T(8,128)(2,1)}, f32[8,208,384]{2,1,0:T(8,128)}, bf16[8,208,384]{2,1,0:T(8,128)(2,1)}, bf16[2,2,448,384]{3,2,1,0:T(8,128)(2,1)}, bf16[2,2,448,384]{3,2,1,0:T(8,128)(2,1)}) custom-call(s32[4]{0:T(128)} %pad_add_fusion.index, bf16[8,197,384]{2,1,0:T(8,128)(2,1)} %copy.31.tok_ref, bf16[8,197,384]{2,1,0:T(8,128)(2,1)} %copy.32.cot_ref, ...), custom_call_target="tpu_custom_call" | custom-call | flops 1000 | bytes 1 | tf_op jit(solution)/shard_map/mlp/pallas_call | solution.py:523
  56.9 0.2 collective-permute-start.6
  57.1 7.0 %back.2 = (bf16[8,197,384]{2,1,0:T(8,128)(2,1)}, f32[384,1152]{1,0:T(8,128)}, f32[8,1152]{1,0:T(8,128)}, f32[2,384]{1,0:T(2,128)}) custom-call(s32[4]{0:T(128)} %pad_add_fusion.index, bf16[8,197,384]{2,1,0:T(8,128)(2,1)} %copy.31.tok_ref, bf16[8,208,1152]{2,1,0:T(8,128)(2,1)} %get-tuple-element.112.proj_ref, ...), custom_call_target="tpu_custom_call" | custom-call | flops 1000 | bytes 1 | tf_op jit(solution)/shard_map/back/pallas_call | solution.py:581
  64.1 0.9 slice_add_fusion
  65.0 1.8 %collective-permute-start.7 = (bf16[448,384]{1,0:T(8,128)(2,1)}, bf16[448,384]{1,0:T(8,128)(2,1)S(1)}, u32[]{:S(2)}, u32[]{:S(2)}) collective-permute-start(bf16[448,384]{1,0:T(8,128)(2,1)} %get-tuple-element.130), channel_id=1, source_target_pairs={{0,1},{1,0},{2,3},{3,2},{4,5},{5,4},{6,7},{7,6},{8,9},{9,8},{10,11... | collective-permute-start | bytes 1032200 | tf_op jit(solution)/shard_map/ppermute | solution.py:638
  66.7 1.5 %collective-permute-start.8 = (bf16[448,384]{1,0:T(8,128)(2,1)S(1)}, bf16[448,384]{1,0:T(8,128)(2,1)S(1)}, u32[]{:S(2)}, u32[]{:S(2)}) collective-permute-start(bf16[448,384]{1,0:T(8,128)(2,1)S(1)} %get-tuple-element.131), channel_id=1, source_target_pairs={{0,4},{1,5},{2,6},{3,7},{4,0},{5,1},{6,2},{7,3},{8,12},{9,13},{10,... | collective-permute-start | bytes 1032200 | tf_op jit(solution)/shard_map/ppermute | solution.py:638
  68.3 0.2 collective-permute-start.9
  68.5 17.1 %back.3 = (bf16[8,197,384]{2,1,0:T(8,128)(2,1)}, bf16[2,2,152,384]{3,2,1,0:T(8,128)(2,1)}, bf16[2,2,152,384]{3,2,1,0:T(8,128)(2,1)}) custom-call(s32[4]{0:T(128)} %pad_add_fusion.index, bf16[8,197,384]{2,1,0:T(8,128)(2,1)} %copy.31.tok_ref, bf16[8,208,1152]{2,1,0:T(8,128)(2,1)} %get-tuple-element.112.proj_ref, ...), custom_call_target="tpu_custom_call", output_to_operand_aliasing={{0}: (11, {})} | custom-call | flops 1000 | bytes 1 | tf_op jit(solution)/shard_map/back/pallas_call | solution.py:581
  85.6 0.1 collective-permute-start.11
  85.7 0.1 fusion.1
  85.8 1.9 %collective-permute-start.10 = (bf16[224,384]{1,0:T(8,128)(2,1)S(1)}, bf16[224,384]{1,0:T(8,128)(2,1)S(1)}, u32[]{:S(2)}, u32[]{:S(2)}) collective-permute-start(bf16[224,384]{1,0:T(8,128)(2,1)S(1)} %fusion.1), channel_id=1, source_target_pairs={{0,8},{1,9},{2,10},{3,11},{4,12},{5,13},{6,14},{7,15},{8,0},{9,1},... | collective-permute-start | bytes 516104 | tf_op jit(solution)/shard_map/ppermute | solution.py:638
  87.7 0.0 collective-permute-done.11
  87.7 1.1 add_bitcast_fusion.3
  88.8 2.8 %collective-permute-start.15 = (bf16[152,384]{1,0:T(8,128)(2,1)S(1)}, bf16[152,384]{1,0:T(8,128)(2,1)S(1)}, u32[]{:S(2)}, u32[]{:S(2)}) collective-permute-start(bf16[152,384]{1,0:T(8,128)(2,1)S(1)} %get-tuple-element.187), channel_id=1, source_target_pairs={{0,5},{1,4},{2,7},{3,6},{4,1},{5,0},{6,3},{7,2},{8,13},{9,12},{10,... | collective-permute-start | bytes 350216 | tf_op jit(solution)/shard_map/ppermute | solution.py:638
  91.6 0.5 collective-permute-start.14
  92.1 0.3 collective-permute-start.13
  92.4 0.4 collective-permute-done.10
  92.7 0.1 fusion.4
  92.9 2.8 %collective-permute-start.12 = (bf16[224,384]{1,0:T(8,128)(2,1)S(1)}, bf16[224,384]{1,0:T(8,128)(2,1)S(1)}, u32[]{:S(2)}, u32[]{:S(2)}) collective-permute-start(bf16[224,384]{1,0:T(8,128)(2,1)S(1)} %fusion.4), channel_id=1, source_target_pairs={{0,16},{1,17},{2,18},{3,19},{4,20},{5,21},{6,22},{7,23},{8,24},{9,... | collective-permute-start | bytes 516104 | tf_op jit(solution)/shard_map/ppermute | solution.py:638
  95.7 1.9 %collective-permute-done.14 = bf16[152,384]{1,0:T(8,128)(2,1)S(1)} collective-permute-done((bf16[152,384]{1,0:T(8,128)(2,1)S(1)}, bf16[152,384]{1,0:T(8,128)(2,1)S(1)}, u32[]{:S(2)}, u32[]{:S(2)}) %collective-permute-start.14) | collective-permute-done | bytes 116768 | tf_op jit(solution)/shard_map/ppermute | solution.py:638
  97.6 0.3 collective-permute-done.13
  97.8 1.0 fusion.6
  98.8 1.6 %collective-permute-start.16 = (bf16[152,384]{1,0:T(8,128)(2,1)S(1)}, bf16[152,384]{1,0:T(8,128)(2,1)S(1)}, u32[]{:S(2)}, u32[]{:S(2)}) collective-permute-start(bf16[152,384]{1,0:T(8,128)(2,1)S(1)} %fusion.6), channel_id=1, source_target_pairs={{0,8},{1,9},{2,10},{3,11},{4,12},{5,13},{6,14},{7,15},{8,0},{9,1},... | collective-permute-start | bytes 350216 | tf_op jit(solution)/shard_map/ppermute | solution.py:638
  100.4 3.3 %collective-permute-done.12 = bf16[224,384]{1,0:T(8,128)(2,1)S(1)} collective-permute-done((bf16[224,384]{1,0:T(8,128)(2,1)S(1)}, bf16[224,384]{1,0:T(8,128)(2,1)S(1)}, u32[]{:S(2)}, u32[]{:S(2)}) %collective-permute-start.12) | collective-permute-done | bytes 172064 | tf_op jit(solution)/shard_map/ppermute | solution.py:638
  103.7 2.4 %collective-permute-done.16 = bf16[152,384]{1,0:T(8,128)(2,1)S(1)} collective-permute-done((bf16[152,384]{1,0:T(8,128)(2,1)S(1)}, bf16[152,384]{1,0:T(8,128)(2,1)S(1)}, u32[]{:S(2)}, u32[]{:S(2)}) %collective-permute-start.16) | collective-permute-done | bytes 116768 | tf_op jit(solution)/shard_map/ppermute | solution.py:638
  106.2 0.1 collective-permute-start.20
  106.3 1.6 %collective-permute-start.19 = (bf16[224,384]{1,0:T(8,128)(2,1)S(1)}, bf16[224,384]{1,0:T(8,128)(2,1)S(1)}, u32[]{:S(2)}, u32[]{:S(2)}) collective-permute-start(bf16[224,384]{1,0:T(8,128)(2,1)S(1)} %add.124.refs_0_), channel_id=1, source_target_pairs={{0,4},{1,5},{2,6},{3,7},{4,0},{5,1},{6,2},{7,3},{8,12},{9,13},{10,... | collective-permute-start | bytes 516104 | tf_op jit(solution)/shard_map/ppermute | solution.py:638
  107.9 4.1 %collective-permute-start.18 = (bf16[152,384]{1,0:T(8,128)(2,1)S(1)}, bf16[152,384]{1,0:T(8,128)(2,1)S(1)}, u32[]{:S(2)}, u32[]{:S(2)}) collective-permute-start(bf16[152,384]{1,0:T(8,128)(2,1)S(1)} %add.125), channel_id=1, source_target_pairs={{0,16},{1,17},{2,18},{3,19},{4,20},{5,21},{6,22},{7,23},{8,24},{9,... | collective-permute-start | bytes 350216 | tf_op jit(solution)/shard_map/ppermute | solution.py:638
  112.0 1.2 copy.38
  113.2 1.2 copy.37
  114.4 1.0 collective-permute-done.18
  115.4 1.5 %collective-permute-done.17.refs_1_ = bf16[224,384]{1,0:T(8,128)(2,1)S(1)} collective-permute-done((bf16[224,384]{1,0:T(8,128)(2,1)S(1)}, bf16[224,384]{1,0:T(8,128)(2,1)S(1)}, u32[]{:S(2)}, u32[]{:S(2)}) %collective-permute-start.17) | collective-permute-done | bytes 172064 | tf_op jit(solution)/shard_map/ppermute | solution.py:638
  116.9 0.5 collective-permute-start.21
  117.4 0.1 collective-permute-start.23
  117.5 1.6 %collective-permute-start.22 = (bf16[152,384]{1,0:T(8,128)(2,1)S(1)}, bf16[152,384]{1,0:T(8,128)(2,1)S(1)}, u32[]{:S(2)}, u32[]{:S(2)}) collective-permute-start(bf16[152,384]{1,0:T(8,128)(2,1)S(1)} %add.126.refs_8_), channel_id=1, source_target_pairs={{0,4},{1,5},{2,6},{3,7},{4,0},{5,1},{6,2},{7,3},{8,12},{9,13},{10,... | collective-permute-start | bytes 350216 | tf_op jit(solution)/shard_map/ppermute | solution.py:638
  119.1 0.2 collective-permute-start.24
  119.3 0.3 collective-permute-start.25
  119.6 5.4 %collective-permute-done.22.refs_9_ = bf16[152,384]{1,0:T(8,128)(2,1)S(1)} collective-permute-done((bf16[152,384]{1,0:T(8,128)(2,1)S(1)}, bf16[152,384]{1,0:T(8,128)(2,1)S(1)}, u32[]{:S(2)}, u32[]{:S(2)}) %collective-permute-start.22) | collective-permute-done | bytes 116768 | tf_op jit(solution)/shard_map/ppermute | solution.py:638
  125.0 0.1 collective-permute-start.26
  125.1 0.5 collective-permute-start.27
  125.6 1.0 collective-permute-done.27.refs_11_
  126.7 0.6 copy-done.22
  127.3 0.7 copy-done.19
  128.0 3.7 %unpack.1 = (f32[768,384]{1,0:T(8,128)}, f32[192,1536]{1,0:T(8,128)}, f32[192,384]{1,0:T(8,128)}, f32[192]{0:T(256)}, f32[192]{0:T(256)}, /*index=5*/f32[192]{0:...) custom-call(s32[4]{0:T(128)} %pad_add_fusion.index, ...), custom_call_target="tpu_custom_call" | custom-call | flops 1000 | bytes 1 | tf_op jit(solution)/shard_map/unpack/pallas_call | solution.py:609
  (58 shorter events, 0.2 us)
Async XLA Ops:
  0.6 9.7 %copy-start.3 = (bf16[8,197,384]{2,0,1:T(8,128)(2,1)S(1)}, bf16[8,197,384]{2,0,1:T(8,128)(2,1)}, u32[]{:S(2)}) copy-start(bf16[8,197,384]{2,0,1:T(8,128)(2,1)} %param.15) | copy-start | bytes 3631108
  3.2 9.8 %collective-permute-start = (bf16[104,1152]{1,0:T(8,128)(2,1)}, bf16[104,1152]{1,0:T(8,128)(2,1)S(1)}, u32[]{:S(2)}, u32[]{:S(2)}) collective-permute-start(bf16[104,1152]{1,0:T(8,128)(2,1)} %pack_first.1.packed), channel_id=1, source_target_pairs={{0,1},{1,0},{2,3},{3,2},{4,5},{5,4},{6,7},{7,6},{8,9},{9,8},{10,11... | collective-permute-start | bytes 718856 | tf_op jit(solution)/shard_map/ppermute | solution.py:638
  8.3 18.1 %collective-permute-start.3 = (bf16[480,384]{1,0:T(8,128)(2,1)}, bf16[480,384]{1,0:T(8,128)(2,1)S(1)}, u32[]{:S(2)}, u32[]{:S(2)}) collective-permute-start(bf16[480,384]{1,0:T(8,128)(2,1)} %get-tuple-element.106), channel_id=1, source_target_pairs={{0,1},{1,0},{2,3},{3,2},{4,5},{5,4},{6,7},{7,6},{8,9},{9,8},{10,11... | collective-permute-start | bytes 1105928 | tf_op jit(solution)/shard_map/ppermute | solution.py:638
  8.3 18.1 %collective-permute-start.2 = (bf16[96,1536]{1,0:T(8,128)(2,1)}, bf16[96,1536]{1,0:T(8,128)(2,1)S(1)}, u32[]{:S(2)}, u32[]{:S(2)}) collective-permute-start(bf16[96,1536]{1,0:T(8,128)(2,1)} %get-tuple-element.105), channel_id=1, source_target_pairs={{0,1},{1,0},{2,3},{3,2},{4,5},{5,4},{6,7},{7,6},{8,9},{9,8},{10,11... | collective-permute-start | bytes 884744 | tf_op jit(solution)/shard_map/ppermute | solution.py:638
  11.5 15.4 %copy-start.4 = (bf16[8,197,384]{2,0,1:T(8,128)(2,1)S(1)}, bf16[8,197,384]{2,0,1:T(8,128)(2,1)}, u32[]{:S(2)}) copy-start(bf16[8,197,384]{2,0,1:T(8,128)(2,1)} %param.29) | copy-start | bytes 3631108
  13.0 1.5 %copy-start.11 = (bf16[104,1152]{1,0:T(8,128)(2,1)}, bf16[104,1152]{1,0:T(8,128)(2,1)S(1)}, u32[]{:S(2)}) copy-start(bf16[104,1152]{1,0:T(8,128)(2,1)S(1)} %collective-permute-done.near) | copy-start | bytes 718852
  13.0 1.5 %collective-permute-start.1 = (bf16[104,1152]{1,0:T(8,128)(2,1)S(1)}, bf16[104,1152]{1,0:T(8,128)(2,1)S(1)}, u32[]{:S(2)}, u32[]{:S(2)}) collective-permute-start(bf16[104,1152]{1,0:T(8,128)(2,1)S(1)} %collective-permute-done.near), channel_id=1, source_target_pairs={{0,2},{1,3},{2,0},{3,1},{4,6},{5,7},{6,4},{7,5},{8,10},{9,11},{10,... | collective-permute-start | bytes 718856 | tf_op jit(solution)/shard_map/ppermute | solution.py:638
  14.5 0.7 copy-start.12
  26.4 2.2 %copy-start.9 = (bf16[96,1536]{1,0:T(8,128)(2,1)}, bf16[96,1536]{1,0:T(8,128)(2,1)S(1)}, u32[]{:S(2)}) copy-start(bf16[96,1536]{1,0:T(8,128)(2,1)S(1)} %collective-permute-done.2.lift_near) | copy-start | bytes 884740
  26.4 2.2 %copy-start.7 = (bf16[480,384]{1,0:T(8,128)(2,1)}, bf16[480,384]{1,0:T(8,128)(2,1)S(1)}, u32[]{:S(2)}) copy-start(bf16[480,384]{1,0:T(8,128)(2,1)S(1)} %collective-permute-done.3.both_near) | copy-start | bytes 1105924
  26.4 2.2 %collective-permute-start.5 = (bf16[480,384]{1,0:T(8,128)(2,1)S(1)}, bf16[480,384]{1,0:T(8,128)(2,1)S(1)}, u32[]{:S(2)}, u32[]{:S(2)}) collective-permute-start(bf16[480,384]{1,0:T(8,128)(2,1)S(1)} %collective-permute-done.3.both_near), channel_id=1, source_target_pairs={{0,2},{1,3},{2,0},{3,1},{4,6},{5,7},{6,4},{7,5},{8,10},{9,11},{10,... | collective-permute-start | bytes 1105928 | tf_op jit(solution)/shard_map/ppermute | solution.py:638
  26.5 2.1 %collective-permute-start.4 = (bf16[96,1536]{1,0:T(8,128)(2,1)S(1)}, bf16[96,1536]{1,0:T(8,128)(2,1)S(1)}, u32[]{:S(2)}, u32[]{:S(2)}) collective-permute-start(bf16[96,1536]{1,0:T(8,128)(2,1)S(1)} %collective-permute-done.2.lift_near), channel_id=1, source_target_pairs={{0,2},{1,3},{2,0},{3,1},{4,6},{5,7},{6,4},{7,5},{8,10},{9,11},{10,... | collective-permute-start | bytes 884744 | tf_op jit(solution)/shard_map/ppermute | solution.py:638
  28.6 0.7 copy-start.10
  28.6 0.8 copy-start.8
  56.9 7.2 %collective-permute-start.6 = (bf16[2,2,448,384]{3,2,1,0:T(8,128)(2,1)}, bf16[2,2,448,384]{3,2,1,0:T(8,128)(2,1)S(1)}, u32[]{:S(2)}, u32[]{:S(2)}) collective-permute-start(bf16[2,2,448,384]{3,2,1,0:T(8,128)(2,1)} %get-tuple-element.120), channel_id=1, source_target_pairs={{0,2},{1,3},{2,0},{3,1},{4,6},{5,7},{6,4},{7,5},{8,10},{9,11},{10,... | collective-permute-start | bytes 4128776 | tf_op jit(solution)/shard_map/ppermute | solution.py:638
  57.1 7.0 %copy-start.1 = (bf16[2,2,448,384]{3,2,1,0:T(8,128)(2,1)S(1)}, bf16[2,2,448,384]{3,2,1,0:T(8,128)(2,1)}, u32[]{:S(2)}) copy-start(bf16[2,2,448,384]{3,2,1,0:T(8,128)(2,1)} %get-tuple-element.111) | copy-start | bytes 4128772
  65.0 20.6 %collective-permute-start.7 = (bf16[448,384]{1,0:T(8,128)(2,1)}, bf16[448,384]{1,0:T(8,128)(2,1)S(1)}, u32[]{:S(2)}, u32[]{:S(2)}) collective-permute-start(bf16[448,384]{1,0:T(8,128)(2,1)} %get-tuple-element.130), channel_id=1, source_target_pairs={{0,1},{1,0},{2,3},{3,2},{4,5},{5,4},{6,7},{7,6},{8,9},{9,8},{10,11... | collective-permute-start | bytes 1032200 | tf_op jit(solution)/shard_map/ppermute | solution.py:638
  66.7 18.9 %collective-permute-start.8 = (bf16[448,384]{1,0:T(8,128)(2,1)S(1)}, bf16[448,384]{1,0:T(8,128)(2,1)S(1)}, u32[]{:S(2)}, u32[]{:S(2)}) collective-permute-start(bf16[448,384]{1,0:T(8,128)(2,1)S(1)} %get-tuple-element.131), channel_id=1, source_target_pairs={{0,4},{1,5},{2,6},{3,7},{4,0},{5,1},{6,2},{7,3},{8,12},{9,13},{10,... | collective-permute-start | bytes 1032200 | tf_op jit(solution)/shard_map/ppermute | solution.py:638
  68.3 17.4 %collective-permute-start.9 = (bf16[448,384]{1,0:T(8,128)(2,1)S(1)}, bf16[448,384]{1,0:T(8,128)(2,1)S(1)}, u32[]{:S(2)}, u32[]{:S(2)}) collective-permute-start(bf16[448,384]{1,0:T(8,128)(2,1)S(1)} %get-tuple-element.132), channel_id=1, source_target_pairs={{0,5},{1,4},{2,7},{3,6},{4,1},{5,0},{6,3},{7,2},{8,13},{9,12},{10,... | collective-permute-start | bytes 1032200 | tf_op jit(solution)/shard_map/ppermute | solution.py:638
  85.6 2.1 %collective-permute-start.11 = (bf16[2,2,152,384]{3,2,1,0:T(8,128)(2,1)}, bf16[2,2,152,384]{3,2,1,0:T(8,128)(2,1)S(1)}, u32[]{:S(2)}, u32[]{:S(2)}) collective-permute-start(bf16[2,2,152,384]{3,2,1,0:T(8,128)(2,1)} %get-tuple-element.137), channel_id=1, source_target_pairs={{0,2},{1,3},{2,0},{3,1},{4,6},{5,7},{6,4},{7,5},{8,10},{9,11},{10,... | collective-permute-start | bytes 1400840 | tf_op jit(solution)/shard_map/ppermute | solution.py:638
  85.8 6.9 %collective-permute-start.10 = (bf16[224,384]{1,0:T(8,128)(2,1)S(1)}, bf16[224,384]{1,0:T(8,128)(2,1)S(1)}, u32[]{:S(2)}, u32[]{:S(2)}) collective-permute-start(bf16[224,384]{1,0:T(8,128)(2,1)S(1)} %fusion.1), channel_id=1, source_target_pairs={{0,8},{1,9},{2,10},{3,11},{4,12},{5,13},{6,14},{7,15},{8,0},{9,1},... | collective-permute-start | bytes 516104 | tf_op jit(solution)/shard_map/ppermute | solution.py:638
  88.8 6.9 %collective-permute-start.15 = (bf16[152,384]{1,0:T(8,128)(2,1)S(1)}, bf16[152,384]{1,0:T(8,128)(2,1)S(1)}, u32[]{:S(2)}, u32[]{:S(2)}) collective-permute-start(bf16[152,384]{1,0:T(8,128)(2,1)S(1)} %get-tuple-element.187), channel_id=1, source_target_pairs={{0,5},{1,4},{2,7},{3,6},{4,1},{5,0},{6,3},{7,2},{8,13},{9,12},{10,... | collective-permute-start | bytes 350216 | tf_op jit(solution)/shard_map/ppermute | solution.py:638
  91.6 6.0 %collective-permute-start.14 = (bf16[152,384]{1,0:T(8,128)(2,1)S(1)}, bf16[152,384]{1,0:T(8,128)(2,1)S(1)}, u32[]{:S(2)}, u32[]{:S(2)}) collective-permute-start(bf16[152,384]{1,0:T(8,128)(2,1)S(1)} %get-tuple-element.188), channel_id=1, source_target_pairs={{0,4},{1,5},{2,6},{3,7},{4,0},{5,1},{6,2},{7,3},{8,12},{9,13},{10,... | collective-permute-start | bytes 350216 | tf_op jit(solution)/shard_map/ppermute | solution.py:638
  92.1 19.9 %copy-start.2 = (bf16[8,197,384]{2,1,0:T(8,128)(2,1)S(1)}, bf16[8,197,384]{2,1,0:T(8,128)(2,1)}, u32[]{:S(2)}) copy-start(bf16[8,197,384]{2,1,0:T(8,128)(2,1)} %get-tuple-element.147) | copy-start | bytes 3631108
  92.1 5.7 %collective-permute-start.13 = (bf16[152,384]{1,0:T(8,128)(2,1)S(1)}, bf16[152,384]{1,0:T(8,128)(2,1)S(1)}, u32[]{:S(2)}, u32[]{:S(2)}) collective-permute-start(bf16[152,384]{1,0:T(8,128)(2,1)S(1)} %get-tuple-element.189), channel_id=1, source_target_pairs={{0,1},{1,0},{2,3},{3,2},{4,5},{5,4},{6,7},{7,6},{8,9},{9,8},{10,11... | collective-permute-start | bytes 350216 | tf_op jit(solution)/shard_map/ppermute | solution.py:638
  92.9 10.8 %collective-permute-start.12 = (bf16[224,384]{1,0:T(8,128)(2,1)S(1)}, bf16[224,384]{1,0:T(8,128)(2,1)S(1)}, u32[]{:S(2)}, u32[]{:S(2)}) collective-permute-start(bf16[224,384]{1,0:T(8,128)(2,1)S(1)} %fusion.4), channel_id=1, source_target_pairs={{0,16},{1,17},{2,18},{3,19},{4,20},{5,21},{6,22},{7,23},{8,24},{9,... | collective-permute-start | bytes 516104 | tf_op jit(solution)/shard_map/ppermute | solution.py:638
  98.8 7.3 %collective-permute-start.16 = (bf16[152,384]{1,0:T(8,128)(2,1)S(1)}, bf16[152,384]{1,0:T(8,128)(2,1)S(1)}, u32[]{:S(2)}, u32[]{:S(2)}) collective-permute-start(bf16[152,384]{1,0:T(8,128)(2,1)S(1)} %fusion.6), channel_id=1, source_target_pairs={{0,8},{1,9},{2,10},{3,11},{4,12},{5,13},{6,14},{7,15},{8,0},{9,1},... | collective-permute-start | bytes 350216 | tf_op jit(solution)/shard_map/ppermute | solution.py:638
  106.2 7.0 %copy-start.5 = (bf16[224,384]{1,0:T(8,128)(2,1)}, bf16[224,384]{1,0:T(8,128)(2,1)S(1)}, u32[]{:S(2)}) copy-start(bf16[224,384]{1,0:T(8,128)(2,1)S(1)} %add.124.refs_0_) | copy-start | bytes 516100
  106.2 7.0 %copy-start = (bf16[8,197,384]{2,1,0:T(8,128)(2,1)S(1)}, bf16[8,197,384]{2,1,0:T(8,128)(2,1)}, u32[]{:S(2)}) copy-start(bf16[8,197,384]{2,1,0:T(8,128)(2,1)} %get-tuple-element.148) | copy-start | bytes 3631108
  106.2 9.1 %collective-permute-start.20 = (bf16[224,384]{1,0:T(8,128)(2,1)S(1)}, bf16[224,384]{1,0:T(8,128)(2,1)S(1)}, u32[]{:S(2)}, u32[]{:S(2)}) collective-permute-start(bf16[224,384]{1,0:T(8,128)(2,1)S(1)} %add.124.refs_0_), channel_id=1, source_target_pairs={{0,2},{1,3},{2,0},{3,1},{4,6},{5,7},{6,4},{7,5},{8,10},{9,11},{10,... | collective-permute-start | bytes 516104 | tf_op jit(solution)/shard_map/ppermute | solution.py:638
  106.3 9.0 %collective-permute-start.19 = (bf16[224,384]{1,0:T(8,128)(2,1)S(1)}, bf16[224,384]{1,0:T(8,128)(2,1)S(1)}, u32[]{:S(2)}, u32[]{:S(2)}) collective-permute-start(bf16[224,384]{1,0:T(8,128)(2,1)S(1)} %add.124.refs_0_), channel_id=1, source_target_pairs={{0,4},{1,5},{2,6},{3,7},{4,0},{5,1},{6,2},{7,3},{8,12},{9,13},{10,... | collective-permute-start | bytes 516104 | tf_op jit(solution)/shard_map/ppermute | solution.py:638
  107.9 8.9 %collective-permute-start.17 = (bf16[224,384]{1,0:T(8,128)(2,1)S(1)}, bf16[224,384]{1,0:T(8,128)(2,1)S(1)}, u32[]{:S(2)}, u32[]{:S(2)}) collective-permute-start(bf16[224,384]{1,0:T(8,128)(2,1)S(1)} %add.124.refs_0_), channel_id=1, source_target_pairs={{0,8},{1,9},{2,10},{3,11},{4,12},{5,13},{6,14},{7,15},{8,0},{9,1},... | collective-permute-start | bytes 516104 | tf_op jit(solution)/shard_map/ppermute | solution.py:638
  107.9 7.4 %collective-permute-start.18 = (bf16[152,384]{1,0:T(8,128)(2,1)S(1)}, bf16[152,384]{1,0:T(8,128)(2,1)S(1)}, u32[]{:S(2)}, u32[]{:S(2)}) collective-permute-start(bf16[152,384]{1,0:T(8,128)(2,1)S(1)} %add.125), channel_id=1, source_target_pairs={{0,16},{1,17},{2,18},{3,19},{4,20},{5,21},{6,22},{7,23},{8,24},{9,... | collective-permute-start | bytes 350216 | tf_op jit(solution)/shard_map/ppermute | solution.py:638
  115.3 11.3 %copy-start.13 = (bf16[224,384]{1,0:T(8,128)(2,1)}, bf16[224,384]{1,0:T(8,128)(2,1)S(1)}, u32[]{:S(2)}) copy-start(bf16[224,384]{1,0:T(8,128)(2,1)S(1)} %collective-permute-done.20.refs_4_) | copy-start | bytes 516100
  115.3 11.3 %copy-start.14 = (bf16[224,384]{1,0:T(8,128)(2,1)}, bf16[224,384]{1,0:T(8,128)(2,1)S(1)}, u32[]{:S(2)}) copy-start(bf16[224,384]{1,0:T(8,128)(2,1)S(1)} %collective-permute-done.19.refs_2_) | copy-start | bytes 516100
  116.9 9.8 %copy-start.15 = (bf16[224,384]{1,0:T(8,128)(2,1)}, bf16[224,384]{1,0:T(8,128)(2,1)S(1)}, u32[]{:S(2)}) copy-start(bf16[224,384]{1,0:T(8,128)(2,1)S(1)} %collective-permute-done.17.refs_1_) | copy-start | bytes 516100
  116.9 8.1 %collective-permute-start.21 = (bf16[224,384]{1,0:T(8,128)(2,1)S(1)}, bf16[224,384]{1,0:T(8,128)(2,1)S(1)}, u32[]{:S(2)}, u32[]{:S(2)}) collective-permute-start(bf16[224,384]{1,0:T(8,128)(2,1)S(1)} %collective-permute-done.17.refs_1_), channel_id=1, source_target_pairs={{0,4},{1,5},{2,6},{3,7},{4,0},{5,1},{6,2},{7,3},{8,12},{9,13},{10,... | collective-permute-start | bytes 516104 | tf_op jit(solution)/shard_map/ppermute | solution.py:638
  117.4 9.3 %copy-start.6 = (bf16[152,384]{1,0:T(8,128)(2,1)}, bf16[152,384]{1,0:T(8,128)(2,1)S(1)}, u32[]{:S(2)}) copy-start(bf16[152,384]{1,0:T(8,128)(2,1)S(1)} %add.126.refs_8_) | copy-start | bytes 350212
  117.4 2.2 %collective-permute-start.23 = (bf16[152,384]{1,0:T(8,128)(2,1)S(1)}, bf16[152,384]{1,0:T(8,128)(2,1)S(1)}, u32[]{:S(2)}, u32[]{:S(2)}) collective-permute-start(bf16[152,384]{1,0:T(8,128)(2,1)S(1)} %add.126.refs_8_), channel_id=1, source_target_pairs={{0,2},{1,3},{2,0},{3,1},{4,6},{5,7},{6,4},{7,5},{8,10},{9,11},{10,... | collective-permute-start | bytes 350216 | tf_op jit(solution)/shard_map/ppermute | solution.py:638
  117.5 7.5 %collective-permute-start.22 = (bf16[152,384]{1,0:T(8,128)(2,1)S(1)}, bf16[152,384]{1,0:T(8,128)(2,1)S(1)}, u32[]{:S(2)}, u32[]{:S(2)}) collective-permute-start(bf16[152,384]{1,0:T(8,128)(2,1)S(1)} %add.126.refs_8_), channel_id=1, source_target_pairs={{0,4},{1,5},{2,6},{3,7},{4,0},{5,1},{6,2},{7,3},{8,12},{9,13},{10,... | collective-permute-start | bytes 350216 | tf_op jit(solution)/shard_map/ppermute | solution.py:638
  119.1 6.5 %collective-permute-start.24 = (bf16[224,384]{1,0:T(8,128)(2,1)S(1)}, bf16[224,384]{1,0:T(8,128)(2,1)S(1)}, u32[]{:S(2)}, u32[]{:S(2)}) collective-permute-start(bf16[224,384]{1,0:T(8,128)(2,1)S(1)} %collective-permute-done.17.refs_1_), channel_id=1, source_target_pairs={{0,2},{1,3},{2,0},{3,1},{4,6},{5,7},{6,4},{7,5},{8,10},{9,11},{10,... | collective-permute-start | bytes 516104 | tf_op jit(solution)/shard_map/ppermute | solution.py:638
  119.3 6.3 %collective-permute-start.25 = (bf16[224,384]{1,0:T(8,128)(2,1)S(1)}, bf16[224,384]{1,0:T(8,128)(2,1)S(1)}, u32[]{:S(2)}, u32[]{:S(2)}) collective-permute-start(bf16[224,384]{1,0:T(8,128)(2,1)S(1)} %collective-permute-done.19.refs_2_), channel_id=1, source_target_pairs={{0,2},{1,3},{2,0},{3,1},{4,6},{5,7},{6,4},{7,5},{8,10},{9,11},{10,... | collective-permute-start | bytes 516104 | tf_op jit(solution)/shard_map/ppermute | solution.py:638
  119.6 7.1 %copy-start.20 = (bf16[152,384]{1,0:T(8,128)(2,1)}, bf16[152,384]{1,0:T(8,128)(2,1)S(1)}, u32[]{:S(2)}) copy-start(bf16[152,384]{1,0:T(8,128)(2,1)S(1)} %collective-permute-done.23.refs_10_) | copy-start | bytes 350212
  125.0 1.7 %copy-start.21 = (bf16[152,384]{1,0:T(8,128)(2,1)}, bf16[152,384]{1,0:T(8,128)(2,1)S(1)}, u32[]{:S(2)}) copy-start(bf16[152,384]{1,0:T(8,128)(2,1)S(1)} %collective-permute-done.22.refs_9_) | copy-start | bytes 350212
  125.0 1.7 %copy-start.16 = (bf16[224,384]{1,0:T(8,128)(2,1)}, bf16[224,384]{1,0:T(8,128)(2,1)S(1)}, u32[]{:S(2)}) copy-start(bf16[224,384]{1,0:T(8,128)(2,1)S(1)} %collective-permute-done.21.refs_3_) | copy-start | bytes 516100
  125.0 1.6 %collective-permute-start.26 = (bf16[224,384]{1,0:T(8,128)(2,1)S(1)}, bf16[224,384]{1,0:T(8,128)(2,1)S(1)}, u32[]{:S(2)}, u32[]{:S(2)}) collective-permute-start(bf16[224,384]{1,0:T(8,128)(2,1)S(1)} %collective-permute-done.21.refs_3_), channel_id=1, source_target_pairs={{0,2},{1,3},{2,0},{3,1},{4,6},{5,7},{6,4},{7,5},{8,10},{9,11},{10,... | collective-permute-start | bytes 516104 | tf_op jit(solution)/shard_map/ppermute | solution.py:638
  125.1 1.6 %collective-permute-start.27 = (bf16[152,384]{1,0:T(8,128)(2,1)S(1)}, bf16[152,384]{1,0:T(8,128)(2,1)S(1)}, u32[]{:S(2)}, u32[]{:S(2)}) collective-permute-start(bf16[152,384]{1,0:T(8,128)(2,1)S(1)} %collective-permute-done.22.refs_9_), channel_id=1, source_target_pairs={{0,2},{1,3},{2,0},{3,1},{4,6},{5,7},{6,4},{7,5},{8,10},{9,11},{10,... | collective-permute-start | bytes 350216 | tf_op jit(solution)/shard_map/ppermute | solution.py:638
  125.6 1.1 copy-start.18
  125.6 1.1 copy-start.17
  126.6 0.7 copy-start.22
  127.3 0.7 copy-start.19

commit v11 on v9

--- a/solution.py
+++ b/solution.py
@@ -431,7 +431,7 @@
         ref[...] = own_half(index, vectors[i : i + 1, :])
 
 
-VMEM_LIMIT = 60 * 1024 * 1024
+VMEM_LIMIT = 40 * 1024 * 1024
 PARAMS = pltpu.CompilerParams(vmem_limit_bytes=VMEM_LIMIT)
 SCALARS = pl.BlockSpec(memory_space=pltpu.SMEM)
 

time: 131 us -> 130 us (level)
  Pallas kernels: 69.2 us -> 54.5 us
  local copies, waits for them, and re-layouts: 7.62 us -> 16.1 us
  waiting for transfers between devices: 23 us -> 26.9 us
  other arithmetic: 2.36 us -> 3.8 us
    unnamed x50 -> x54, local copies, waits for them, and re-layouts: 5.2 us -> 13.7 us
    pallas_call x2, Pallas kernels: 24.1 us -> 19.3 us  [attention_backward(): pl.pallas_call(functools.partial(back_kernel, length, first, last), grid=...]
    ppermute x28, waiting for transfers between devices: 23 us -> 26.9 us  [swap(): return lax.ppermute(v, AXES, pairs)]
    pallas_call x1, Pallas kernels: 27.4 us -> 24.1 us  [mlp_both_ways(): pl.pallas_call(functools.partial(mlp_kernel, length, 512), grid=(images /...]
    pallas_call x1, Pallas kernels: 9.91 us -> 7.19 us  [forward_attention(): pl.pallas_call(functools.partial(attend_kernel, length), grid=(images //...]
    pallas_call x1, Pallas kernels: 2.19 us -> 0.6 us  [pack_rest(): pl.pallas_call(pack_rest_kernel, grid=(1,), in_specs=[SCALARS, *whole_lik...]
  transfers between devices with their start and end apart: 28 -> 28, of which waited for: 13 -> 14; matrix products, arithmetic and copies ran while one was open for 5% -> 5% of each run, Pallas kernels for 28% -> 21%
where the time goes in v11:
time: 130 us; the launch traced here: 129 us
  Pallas kernels  54.5 us (42%)
  starting transfers between devices  27 us (21%)
  waiting for transfers between devices  26.9 us (21%)
  local copies, waits for them, and re-layouts  16.1 us (12%)
  other arithmetic  3.8 us (3%)
    ppermute x28, starting transfers between devices, swap(): return lax.ppermute(v, AXES, pairs)  27 us
    ppermute x28, waiting for transfers between devices, swap(): return lax.ppermute(v, AXES, pairs)  26.9 us
    pallas_call x1, Pallas kernels, mlp_both_ways(): pl.pallas_call(functools.partial(mlp_kernel, length, 512), grid=(images /...  24.1 us
    pallas_call x2, Pallas kernels, attention_backward(): pl.pallas_call(functools.partial(back_kernel, length, first, last), grid=...  19.3 us
    unnamed x54, local copies, waits for them, and re-layouts  13.7 us
    pallas_call x1, Pallas kernels, forward_attention(): pl.pallas_call(functools.partial(attend_kernel, length), grid=(images //...  7.19 us
    pallas_call x1, Pallas kernels, unpack(): pl.pallas_call(unpack_kernel, grid=(1,), in_specs=[SCALARS, *whole_like((...  2.69 us
  transfers between devices with their start and end apart: 28, of which 14 were waited for; matrix products, arithmetic and copies ran while one was open for 5% of the time, Pallas kernels for 21%

profile of v11, /device:TPU:0, one launch (start us, length us, event | category | flops | bytes accessed | tf_op | source)
XLA Modules:
  0.0 129.1 jit_solution(1802404543843369542)
XLA Ops:
  0.7 1.0 copy-done.7
  1.7 0.7 copy-done.11
  2.4 0.7 copy-done.12
  3.1 0.7 copy-done.13
  3.7 0.7 copy-done.14
  4.4 0.7 copy-done.15
  5.1 0.7 copy-done.16
  5.7 0.7 copy-done.17
  6.4 0.7 copy-done.18
  7.0 0.7 copy-done.19
  7.7 0.6 pack_first.1.packed
  8.3 3.0 %collective-permute-start = (bf16[104,1152]{1,0:T(8,128)(2,1)S(1)}, bf16[104,1152]{1,0:T(8,128)(2,1)S(1)}, u32[]{:S(2)}, u32[]{:S(2)}) collective-permute-start(bf16[104,1152]{1,0:T(8,128)(2,1)S(1)} %pack_first.1.packed), channel_id=1, source_target_pairs={{0,1},{1,0},{2,3},{3,2},{4,5},{5,4},{6,7},{7,6},{8,9},{9,8},{10,11... | collective-permute-start | bytes 718856 | tf_op jit(solution)/shard_map/ppermute | solution.py:638
  11.3 1.1 copy-done.3
  12.3 1.1 copy-done.5
  13.4 0.9 copy-done.9
  14.3 0.6 pack_rest.1
  15.0 2.0 %collective-permute-start.2 = (bf16[96,1536]{1,0:T(8,128)(2,1)S(1)}, bf16[96,1536]{1,0:T(8,128)(2,1)S(1)}, u32[]{:S(2)}, u32[]{:S(2)}) collective-permute-start(bf16[96,1536]{1,0:T(8,128)(2,1)S(1)} %get-tuple-element.105), channel_id=1, source_target_pairs={{0,1},{1,0},{2,3},{3,2},{4,5},{5,4},{6,7},{7,6},{8,9},{9,8},{10,11... | collective-permute-start | bytes 884744 | tf_op jit(solution)/shard_map/ppermute | solution.py:638
  17.0 0.2 copy.31.tok_ref
  17.2 0.3 collective-permute-done.near
  17.5 1.5 %collective-permute-done.1.far = bf16[104,1152]{1,0:T(8,128)(2,1)S(1)} collective-permute-done((bf16[104,1152]{1,0:T(8,128)(2,1)S(1)}, bf16[104,1152]{1,0:T(8,128)(2,1)S(1)}, u32[]{:S(2)}, u32[]{:S(2)}) %collective-permute-start.1) | collective-permute-done | bytes 239648 | tf_op jit(solution)/shard_map/ppermute | solution.py:638
  19.0 7.2 %attend.1 = (bf16[8,208,384]{2,1,0:T(8,128)(2,1)S(1)}, bf16[8,208,1152]{2,1,0:T(8,128)(2,1)S(1)}, bf16[8,208,384]{2,1,0:T(8,128)(2,1)S(1)}, bf16[384,1152]{1,0:T(8,128)(2,1)S(1)}, f32[12,384]{1,0:T(8,128)S(1)}) custom-call(s32[4]{0:T(128)S(1)} %pad_add_fusion.index, bf16[8,197,384]{2,1,0:T(8,128)(2,1)S(1)} %copy.31.tok_ref, ...), custom_call_target="tpu_custom_call" | custom-call | flops 1000 | bytes 1 | tf_op jit(solution)/shard_map/attend/pallas_call | solution.py:493
  26.2 5.1 %collective-permute-done.2.lift_near = bf16[96,1536]{1,0:T(8,128)(2,1)S(1)} collective-permute-done((bf16[96,1536]{1,0:T(8,128)(2,1)S(1)}, bf16[96,1536]{1,0:T(8,128)(2,1)S(1)}, u32[]{:S(2)}, u32[]{:S(2)}) %collective-permute-start.2) | collective-permute-done | bytes 294944 | tf_op jit(solution)/shard_map/ppermute | solution.py:638
  31.4 0.5 collective-permute-start.4
  31.9 0.2 copy.32.cot_ref
  32.0 1.4 %collective-permute-done.4.lift_far = bf16[96,1536]{1,0:T(8,128)(2,1)S(1)} collective-permute-done((bf16[96,1536]{1,0:T(8,128)(2,1)S(1)}, bf16[96,1536]{1,0:T(8,128)(2,1)S(1)}, u32[]{:S(2)}, u32[]{:S(2)}) %collective-permute-start.4) | collective-permute-done | bytes 294944 | tf_op jit(solution)/shard_map/ppermute | solution.py:638
  33.5 24.1 %mlp.1 = (bf16[8,197,384]{2,1,0:T(8,128)(2,1)S(1)}, f32[8,208,384]{2,1,0:T(8,128)S(1)}, bf16[8,208,384]{2,1,0:T(8,128)(2,1)S(1)}, bf16[2,2,448,384]{3,2,1,0:T(8,128)(2,1)S(1)}, bf16[2,2,448,384]{3,2,1,0:T(8,128)(2,1)S(1)}) custom-call(s32[4]{0:T(128)S(1)} %pad_add_fusion.index, bf16[8,197,384]{2,1,0:T(8,128)(2,1)S(1)} %copy.31.tok_ref, ...), custom_call_target="tpu_custom_call" | custom-call | flops 1000 | bytes 1 | tf_op jit(solution)/shard_map/mlp/pallas_call | solution.py:523
  57.6 0.2 collective-permute-start.6
  57.9 4.9 %back.2 = (bf16[8,197,384]{2,1,0:T(8,128)(2,1)S(1)}, f32[384,1152]{1,0:T(8,128)S(1)}, f32[8,1152]{1,0:T(8,128)S(1)}, f32[2,384]{1,0:T(2,128)S(1)}) custom-call(s32[4]{0:T(128)S(1)} %pad_add_fusion.index, bf16[8,197,384]{2,1,0:T(8,128)(2,1)S(1)} %copy.31.tok_ref, bf16[8,208,1152]{2,1,0:T(8,128)(2,1)S(1)} %get-tuple-element.112.proj_ref, ...), custom_call_target="tpu_custom_call" | custom-call | flops 1000 | bytes 1 | tf_op jit(solution)/shard_map/back/pallas_call | solution.py:581
  62.9 1.0 copy-done.20
  63.8 1.7 %collective-permute-start.7 = (bf16[448,384]{1,0:T(8,128)(2,1)S(1)}, bf16[448,384]{1,0:T(8,128)(2,1)S(1)}, u32[]{:S(2)}, u32[]{:S(2)}) collective-permute-start(bf16[448,384]{1,0:T(8,128)(2,1)S(1)} %get-tuple-element.130), channel_id=1, source_target_pairs={{0,1},{1,0},{2,3},{3,2},{4,5},{5,4},{6,7},{7,6},{8,9},{9,8},{10,11... | collective-permute-start | bytes 1032200 | tf_op jit(solution)/shard_map/ppermute | solution.py:638
  65.6 1.5 %collective-permute-start.8 = (bf16[448,384]{1,0:T(8,128)(2,1)S(1)}, bf16[448,384]{1,0:T(8,128)(2,1)S(1)}, u32[]{:S(2)}, u32[]{:S(2)}) collective-permute-start(bf16[448,384]{1,0:T(8,128)(2,1)S(1)} %get-tuple-element.131), channel_id=1, source_target_pairs={{0,4},{1,5},{2,6},{3,7},{4,0},{5,1},{6,2},{7,3},{8,12},{9,13},{10,... | collective-permute-start | bytes 1032200 | tf_op jit(solution)/shard_map/ppermute | solution.py:638
  67.1 0.3 collective-permute-start.9
  67.4 14.4 %back.3 = (bf16[8,197,384]{2,1,0:T(8,128)(2,1)S(1)}, bf16[2,2,152,384]{3,2,1,0:T(8,128)(2,1)S(1)}, bf16[2,2,152,384]{3,2,1,0:T(8,128)(2,1)S(1)}) custom-call(s32[4]{0:T(128)S(1)} %pad_add_fusion.index, bf16[8,197,384]{2,1,0:T(8,128)(2,1)S(1)} %copy.31.tok_ref, bf16[8,208,1152]{2,1,0:T(8,128)(2,1)} %copy-done, ...), custom_call_target="tpu_custom_call", output_to_operand_aliasing={{0}: (11, {})} | custom-call | flops 1000 | bytes 1 | tf_op jit(solution)/shard_map/back/pallas_call | solution.py:581
  81.8 1.1 copy-done.1
  82.8 0.1 collective-permute-done.8
  83.0 0.6 copy-done.23
  83.7 0.6 copy-done.25
  84.3 1.4 %fusion.1 = bf16[448,384]{1,0:T(8,128)(2,1)S(1)} fusion(bf16[448,384]{1,0:T(8,128)(2,1)} %copy-done.25, bf16[448,384]{1,0:T(8,128)(2,1)} %copy-done.24, bf16[448,384]{1,0:T(8,128)(2,1)} %copy-done.23, bf16[2,2,448,384]{3,2,1,0:T(8,128)(2,1)} %copy-done.20, bf16[2,2,448,384]{3,2,1,0:T(8,128)(2,1)S(1)} %get-tuple-element.111), kind=kLoop, calls=%fused_computation.4 | loop fusion | flops 688128 | bytes 2064384 | tf_op jit(solution)/shard_map/add | solution.py:785
  85.8 1.8 %collective-permute-start.10 = (bf16[224,384]{1,0:T(8,128)(2,1)S(1)}, bf16[224,384]{1,0:T(8,128)(2,1)S(1)}, u32[]{:S(2)}, u32[]{:S(2)}) collective-permute-start(bf16[224,384]{1,0:T(8,128)(2,1)S(1)} %get-tuple-element.189), channel_id=1, source_target_pairs={{0,8},{1,9},{2,10},{3,11},{4,12},{5,13},{6,14},{7,15},{8,0},{9,1},... | collective-permute-start | bytes 516104 | tf_op jit(solution)/shard_map/ppermute | solution.py:638
  87.6 1.1 add_bitcast_fusion.3
  88.7 2.5 %collective-permute-start.15 = (bf16[152,384]{1,0:T(8,128)(2,1)S(1)}, bf16[152,384]{1,0:T(8,128)(2,1)S(1)}, u32[]{:S(2)}, u32[]{:S(2)}) collective-permute-start(bf16[152,384]{1,0:T(8,128)(2,1)S(1)} %get-tuple-element.186), channel_id=1, source_target_pairs={{0,5},{1,4},{2,7},{3,6},{4,1},{5,0},{6,3},{7,2},{8,13},{9,12},{10,... | collective-permute-start | bytes 350216 | tf_op jit(solution)/shard_map/ppermute | solution.py:638
  91.2 0.5 collective-permute-start.14
  91.7 0.5 collective-permute-start.13
  92.3 0.4 collective-permute-done.10
  92.7 2.8 %collective-permute-start.12 = (bf16[224,384]{1,0:T(8,128)(2,1)S(1)}, bf16[224,384]{1,0:T(8,128)(2,1)S(1)}, u32[]{:S(2)}, u32[]{:S(2)}) collective-permute-start(bf16[224,384]{1,0:T(8,128)(2,1)S(1)} %add.103), channel_id=1, source_target_pairs={{0,16},{1,17},{2,18},{3,19},{4,20},{5,21},{6,22},{7,23},{8,24},{9,... | collective-permute-start | bytes 516104 | tf_op jit(solution)/shard_map/ppermute | solution.py:638
  95.5 2.0 %collective-permute-done.14 = bf16[152,384]{1,0:T(8,128)(2,1)S(1)} collective-permute-done((bf16[152,384]{1,0:T(8,128)(2,1)S(1)}, bf16[152,384]{1,0:T(8,128)(2,1)S(1)}, u32[]{:S(2)}, u32[]{:S(2)}) %collective-permute-start.14) | collective-permute-done | bytes 116768 | tf_op jit(solution)/shard_map/ppermute | solution.py:638
  97.6 1.0 fusion.3
  98.5 0.5 collective-permute-start.16
  99.0 4.6 %collective-permute-done.12 = bf16[224,384]{1,0:T(8,128)(2,1)S(1)} collective-permute-done((bf16[224,384]{1,0:T(8,128)(2,1)S(1)}, bf16[224,384]{1,0:T(8,128)(2,1)S(1)}, u32[]{:S(2)}, u32[]{:S(2)}) %collective-permute-start.12) | collective-permute-done | bytes 172064 | tf_op jit(solution)/shard_map/ppermute | solution.py:638
  103.6 2.4 %collective-permute-done.16 = bf16[152,384]{1,0:T(8,128)(2,1)S(1)} collective-permute-done((bf16[152,384]{1,0:T(8,128)(2,1)S(1)}, bf16[152,384]{1,0:T(8,128)(2,1)S(1)}, u32[]{:S(2)}, u32[]{:S(2)}) %collective-permute-start.16) | collective-permute-done | bytes 116768 | tf_op jit(solution)/shard_map/ppermute | solution.py:638
  106.2 1.6 %collective-permute-start.19 = (bf16[224,384]{1,0:T(8,128)(2,1)S(1)}, bf16[224,384]{1,0:T(8,128)(2,1)S(1)}, u32[]{:S(2)}, u32[]{:S(2)}) collective-permute-start(bf16[224,384]{1,0:T(8,128)(2,1)S(1)} %add.109.refs_0_), channel_id=1, source_target_pairs={{0,4},{1,5},{2,6},{3,7},{4,0},{5,1},{6,2},{7,3},{8,12},{9,13},{10,... | collective-permute-start | bytes 516104 | tf_op jit(solution)/shard_map/ppermute | solution.py:638
  107.8 4.1 %collective-permute-start.18 = (bf16[152,384]{1,0:T(8,128)(2,1)S(1)}, bf16[152,384]{1,0:T(8,128)(2,1)S(1)}, u32[]{:S(2)}, u32[]{:S(2)}) collective-permute-start(bf16[152,384]{1,0:T(8,128)(2,1)S(1)} %add.110), channel_id=1, source_target_pairs={{0,16},{1,17},{2,18},{3,19},{4,20},{5,21},{6,22},{7,23},{8,24},{9,... | collective-permute-start | bytes 350216 | tf_op jit(solution)/shard_map/ppermute | solution.py:638
  111.9 1.2 copy.38
  113.0 1.2 copy.37
  114.2 1.0 collective-permute-done.18
  115.2 1.5 %collective-permute-done.17.refs_1_ = bf16[224,384]{1,0:T(8,128)(2,1)S(1)} collective-permute-done((bf16[224,384]{1,0:T(8,128)(2,1)S(1)}, bf16[224,384]{1,0:T(8,128)(2,1)S(1)}, u32[]{:S(2)}, u32[]{:S(2)}) %collective-permute-start.17) | collective-permute-done | bytes 172064 | tf_op jit(solution)/shard_map/ppermute | solution.py:638
  116.7 0.5 collective-permute-start.21
  117.3 1.6 %collective-permute-start.22 = (bf16[152,384]{1,0:T(8,128)(2,1)S(1)}, bf16[152,384]{1,0:T(8,128)(2,1)S(1)}, u32[]{:S(2)}, u32[]{:S(2)}) collective-permute-start(bf16[152,384]{1,0:T(8,128)(2,1)S(1)} %add.111.refs_8_), channel_id=1, source_target_pairs={{0,4},{1,5},{2,6},{3,7},{4,0},{5,1},{6,2},{7,3},{8,12},{9,13},{10,... | collective-permute-start | bytes 350216 | tf_op jit(solution)/shard_map/ppermute | solution.py:638
  119.0 0.2 collective-permute-start.24
  119.1 0.3 collective-permute-start.25
  119.5 5.4 %collective-permute-done.22.refs_9_ = bf16[152,384]{1,0:T(8,128)(2,1)S(1)} collective-permute-done((bf16[152,384]{1,0:T(8,128)(2,1)S(1)}, bf16[152,384]{1,0:T(8,128)(2,1)S(1)}, u32[]{:S(2)}, u32[]{:S(2)}) %collective-permute-start.22) | collective-permute-done | bytes 116768 | tf_op jit(solution)/shard_map/ppermute | solution.py:638
  124.9 0.5 collective-permute-start.27
  125.4 1.1 collective-permute-done.27.refs_11_
  126.4 2.7 %unpack.1 = (f32[768,384]{1,0:T(8,128)}, f32[192,1536]{1,0:T(8,128)}, f32[192,384]{1,0:T(8,128)}, f32[192]{0:T(256)}, f32[192]{0:T(256)}, /*index=5*/f32[192]{0:...) custom-call(s32[4]{0:T(128)S(1)} %pad_add_fusion.index, ...), custom_call_target="tpu_custom_call" | custom-call | flops 1000 | bytes 1 | tf_op jit(solution)/shard_map/unpack/pallas_call | solution.py:609
  (65 shorter events, 1.0 us)
Async XLA Ops:
  0.7 1.0 copy-start.7
  1.7 0.7 copy-start.11
  2.4 0.7 copy-start.12
  3.1 0.7 copy-start.13
  3.7 0.7 copy-start.14
  4.4 0.7 copy-start.15
  5.0 0.7 copy-start.16
  5.7 0.7 copy-start.17
  6.4 0.7 copy-start.18
  7.0 0.7 copy-start.19
  8.3 9.2 %collective-permute-start = (bf16[104,1152]{1,0:T(8,128)(2,1)S(1)}, bf16[104,1152]{1,0:T(8,128)(2,1)S(1)}, u32[]{:S(2)}, u32[]{:S(2)}) collective-permute-start(bf16[104,1152]{1,0:T(8,128)(2,1)S(1)} %pack_first.1.packed), channel_id=1, source_target_pairs={{0,1},{1,0},{2,3},{3,2},{4,5},{5,4},{6,7},{7,6},{8,9},{9,8},{10,11... | collective-permute-start | bytes 718856 | tf_op jit(solution)/shard_map/ppermute | solution.py:638
  11.3 1.1 copy-start.3
  12.3 1.1 copy-start.5
  13.4 0.9 copy-start.9
  14.3 2.7 %copy-start.21 = (bf16[8,197,384]{2,0,1:T(8,128)(2,1)S(1)}, bf16[8,197,384]{2,0,1:T(8,128)(2,1)}, u32[]{:S(2)}) copy-start(bf16[8,197,384]{2,0,1:T(8,128)(2,1)} %param.15) | copy-start | bytes 3631108
  14.9 4.1 %copy-start.8 = (bf16[192,1152]{1,0:T(8,128)(2,1)S(1)}, bf16[192,1152]{1,0:T(8,128)(2,1)}, u32[]{:S(2)}) copy-start(bf16[192,1152]{1,0:T(8,128)(2,1)} %own.1) | copy-start | bytes 1327108
  14.9 16.4 %collective-permute-start.3 = (bf16[480,384]{1,0:T(8,128)(2,1)S(1)}, bf16[480,384]{1,0:T(8,128)(2,1)S(1)}, u32[]{:S(2)}, u32[]{:S(2)}) collective-permute-start(bf16[480,384]{1,0:T(8,128)(2,1)S(1)} %get-tuple-element.106), channel_id=1, source_target_pairs={{0,1},{1,0},{2,3},{3,2},{4,5},{5,4},{6,7},{7,6},{8,9},{9,8},{10,11... | collective-permute-start | bytes 1105928 | tf_op jit(solution)/shard_map/ppermute | solution.py:638
  15.0 16.4 %collective-permute-start.2 = (bf16[96,1536]{1,0:T(8,128)(2,1)S(1)}, bf16[96,1536]{1,0:T(8,128)(2,1)S(1)}, u32[]{:S(2)}, u32[]{:S(2)}) collective-permute-start(bf16[96,1536]{1,0:T(8,128)(2,1)S(1)} %get-tuple-element.105), channel_id=1, source_target_pairs={{0,1},{1,0},{2,3},{3,2},{4,5},{5,4},{6,7},{7,6},{8,9},{9,8},{10,11... | collective-permute-start | bytes 884744 | tf_op jit(solution)/shard_map/ppermute | solution.py:638
  17.2 14.7 %copy-start.22 = (bf16[8,197,384]{2,0,1:T(8,128)(2,1)S(1)}, bf16[8,197,384]{2,0,1:T(8,128)(2,1)}, u32[]{:S(2)}) copy-start(bf16[8,197,384]{2,0,1:T(8,128)(2,1)} %param.29) | copy-start | bytes 3631108
  17.5 1.5 %collective-permute-start.1 = (bf16[104,1152]{1,0:T(8,128)(2,1)S(1)}, bf16[104,1152]{1,0:T(8,128)(2,1)S(1)}, u32[]{:S(2)}, u32[]{:S(2)}) collective-permute-start(bf16[104,1152]{1,0:T(8,128)(2,1)S(1)} %collective-permute-done.near), channel_id=1, source_target_pairs={{0,2},{1,3},{2,0},{3,1},{4,6},{5,7},{6,4},{7,5},{8,10},{9,11},{10,... | collective-permute-start | bytes 718856 | tf_op jit(solution)/shard_map/ppermute | solution.py:638
  26.2 31.7 %copy-start = (bf16[8,208,1152]{2,1,0:T(8,128)(2,1)}, bf16[8,208,1152]{2,1,0:T(8,128)(2,1)S(1)}, u32[]{:S(2)}) copy-start(bf16[8,208,1152]{2,1,0:T(8,128)(2,1)S(1)} %get-tuple-element.112.proj_ref) | copy-start | bytes 11501572
  26.2 7.3 %copy-start.4 = (bf16[192,1536]{1,0:T(8,128)(2,1)S(1)}, bf16[192,1536]{1,0:T(8,128)(2,1)}, u32[]{:S(2)}) copy-start(bf16[192,1536]{1,0:T(8,128)(2,1)} %lift_own.2) | copy-start | bytes 1769476
  26.2 7.3 %copy-start.6 = (bf16[768,384]{1,0:T(8,128)(2,1)S(1)}, bf16[768,384]{1,0:T(8,128)(2,1)}, u32[]{:S(2)}) copy-start(bf16[768,384]{1,0:T(8,128)(2,1)} %drop_own.2) | copy-start | bytes 1769476
  26.2 7.2 %copy-start.10 = (bf16[192,384]{1,0:T(8,128)(2,1)S(1)}, bf16[192,384]{1,0:T(8,128)(2,1)}, u32[]{:S(2)}) copy-start(bf16[192,384]{1,0:T(8,128)(2,1)} %out_own.2) | copy-start | bytes 442372
  31.4 2.1 %collective-permute-start.5 = (bf16[480,384]{1,0:T(8,128)(2,1)S(1)}, bf16[480,384]{1,0:T(8,128)(2,1)S(1)}, u32[]{:S(2)}, u32[]{:S(2)}) collective-permute-start(bf16[480,384]{1,0:T(8,128)(2,1)S(1)} %collective-permute-done.3.both_near), channel_id=1, source_target_pairs={{0,2},{1,3},{2,0},{3,1},{4,6},{5,7},{6,4},{7,5},{8,10},{9,11},{10,... | collective-permute-start | bytes 1105928 | tf_op jit(solution)/shard_map/ppermute | solution.py:638
  31.4 2.1 %collective-permute-start.4 = (bf16[96,1536]{1,0:T(8,128)(2,1)S(1)}, bf16[96,1536]{1,0:T(8,128)(2,1)S(1)}, u32[]{:S(2)}, u32[]{:S(2)}) collective-permute-start(bf16[96,1536]{1,0:T(8,128)(2,1)S(1)} %collective-permute-done.2.lift_near), channel_id=1, source_target_pairs={{0,2},{1,3},{2,0},{3,1},{4,6},{5,7},{6,4},{7,5},{8,10},{9,11},{10,... | collective-permute-start | bytes 884744 | tf_op jit(solution)/shard_map/ppermute | solution.py:638
  57.6 5.1 %collective-permute-start.6 = (bf16[2,2,448,384]{3,2,1,0:T(8,128)(2,1)S(1)}, bf16[2,2,448,384]{3,2,1,0:T(8,128)(2,1)S(1)}, u32[]{:S(2)}, u32[]{:S(2)}) collective-permute-start(bf16[2,2,448,384]{3,2,1,0:T(8,128)(2,1)S(1)} %get-tuple-element.120), channel_id=1, source_target_pairs={{0,2},{1,3},{2,0},{3,1},{4,6},{5,7},{6,4},{7,5},{8,10},{9,11},{10,... | collective-permute-start | bytes 4128776 | tf_op jit(solution)/shard_map/ppermute | solution.py:638
  62.7 1.1 copy-start.20
  63.8 19.0 %collective-permute-start.7 = (bf16[448,384]{1,0:T(8,128)(2,1)S(1)}, bf16[448,384]{1,0:T(8,128)(2,1)S(1)}, u32[]{:S(2)}, u32[]{:S(2)}) collective-permute-start(bf16[448,384]{1,0:T(8,128)(2,1)S(1)} %get-tuple-element.130), channel_id=1, source_target_pairs={{0,1},{1,0},{2,3},{3,2},{4,5},{5,4},{6,7},{7,6},{8,9},{9,8},{10,11... | collective-permute-start | bytes 1032200 | tf_op jit(solution)/shard_map/ppermute | solution.py:638
  65.6 17.4 %collective-permute-start.8 = (bf16[448,384]{1,0:T(8,128)(2,1)S(1)}, bf16[448,384]{1,0:T(8,128)(2,1)S(1)}, u32[]{:S(2)}, u32[]{:S(2)}) collective-permute-start(bf16[448,384]{1,0:T(8,128)(2,1)S(1)} %get-tuple-element.131), channel_id=1, source_target_pairs={{0,4},{1,5},{2,6},{3,7},{4,0},{5,1},{6,2},{7,3},{8,12},{9,13},{10,... | collective-permute-start | bytes 1032200 | tf_op jit(solution)/shard_map/ppermute | solution.py:638
  67.1 15.9 %collective-permute-start.9 = (bf16[448,384]{1,0:T(8,128)(2,1)S(1)}, bf16[448,384]{1,0:T(8,128)(2,1)S(1)}, u32[]{:S(2)}, u32[]{:S(2)}) collective-permute-start(bf16[448,384]{1,0:T(8,128)(2,1)S(1)} %get-tuple-element.132), channel_id=1, source_target_pairs={{0,5},{1,4},{2,7},{3,6},{4,1},{5,0},{6,3},{7,2},{8,13},{9,12},{10,... | collective-permute-start | bytes 1032200 | tf_op jit(solution)/shard_map/ppermute | solution.py:638
  81.8 1.1 copy-start.1
  82.8 0.7 copy-start.23
  83.0 0.7 copy-start.24
  83.6 0.7 copy-start.25
  84.3 3.3 %collective-permute-start.11 = (bf16[2,2,152,384]{3,2,1,0:T(8,128)(2,1)S(1)}, bf16[2,2,152,384]{3,2,1,0:T(8,128)(2,1)}, u32[]{:S(2)}, u32[]{:S(2)}) collective-permute-start(bf16[2,2,152,384]{3,2,1,0:T(8,128)(2,1)S(1)} %get-tuple-element.137), channel_id=1, source_target_pairs={{0,2},{1,3},{2,0},{3,1},{4,6},{5,7},{6,4},{7,5},{8,10},{9,11},{10,... | collective-permute-start | bytes 1400840 | tf_op jit(solution)/shard_map/ppermute | solution.py:638
  85.8 6.9 %collective-permute-start.10 = (bf16[224,384]{1,0:T(8,128)(2,1)S(1)}, bf16[224,384]{1,0:T(8,128)(2,1)S(1)}, u32[]{:S(2)}, u32[]{:S(2)}) collective-permute-start(bf16[224,384]{1,0:T(8,128)(2,1)S(1)} %get-tuple-element.189), channel_id=1, source_target_pairs={{0,8},{1,9},{2,10},{3,11},{4,12},{5,13},{6,14},{7,15},{8,0},{9,1},... | collective-permute-start | bytes 516104 | tf_op jit(solution)/shard_map/ppermute | solution.py:638
  88.7 6.8 %collective-permute-start.15 = (bf16[152,384]{1,0:T(8,128)(2,1)S(1)}, bf16[152,384]{1,0:T(8,128)(2,1)S(1)}, u32[]{:S(2)}, u32[]{:S(2)}) collective-permute-start(bf16[152,384]{1,0:T(8,128)(2,1)S(1)} %get-tuple-element.186), channel_id=1, source_target_pairs={{0,5},{1,4},{2,7},{3,6},{4,1},{5,0},{6,3},{7,2},{8,13},{9,12},{10,... | collective-permute-start | bytes 350216 | tf_op jit(solution)/shard_map/ppermute | solution.py:638
  91.2 6.3 %collective-permute-start.14 = (bf16[152,384]{1,0:T(8,128)(2,1)S(1)}, bf16[152,384]{1,0:T(8,128)(2,1)S(1)}, u32[]{:S(2)}, u32[]{:S(2)}) collective-permute-start(bf16[152,384]{1,0:T(8,128)(2,1)S(1)} %get-tuple-element.187), channel_id=1, source_target_pairs={{0,4},{1,5},{2,6},{3,7},{4,0},{5,1},{6,2},{7,3},{8,12},{9,13},{10,... | collective-permute-start | bytes 350216 | tf_op jit(solution)/shard_map/ppermute | solution.py:638
  91.7 5.8 %collective-permute-start.13 = (bf16[152,384]{1,0:T(8,128)(2,1)S(1)}, bf16[152,384]{1,0:T(8,128)(2,1)S(1)}, u32[]{:S(2)}, u32[]{:S(2)}) collective-permute-start(bf16[152,384]{1,0:T(8,128)(2,1)S(1)} %get-tuple-element.188), channel_id=1, source_target_pairs={{0,1},{1,0},{2,3},{3,2},{4,5},{5,4},{6,7},{7,6},{8,9},{9,8},{10,11... | collective-permute-start | bytes 350216 | tf_op jit(solution)/shard_map/ppermute | solution.py:638
  92.7 10.9 %collective-permute-start.12 = (bf16[224,384]{1,0:T(8,128)(2,1)S(1)}, bf16[224,384]{1,0:T(8,128)(2,1)S(1)}, u32[]{:S(2)}, u32[]{:S(2)}) collective-permute-start(bf16[224,384]{1,0:T(8,128)(2,1)S(1)} %add.103), channel_id=1, source_target_pairs={{0,16},{1,17},{2,18},{3,19},{4,20},{5,21},{6,22},{7,23},{8,24},{9,... | collective-permute-start | bytes 516104 | tf_op jit(solution)/shard_map/ppermute | solution.py:638
  98.5 7.5 %collective-permute-start.16 = (bf16[152,384]{1,0:T(8,128)(2,1)S(1)}, bf16[152,384]{1,0:T(8,128)(2,1)S(1)}, u32[]{:S(2)}, u32[]{:S(2)}) collective-permute-start(bf16[152,384]{1,0:T(8,128)(2,1)S(1)} %fusion.3), channel_id=1, source_target_pairs={{0,8},{1,9},{2,10},{3,11},{4,12},{5,13},{6,14},{7,15},{8,0},{9,1},... | collective-permute-start | bytes 350216 | tf_op jit(solution)/shard_map/ppermute | solution.py:638
  106.1 7.0 %copy-start.2 = (bf16[8,197,384]{2,1,0:T(8,128)(2,1)S(1)}, bf16[8,197,384]{2,1,0:T(8,128)(2,1)}, u32[]{:S(2)}) copy-start(bf16[8,197,384]{2,1,0:T(8,128)(2,1)} %copy-done.1) | copy-start | bytes 3631108
  106.1 9.1 %collective-permute-start.20 = (bf16[224,384]{1,0:T(8,128)(2,1)S(1)}, bf16[224,384]{1,0:T(8,128)(2,1)S(1)}, u32[]{:S(2)}, u32[]{:S(2)}) collective-permute-start(bf16[224,384]{1,0:T(8,128)(2,1)S(1)} %add.109.refs_0_), channel_id=1, source_target_pairs={{0,2},{1,3},{2,0},{3,1},{4,6},{5,7},{6,4},{7,5},{8,10},{9,11},{10,... | collective-permute-start | bytes 516104 | tf_op jit(solution)/shard_map/ppermute | solution.py:638
  106.2 9.0 %collective-permute-start.19 = (bf16[224,384]{1,0:T(8,128)(2,1)S(1)}, bf16[224,384]{1,0:T(8,128)(2,1)S(1)}, u32[]{:S(2)}, u32[]{:S(2)}) collective-permute-start(bf16[224,384]{1,0:T(8,128)(2,1)S(1)} %add.109.refs_0_), channel_id=1, source_target_pairs={{0,4},{1,5},{2,6},{3,7},{4,0},{5,1},{6,2},{7,3},{8,12},{9,13},{10,... | collective-permute-start | bytes 516104 | tf_op jit(solution)/shard_map/ppermute | solution.py:638
  107.8 8.9 %collective-permute-start.17 = (bf16[224,384]{1,0:T(8,128)(2,1)S(1)}, bf16[224,384]{1,0:T(8,128)(2,1)S(1)}, u32[]{:S(2)}, u32[]{:S(2)}) collective-permute-start(bf16[224,384]{1,0:T(8,128)(2,1)S(1)} %add.109.refs_0_), channel_id=1, source_target_pairs={{0,8},{1,9},{2,10},{3,11},{4,12},{5,13},{6,14},{7,15},{8,0},{9,1},... | collective-permute-start | bytes 516104 | tf_op jit(solution)/shard_map/ppermute | solution.py:638
  107.8 7.4 %collective-permute-start.18 = (bf16[152,384]{1,0:T(8,128)(2,1)S(1)}, bf16[152,384]{1,0:T(8,128)(2,1)S(1)}, u32[]{:S(2)}, u32[]{:S(2)}) collective-permute-start(bf16[152,384]{1,0:T(8,128)(2,1)S(1)} %add.110), channel_id=1, source_target_pairs={{0,16},{1,17},{2,18},{3,19},{4,20},{5,21},{6,22},{7,23},{8,24},{9,... | collective-permute-start | bytes 350216 | tf_op jit(solution)/shard_map/ppermute | solution.py:638
  116.7 8.1 %collective-permute-start.21 = (bf16[224,384]{1,0:T(8,128)(2,1)S(1)}, bf16[224,384]{1,0:T(8,128)(2,1)S(1)}, u32[]{:S(2)}, u32[]{:S(2)}) collective-permute-start(bf16[224,384]{1,0:T(8,128)(2,1)S(1)} %collective-permute-done.17.refs_1_), channel_id=1, source_target_pairs={{0,4},{1,5},{2,6},{3,7},{4,0},{5,1},{6,2},{7,3},{8,12},{9,13},{10,... | collective-permute-start | bytes 516104 | tf_op jit(solution)/shard_map/ppermute | solution.py:638
  117.2 2.2 %collective-permute-start.23 = (bf16[152,384]{1,0:T(8,128)(2,1)S(1)}, bf16[152,384]{1,0:T(8,128)(2,1)S(1)}, u32[]{:S(2)}, u32[]{:S(2)}) collective-permute-start(bf16[152,384]{1,0:T(8,128)(2,1)S(1)} %add.111.refs_8_), channel_id=1, source_target_pairs={{0,2},{1,3},{2,0},{3,1},{4,6},{5,7},{6,4},{7,5},{8,10},{9,11},{10,... | collective-permute-start | bytes 350216 | tf_op jit(solution)/shard_map/ppermute | solution.py:638
  117.3 7.5 %collective-permute-start.22 = (bf16[152,384]{1,0:T(8,128)(2,1)S(1)}, bf16[152,384]{1,0:T(8,128)(2,1)S(1)}, u32[]{:S(2)}, u32[]{:S(2)}) collective-permute-start(bf16[152,384]{1,0:T(8,128)(2,1)S(1)} %add.111.refs_8_), channel_id=1, source_target_pairs={{0,4},{1,5},{2,6},{3,7},{4,0},{5,1},{6,2},{7,3},{8,12},{9,13},{10,... | collective-permute-start | bytes 350216 | tf_op jit(solution)/shard_map/ppermute | solution.py:638
  119.0 6.4 %collective-permute-start.24 = (bf16[224,384]{1,0:T(8,128)(2,1)S(1)}, bf16[224,384]{1,0:T(8,128)(2,1)S(1)}, u32[]{:S(2)}, u32[]{:S(2)}) collective-permute-start(bf16[224,384]{1,0:T(8,128)(2,1)S(1)} %collective-permute-done.17.refs_1_), channel_id=1, source_target_pairs={{0,2},{1,3},{2,0},{3,1},{4,6},{5,7},{6,4},{7,5},{8,10},{9,11},{10,... | collective-permute-start | bytes 516104 | tf_op jit(solution)/shard_map/ppermute | solution.py:638
  119.1 6.3 %collective-permute-start.25 = (bf16[224,384]{1,0:T(8,128)(2,1)S(1)}, bf16[224,384]{1,0:T(8,128)(2,1)S(1)}, u32[]{:S(2)}, u32[]{:S(2)}) collective-permute-start(bf16[224,384]{1,0:T(8,128)(2,1)S(1)} %collective-permute-done.19.refs_2_), channel_id=1, source_target_pairs={{0,2},{1,3},{2,0},{3,1},{4,6},{5,7},{6,4},{7,5},{8,10},{9,11},{10,... | collective-permute-start | bytes 516104 | tf_op jit(solution)/shard_map/ppermute | solution.py:638
  124.9 1.6 %collective-permute-start.26 = (bf16[224,384]{1,0:T(8,128)(2,1)S(1)}, bf16[224,384]{1,0:T(8,128)(2,1)S(1)}, u32[]{:S(2)}, u32[]{:S(2)}) collective-permute-start(bf16[224,384]{1,0:T(8,128)(2,1)S(1)} %collective-permute-done.21.refs_3_), channel_id=1, source_target_pairs={{0,2},{1,3},{2,0},{3,1},{4,6},{5,7},{6,4},{7,5},{8,10},{9,11},{10,... | collective-permute-start | bytes 516104 | tf_op jit(solution)/shard_map/ppermute | solution.py:638
  124.9 1.6 %collective-permute-start.27 = (bf16[152,384]{1,0:T(8,128)(2,1)S(1)}, bf16[152,384]{1,0:T(8,128)(2,1)S(1)}, u32[]{:S(2)}, u32[]{:S(2)}) collective-permute-start(bf16[152,384]{1,0:T(8,128)(2,1)S(1)} %collective-permute-done.22.refs_9_), channel_id=1, source_target_pairs={{0,2},{1,3},{2,0},{3,1},{4,6},{5,7},{6,4},{7,5},{8,10},{9,11},{10,... | collective-permute-start | bytes 350216 | tf_op jit(solution)/shard_map/ppermute | solution.py:638
